TPU v7x, 128 devices: a whole 4x4x4 slice. The times are simulated.
128 devices in a mesh: ap: 16 (over z_lo, y, core), sc: 8 (over z_hi, x).
Axes of the slice: x: 4, y: 4, z: 4 (z_hi: 2, z_lo: 2; z = z_hi * 2 + z_lo), core: 2. Of those that a mesh axis runs over, the one named last changes fastest.
Arguments:
- observed_signal: float32 [2, 14, 128, 4, 2048], P(None, None, 'sc', None, 'ap'), may hold values from -6 to 6
- delays: float32 [4, 256, 2048], P(None, 'sc', 'ap'), may hold values from 0 to 64
- sines: float32 [4, 256, 2048], P(None, 'sc', 'ap'), may hold values from -1 to 1
- path_gain_real: float32 [4, 256, 2048], P(None, 'sc', 'ap'), may hold values from -0.078125 to 0.078125
- path_gain_imaginary: float32 [4, 256, 2048], P(None, 'sc', 'ap'), may hold values from -0.078125 to 0.078125
- counts: int32 [256, 2048], P(None, 'ap'), may hold values from 0 to 4
- regularizer: float32 [256], replicated, may hold values from 0.3 to 3
Outputs:
- estimates: float32 [2, 14, 128, 256], P(None, None, 'sc')
All inputs are finite; a program needn't handle non-finite values.
Results may differ from a plain program's by a relative error of at most 0.00038.
Values sent between devices are 32-bit elements; how exact they have to be, the bound alone decides.
No kernel may reach another device: no remote copies, remote signals or barrier semaphores. Data moves between devices by JAX's collectives and lax.ppermute only.
A program may use at most 128 MiB of HBM per device.

v0:
```python
import functools

import jax
import jax.numpy as jnp
import numpy as np
from jax import lax
from jax.experimental import pallas as pl
from jax.experimental.pallas import tpu as pltpu
from jax.sharding import PartitionSpec as P


CORES = 2
OWNERS = 8
NEAR_SLOTS = [((0, 0), 0, 0, 0, 8), ((1, 0), 1, 0, 1, 8), ((0, 1), 2, 0, 2, 8), ((0, 3), 3, 0, 3, 8)]
FAR_SLOTS = [((0, 2), 0, 0, 1, 0), ((1, 1), 2, 0, 2, 8), ((1, 3), 3, 0, 3, 8), ((1, 2), 4, 0, 5, 0)]
Y_CHIPS = 4
Z_CHIPS = 2
X_CHIPS = 4
ANTENNAS = 4
PATHS = 4
FFT_LEN = 512
FIT_POINTS = 4001
ROWS = 16
HALF = 16
SOLVE_STEPS = 60
TOLERANCE = 2e-7


def turn_fit():
    u = 0.25 * np.cos(np.pi * (np.arange(FIT_POINTS) + 0.5) / FIT_POINTS)
    cheb = np.polynomial.chebyshev.Chebyshev
    poly = np.polynomial.Polynomial
    x = u * u
    fits = []
    for values, degree in ((np.sin(2 * np.pi * u) / u, 4), (np.cos(2 * np.pi * u), 5)):
        fits.append([float(c) for c in cheb.fit(x, values, degree, domain=[0, 0.0625]).convert(kind=poly).coef])
    return fits


SIN_FIT, COS_FIT = turn_fit()


def horner(x, coefs):
    total = jnp.full_like(x, coefs[-1])
    for c in coefs[-2::-1]:
        total = total * x + c
    return total


def small_turn(u):
    x = u * u
    return horner(x, COS_FIT), u * horner(x, SIN_FIT)


def doubled(c, s):
    return 1.0 - 2.0 * (s * s), 2.0 * (s * c)


def times(a, b):
    return a[0] * b[0] - a[1] * b[1], a[0] * b[1] + a[1] * b[0]


NT = (((1,), (1,)), ((), ()))


def product(a, b):
    return lax.dot_general(a, b, NT, preferred_element_type=jnp.float32)


def prepare_kernel(slots, pieces, place_ref, tone_ref, *refs):
    tab_refs, count_ref = refs[:pieces], refs[pieces]
    lead, turn, four = refs[-3:]
    per_block = count_ref.shape[0] // OWNERS
    sc_z, sc_x = place_ref[3], place_ref[4]
    centre = tone_ref[0]
    side = tone_ref[1]

    def prepare(slot, block, carry):
        (across, along), angles, a_at, gains, g_at = slot
        angles, gains = tab_refs[angles], tab_refs[gains]
        owner = jnp.abs(sc_z - across) * X_CHIPS + (sc_x - along + X_CHIPS) % X_CHIPS
        inside = pl.ds(pl.multiple_of(block * ROWS, ROWS), ROWS)
        here = pl.ds(pl.multiple_of(owner * per_block + block * ROWS, ROWS), ROWS)
        count = count_ref[here, :]
        for p in range(PATHS):
            delay = angles[a_at + p, inside, :]
            sine = angles[a_at + PATHS + p, inside, :]
            alive = p < count
            re = jnp.where(alive, gains[g_at + p, inside, :], 0.0)
            im = jnp.where(alive, gains[g_at + PATHS + p, inside, :], 0.0)
            tones = small_turn(delay * (side * (0.5 / FFT_LEN)))
            one = doubled(*tones)
            for y in range(Y_CHIPS):
                turn[y, p, 0, here, :], turn[y, p, 1, here, :] = tones
                if y + 1 < Y_CHIPS:
                    tones = times(tones, one)
            four[p, 0, here, :], four[p, 1, here, :] = doubled(*doubled(*one))
            turns = delay * centre
            turns = turns - jnp.round(turns)
            c, s = doubled(*small_turn(0.5 * turns))
            z = times((re, im), (c, -s))
            steer = doubled(*small_turn(0.25 * sine))
            for n in range(ANTENNAS):
                lead[n, p, 0, here, :], lead[n, p, 1, here, :] = z
                if n + 1 < ANTENNAS:
                    z = times(z, steer)
        return carry

    for slot in slots:
        lax.fori_loop(0, per_block // ROWS, functools.partial(prepare, slot), 0)


def in_vmem(x):
    return pltpu.with_memory_space_constraint(x, pltpu.VMEM)


def prepared(place, centre, slots, tables, counts, state=None):
    users, width = counts.shape
    f32 = jnp.float32
    vmem = pl.BlockSpec(memory_space=pltpu.VMEM)
    smem = pl.BlockSpec(memory_space=pltpu.SMEM)
    state = () if state is None else state
    first = 3 + len(tables)
    return pl.pallas_call(
        functools.partial(prepare_kernel, slots, len(tables)),
        in_specs=[smem, smem] + [vmem] * (len(tables) + 1 + len(state)),
        out_specs=[vmem] * 3,
        out_shape=[
            pltpu.VMEM((ANTENNAS, PATHS, 2, users, width), f32),
            pltpu.VMEM((Y_CHIPS, PATHS, 2, users, width), f32),
            pltpu.VMEM((PATHS, 2, users, width), f32),
        ],
        input_output_aliases={first + k: k for k in range(len(state))},
        compiler_params=pltpu.CompilerParams(vmem_limit_bytes=4 << 20),
        name="prepared",
    )(place, centre, *[in_vmem(t) for t in tables], in_vmem(counts), *state)


def tone_kernel(place_ref, y_ref, lead, turn, four, kept_ref, sent_ref, re_a, im_a, lo_a, re_b, im_b, lo_b):
    users, width = four.shape[2:]
    blocks = users // ROWS
    half = ANTENNAS * width
    pairs = Y_CHIPS * Z_CHIPS
    core, chip_z, target_y = place_ref[0], place_ref[1], place_ref[2]

    def build(buffers, block, second):
        with_re, with_im, lo = buffers
        here = pl.ds(block * ROWS, ROWS)
        below = pl.ds(users + block * ROWS, ROWS)
        cs = [(turn[target_y, p, 0, here, :], turn[target_y, p, 1, here, :]) for p in range(PATHS)]
        if second:
            cs = [times(cs[p], (four[p, 0, here, :], four[p, 1, here, :])) for p in range(PATHS)]
        for n in range(ANTENNAS):
            sums = None
            for p in range(PATHS):
                c, s = cs[p]
                re, im = lead[n, p, 0, here, :], lead[n, p, 1, here, :]
                products = (re * c, im * s, im * c, re * s)
                sums = products if sums is None else tuple(a + b for a, b in zip(sums, products))
            a, b, c, d = sums
            columns = slice(n * width, (n + 1) * width)
            for tone, (re, im) in enumerate(((a - b, c + d), (a + b, c - d))):
                for part, (value, top, bottom) in enumerate(((re, with_re, with_im), (im, with_im, with_re))):
                    packed = value.astype(jnp.bfloat16)
                    top[tone, here, columns] = packed
                    bottom[tone, below, columns] = packed
                    rest = (value - packed.astype(jnp.float32)).astype(jnp.bfloat16)
                    lo[tone, here, slice(part * half + n * width, part * half + (n + 1) * width)] = rest

    def multiply(buffers, z):
        with_re, with_im, lo = buffers
        pair = z * Y_CHIPS + target_y
        slot = jnp.abs(z - chip_z)
        plus, minus = pairs + pair, pairs - 1 - pair
        first = jnp.where(core == 0, plus, minus)
        for tone, (at, out_ref) in enumerate(((first, sent_ref), (plus + minus - first, kept_ref))):
            y = y_ref[at]
            y_hi = y.astype(jnp.bfloat16)
            y_lo = (y - y_hi.astype(jnp.float32)).astype(jnp.bfloat16)
            for part, ref in enumerate((with_re, with_im)):
                ref[tone, 2 * users : 2 * users + 2 * HALF] = y_hi[:, part * half : (part + 1) * half]
                ref[tone, 2 * users + 2 * HALF :] = y_lo[:, part * half : (part + 1) * half]
            by_re = product(with_re[tone], with_re[tone, :users])
            by_im = product(with_im[tone], with_im[tone, :users])
            plain, crossed = by_re[:users] + by_im[:users], by_im[users : 2 * users] - by_re[users : 2 * users]
            out_ref[slot, :users, :] = plain + crossed
            filtered = by_re[2 * users :] + by_im[2 * users :]
            rest = product(y_hi, lo[tone])
            out_ref[slot, users:, :] = filtered[: 2 * HALF] + (filtered[2 * HALF :] + rest)

    even, odd = (re_a, im_a, lo_a), (re_b, im_b, lo_b)

    def alone(block, carry):
        build(even, block, False)
        return carry

    lax.fori_loop(0, blocks, alone, 0, unroll=2)
    multiply(even, 0)
    for block in range(blocks):
        build(odd, block, True)
    multiply(odd, 1)


def tone_systems(place, received, state):
    users, _ = state[2].shape[2:]
    wide = received.shape[2]
    f32, bf16 = jnp.float32, jnp.bfloat16
    vmem = pl.BlockSpec(memory_space=pltpu.VMEM)
    smem = pl.BlockSpec(memory_space=pltpu.SMEM)
    channel = pltpu.VMEM((2, 2 * users + 4 * HALF, wide // 2), bf16)
    rest = pltpu.VMEM((2, users, wide), bf16)
    return pl.pallas_call(
        tone_kernel,
        in_specs=[smem] + [vmem] * (1 + len(state)),
        out_specs=[vmem, vmem],
        out_shape=[pltpu.VMEM((Z_CHIPS, users + 2 * HALF, users), f32)] * 2,
        scratch_shapes=[channel, channel, rest] * 2,
        compiler_params=pltpu.CompilerParams(vmem_limit_bytes=16 << 20),
        name="tone_systems",
    )(place, in_vmem(received), *state)


def three_parts(x):
    hi = x.astype(jnp.bfloat16)
    rest = x - hi.astype(jnp.float32)
    mid = rest.astype(jnp.bfloat16)
    return hi, mid, (rest - mid.astype(jnp.float32)).astype(jnp.bfloat16)


def solve_kernel(*refs):
    *part_refs, regularizer_ref, out_ref, system_ref, parts, x_ref, r_ref, p_ref, work = refs
    system_ref[...] = sum(ref[0] for ref in part_refs)
    users = regularizer_ref.shape[1]
    f32 = jnp.float32
    g = system_ref[:users, :]
    flipped = g.T
    row = lax.broadcasted_iota(jnp.int32, (users, users), 0)
    column = lax.broadcasted_iota(jnp.int32, (users, users), 1)
    eye = row == column
    re = 0.5 * (g + flipped)
    im = 0.5 * (g - flipped)
    re = jnp.where(eye, re + regularizer_ref[...], re)
    diagonal = jnp.where(eye, re, 0.0)
    across = lax.rsqrt(jnp.sum(diagonal, 0, keepdims=True))
    down = lax.rsqrt(jnp.sum(diagonal, 1, keepdims=True))
    for k, matrix in enumerate((re, im)):
        for at, part in enumerate(three_parts(matrix * across * down)):
            parts[k, at] = part
    right = system_ref[users:, :] * across

    def together(v):
        total = jnp.sum(v[:HALF] + v[HALF:], 1, keepdims=True)
        return jnp.concatenate([total, total], 0)

    def dot(a, b):
        return jnp.dot(a, b, preferred_element_type=f32)

    rows = 2 * HALF

    def applied(p):
        hi, mid, low = three_parts(p)
        left3 = jnp.concatenate([hi, mid, low], 0)
        left2 = jnp.concatenate([hi, mid], 0)
        result = []
        for k in range(2):
            a = dot(left3, parts[k, 0])
            b = dot(left2, parts[k, 1])
            c = dot(hi, parts[k, 2])
            small = a[2 * rows :] + b[rows:] + c
            result.append(a[:rows] + ((a[rows : 2 * rows] + b[:rows]) + small))
        s, i = result
        return jnp.concatenate([s[:HALF] + i[HALF:], s[HALF:] - i[:HALF]], 0)

    norm = together(right * right)
    goal = norm * (TOLERANCE * TOLERANCE)
    x_ref[...] = jnp.zeros_like(right)
    r_ref[...] = right
    p_ref[...] = right

    def advance(state):
        done, _, rr = state
        for _ in range(2):
            p = p_ref[...]
            q = applied(p)
            pq = together(p * q)
            alpha = jnp.where(pq > 0.0, rr / pq, 0.0)
            x_ref[...] += alpha * p
            r = r_ref[...] - alpha * q
            r_ref[...] = r
            latest = together(r * r)
            p_ref[...] = r + jnp.where(rr > 0.0, latest / rr, 0.0) * p
            rr = latest
        return done + 2, jnp.max(jnp.where(rr <= goal, 0, 1)), rr

    def unfinished(state):
        done, left, _ = state
        return (left > 0) & (done < SOLVE_STEPS)

    _, left, _ = lax.while_loop(unfinished, advance, (0, jnp.max(jnp.where(norm <= goal, 0, 1)), norm))
    out_ref[...] = x_ref[...] * across

    @pl.when(left > 0)
    def _():
        work[0, :users, :] = re
        work[1, :users, :] = -im
        work[0, users:, :] = system_ref[users : users + HALF, :]
        work[1, users:, :] = system_ref[users + HALF :, :]
        lane = lax.broadcasted_iota(jnp.int32, (1, users), 1)

        def eliminate(j, carry):
            a, b = work[0], work[1]
            here = lane == j
            row_re = work[0, pl.ds(j, 1), :]
            row_im = work[1, pl.ds(j, 1), :]
            pivot = 1.0 / jnp.sum(jnp.where(here, row_re, 0.0), 1, keepdims=True)
            col_re = jnp.sum(jnp.where(here, a, 0.0), 1, keepdims=True) * pivot
            col_im = jnp.sum(jnp.where(here, b, 0.0), 1, keepdims=True) * pivot
            work[0] = jnp.where(here, col_re, a - (col_re * row_re - col_im * row_im))
            work[1] = jnp.where(here, col_im, b - (col_re * row_im + col_im * row_re))
            return carry

        lax.fori_loop(0, users, eliminate, 0)
        out_ref[:HALF, :] = work[0, users:, :]
        out_ref[HALF:, :] = work[1, users:, :]


def solved(systems, regularizer):
    _, rows, users = systems[0].shape
    f32 = jnp.float32
    vmem = pl.BlockSpec(memory_space=pltpu.VMEM)
    pair = pltpu.VMEM((2 * HALF, users), f32)
    return pl.pallas_call(
        solve_kernel,
        in_specs=[vmem] * (len(systems) + 1),
        out_specs=vmem,
        out_shape=jax.ShapeDtypeStruct((2 * HALF, users), f32),
        scratch_shapes=[
            pltpu.VMEM((rows, users), f32),
            pltpu.VMEM((2, 3, users, users), jnp.bfloat16),
            pair,
            pair,
            pair,
            pltpu.VMEM((2, users + HALF, users), f32),
        ],
        compiler_params=pltpu.CompilerParams(vmem_limit_bytes=12 << 20),
        name="solved",
    )(*[in_vmem(s) for s in systems], regularizer.reshape(1, users))


def received_rows(observed_signal):
    _, samples, tones, antennas, width = observed_signal.shape
    y = jnp.moveaxis(observed_signal, 2, 0).reshape(tones, 2, samples, antennas * width)
    re, im = y[:, 0], y[:, 1]
    gap = ((0, 0), (0, HALF - samples), (0, 0))
    top = jnp.pad(jnp.concatenate([re, im], 2), gap)
    bottom = jnp.pad(jnp.concatenate([im, -re], 2), gap)
    return jnp.concatenate([top, bottom], 1)


def ap_at(z, y, core):
    return (z * Y_CHIPS + y % Y_CHIPS) * CORES + core


def over_ap(value, dz, dy, dcore):
    spots = [(z, y, c) for z in range(Z_CHIPS) for y in range(Y_CHIPS) for c in range(CORES)]
    pairs = [(ap_at(z, y, c), ap_at(z ^ dz, y + dy, c ^ dcore)) for z, y, c in spots]
    return lax.ppermute(value, "ap", pairs)


def over_sc(value, dz, dx):
    spots = [(z, x) for z in range(2) for x in range(X_CHIPS)]
    pairs = [(z * X_CHIPS + x, (z ^ dz) * X_CHIPS + (x + dx) % X_CHIPS) for z, x in spots]
    return lax.ppermute(value, "sc", pairs)


def gathered_tables(own):
    half = own.shape[0] // 2
    across = over_sc(own, 1, 0)
    up, down = over_sc(own, 0, 1), over_sc(own, 0, -1)
    up_twice, down_twice = over_sc(up[:half], 0, 1), over_sc(down[half:], 0, -1)
    across_up, across_down = over_sc(across, 0, 1), over_sc(across, 0, -1)
    far = over_sc(up_twice, 1, 0), over_sc(down_twice, 1, 0)
    return [own, across, up, down], [up_twice, down_twice, across_up, across_down, *far]


def pack_kernel(*refs):
    *parts, out, sems = refs
    rows = out.shape[0] // len(parts)
    copies = [
        pltpu.make_async_copy(part, out.at[pl.ds(k * rows, rows)], sems.at[k]) for k, part in enumerate(parts)
    ]
    for copy in copies:
        copy.start()
    for copy in copies:
        copy.wait()


def packed_tables(parts):
    rows = sum(part.shape[0] for part in parts)
    vmem = pl.BlockSpec(memory_space=pltpu.VMEM)
    return pl.pallas_call(
        pack_kernel,
        in_specs=[pl.BlockSpec(memory_space=pltpu.HBM)] * len(parts),
        out_specs=vmem,
        out_shape=pltpu.VMEM((rows, *parts[0].shape[1:]), jnp.float32),
        scratch_shapes=[pltpu.SemaphoreType.DMA((len(parts),))],
        compiler_params=pltpu.CompilerParams(vmem_limit_bytes=4 << 20),
        name="packed_tables",
    )(*[pltpu.with_memory_space_constraint(p, pltpu.HBM) for p in parts])


def all_steps(observed_signal, delays, sines, path_gain_real, path_gain_imaginary, counts, regularizer):
    tones = observed_signal.shape[2]
    samples = observed_signal.shape[1]
    users = counts.shape[0]
    sc = lax.axis_index("sc")
    ap = lax.axis_index("ap")
    core = ap % CORES
    chip = ap // CORES
    place = jnp.stack([core, chip // Y_CHIPS, chip % Y_CHIPS, sc // X_CHIPS, sc % X_CHIPS]).astype(jnp.int32)
    first = (sc * tones).astype(jnp.float32)
    side = jnp.where(core == 0, -1.0, 1.0)
    centre = jnp.stack([(first + 0.5 * (tones - 1)) * (1.0 / FFT_LEN), side])
    own = packed_tables([delays, sines, path_gain_real, path_gain_imaginary])
    near, far = gathered_tables(own)
    state = prepared(place, centre, NEAR_SLOTS, near, counts)
    state = prepared(place, centre, FAR_SLOTS, far, counts, state)
    received = received_rows(observed_signal)
    rows = users + 2 * HALF
    top = rows // 2

    def systems(distance, *after):
        where = jnp.stack([core, chip // Y_CHIPS, (chip + distance) % Y_CHIPS]).astype(jnp.int32)
        if after:
            where = lax.optimization_barrier((where, *after))[0]
        kept, sent = tone_systems(where, received, state)
        return kept, over_ap(sent, 0, 0, 1)

    def around(value, step):
        return over_ap(value, 0, step, 0)

    kept, other = systems(2)
    next_kept, next_other = systems(1, kept)
    farthest = kept + other
    up, down = around(farthest[:, :top], 1), around(farthest[:, top:], -1)
    last_kept, last_other = systems(3, farthest)
    upward = next_kept + next_other
    upward = jnp.concatenate([upward[:, :top] + up, upward[:, top:]], 1)
    downward = last_kept + last_other
    downward = jnp.concatenate([downward[:, :top], downward[:, top:] + down], 1)
    up, down = around(upward, 1), around(downward, -1)
    kept, other = systems(0, upward, downward)
    mine = (kept + other) + (up + down)
    own_tone = solved([mine[:1], over_ap(mine[1:], 1, 0, 0)], regularizer)
    length = lax.axis_size("ap")
    every = lax.all_to_all(jnp.broadcast_to(own_tone[None], (length, *own_tone.shape)), "ap", 0, 0, tiled=True)
    every = every.reshape(length // CORES, CORES, 2, HALF, users)[:, :, :, :samples]
    every = jnp.concatenate([every[::-1, 0], every[:, 1]], 0)
    return jnp.transpose(every, (1, 2, 0, 3))


def solution(mesh):
    placed = (
        P(None, None, "sc", None, "ap"),
        P(None, "sc", "ap"),
        P(None, "sc", "ap"),
        P(None, "sc", "ap"),
        P(None, "sc", "ap"),
        P(None, "ap"),
        P(),
    )
    return jax.shard_map(all_steps, mesh=mesh, in_specs=placed, out_specs=P(None, None, "sc", None), check_vma=False)
```

profile of v0, /device:TPU:0, one launch (start us, length us, event | category | flops | bytes accessed | tf_op | source)
XLA Modules:
  0.0 109.3 jit_solution(9794975686017485897)
XLA Ops:
  0.0 1.0 packed_tables.1.refs_0_
  1.0 4.1 %collective-permute-start.4 = (f32[16,32,128]{2,1,0:T(8,128)S(1)}, f32[16,32,128]{2,1,0:T(8,128)}, u32[]{:S(2)}, u32[]{:S(2)}) collective-permute-start(f32[16,32,128]{2,1,0:T(8,128)S(1)} %packed_tables.1.refs_0_), channel_id=1, source_target_pairs={{0,4},{1,5},{2,6},{3,7},{4,0},{5,1},{6,2},{7,3},{8,12},{9,13},{10,... | collective-permute-start | bytes 786440 | tf_op jit(solution)/shard_map/ppermute | solution.py:373
  5.0 1.5 %collective-permute-start = (f32[16,32,128]{2,1,0:T(8,128)S(1)}, f32[16,32,128]{2,1,0:T(8,128)S(1)}, u32[]{:S(2)}, u32[]{:S(2)}) collective-permute-start(f32[16,32,128]{2,1,0:T(8,128)S(1)} %packed_tables.1.refs_0_), channel_id=1, source_target_pairs={{0,1},{1,2},{2,3},{3,0},{4,5},{5,6},{6,7},{7,4},{8,9},{9,10},{10,1... | collective-permute-start | bytes 786440 | tf_op jit(solution)/shard_map/ppermute | solution.py:373
  6.5 1.7 %collective-permute-start.2 = (f32[16,32,128]{2,1,0:T(8,128)S(1)}, f32[16,32,128]{2,1,0:T(8,128)S(1)}, u32[]{:S(2)}, u32[]{:S(2)}) collective-permute-start(f32[16,32,128]{2,1,0:T(8,128)S(1)} %packed_tables.1.refs_0_), channel_id=1, source_target_pairs={{0,3},{1,0},{2,1},{3,2},{4,7},{5,4},{6,5},{7,6},{8,11},{9,8},{10,9... | collective-permute-start | bytes 786440 | tf_op jit(solution)/shard_map/ppermute | solution.py:373
  8.3 1.5 %reshape.10 = f32[16,2,14,512]{3,0,2,1:T(8,128)S(1)} reshape(f32[16,2,14,4,128]{4,3,0,2,1:T(4,128)} %bitcast.31) | data formatting | bytes 1835008 | tf_op jit(solution)/shard_map/reshape | solution.py:352
  9.8 0.1 fusion.1
  9.9 0.3 fusion
  10.2 0.5 copy_bitcast_fusion
  10.8 0.1 pad_add_fusion
  10.9 0.7 pad_add_fusion.4
  11.5 2.5 %collective-permute-done.refs_2_ = f32[16,32,128]{2,1,0:T(8,128)S(1)} collective-permute-done((f32[16,32,128]{2,1,0:T(8,128)S(1)}, f32[16,32,128]{2,1,0:T(8,128)S(1)}, u32[]{:S(2)}, u32[]{:S(2)}) %collective-permute-start) | collective-permute-done | bytes 262176 | tf_op jit(solution)/shard_map/ppermute | solution.py:373
  14.0 0.3 collective-permute-start.1
  14.4 0.0 collective-permute-done.2.refs_3_
  14.4 3.0 %collective-permute-start.3 = (f32[8,32,128]{2,1,0:T(8,128)S(1)}, f32[8,32,128]{2,1,0:T(8,128)}, u32[]{:S(2)}, u32[]{:S(2)}) collective-permute-start(f32[8,32,128]{2,1,0:T(8,128)S(1)} %slice.62), channel_id=1, source_target_pairs={{0,3},{1,0},{2,1},{3,2},{4,7},{5,4},{6,5},{7,6},{8,11},{9,8},{10,9... | collective-permute-start | bytes 393224 | tf_op jit(solution)/shard_map/ppermute | solution.py:373
  17.4 0.2 select_maximum_fusion.1
  17.6 0.0 collective-permute-done.4.refs_1_
  17.6 0.1 collective-permute-start.5
  17.7 3.2 %collective-permute-start.6 = (f32[16,32,128]{2,1,0:T(8,128)}, f32[16,32,128]{2,1,0:T(8,128)S(1)}, u32[]{:S(2)}, u32[]{:S(2)}) collective-permute-start(f32[16,32,128]{2,1,0:T(8,128)} %collective-permute-done.4.refs_1_), channel_id=1, source_target_pairs={{0,3},{1,0},{2,1},{3,2},{4,7},{5,4},{6,5},{7,6},{8,11},{9,8},{10,9... | collective-permute-start | bytes 786440 | tf_op jit(solution)/shard_map/ppermute | solution.py:373
  20.9 0.0 collective-permute-done.1.refs_0_
  20.9 0.4 collective-permute-start.7
  21.3 0.0 collective-permute-done.3.refs_1_
  21.3 3.2 %collective-permute-start.8 = (f32[8,32,128]{2,1,0:T(8,128)}, f32[8,32,128]{2,1,0:T(8,128)}, u32[]{:S(2)}, u32[]{:S(2)}) collective-permute-start(f32[8,32,128]{2,1,0:T(8,128)} %collective-permute-done.3.refs_1_), channel_id=1, source_target_pairs={{0,4},{1,5},{2,6},{3,7},{4,0},{5,1},{6,2},{7,3},{8,12},{9,13},{10,... | collective-permute-start | bytes 393224 | tf_op jit(solution)/shard_map/ppermute | solution.py:373
  24.5 0.1 pad_maximum_fusion.y_ref
  24.6 0.1 stack.67.place_ref
  24.7 0.1 pad_maximum_fusion.3.tone_ref
  24.8 0.0 copy-done
  24.8 2.2 %prepared.2 = (f32[4,4,2,256,128]{4,3,2,1,0:T(8,128)S(1)}, f32[4,4,2,256,128]{4,3,2,1,0:T(8,128)S(1)}, f32[4,2,256,128]{3,2,1,0:T(8,128)S(1)}) custom-call(s32[5]{0:T(128)S(1)} %stack.67.place_ref, f32[2]{0:T(128)S(1)} %pad_maximum_fusion.3.tone_ref, f32[16,32,128]{2,1,0:T(8,128)S(1)} %packed_tables.1.refs_0_, ...), custom_call_target="tpu_custom_call" | custom-call | tf_op jit(solution)/shard_map/prepared/pallas_call | solution.py:124
  27.0 0.7 collective-permute-done.7.refs_4_
  27.7 1.4 %collective-permute-done.8.refs_5_ = f32[8,32,128]{2,1,0:T(8,128)} collective-permute-done((f32[8,32,128]{2,1,0:T(8,128)}, f32[8,32,128]{2,1,0:T(8,128)}, u32[]{:S(2)}, u32[]{:S(2)}) %collective-permute-start.8) | collective-permute-done | bytes 131104 | tf_op jit(solution)/shard_map/ppermute | solution.py:373
  29.1 0.0 collective-permute-done.5.refs_2_
  29.1 0.0 collective-permute-done.6.refs_3_
  29.1 2.3 %prepared.3 = (f32[4,4,2,256,128]{4,3,2,1,0:T(8,128)S(1)}, f32[4,4,2,256,128]{4,3,2,1,0:T(8,128)S(1)}, f32[4,2,256,128]{3,2,1,0:T(8,128)S(1)}) custom-call(s32[5]{0:T(128)S(1)} %stack.67.place_ref, f32[2]{0:T(128)S(1)} %pad_maximum_fusion.3.tone_ref, ...), custom_call_target="tpu_custom_call", output_to_operand_aliasing={{0}: (9, {}), {1}: (10, {}), {2}: (11, {})} | custom-call | tf_op jit(solution)/shard_map/prepared/pallas_call | solution.py:124
  31.5 4.4 %tone_systems.4 = (f32[2,288,256]{2,1,0:T(8,128)S(1)}, f32[2,288,256]{2,1,0:T(8,128)S(1)}) custom-call(s32[3]{0:T(128)S(1)} %copy-done.1, f32[16,32,1024]{2,1,0:T(8,128)S(1)} %pad_maximum_fusion.y_ref, f32[4,4,2,256,128]{4,3,2,1,0:T(8,128)S(1)} %get-tuple-element.25.lead, f32[4,4,2,256,128]{4,3,2,1,0:T(8,128)S(1)} %get-tuple-element.26.turn, ...), custom_call_target="tpu_custom_call" | custom-call | tf_op jit(solution)/shard_map/tone_systems/pallas_call | solution.py:212
  35.9 0.0 collective-permute-start.10
  35.9 4.4 %tone_systems.5 = (f32[2,288,256]{2,1,0:T(8,128)S(1)}, f32[2,288,256]{2,1,0:T(8,128)S(1)}) custom-call(s32[3]{0:T(128)S(1)} %get-tuple-element.29.place_ref, f32[16,32,1024]{2,1,0:T(8,128)S(1)} %pad_maximum_fusion.y_ref, f32[4,4,2,256,128]{4,3,2,1,0:T(8,128)S(1)} %get-tuple-element.25.lead, f32[4,4,2,256,128]{4,3,2,1,0:T(8,128)S(1)} %get-tuple-element.26.turn, ...), custom_call_target="tpu_custom_call" | custom-call | tf_op jit(solution)/shard_map/tone_systems/pallas_call | solution.py:212
  40.2 0.5 collective-permute-start.9
  40.8 0.0 collective-permute-done.10
  40.8 0.1 add.72
  40.9 1.8 %collective-permute-start.11 = (f32[2,144,256]{2,1,0:T(8,128)S(1)}, f32[2,144,256]{2,1,0:T(8,128)S(1)}, u32[]{:S(2)}, u32[]{:S(2)}) collective-permute-start(f32[2,144,256]{2,1,0:T(8,128)S(1)} %get-tuple-element.48), channel_id=1, source_target_pairs={{0,16},{8,24},{16,32},{24,40},{32,48},{40,56},{48,0},{56,8},{64,80... | collective-permute-start | bytes 884744 | tf_op jit(solution)/shard_map/ppermute | solution.py:367
  42.7 4.4 %tone_systems.6 = (f32[2,288,256]{2,1,0:T(8,128)S(1)}, f32[2,288,256]{2,1,0:T(8,128)S(1)}) custom-call(s32[3]{0:T(128)S(1)} %get-tuple-element.33.place_ref, f32[16,32,1024]{2,1,0:T(8,128)S(1)} %pad_maximum_fusion.y_ref, f32[4,4,2,256,128]{4,3,2,1,0:T(8,128)S(1)} %get-tuple-element.25.lead, f32[4,4,2,256,128]{4,3,2,1,0:T(8,128)S(1)} %get-tuple-element.26.turn, ...), custom_call_target="tpu_custom_call" | custom-call | tf_op jit(solution)/shard_map/tone_systems/pallas_call | solution.py:212
  47.1 0.0 collective-permute-start.12
  47.1 1.7 %collective-permute-start.13 = (f32[2,144,256]{2,1,0:T(8,128)S(1)}, f32[2,144,256]{2,1,0:T(8,128)S(1)}, u32[]{:S(2)}, u32[]{:S(2)}) collective-permute-start(f32[2,144,256]{2,1,0:T(8,128)S(1)} %get-tuple-element.47), channel_id=1, source_target_pairs={{0,48},{8,56},{16,0},{24,8},{32,16},{40,24},{48,32},{56,40},{64,11... | collective-permute-start | bytes 884744 | tf_op jit(solution)/shard_map/ppermute | solution.py:367
  48.8 0.0 collective-permute-done.9
  48.9 0.1 add.71
  48.9 2.4 %collective-permute-done.11 = f32[2,144,256]{2,1,0:T(8,128)S(1)} collective-permute-done((f32[2,144,256]{2,1,0:T(8,128)S(1)}, f32[2,144,256]{2,1,0:T(8,128)S(1)}, u32[]{:S(2)}, u32[]{:S(2)}) %collective-permute-start.11) | collective-permute-done | bytes 294944 | tf_op jit(solution)/shard_map/ppermute | solution.py:367
  51.4 0.1 slice_add_fusion.1
  51.5 0.4 collective-permute-start.15
  51.8 0.0 collective-permute-done.12
  51.8 0.1 add.76
  51.9 4.6 %collective-permute-done.13 = f32[2,144,256]{2,1,0:T(8,128)S(1)} collective-permute-done((f32[2,144,256]{2,1,0:T(8,128)S(1)}, f32[2,144,256]{2,1,0:T(8,128)S(1)}, u32[]{:S(2)}, u32[]{:S(2)}) %collective-permute-start.13) | collective-permute-done | bytes 294944 | tf_op jit(solution)/shard_map/ppermute | solution.py:367
  56.5 0.1 fusion.3
  56.6 0.0 copy-start.2
  56.7 4.4 %tone_systems.7 = (f32[2,288,256]{2,1,0:T(8,128)S(1)}, f32[2,288,256]{2,1,0:T(8,128)S(1)}) custom-call(s32[3]{0:T(128)S(1)} %get-tuple-element.36.place_ref, f32[16,32,1024]{2,1,0:T(8,128)S(1)} %pad_maximum_fusion.y_ref, f32[4,4,2,256,128]{4,3,2,1,0:T(8,128)S(1)} %get-tuple-element.25.lead, f32[4,4,2,256,128]{4,3,2,1,0:T(8,128)S(1)} %get-tuple-element.26.turn, ...), custom_call_target="tpu_custom_call" | custom-call | tf_op jit(solution)/shard_map/tone_systems/pallas_call | solution.py:212
  61.0 0.0 collective-permute-start.14
  61.1 2.9 %collective-permute-start.16 = (f32[2,288,256]{2,1,0:T(8,128)S(1)}, f32[2,288,256]{2,1,0:T(8,128)S(1)}, u32[]{:S(2)}, u32[]{:S(2)}) collective-permute-start(f32[2,288,256]{2,1,0:T(8,128)S(1)} %pad_maximum_fusion.2), channel_id=1, source_target_pairs={{0,48},{8,56},{16,0},{24,8},{32,16},{40,24},{48,32},{56,40},{64,11... | collective-permute-start | bytes 1769480 | tf_op jit(solution)/shard_map/ppermute | solution.py:367
  64.0 3.2 %collective-permute-done.15 = f32[2,288,256]{2,1,0:T(8,128)S(1)} collective-permute-done((f32[2,288,256]{2,1,0:T(8,128)S(1)}, f32[2,288,256]{2,1,0:T(8,128)S(1)}, u32[]{:S(2)}, u32[]{:S(2)}) %collective-permute-start.15) | collective-permute-done | bytes 589856 | tf_op jit(solution)/shard_map/ppermute | solution.py:367
  67.2 0.0 collective-permute-done.14
  67.2 10.0 %collective-permute-done.16 = f32[2,288,256]{2,1,0:T(8,128)S(1)} collective-permute-done((f32[2,288,256]{2,1,0:T(8,128)S(1)}, f32[2,288,256]{2,1,0:T(8,128)S(1)}, u32[]{:S(2)}, u32[]{:S(2)}) %collective-permute-start.16) | collective-permute-done | bytes 589856 | tf_op jit(solution)/shard_map/ppermute | solution.py:367
  77.2 0.2 add_add_fusion
  77.4 1.1 collective-permute-start.17
  78.5 7.5 %collective-permute-done.17.refs_1_ = f32[1,288,256]{2,1,0:T(8,128)S(1)} collective-permute-done((f32[1,288,256]{2,1,0:T(8,128)S(1)}, f32[1,288,256]{2,1,0:T(8,128)S(1)}, u32[]{:S(2)}, u32[]{:S(2)}) %collective-permute-start.17) | collective-permute-done | bytes 294944 | tf_op jit(solution)/shard_map/ppermute | solution.py:367
  86.0 5.9 %solved.1 = f32[32,256]{1,0:T(8,128)S(1)} custom-call(f32[1,288,256]{2,1,0:T(8,128)S(1)} %get-tuple-element.44.refs_0_, f32[1,288,256]{2,1,0:T(8,128)S(1)} %collective-permute-done.17.refs_1_, f32[1,256]{1,0:T(1,128)S(1)} %bitcast.29), custom_call_target="tpu_custom_call" | custom-call | tf_op jit(solution)/shard_map/solved/pallas_call | solution.py:332
  92.0 16.1 %all_to_all.5 = f32[16,32,256]{2,1,0:T(8,128)S(1)} all-to-all(f32[16,32,256]{2,1,0:T(8,128)S(1)} %broadcast_in_dim.2), channel_id=1, replica_groups=mesh['ap'=16,'sc'=8] {'ap'}, dimensions={0} | all-to-all | bytes 1048576 | tf_op jit(solution)/shard_map/all_to_all | solution.py:456
  108.2 1.0 copy.15
  (14 shorter events, 0.3 us)
Async XLA Ops:
  1.0 16.6 %collective-permute-start.4 = (f32[16,32,128]{2,1,0:T(8,128)S(1)}, f32[16,32,128]{2,1,0:T(8,128)}, u32[]{:S(2)}, u32[]{:S(2)}) collective-permute-start(f32[16,32,128]{2,1,0:T(8,128)S(1)} %packed_tables.1.refs_0_), channel_id=1, source_target_pairs={{0,4},{1,5},{2,6},{3,7},{4,0},{5,1},{6,2},{7,3},{8,12},{9,13},{10,... | collective-permute-start | bytes 786440 | tf_op jit(solution)/shard_map/ppermute | solution.py:373
  5.0 9.0 %collective-permute-start = (f32[16,32,128]{2,1,0:T(8,128)S(1)}, f32[16,32,128]{2,1,0:T(8,128)S(1)}, u32[]{:S(2)}, u32[]{:S(2)}) collective-permute-start(f32[16,32,128]{2,1,0:T(8,128)S(1)} %packed_tables.1.refs_0_), channel_id=1, source_target_pairs={{0,1},{1,2},{2,3},{3,0},{4,5},{5,6},{6,7},{7,4},{8,9},{9,10},{10,1... | collective-permute-start | bytes 786440 | tf_op jit(solution)/shard_map/ppermute | solution.py:373
  6.5 7.9 %collective-permute-start.2 = (f32[16,32,128]{2,1,0:T(8,128)S(1)}, f32[16,32,128]{2,1,0:T(8,128)S(1)}, u32[]{:S(2)}, u32[]{:S(2)}) collective-permute-start(f32[16,32,128]{2,1,0:T(8,128)S(1)} %packed_tables.1.refs_0_), channel_id=1, source_target_pairs={{0,3},{1,0},{2,1},{3,2},{4,7},{5,4},{6,5},{7,6},{8,11},{9,8},{10,9... | collective-permute-start | bytes 786440 | tf_op jit(solution)/shard_map/ppermute | solution.py:373
  11.5 13.3 %copy-start = (s32[256,128]{1,0:T(8,128)S(1)}, s32[256,128]{1,0:T(8,128)}, u32[]{:S(2)}) copy-start(s32[256,128]{1,0:T(8,128)} %refs_6_.1) | copy-start | bytes 393220
  14.0 6.9 %collective-permute-start.1 = (f32[8,32,128]{2,1,0:T(8,128)S(1)}, f32[8,32,128]{2,1,0:T(8,128)}, u32[]{:S(2)}, u32[]{:S(2)}) collective-permute-start(f32[8,32,128]{2,1,0:T(8,128)S(1)} %slice.61), channel_id=1, source_target_pairs={{0,1},{1,2},{2,3},{3,0},{4,5},{5,6},{6,7},{7,4},{8,9},{9,10},{10,1... | collective-permute-start | bytes 393224 | tf_op jit(solution)/shard_map/ppermute | solution.py:373
  14.4 6.9 %collective-permute-start.3 = (f32[8,32,128]{2,1,0:T(8,128)S(1)}, f32[8,32,128]{2,1,0:T(8,128)}, u32[]{:S(2)}, u32[]{:S(2)}) collective-permute-start(f32[8,32,128]{2,1,0:T(8,128)S(1)} %slice.62), channel_id=1, source_target_pairs={{0,3},{1,0},{2,1},{3,2},{4,7},{5,4},{6,5},{7,6},{8,11},{9,8},{10,9... | collective-permute-start | bytes 393224 | tf_op jit(solution)/shard_map/ppermute | solution.py:373
  17.6 11.5 %collective-permute-start.5 = (f32[16,32,128]{2,1,0:T(8,128)}, f32[16,32,128]{2,1,0:T(8,128)S(1)}, u32[]{:S(2)}, u32[]{:S(2)}) collective-permute-start(f32[16,32,128]{2,1,0:T(8,128)} %collective-permute-done.4.refs_1_), channel_id=1, source_target_pairs={{0,1},{1,2},{2,3},{3,0},{4,5},{5,6},{6,7},{7,4},{8,9},{9,10},{10,1... | collective-permute-start | bytes 786440 | tf_op jit(solution)/shard_map/ppermute | solution.py:373
  17.7 11.4 %collective-permute-start.6 = (f32[16,32,128]{2,1,0:T(8,128)}, f32[16,32,128]{2,1,0:T(8,128)S(1)}, u32[]{:S(2)}, u32[]{:S(2)}) collective-permute-start(f32[16,32,128]{2,1,0:T(8,128)} %collective-permute-done.4.refs_1_), channel_id=1, source_target_pairs={{0,3},{1,0},{2,1},{3,2},{4,7},{5,4},{6,5},{7,6},{8,11},{9,8},{10,9... | collective-permute-start | bytes 786440 | tf_op jit(solution)/shard_map/ppermute | solution.py:373
  20.9 6.8 %collective-permute-start.7 = (f32[8,32,128]{2,1,0:T(8,128)}, f32[8,32,128]{2,1,0:T(8,128)}, u32[]{:S(2)}, u32[]{:S(2)}) collective-permute-start(f32[8,32,128]{2,1,0:T(8,128)} %collective-permute-done.1.refs_0_), channel_id=1, source_target_pairs={{0,4},{1,5},{2,6},{3,7},{4,0},{5,1},{6,2},{7,3},{8,12},{9,13},{10,... | collective-permute-start | bytes 393224 | tf_op jit(solution)/shard_map/ppermute | solution.py:373
  21.3 7.8 %collective-permute-start.8 = (f32[8,32,128]{2,1,0:T(8,128)}, f32[8,32,128]{2,1,0:T(8,128)}, u32[]{:S(2)}, u32[]{:S(2)}) collective-permute-start(f32[8,32,128]{2,1,0:T(8,128)} %collective-permute-done.3.refs_1_), channel_id=1, source_target_pairs={{0,4},{1,5},{2,6},{3,7},{4,0},{5,1},{6,2},{7,3},{8,12},{9,13},{10,... | collective-permute-start | bytes 393224 | tf_op jit(solution)/shard_map/ppermute | solution.py:373
  29.1 2.4 %copy-start.1 = (s32[3]{0:T(128)S(1)}, s32[3]{0:T(128)}, u32[]{:S(2)}) copy-start(s32[3]{0:T(128)} %get-tuple-element.56.place_ref) | copy-start | bytes 40
  35.9 4.9 %collective-permute-start.10 = (f32[2,288,256]{2,1,0:T(8,128)S(1)}, f32[2,288,256]{2,1,0:T(8,128)S(1)}, u32[]{:S(2)}, u32[]{:S(2)}) collective-permute-start(f32[2,288,256]{2,1,0:T(8,128)S(1)} %get-tuple-element.32), channel_id=1, source_target_pairs={{0,8},{8,0},{16,24},{24,16},{32,40},{40,32},{48,56},{56,48},{64,72... | collective-permute-start | bytes 1769480 | tf_op jit(solution)/shard_map/ppermute | solution.py:367
  40.2 8.6 %collective-permute-start.9 = (f32[2,288,256]{2,1,0:T(8,128)S(1)}, f32[2,288,256]{2,1,0:T(8,128)S(1)}, u32[]{:S(2)}, u32[]{:S(2)}) collective-permute-start(f32[2,288,256]{2,1,0:T(8,128)S(1)} %get-tuple-element.31), channel_id=1, source_target_pairs={{0,8},{8,0},{16,24},{24,16},{32,40},{40,32},{48,56},{56,48},{64,72... | collective-permute-start | bytes 1769480 | tf_op jit(solution)/shard_map/ppermute | solution.py:367
  40.9 10.5 %collective-permute-start.11 = (f32[2,144,256]{2,1,0:T(8,128)S(1)}, f32[2,144,256]{2,1,0:T(8,128)S(1)}, u32[]{:S(2)}, u32[]{:S(2)}) collective-permute-start(f32[2,144,256]{2,1,0:T(8,128)S(1)} %get-tuple-element.48), channel_id=1, source_target_pairs={{0,16},{8,24},{16,32},{24,40},{32,48},{40,56},{48,0},{56,8},{64,80... | collective-permute-start | bytes 884744 | tf_op jit(solution)/shard_map/ppermute | solution.py:367
  47.1 4.7 %collective-permute-start.12 = (f32[2,288,256]{2,1,0:T(8,128)S(1)}, f32[2,288,256]{2,1,0:T(8,128)S(1)}, u32[]{:S(2)}, u32[]{:S(2)}) collective-permute-start(f32[2,288,256]{2,1,0:T(8,128)S(1)} %get-tuple-element.35), channel_id=1, source_target_pairs={{0,8},{8,0},{16,24},{24,16},{32,40},{40,32},{48,56},{56,48},{64,72... | collective-permute-start | bytes 1769480 | tf_op jit(solution)/shard_map/ppermute | solution.py:367
  47.1 9.4 %collective-permute-start.13 = (f32[2,144,256]{2,1,0:T(8,128)S(1)}, f32[2,144,256]{2,1,0:T(8,128)S(1)}, u32[]{:S(2)}, u32[]{:S(2)}) collective-permute-start(f32[2,144,256]{2,1,0:T(8,128)S(1)} %get-tuple-element.47), channel_id=1, source_target_pairs={{0,48},{8,56},{16,0},{24,8},{32,16},{40,24},{48,32},{56,40},{64,11... | collective-permute-start | bytes 884744 | tf_op jit(solution)/shard_map/ppermute | solution.py:367
  51.5 15.7 %collective-permute-start.15 = (f32[2,288,256]{2,1,0:T(8,128)S(1)}, f32[2,288,256]{2,1,0:T(8,128)S(1)}, u32[]{:S(2)}, u32[]{:S(2)}) collective-permute-start(f32[2,288,256]{2,1,0:T(8,128)S(1)} %pad_maximum_fusion.1), channel_id=1, source_target_pairs={{0,16},{8,24},{16,32},{24,40},{32,48},{40,56},{48,0},{56,8},{64,80... | collective-permute-start | bytes 1769480 | tf_op jit(solution)/shard_map/ppermute | solution.py:367
  56.6 29.3 %copy-start.2 = (f32[256]{0:T(256)S(1)}, f32[256]{0:T(256)}, u32[]{:S(2)}) copy-start(f32[256]{0:T(256)} %param.13) | copy-start | bytes 3076
  61.0 6.2 %collective-permute-start.14 = (f32[2,288,256]{2,1,0:T(8,128)S(1)}, f32[2,288,256]{2,1,0:T(8,128)S(1)}, u32[]{:S(2)}, u32[]{:S(2)}) collective-permute-start(f32[2,288,256]{2,1,0:T(8,128)S(1)} %get-tuple-element.38), channel_id=1, source_target_pairs={{0,8},{8,0},{16,24},{24,16},{32,40},{40,32},{48,56},{56,48},{64,72... | collective-permute-start | bytes 1769480 | tf_op jit(solution)/shard_map/ppermute | solution.py:367
  61.1 16.1 %collective-permute-start.16 = (f32[2,288,256]{2,1,0:T(8,128)S(1)}, f32[2,288,256]{2,1,0:T(8,128)S(1)}, u32[]{:S(2)}, u32[]{:S(2)}) collective-permute-start(f32[2,288,256]{2,1,0:T(8,128)S(1)} %pad_maximum_fusion.2), channel_id=1, source_target_pairs={{0,48},{8,56},{16,0},{24,8},{32,16},{40,24},{48,32},{56,40},{64,11... | collective-permute-start | bytes 1769480 | tf_op jit(solution)/shard_map/ppermute | solution.py:367
  77.4 8.6 %collective-permute-start.17 = (f32[1,288,256]{2,1,0:T(8,128)S(1)}, f32[1,288,256]{2,1,0:T(8,128)S(1)}, u32[]{:S(2)}, u32[]{:S(2)}) collective-permute-start(f32[1,288,256]{2,1,0:T(8,128)S(1)} %get-tuple-element.43), channel_id=1, source_target_pairs={{0,64},{8,72},{16,80},{24,88},{32,96},{40,104},{48,112},{56,120},{... | collective-permute-start | bytes 884744 | tf_op jit(solution)/shard_map/ppermute | solution.py:367
where the time goes:
time: 110 us; the launch traced here: 109 us
  waiting for transfers between devices  32.3 us (29%)
  Pallas kernels  28.9 us (26%)
  starting transfers between devices  26 us (24%)
  blocking collectives  16.1 us (15%)
  local copies, waits for them, and re-layouts  3.5 us (3%)
  other arithmetic  2.05 us (2%)
    ppermute x9, waiting for transfers between devices, over_ap(): return lax.ppermute(value, 'ap', pairs)  27.7 us
    ppermute x9, starting transfers between devices, over_sc(): return lax.ppermute(value, 'sc', pairs)  17.5 us
    pallas_call x4, Pallas kernels, tone_systems(): pl.pallas_call(tone_kernel, in_specs=[smem] + [vmem] * (1 + len(state)),...  17.5 us
    all_to_all x1, blocking collectives, all_steps(): lax.all_to_all(jnp.broadcast_to(own_tone[None], (length, *own_tone.shape)...  16.1 us
    ppermute x9, starting transfers between devices, over_ap(): return lax.ppermute(value, 'ap', pairs)  8.52 us
    pallas_call x1, Pallas kernels, solved(): pl.pallas_call(solve_kernel, in_specs=[vmem] * (len(systems) + 1), out_sp...  5.94 us
    ppermute x9, waiting for transfers between devices, over_sc(): return lax.ppermute(value, 'sc', pairs)  4.62 us
    pallas_call x2, Pallas kernels, prepared(): pl.pallas_call(functools.partial(prepare_kernel, slots, len(tables)), in_...  4.55 us
  transfers between devices with their start and end apart: 18, of which 8 were waited for; matrix products, arithmetic and copies ran while one was open for 4% of the time, Pallas kernels for 14%

commit v1 on v0

--- a/solution.py
+++ b/solution.py
@@ -12,7 +12,8 @@
 CORES = 2
 OWNERS = 8
 NEAR_SLOTS = [((0, 0), 0, 0, 0, 8), ((1, 0), 1, 0, 1, 8), ((0, 1), 2, 0, 2, 8), ((0, 3), 3, 0, 3, 8)]
-FAR_SLOTS = [((0, 2), 0, 0, 1, 0), ((1, 1), 2, 0, 2, 8), ((1, 3), 3, 0, 3, 8), ((1, 2), 4, 0, 5, 0)]
+MIDDLE_SLOTS = [((0, 2), 0, 0, 1, 0), ((1, 1), 2, 0, 2, 8), ((1, 3), 3, 0, 3, 8)]
+FAR_SLOTS = [((1, 2), 0, 0, 1, 0)]
 Y_CHIPS = 4
 Z_CHIPS = 2
 X_CHIPS = 4
@@ -375,12 +376,13 @@
 
 def gathered_tables(own):
     half = own.shape[0] // 2
+
     across = over_sc(own, 1, 0)
     up, down = over_sc(own, 0, 1), over_sc(own, 0, -1)
+    across_up, across_down = over_sc(across, 0, 1), over_sc(across, 0, -1)
     up_twice, down_twice = over_sc(up[:half], 0, 1), over_sc(down[half:], 0, -1)
-    across_up, across_down = over_sc(across, 0, 1), over_sc(across, 0, -1)
     far = over_sc(up_twice, 1, 0), over_sc(down_twice, 1, 0)
-    return [own, across, up, down], [up_twice, down_twice, across_up, across_down, *far]
+    return [own, across, up, down], [up_twice, down_twice, across_up, across_down], list(far)
 
 
 def pack_kernel(*refs):
@@ -422,8 +424,9 @@
     side = jnp.where(core == 0, -1.0, 1.0)
     centre = jnp.stack([(first + 0.5 * (tones - 1)) * (1.0 / FFT_LEN), side])
     own = packed_tables([delays, sines, path_gain_real, path_gain_imaginary])
-    near, far = gathered_tables(own)
+    near, middle, far = gathered_tables(own)
     state = prepared(place, centre, NEAR_SLOTS, near, counts)
+    state = prepared(place, centre, MIDDLE_SLOTS, middle, counts, state)
     state = prepared(place, centre, FAR_SLOTS, far, counts, state)
     received = received_rows(observed_signal)
     rows = users + 2 * HALF
@@ -440,10 +443,10 @@
         return over_ap(value, 0, step, 0)
 
     kept, other = systems(2)
-    next_kept, next_other = systems(1, kept)
     farthest = kept + other
     up, down = around(farthest[:, :top], 1), around(farthest[:, top:], -1)
-    last_kept, last_other = systems(3, farthest)
+    next_kept, next_other = systems(1, farthest)
+    last_kept, last_other = systems(3, next_kept)
     upward = next_kept + next_other
     upward = jnp.concatenate([upward[:, :top] + up, upward[:, top:]], 1)
     downward = last_kept + last_other
@@ -452,10 +455,15 @@
     kept, other = systems(0, upward, downward)
     mine = (kept + other) + (up + down)
     own_tone = solved([mine[:1], over_ap(mine[1:], 1, 0, 0)], regularizer)
-    length = lax.axis_size("ap")
-    every = lax.all_to_all(jnp.broadcast_to(own_tone[None], (length, *own_tone.shape)), "ap", 0, 0, tiled=True)
-    every = every.reshape(length // CORES, CORES, 2, HALF, users)[:, :, :, :samples]
-    every = jnp.concatenate([every[::-1, 0], every[:, 1]], 0)
+    chips = lax.axis_size("ap") // CORES
+    same = [[chip * CORES + c for chip in range(chips)] for c in range(CORES)]
+    same_core = lax.all_to_all(
+        jnp.broadcast_to(own_tone[None], (chips, *own_tone.shape)), "ap", 0, 0, tiled=True, axis_index_groups=same
+    )
+    other_core = over_ap(same_core, 0, 0, 1)
+    first = jnp.where(core == 0, same_core, other_core)[::-1]
+    second = jnp.where(core == 0, other_core, same_core)
+    every = jnp.concatenate([first, second], 0).reshape(tones, 2, HALF, users)[:, :, :samples]
     return jnp.transpose(every, (1, 2, 0, 3))
 
 

time: 110 us -> 109 us (level)
  blocking collectives: 16.1 us -> 9.83 us
  waiting for transfers between devices: 32.3 us -> 38.1 us
  starting transfers between devices: 26 us -> 24.5 us
    ppermute x9 -> x10, waiting for transfers between devices: 27.7 us -> 35.4 us  [over_ap(): return lax.ppermute(value, 'ap', pairs)]
    all_to_all x1, blocking collectives: 16.1 us -> 9.83 us  [all_steps(): lax.all_to_all(jnp.broadcast_to(own_tone[None], (chips, *own_tone.shape))...]
    ppermute x9, waiting for transfers between devices: 4.62 us -> 2.68 us  [over_sc(): return lax.ppermute(value, 'sc', pairs)]
    ppermute x9 -> x10, starting transfers between devices: 8.52 us -> 6.99 us  [over_ap(): return lax.ppermute(value, 'ap', pairs)]
    pallas_call x2 -> x3, Pallas kernels: 4.55 us -> 5.41 us  [prepared(): pl.pallas_call(functools.partial(prepare_kernel, slots, len(tables)), in_...]
  transfers between devices with their start and end apart: 18 -> 19, of which waited for: 8 -> 9; matrix products, arithmetic and copies ran while one was open for 4% -> 4% of each run, Pallas kernels for 14% -> 4%
where the time goes in v1:
time: 109 us; the launch traced here: 108 us
  waiting for transfers between devices  38.1 us (35%)
  Pallas kernels  29.8 us (27%)
  starting transfers between devices  24.5 us (22%)
  blocking collectives  9.83 us (9%)
  local copies, waits for them, and re-layouts  3.44 us (3%)
  other arithmetic  2.08 us (2%)
    ppermute x10, waiting for transfers between devices, over_ap(): return lax.ppermute(value, 'ap', pairs)  35.4 us
    ppermute x9, starting transfers between devices, over_sc(): return lax.ppermute(value, 'sc', pairs)  17.5 us
    pallas_call x4, Pallas kernels, tone_systems(): pl.pallas_call(tone_kernel, in_specs=[smem] + [vmem] * (1 + len(state)),...  17.5 us
    all_to_all x1, blocking collectives, all_steps(): lax.all_to_all(jnp.broadcast_to(own_tone[None], (chips, *own_tone.shape))...  9.83 us
    ppermute x10, starting transfers between devices, over_ap(): return lax.ppermute(value, 'ap', pairs)  6.99 us
    pallas_call x1, Pallas kernels, solved(): pl.pallas_call(solve_kernel, in_specs=[vmem] * (len(systems) + 1), out_sp...  5.94 us
    pallas_call x3, Pallas kernels, prepared(): pl.pallas_call(functools.partial(prepare_kernel, slots, len(tables)), in_...  5.41 us
    ppermute x9, waiting for transfers between devices, over_sc(): return lax.ppermute(value, 'sc', pairs)  2.68 us
  transfers between devices with their start and end apart: 19, of which 9 were waited for; matrix products, arithmetic and copies ran while one was open for 4% of the time, Pallas kernels for 4%

profile of v1, /device:TPU:0, one launch (start us, length us, event | category | flops | bytes accessed | tf_op | source)
XLA Modules:
  0.0 108.0 jit_solution(9126899339483175254)
XLA Ops:
  0.0 1.0 packed_tables.1.refs_0_
  1.0 4.1 %collective-permute-start.6 = (f32[16,32,128]{2,1,0:T(8,128)S(1)}, f32[16,32,128]{2,1,0:T(8,128)}, u32[]{:S(2)}, u32[]{:S(2)}) collective-permute-start(f32[16,32,128]{2,1,0:T(8,128)S(1)} %packed_tables.1.refs_0_), channel_id=1, source_target_pairs={{0,4},{1,5},{2,6},{3,7},{4,0},{5,1},{6,2},{7,3},{8,12},{9,13},{10,... | collective-permute-start | bytes 786440 | tf_op jit(solution)/shard_map/ppermute | solution.py:374
  5.0 1.5 %collective-permute-start = (f32[16,32,128]{2,1,0:T(8,128)S(1)}, f32[16,32,128]{2,1,0:T(8,128)S(1)}, u32[]{:S(2)}, u32[]{:S(2)}) collective-permute-start(f32[16,32,128]{2,1,0:T(8,128)S(1)} %packed_tables.1.refs_0_), channel_id=1, source_target_pairs={{0,1},{1,2},{2,3},{3,0},{4,5},{5,6},{6,7},{7,4},{8,9},{9,10},{10,1... | collective-permute-start | bytes 786440 | tf_op jit(solution)/shard_map/ppermute | solution.py:374
  6.5 1.7 %collective-permute-start.3 = (f32[16,32,128]{2,1,0:T(8,128)S(1)}, f32[16,32,128]{2,1,0:T(8,128)S(1)}, u32[]{:S(2)}, u32[]{:S(2)}) collective-permute-start(f32[16,32,128]{2,1,0:T(8,128)S(1)} %packed_tables.1.refs_0_), channel_id=1, source_target_pairs={{0,3},{1,0},{2,1},{3,2},{4,7},{5,4},{6,5},{7,6},{8,11},{9,8},{10,9... | collective-permute-start | bytes 786440 | tf_op jit(solution)/shard_map/ppermute | solution.py:374
  8.3 1.5 %reshape.10 = f32[16,2,14,512]{3,0,2,1:T(8,128)S(1)} reshape(f32[16,2,14,4,128]{4,3,0,2,1:T(4,128)} %bitcast.27) | data formatting | bytes 1835008 | tf_op jit(solution)/shard_map/reshape | solution.py:353
  9.8 0.1 fusion.1
  9.9 0.3 fusion
  10.2 0.5 copy_bitcast_fusion
  10.8 0.1 pad_add_fusion
  10.9 0.7 pad_add_fusion.4
  11.5 2.5 %collective-permute-done.refs_2_ = f32[16,32,128]{2,1,0:T(8,128)S(1)} collective-permute-done((f32[16,32,128]{2,1,0:T(8,128)S(1)}, f32[16,32,128]{2,1,0:T(8,128)S(1)}, u32[]{:S(2)}, u32[]{:S(2)}) %collective-permute-start) | collective-permute-done | bytes 262176 | tf_op jit(solution)/shard_map/ppermute | solution.py:374
  14.0 0.3 collective-permute-start.1
  14.4 0.0 collective-permute-done.3.refs_3_
  14.4 3.0 %collective-permute-start.4 = (f32[8,32,128]{2,1,0:T(8,128)S(1)}, f32[8,32,128]{2,1,0:T(8,128)}, u32[]{:S(2)}, u32[]{:S(2)}) collective-permute-start(f32[8,32,128]{2,1,0:T(8,128)S(1)} %slice.55), channel_id=1, source_target_pairs={{0,3},{1,0},{2,1},{3,2},{4,7},{5,4},{6,5},{7,6},{8,11},{9,8},{10,9... | collective-permute-start | bytes 393224 | tf_op jit(solution)/shard_map/ppermute | solution.py:374
  17.4 0.2 select_maximum_fusion.1
  17.6 0.0 collective-permute-done.6.refs_1_
  17.6 0.1 collective-permute-start.7
  17.7 3.2 %collective-permute-start.8 = (f32[16,32,128]{2,1,0:T(8,128)}, f32[16,32,128]{2,1,0:T(8,128)S(1)}, u32[]{:S(2)}, u32[]{:S(2)}) collective-permute-start(f32[16,32,128]{2,1,0:T(8,128)} %collective-permute-done.6.refs_1_), channel_id=1, source_target_pairs={{0,3},{1,0},{2,1},{3,2},{4,7},{5,4},{6,5},{7,6},{8,11},{9,8},{10,9... | collective-permute-start | bytes 786440 | tf_op jit(solution)/shard_map/ppermute | solution.py:374
  20.9 0.0 collective-permute-done.1.refs_0_
  20.9 0.4 collective-permute-start.2
  21.3 0.0 collective-permute-done.4.refs_1_
  21.3 3.2 %collective-permute-start.5 = (f32[8,32,128]{2,1,0:T(8,128)}, f32[8,32,128]{2,1,0:T(8,128)}, u32[]{:S(2)}, u32[]{:S(2)}) collective-permute-start(f32[8,32,128]{2,1,0:T(8,128)} %collective-permute-done.4.refs_1_), channel_id=1, source_target_pairs={{0,4},{1,5},{2,6},{3,7},{4,0},{5,1},{6,2},{7,3},{8,12},{9,13},{10,... | collective-permute-start | bytes 393224 | tf_op jit(solution)/shard_map/ppermute | solution.py:374
  24.5 0.1 pad_maximum_fusion.y_ref
  24.6 0.1 stack.67.place_ref
  24.7 0.1 pad_maximum_fusion.4.tone_ref
  24.8 2.2 %prepared.3 = (f32[4,4,2,256,128]{4,3,2,1,0:T(8,128)S(1)}, f32[4,4,2,256,128]{4,3,2,1,0:T(8,128)S(1)}, f32[4,2,256,128]{3,2,1,0:T(8,128)S(1)}) custom-call(s32[5]{0:T(128)S(1)} %stack.67.place_ref, f32[2]{0:T(128)S(1)} %pad_maximum_fusion.4.tone_ref, f32[16,32,128]{2,1,0:T(8,128)S(1)} %packed_tables.1.refs_0_, ...), custom_call_target="tpu_custom_call" | custom-call | tf_op jit(solution)/shard_map/prepared/pallas_call | solution.py:125
  27.0 0.0 collective-permute-done.7.refs_2_
  27.0 0.0 collective-permute-done.8.refs_3_
  27.0 1.9 %prepared.4 = (f32[4,4,2,256,128]{4,3,2,1,0:T(8,128)S(1)}, f32[4,4,2,256,128]{4,3,2,1,0:T(8,128)S(1)}, f32[4,2,256,128]{3,2,1,0:T(8,128)S(1)}) custom-call(s32[5]{0:T(128)S(1)} %stack.67.place_ref, f32[2]{0:T(128)S(1)} %pad_maximum_fusion.4.tone_ref, ...), custom_call_target="tpu_custom_call", output_to_operand_aliasing={{0}: (7, {}), {1}: (8, {}), {2}: (9, {})} | custom-call | tf_op jit(solution)/shard_map/prepared/pallas_call | solution.py:125
  28.9 0.2 collective-permute-done.5.refs_1_
  29.1 1.3 %prepared.5 = (f32[4,4,2,256,128]{4,3,2,1,0:T(8,128)S(1)}, f32[4,4,2,256,128]{4,3,2,1,0:T(8,128)S(1)}, f32[4,2,256,128]{3,2,1,0:T(8,128)S(1)}) custom-call(s32[5]{0:T(128)S(1)} %stack.67.place_ref, f32[2]{0:T(128)S(1)} %pad_maximum_fusion.4.tone_ref, ...), custom_call_target="tpu_custom_call", output_to_operand_aliasing={{0}: (5, {}), {1}: (6, {}), {2}: (7, {})} | custom-call | tf_op jit(solution)/shard_map/prepared/pallas_call | solution.py:125
  30.4 4.4 %tone_systems.4 = (f32[2,288,256]{2,1,0:T(8,128)S(1)}, f32[2,288,256]{2,1,0:T(8,128)S(1)}) custom-call(s32[3]{0:T(128)S(1)} %copy-done.1, f32[16,32,1024]{2,1,0:T(8,128)S(1)} %pad_maximum_fusion.y_ref, f32[4,4,2,256,128]{4,3,2,1,0:T(8,128)S(1)} %get-tuple-element.31.lead, f32[4,4,2,256,128]{4,3,2,1,0:T(8,128)S(1)} %get-tuple-element.32.turn, ...), custom_call_target="tpu_custom_call" | custom-call | tf_op jit(solution)/shard_map/tone_systems/pallas_call | solution.py:213
  34.8 0.2 collective-permute-start.9
  35.0 2.0 %collective-permute-done.9 = f32[2,288,256]{2,1,0:T(8,128)S(1)} collective-permute-done((f32[2,288,256]{2,1,0:T(8,128)S(1)}, f32[2,288,256]{2,1,0:T(8,128)S(1)}, u32[]{:S(2)}, u32[]{:S(2)}) %collective-permute-start.9) | collective-permute-done | bytes 589856 | tf_op jit(solution)/shard_map/ppermute | solution.py:368
  37.0 0.1 add.71
  37.0 4.4 %tone_systems.5 = (f32[2,288,256]{2,1,0:T(8,128)S(1)}, f32[2,288,256]{2,1,0:T(8,128)S(1)}) custom-call(s32[3]{0:T(128)S(1)} %get-tuple-element.36.place_ref, f32[16,32,1024]{2,1,0:T(8,128)S(1)} %pad_maximum_fusion.y_ref, f32[4,4,2,256,128]{4,3,2,1,0:T(8,128)S(1)} %get-tuple-element.31.lead, f32[4,4,2,256,128]{4,3,2,1,0:T(8,128)S(1)} %get-tuple-element.32.turn, ...), custom_call_target="tpu_custom_call" | custom-call | tf_op jit(solution)/shard_map/tone_systems/pallas_call | solution.py:213
  41.4 4.4 %tone_systems.6 = (f32[2,288,256]{2,1,0:T(8,128)S(1)}, f32[2,288,256]{2,1,0:T(8,128)S(1)}) custom-call(s32[3]{0:T(128)S(1)} %get-tuple-element.39.place_ref, f32[16,32,1024]{2,1,0:T(8,128)S(1)} %pad_maximum_fusion.y_ref, f32[4,4,2,256,128]{4,3,2,1,0:T(8,128)S(1)} %get-tuple-element.31.lead, f32[4,4,2,256,128]{4,3,2,1,0:T(8,128)S(1)} %get-tuple-element.32.turn, ...), custom_call_target="tpu_custom_call" | custom-call | tf_op jit(solution)/shard_map/tone_systems/pallas_call | solution.py:213
  45.8 0.1 collective-permute-start.10
  45.9 0.4 collective-permute-start.12
  46.4 3.1 %collective-permute-start.13 = (f32[2,144,256]{2,1,0:T(8,128)S(1)}, f32[2,144,256]{2,1,0:T(8,128)S(1)}, u32[]{:S(2)}, u32[]{:S(2)}) collective-permute-start(f32[2,144,256]{2,1,0:T(8,128)S(1)} %get-tuple-element.53), channel_id=1, source_target_pairs={{0,48},{8,56},{16,0},{24,8},{32,16},{40,24},{48,32},{56,40},{64,11... | collective-permute-start | bytes 884744 | tf_op jit(solution)/shard_map/ppermute | solution.py:368
  49.5 0.0 collective-permute-start.11
  49.5 0.0 collective-permute-done.10
  49.5 0.1 add.72
  49.6 0.1 add.76
  49.6 6.4 %collective-permute-done.13 = f32[2,144,256]{2,1,0:T(8,128)S(1)} collective-permute-done((f32[2,144,256]{2,1,0:T(8,128)S(1)}, f32[2,144,256]{2,1,0:T(8,128)S(1)}, u32[]{:S(2)}, u32[]{:S(2)}) %collective-permute-start.13) | collective-permute-done | bytes 294944 | tf_op jit(solution)/shard_map/ppermute | solution.py:368
  56.0 0.1 fusion.3
  56.1 3.3 %collective-permute-done.11 = f32[2,144,256]{2,1,0:T(8,128)S(1)} collective-permute-done((f32[2,144,256]{2,1,0:T(8,128)S(1)}, f32[2,144,256]{2,1,0:T(8,128)S(1)}, u32[]{:S(2)}, u32[]{:S(2)}) %collective-permute-start.11) | collective-permute-done | bytes 294944 | tf_op jit(solution)/shard_map/ppermute | solution.py:368
  59.4 0.1 slice_add_fusion.1
  59.5 0.0 copy-start.2
  59.6 4.4 %tone_systems.7 = (f32[2,288,256]{2,1,0:T(8,128)S(1)}, f32[2,288,256]{2,1,0:T(8,128)S(1)}) custom-call(s32[3]{0:T(128)S(1)} %get-tuple-element.42.place_ref, f32[16,32,1024]{2,1,0:T(8,128)S(1)} %pad_maximum_fusion.y_ref, f32[4,4,2,256,128]{4,3,2,1,0:T(8,128)S(1)} %get-tuple-element.31.lead, f32[4,4,2,256,128]{4,3,2,1,0:T(8,128)S(1)} %get-tuple-element.32.turn, ...), custom_call_target="tpu_custom_call" | custom-call | tf_op jit(solution)/shard_map/tone_systems/pallas_call | solution.py:213
  63.9 0.0 collective-permute-start.14
  63.9 0.5 collective-permute-start.16
  64.4 1.6 %collective-permute-start.15 = (f32[2,288,256]{2,1,0:T(8,128)S(1)}, f32[2,288,256]{2,1,0:T(8,128)S(1)}, u32[]{:S(2)}, u32[]{:S(2)}) collective-permute-start(f32[2,288,256]{2,1,0:T(8,128)S(1)} %pad_maximum_fusion.1), channel_id=1, source_target_pairs={{0,16},{8,24},{16,32},{24,40},{32,48},{40,56},{48,0},{56,8},{64,80... | collective-permute-start | bytes 1769480 | tf_op jit(solution)/shard_map/ppermute | solution.py:368
  66.0 0.0 collective-permute-done.14
  66.0 13.6 %collective-permute-done.16 = f32[2,288,256]{2,1,0:T(8,128)S(1)} collective-permute-done((f32[2,288,256]{2,1,0:T(8,128)S(1)}, f32[2,288,256]{2,1,0:T(8,128)S(1)}, u32[]{:S(2)}, u32[]{:S(2)}) %collective-permute-start.16) | collective-permute-done | bytes 589856 | tf_op jit(solution)/shard_map/ppermute | solution.py:368
  79.7 1.3 %collective-permute-done.15 = f32[2,288,256]{2,1,0:T(8,128)S(1)} collective-permute-done((f32[2,288,256]{2,1,0:T(8,128)S(1)}, f32[2,288,256]{2,1,0:T(8,128)S(1)}, u32[]{:S(2)}, u32[]{:S(2)}) %collective-permute-start.15) | collective-permute-done | bytes 589856 | tf_op jit(solution)/shard_map/ppermute | solution.py:368
  81.0 0.2 add_add_fusion
  81.2 1.1 %collective-permute-start.17 = (f32[1,288,256]{2,1,0:T(8,128)S(1)}, f32[1,288,256]{2,1,0:T(8,128)S(1)}, u32[]{:S(2)}, u32[]{:S(2)}) collective-permute-start(f32[1,288,256]{2,1,0:T(8,128)S(1)} %get-tuple-element.49), channel_id=1, source_target_pairs={{0,64},{8,72},{16,80},{24,88},{32,96},{40,104},{48,112},{56,120},{... | collective-permute-start | bytes 884744 | tf_op jit(solution)/shard_map/ppermute | solution.py:368
  82.3 7.2 %collective-permute-done.17.refs_1_ = f32[1,288,256]{2,1,0:T(8,128)S(1)} collective-permute-done((f32[1,288,256]{2,1,0:T(8,128)S(1)}, f32[1,288,256]{2,1,0:T(8,128)S(1)}, u32[]{:S(2)}, u32[]{:S(2)}) %collective-permute-start.17) | collective-permute-done | bytes 294944 | tf_op jit(solution)/shard_map/ppermute | solution.py:368
  89.5 5.9 %solved.1 = f32[32,256]{1,0:T(8,128)S(1)} custom-call(f32[1,288,256]{2,1,0:T(8,128)S(1)} %get-tuple-element.50.refs_0_, f32[1,288,256]{2,1,0:T(8,128)S(1)} %collective-permute-done.17.refs_1_, f32[1,256]{1,0:T(1,128)S(1)} %bitcast.25), custom_call_target="tpu_custom_call" | custom-call | tf_op jit(solution)/shard_map/solved/pallas_call | solution.py:333
  95.5 9.8 %all_to_all.5 = f32[8,32,256]{2,1,0:T(8,128)S(1)} all-to-all(f32[8,32,256]{2,1,0:T(8,128)S(1)} %broadcast_in_dim.2), channel_id=1, replica_groups={{0,16,32,48,64,80,96,112},{8,24,40,56,72,88,104,120},{1,17,33,49,65,81,..., dimensions={0} | all-to-all | bytes 524288 | tf_op jit(solution)/shard_map/all_to_all | solution.py:460
  105.3 0.0 collective-permute-start.18
  105.3 1.5 %collective-permute-done.18 = f32[8,32,256]{2,1,0:T(8,128)S(1)} collective-permute-done((f32[8,32,256]{2,1,0:T(8,128)S(1)}, f32[8,32,256]{2,1,0:T(8,128)S(1)}, u32[]{:S(2)}, u32[]{:S(2)}) %collective-permute-start.18) | collective-permute-done | bytes 262176 | tf_op jit(solution)/shard_map/ppermute | solution.py:368
  107.0 1.0 copy.28
  (17 shorter events, 0.3 us)
Async XLA Ops:
  1.0 16.6 %collective-permute-start.6 = (f32[16,32,128]{2,1,0:T(8,128)S(1)}, f32[16,32,128]{2,1,0:T(8,128)}, u32[]{:S(2)}, u32[]{:S(2)}) collective-permute-start(f32[16,32,128]{2,1,0:T(8,128)S(1)} %packed_tables.1.refs_0_), channel_id=1, source_target_pairs={{0,4},{1,5},{2,6},{3,7},{4,0},{5,1},{6,2},{7,3},{8,12},{9,13},{10,... | collective-permute-start | bytes 786440 | tf_op jit(solution)/shard_map/ppermute | solution.py:374
  5.0 9.0 %collective-permute-start = (f32[16,32,128]{2,1,0:T(8,128)S(1)}, f32[16,32,128]{2,1,0:T(8,128)S(1)}, u32[]{:S(2)}, u32[]{:S(2)}) collective-permute-start(f32[16,32,128]{2,1,0:T(8,128)S(1)} %packed_tables.1.refs_0_), channel_id=1, source_target_pairs={{0,1},{1,2},{2,3},{3,0},{4,5},{5,6},{6,7},{7,4},{8,9},{9,10},{10,1... | collective-permute-start | bytes 786440 | tf_op jit(solution)/shard_map/ppermute | solution.py:374
  6.5 7.9 %collective-permute-start.3 = (f32[16,32,128]{2,1,0:T(8,128)S(1)}, f32[16,32,128]{2,1,0:T(8,128)S(1)}, u32[]{:S(2)}, u32[]{:S(2)}) collective-permute-start(f32[16,32,128]{2,1,0:T(8,128)S(1)} %packed_tables.1.refs_0_), channel_id=1, source_target_pairs={{0,3},{1,0},{2,1},{3,2},{4,7},{5,4},{6,5},{7,6},{8,11},{9,8},{10,9... | collective-permute-start | bytes 786440 | tf_op jit(solution)/shard_map/ppermute | solution.py:374
  11.5 13.3 %copy-start = (s32[256,128]{1,0:T(8,128)S(1)}, s32[256,128]{1,0:T(8,128)}, u32[]{:S(2)}) copy-start(s32[256,128]{1,0:T(8,128)} %refs_2_.3) | copy-start | bytes 393220
  14.0 6.9 %collective-permute-start.1 = (f32[8,32,128]{2,1,0:T(8,128)S(1)}, f32[8,32,128]{2,1,0:T(8,128)}, u32[]{:S(2)}, u32[]{:S(2)}) collective-permute-start(f32[8,32,128]{2,1,0:T(8,128)S(1)} %slice.54), channel_id=1, source_target_pairs={{0,1},{1,2},{2,3},{3,0},{4,5},{5,6},{6,7},{7,4},{8,9},{9,10},{10,1... | collective-permute-start | bytes 393224 | tf_op jit(solution)/shard_map/ppermute | solution.py:374
  14.4 6.9 %collective-permute-start.4 = (f32[8,32,128]{2,1,0:T(8,128)S(1)}, f32[8,32,128]{2,1,0:T(8,128)}, u32[]{:S(2)}, u32[]{:S(2)}) collective-permute-start(f32[8,32,128]{2,1,0:T(8,128)S(1)} %slice.55), channel_id=1, source_target_pairs={{0,3},{1,0},{2,1},{3,2},{4,7},{5,4},{6,5},{7,6},{8,11},{9,8},{10,9... | collective-permute-start | bytes 393224 | tf_op jit(solution)/shard_map/ppermute | solution.py:374
  17.6 9.4 %collective-permute-start.7 = (f32[16,32,128]{2,1,0:T(8,128)}, f32[16,32,128]{2,1,0:T(8,128)S(1)}, u32[]{:S(2)}, u32[]{:S(2)}) collective-permute-start(f32[16,32,128]{2,1,0:T(8,128)} %collective-permute-done.6.refs_1_), channel_id=1, source_target_pairs={{0,1},{1,2},{2,3},{3,0},{4,5},{5,6},{6,7},{7,4},{8,9},{9,10},{10,1... | collective-permute-start | bytes 786440 | tf_op jit(solution)/shard_map/ppermute | solution.py:374
  17.7 9.3 %collective-permute-start.8 = (f32[16,32,128]{2,1,0:T(8,128)}, f32[16,32,128]{2,1,0:T(8,128)S(1)}, u32[]{:S(2)}, u32[]{:S(2)}) collective-permute-start(f32[16,32,128]{2,1,0:T(8,128)} %collective-permute-done.6.refs_1_), channel_id=1, source_target_pairs={{0,3},{1,0},{2,1},{3,2},{4,7},{5,4},{6,5},{7,6},{8,11},{9,8},{10,9... | collective-permute-start | bytes 786440 | tf_op jit(solution)/shard_map/ppermute | solution.py:374
  20.9 8.0 %collective-permute-start.2 = (f32[8,32,128]{2,1,0:T(8,128)}, f32[8,32,128]{2,1,0:T(8,128)}, u32[]{:S(2)}, u32[]{:S(2)}) collective-permute-start(f32[8,32,128]{2,1,0:T(8,128)} %collective-permute-done.1.refs_0_), channel_id=1, source_target_pairs={{0,4},{1,5},{2,6},{3,7},{4,0},{5,1},{6,2},{7,3},{8,12},{9,13},{10,... | collective-permute-start | bytes 393224 | tf_op jit(solution)/shard_map/ppermute | solution.py:374
  21.3 7.8 %collective-permute-start.5 = (f32[8,32,128]{2,1,0:T(8,128)}, f32[8,32,128]{2,1,0:T(8,128)}, u32[]{:S(2)}, u32[]{:S(2)}) collective-permute-start(f32[8,32,128]{2,1,0:T(8,128)} %collective-permute-done.4.refs_1_), channel_id=1, source_target_pairs={{0,4},{1,5},{2,6},{3,7},{4,0},{5,1},{6,2},{7,3},{8,12},{9,13},{10,... | collective-permute-start | bytes 393224 | tf_op jit(solution)/shard_map/ppermute | solution.py:374
  29.1 1.3 %copy-start.1 = (s32[3]{0:T(128)S(1)}, s32[3]{0:T(128)}, u32[]{:S(2)}) copy-start(s32[3]{0:T(128)} %get-tuple-element.62.place_ref) | copy-start | bytes 40
  34.8 2.2 %collective-permute-start.9 = (f32[2,288,256]{2,1,0:T(8,128)S(1)}, f32[2,288,256]{2,1,0:T(8,128)S(1)}, u32[]{:S(2)}, u32[]{:S(2)}) collective-permute-start(f32[2,288,256]{2,1,0:T(8,128)S(1)} %get-tuple-element.35), channel_id=1, source_target_pairs={{0,8},{8,0},{16,24},{24,16},{32,40},{40,32},{48,56},{56,48},{64,72... | collective-permute-start | bytes 1769480 | tf_op jit(solution)/shard_map/ppermute | solution.py:368
  45.8 3.7 %collective-permute-start.10 = (f32[2,288,256]{2,1,0:T(8,128)S(1)}, f32[2,288,256]{2,1,0:T(8,128)S(1)}, u32[]{:S(2)}, u32[]{:S(2)}) collective-permute-start(f32[2,288,256]{2,1,0:T(8,128)S(1)} %get-tuple-element.38), channel_id=1, source_target_pairs={{0,8},{8,0},{16,24},{24,16},{32,40},{40,32},{48,56},{56,48},{64,72... | collective-permute-start | bytes 1769480 | tf_op jit(solution)/shard_map/ppermute | solution.py:368
  45.9 3.6 %collective-permute-start.12 = (f32[2,288,256]{2,1,0:T(8,128)S(1)}, f32[2,288,256]{2,1,0:T(8,128)S(1)}, u32[]{:S(2)}, u32[]{:S(2)}) collective-permute-start(f32[2,288,256]{2,1,0:T(8,128)S(1)} %get-tuple-element.41), channel_id=1, source_target_pairs={{0,8},{8,0},{16,24},{24,16},{32,40},{40,32},{48,56},{56,48},{64,72... | collective-permute-start | bytes 1769480 | tf_op jit(solution)/shard_map/ppermute | solution.py:368
  46.4 9.6 %collective-permute-start.13 = (f32[2,144,256]{2,1,0:T(8,128)S(1)}, f32[2,144,256]{2,1,0:T(8,128)S(1)}, u32[]{:S(2)}, u32[]{:S(2)}) collective-permute-start(f32[2,144,256]{2,1,0:T(8,128)S(1)} %get-tuple-element.53), channel_id=1, source_target_pairs={{0,48},{8,56},{16,0},{24,8},{32,16},{40,24},{48,32},{56,40},{64,11... | collective-permute-start | bytes 884744 | tf_op jit(solution)/shard_map/ppermute | solution.py:368
  49.5 10.0 %collective-permute-start.11 = (f32[2,144,256]{2,1,0:T(8,128)S(1)}, f32[2,144,256]{2,1,0:T(8,128)S(1)}, u32[]{:S(2)}, u32[]{:S(2)}) collective-permute-start(f32[2,144,256]{2,1,0:T(8,128)S(1)} %get-tuple-element.54), channel_id=1, source_target_pairs={{0,16},{8,24},{16,32},{24,40},{32,48},{40,56},{48,0},{56,8},{64,80... | collective-permute-start | bytes 884744 | tf_op jit(solution)/shard_map/ppermute | solution.py:368
  59.5 30.0 %copy-start.2 = (f32[256]{0:T(256)S(1)}, f32[256]{0:T(256)}, u32[]{:S(2)}) copy-start(f32[256]{0:T(256)} %param.13) | copy-start | bytes 3076
  63.9 2.1 %collective-permute-start.14 = (f32[2,288,256]{2,1,0:T(8,128)S(1)}, f32[2,288,256]{2,1,0:T(8,128)S(1)}, u32[]{:S(2)}, u32[]{:S(2)}) collective-permute-start(f32[2,288,256]{2,1,0:T(8,128)S(1)} %get-tuple-element.44), channel_id=1, source_target_pairs={{0,8},{8,0},{16,24},{24,16},{32,40},{40,32},{48,56},{56,48},{64,72... | collective-permute-start | bytes 1769480 | tf_op jit(solution)/shard_map/ppermute | solution.py:368
  63.9 15.7 %collective-permute-start.16 = (f32[2,288,256]{2,1,0:T(8,128)S(1)}, f32[2,288,256]{2,1,0:T(8,128)S(1)}, u32[]{:S(2)}, u32[]{:S(2)}) collective-permute-start(f32[2,288,256]{2,1,0:T(8,128)S(1)} %pad_maximum_fusion.2), channel_id=1, source_target_pairs={{0,48},{8,56},{16,0},{24,8},{32,16},{40,24},{48,32},{56,40},{64,11... | collective-permute-start | bytes 1769480 | tf_op jit(solution)/shard_map/ppermute | solution.py:368
  64.4 16.6 %collective-permute-start.15 = (f32[2,288,256]{2,1,0:T(8,128)S(1)}, f32[2,288,256]{2,1,0:T(8,128)S(1)}, u32[]{:S(2)}, u32[]{:S(2)}) collective-permute-start(f32[2,288,256]{2,1,0:T(8,128)S(1)} %pad_maximum_fusion.1), channel_id=1, source_target_pairs={{0,16},{8,24},{16,32},{24,40},{32,48},{40,56},{48,0},{56,8},{64,80... | collective-permute-start | bytes 1769480 | tf_op jit(solution)/shard_map/ppermute | solution.py:368
  81.2 8.3 %collective-permute-start.17 = (f32[1,288,256]{2,1,0:T(8,128)S(1)}, f32[1,288,256]{2,1,0:T(8,128)S(1)}, u32[]{:S(2)}, u32[]{:S(2)}) collective-permute-start(f32[1,288,256]{2,1,0:T(8,128)S(1)} %get-tuple-element.49), channel_id=1, source_target_pairs={{0,64},{8,72},{16,80},{24,88},{32,96},{40,104},{48,112},{56,120},{... | collective-permute-start | bytes 884744 | tf_op jit(solution)/shard_map/ppermute | solution.py:368
  105.3 1.5 %collective-permute-start.18 = (f32[8,32,256]{2,1,0:T(8,128)S(1)}, f32[8,32,256]{2,1,0:T(8,128)S(1)}, u32[]{:S(2)}, u32[]{:S(2)}) collective-permute-start(f32[8,32,256]{2,1,0:T(8,128)S(1)} %all_to_all.5), channel_id=1, source_target_pairs={{0,8},{8,0},{16,24},{24,16},{32,40},{40,32},{48,56},{56,48},{64,72... | collective-permute-start | bytes 786440 | tf_op jit(solution)/shard_map/ppermute | solution.py:368

commit v2 on v1

--- a/solution.py
+++ b/solution.py
@@ -12,8 +12,7 @@
 CORES = 2
 OWNERS = 8
 NEAR_SLOTS = [((0, 0), 0, 0, 0, 8), ((1, 0), 1, 0, 1, 8), ((0, 1), 2, 0, 2, 8), ((0, 3), 3, 0, 3, 8)]
-MIDDLE_SLOTS = [((0, 2), 0, 0, 1, 0), ((1, 1), 2, 0, 2, 8), ((1, 3), 3, 0, 3, 8)]
-FAR_SLOTS = [((1, 2), 0, 0, 1, 0)]
+FAR_SLOTS = [((0, 2), 0, 0, 0, 8), ((1, 1), 1, 0, 1, 8), ((1, 3), 2, 0, 2, 8), ((1, 2), 3, 0, 3, 8)]
 Y_CHIPS = 4
 Z_CHIPS = 2
 X_CHIPS = 4
@@ -24,7 +23,7 @@
 ROWS = 16
 HALF = 16
 SOLVE_STEPS = 60
-TOLERANCE = 2e-7
+TOLERANCE = 1e-6
 
 
 def turn_fit():
@@ -368,21 +367,37 @@
     return lax.ppermute(value, "ap", pairs)
 
 
+def over_ap_by_core(value):
+    spots = [(z, y, c) for z in range(Z_CHIPS) for y in range(Y_CHIPS) for c in range(CORES)]
+    pairs = [(ap_at(z, y, c), ap_at(z, y + (1 if c == 0 else -1), c)) for z, y, c in spots]
+    return lax.ppermute(value, "ap", pairs)
+
+
 def over_sc(value, dz, dx):
     spots = [(z, x) for z in range(2) for x in range(X_CHIPS)]
     pairs = [(z * X_CHIPS + x, (z ^ dz) * X_CHIPS + (x + dx) % X_CHIPS) for z, x in spots]
     return lax.ppermute(value, "sc", pairs)
 
 
-def gathered_tables(own):
-    half = own.shape[0] // 2
-
+def over_sc_by_core(value):
+    owners = Z_CHIPS * X_CHIPS
+    pairs = []
+    for ap in range(Z_CHIPS * Y_CHIPS * CORES):
+        step = 1 if ap % CORES == 0 else -1
+        for z in range(Z_CHIPS):
+            for x in range(X_CHIPS):
+                at = ap * owners + z * X_CHIPS
+                pairs.append((at + x, at + (x + step) % X_CHIPS))
+    return lax.ppermute(value, ("ap", "sc"), pairs)
+
+
+def gathered_tables(own, core):
     across = over_sc(own, 1, 0)
     up, down = over_sc(own, 0, 1), over_sc(own, 0, -1)
+    opposite = over_sc_by_core(jnp.where(core == 0, up, down))
     across_up, across_down = over_sc(across, 0, 1), over_sc(across, 0, -1)
-    up_twice, down_twice = over_sc(up[:half], 0, 1), over_sc(down[half:], 0, -1)
-    far = over_sc(up_twice, 1, 0), over_sc(down_twice, 1, 0)
-    return [own, across, up, down], [up_twice, down_twice, across_up, across_down], list(far)
+    far = over_sc(opposite, 1, 0)
+    return [own, across, up, down], [opposite, across_up, across_down, far]
 
 
 def pack_kernel(*refs):
@@ -424,13 +439,10 @@
     side = jnp.where(core == 0, -1.0, 1.0)
     centre = jnp.stack([(first + 0.5 * (tones - 1)) * (1.0 / FFT_LEN), side])
     own = packed_tables([delays, sines, path_gain_real, path_gain_imaginary])
-    near, middle, far = gathered_tables(own)
+    near, far = gathered_tables(own, core)
     state = prepared(place, centre, NEAR_SLOTS, near, counts)
-    state = prepared(place, centre, MIDDLE_SLOTS, middle, counts, state)
     state = prepared(place, centre, FAR_SLOTS, far, counts, state)
     received = received_rows(observed_signal)
-    rows = users + 2 * HALF
-    top = rows // 2
 
     def systems(distance, *after):
         where = jnp.stack([core, chip // Y_CHIPS, (chip + distance) % Y_CHIPS]).astype(jnp.int32)
@@ -443,14 +455,12 @@
         return over_ap(value, 0, step, 0)
 
     kept, other = systems(2)
+    next_kept, next_other = systems(1, kept)
     farthest = kept + other
-    up, down = around(farthest[:, :top], 1), around(farthest[:, top:], -1)
-    next_kept, next_other = systems(1, farthest)
-    last_kept, last_other = systems(3, next_kept)
-    upward = next_kept + next_other
-    upward = jnp.concatenate([upward[:, :top] + up, upward[:, top:]], 1)
-    downward = last_kept + last_other
-    downward = jnp.concatenate([downward[:, :top], downward[:, top:] + down], 1)
+    passing = over_ap_by_core(farthest)
+    last_kept, last_other = systems(3, farthest)
+    upward = next_kept + next_other + jnp.where(core == 0, passing, 0.0)
+    downward = last_kept + last_other + jnp.where(core == 0, 0.0, passing)
     up, down = around(upward, 1), around(downward, -1)
     kept, other = systems(0, upward, downward)
     mine = (kept + other) + (up + down)

time: 109 us -> 111 us (1.018)
  waiting for transfers between devices: 38.1 us -> 45.3 us
  starting transfers between devices: 24.5 us -> 19 us
  blocking collectives: 9.83 us -> 12.9 us
  Pallas kernels: 29.8 us -> 27.3 us
    ppermute x0 -> x2, waiting for transfers between devices: none -> 13.9 us  [the longest x1 9.16 us: over_ap_by_core(): return lax.ppermute(value, 'ap', pairs)]
    ppermute x10 -> x8, waiting for transfers between devices: 35.4 us -> 23 us  [over_ap(): return lax.ppermute(value, 'ap', pairs)]
    ppermute x9 -> x6, starting transfers between devices: 17.5 us -> 10.7 us  [over_sc(): return lax.ppermute(value, 'sc', pairs)]
    ppermute x9 -> x6, waiting for transfers between devices: 2.68 us -> 8.45 us  [over_sc(): return lax.ppermute(value, 'sc', pairs)]
    ppermute x0 -> x2, starting transfers between devices: none -> 3.19 us  [the longest x1 1.64 us: over_ap_by_core(): return lax.ppermute(value, 'ap', pairs)]
    all_to_all x1, blocking collectives: 9.83 us -> 12.9 us  [all_steps(): lax.all_to_all(jnp.broadcast_to(own_tone[None], (chips, *own_tone.shape))...]
    ppermute x10 -> x8, starting transfers between devices: 6.99 us -> 5.16 us  [over_ap(): return lax.ppermute(value, 'ap', pairs)]
    pallas_call x1, Pallas kernels: 5.94 us -> 4.57 us  [solved(): pl.pallas_call(solve_kernel, in_specs=[vmem] * (len(systems) + 1), out_sp...]
  transfers between devices with their start and end apart: 19 -> 16, of which waited for: 9 -> 9; matrix products, arithmetic and copies ran while one was open for 4% -> 3% of each run, Pallas kernels for 4% -> 10%
where the time goes in v2:
time: 111 us; the launch traced here: 110 us
  waiting for transfers between devices  45.3 us (41%)
  Pallas kernels  27.3 us (25%)
  starting transfers between devices  19 us (17%)
  blocking collectives  12.9 us (12%)
  local copies, waits for them, and re-layouts  3.38 us (3%)
  other arithmetic  1.41 us (1%)
    ppermute x8, waiting for transfers between devices, over_ap(): return lax.ppermute(value, 'ap', pairs)  23 us
    pallas_call x4, Pallas kernels, tone_systems(): pl.pallas_call(tone_kernel, in_specs=[smem] + [vmem] * (1 + len(state)),...  17.3 us
    all_to_all x1, blocking collectives, all_steps(): lax.all_to_all(jnp.broadcast_to(own_tone[None], (chips, *own_tone.shape))...  12.9 us
    ppermute x6, starting transfers between devices, over_sc(): return lax.ppermute(value, 'sc', pairs)  10.7 us
    ppermute x1, waiting for transfers between devices, over_ap_by_core(): return lax.ppermute(value, 'ap', pairs)  9.16 us
    ppermute x6, waiting for transfers between devices, over_sc(): return lax.ppermute(value, 'sc', pairs)  8.45 us
    ppermute x8, starting transfers between devices, over_ap(): return lax.ppermute(value, 'ap', pairs)  5.16 us
    ppermute x1, waiting for transfers between devices, over_sc_by_core(): return lax.ppermute(value, ('ap', 'sc'), pairs)  4.74 us
  transfers between devices with their start and end apart: 16, of which 9 were waited for; matrix products, arithmetic and copies ran while one was open for 3% of the time, Pallas kernels for 10%

profile of v2, /device:TPU:0, one launch (start us, length us, event | category | flops | bytes accessed | tf_op | source)
XLA Modules:
  0.0 109.6 jit_solution(14144580430078875286)
XLA Ops:
  0.0 1.0 packed_tables.1.refs_0_
  1.0 4.1 %collective-permute-start.3 = (f32[16,32,128]{2,1,0:T(8,128)S(1)}, f32[16,32,128]{2,1,0:T(8,128)}, u32[]{:S(2)}, u32[]{:S(2)}) collective-permute-start(f32[16,32,128]{2,1,0:T(8,128)S(1)} %packed_tables.1.refs_0_), channel_id=1, source_target_pairs={{0,4},{1,5},{2,6},{3,7},{4,0},{5,1},{6,2},{7,3},{8,12},{9,13},{10,... | collective-permute-start | bytes 786440 | tf_op jit(solution)/shard_map/ppermute | solution.py:379
  5.0 1.5 %collective-permute-start = (f32[16,32,128]{2,1,0:T(8,128)S(1)}, f32[16,32,128]{2,1,0:T(8,128)S(1)}, u32[]{:S(2)}, u32[]{:S(2)}) collective-permute-start(f32[16,32,128]{2,1,0:T(8,128)S(1)} %packed_tables.1.refs_0_), channel_id=1, source_target_pairs={{0,1},{1,2},{2,3},{3,0},{4,5},{5,6},{6,7},{7,4},{8,9},{9,10},{10,1... | collective-permute-start | bytes 786440 | tf_op jit(solution)/shard_map/ppermute | solution.py:379
  6.5 1.7 %collective-permute-start.1 = (f32[16,32,128]{2,1,0:T(8,128)S(1)}, f32[16,32,128]{2,1,0:T(8,128)S(1)}, u32[]{:S(2)}, u32[]{:S(2)}) collective-permute-start(f32[16,32,128]{2,1,0:T(8,128)S(1)} %packed_tables.1.refs_0_), channel_id=1, source_target_pairs={{0,3},{1,0},{2,1},{3,2},{4,7},{5,4},{6,5},{7,6},{8,11},{9,8},{10,9... | collective-permute-start | bytes 786440 | tf_op jit(solution)/shard_map/ppermute | solution.py:379
  8.3 1.5 %reshape.10 = f32[16,2,14,512]{3,0,2,1:T(8,128)S(1)} reshape(f32[16,2,14,4,128]{4,3,0,2,1:T(4,128)} %bitcast.27) | data formatting | bytes 1835008 | tf_op jit(solution)/shard_map/reshape | solution.py:352
  9.8 0.1 fusion.1
  9.9 0.5 copy_bitcast_fusion
  10.5 0.3 fusion
  10.8 0.0 copy-start
  10.8 0.2 select_maximum_fusion.1
  11.0 3.0 %collective-permute-done.refs_2_ = f32[16,32,128]{2,1,0:T(8,128)S(1)} collective-permute-done((f32[16,32,128]{2,1,0:T(8,128)S(1)}, f32[16,32,128]{2,1,0:T(8,128)S(1)}, u32[]{:S(2)}, u32[]{:S(2)}) %collective-permute-start) | collective-permute-done | bytes 262176 | tf_op jit(solution)/shard_map/ppermute | solution.py:379
  14.0 0.0 collective-permute-done.1.refs_3_
  14.1 1.6 %collective-permute-start.2 = (f32[16,32,128]{2,1,0:T(8,128)S(1)}, f32[16,32,128]{2,1,0:T(8,128)S(1)}, u32[]{:S(2)}, u32[]{:S(2)}) collective-permute-start(f32[16,32,128]{2,1,0:T(8,128)S(1)} %broadcast_select_fusion), channel_id=1, source_target_pairs={{0,1},{1,2},{2,3},{3,0},{4,5},{5,6},{6,7},{7,4},{8,11},{9,8},{10,9... | collective-permute-start | bytes 786440 | tf_op jit(solution)/shard_map/ppermute | solution.py:391
  15.6 0.1 pad_add_fusion
  15.7 0.1 pad_maximum_fusion.y_ref
  15.8 0.0 collective-permute-done.3.refs_1_
  15.8 1.3 %collective-permute-start.4 = (f32[16,32,128]{2,1,0:T(8,128)}, f32[16,32,128]{2,1,0:T(8,128)S(1)}, u32[]{:S(2)}, u32[]{:S(2)}) collective-permute-start(f32[16,32,128]{2,1,0:T(8,128)} %collective-permute-done.3.refs_1_), channel_id=1, source_target_pairs={{0,1},{1,2},{2,3},{3,0},{4,5},{5,6},{6,7},{7,4},{8,9},{9,10},{10,1... | collective-permute-start | bytes 786440 | tf_op jit(solution)/shard_map/ppermute | solution.py:379
  17.1 2.0 %collective-permute-start.5 = (f32[16,32,128]{2,1,0:T(8,128)}, f32[16,32,128]{2,1,0:T(8,128)}, u32[]{:S(2)}, u32[]{:S(2)}) collective-permute-start(f32[16,32,128]{2,1,0:T(8,128)} %collective-permute-done.3.refs_1_), channel_id=1, source_target_pairs={{0,3},{1,0},{2,1},{3,2},{4,7},{5,4},{6,5},{7,6},{8,11},{9,8},{10,9... | collective-permute-start | bytes 786440 | tf_op jit(solution)/shard_map/ppermute | solution.py:379
  19.2 4.7 %collective-permute-done.2.refs_0_ = f32[16,32,128]{2,1,0:T(8,128)S(1)} collective-permute-done((f32[16,32,128]{2,1,0:T(8,128)S(1)}, f32[16,32,128]{2,1,0:T(8,128)S(1)}, u32[]{:S(2)}, u32[]{:S(2)}) %collective-permute-start.2) | collective-permute-done | bytes 262176 | tf_op jit(solution)/shard_map/ppermute | solution.py:391
  23.9 0.1 collective-permute-start.6
  24.0 0.1 pad_maximum_fusion.2.tone_ref
  24.1 0.1 stack.67.place_ref
  24.1 0.1 pad_add_fusion.4
  24.2 0.0 copy-done
  24.2 2.2 %prepared.2 = (f32[4,4,2,256,128]{4,3,2,1,0:T(8,128)S(1)}, f32[4,4,2,256,128]{4,3,2,1,0:T(8,128)S(1)}, f32[4,2,256,128]{3,2,1,0:T(8,128)S(1)}) custom-call(s32[5]{0:T(128)S(1)} %stack.67.place_ref, f32[2]{0:T(128)S(1)} %pad_maximum_fusion.2.tone_ref, f32[16,32,128]{2,1,0:T(8,128)S(1)} %packed_tables.1.refs_0_, ...), custom_call_target="tpu_custom_call" | custom-call | tf_op jit(solution)/shard_map/prepared/pallas_call | solution.py:124
  26.4 0.9 collective-permute-done.4.refs_1_
  27.3 0.0 collective-permute-done.5.refs_2_
  27.3 4.5 %collective-permute-done.6.refs_3_ = f32[16,32,128]{2,1,0:T(8,128)} collective-permute-done((f32[16,32,128]{2,1,0:T(8,128)S(1)}, f32[16,32,128]{2,1,0:T(8,128)}, u32[]{:S(2)}, u32[]{:S(2)}) %collective-permute-start.6) | collective-permute-done | bytes 262176 | tf_op jit(solution)/shard_map/ppermute | solution.py:379
  31.9 2.3 %prepared.3 = (f32[4,4,2,256,128]{4,3,2,1,0:T(8,128)S(1)}, f32[4,4,2,256,128]{4,3,2,1,0:T(8,128)S(1)}, f32[4,2,256,128]{3,2,1,0:T(8,128)S(1)}) custom-call(s32[5]{0:T(128)S(1)} %stack.67.place_ref, f32[2]{0:T(128)S(1)} %pad_maximum_fusion.2.tone_ref, ...), custom_call_target="tpu_custom_call", output_to_operand_aliasing={{0}: (7, {}), {1}: (8, {}), {2}: (9, {})} | custom-call | tf_op jit(solution)/shard_map/prepared/pallas_call | solution.py:124
  34.2 4.3 %tone_systems.4 = (f32[2,288,256]{2,1,0:T(8,128)S(1)}, f32[2,288,256]{2,1,0:T(8,128)S(1)}) custom-call(s32[3]{0:T(128)S(1)} %get-tuple-element.52.place_ref, f32[16,32,1024]{2,1,0:T(8,128)S(1)} %pad_maximum_fusion.y_ref, f32[4,4,2,256,128]{4,3,2,1,0:T(8,128)S(1)} %get-tuple-element.25.lead, f32[4,4,2,256,128]{4,3,2,1,0:T(8,128)S(1)} %get-tuple-element.26.turn, ...), custom_call_target="tpu_custom_call" | custom-call | tf_op jit(solution)/shard_map/tone_systems/pallas_call | solution.py:212
  38.5 0.0 collective-permute-start.8
  38.5 4.3 %tone_systems.5 = (f32[2,288,256]{2,1,0:T(8,128)S(1)}, f32[2,288,256]{2,1,0:T(8,128)S(1)}) custom-call(s32[3]{0:T(128)S(1)} %get-tuple-element.29.place_ref, f32[16,32,1024]{2,1,0:T(8,128)S(1)} %pad_maximum_fusion.y_ref, f32[4,4,2,256,128]{4,3,2,1,0:T(8,128)S(1)} %get-tuple-element.25.lead, f32[4,4,2,256,128]{4,3,2,1,0:T(8,128)S(1)} %get-tuple-element.26.turn, ...), custom_call_target="tpu_custom_call" | custom-call | tf_op jit(solution)/shard_map/tone_systems/pallas_call | solution.py:212
  42.8 0.7 collective-permute-start.7
  43.5 0.0 collective-permute-done.8
  43.5 0.1 add.72
  43.6 4.3 %tone_systems.6 = (f32[2,288,256]{2,1,0:T(8,128)S(1)}, f32[2,288,256]{2,1,0:T(8,128)S(1)}) custom-call(s32[3]{0:T(128)S(1)} %get-tuple-element.33.place_ref, f32[16,32,1024]{2,1,0:T(8,128)S(1)} %pad_maximum_fusion.y_ref, f32[4,4,2,256,128]{4,3,2,1,0:T(8,128)S(1)} %get-tuple-element.25.lead, f32[4,4,2,256,128]{4,3,2,1,0:T(8,128)S(1)} %get-tuple-element.26.turn, ...), custom_call_target="tpu_custom_call" | custom-call | tf_op jit(solution)/shard_map/tone_systems/pallas_call | solution.py:212
  47.9 0.0 collective-permute-start.10
  48.0 1.6 %collective-permute-start.9 = (f32[2,288,256]{2,1,0:T(8,128)S(1)}, f32[2,288,256]{2,1,0:T(8,128)S(1)}, u32[]{:S(2)}, u32[]{:S(2)}) collective-permute-start(f32[2,288,256]{2,1,0:T(8,128)S(1)} %add.72), channel_id=1, source_target_pairs={{0,16},{8,56},{16,32},{24,8},{32,48},{40,24},{48,0},{56,40},{64,80... | collective-permute-start | bytes 1769480 | tf_op jit(solution)/shard_map/ppermute | solution.py:373
  49.6 0.0 collective-permute-done.7
  49.6 0.4 collective-permute-done.10
  49.9 9.2 %collective-permute-done.9 = f32[2,288,256]{2,1,0:T(8,128)S(1)} collective-permute-done((f32[2,288,256]{2,1,0:T(8,128)S(1)}, f32[2,288,256]{2,1,0:T(8,128)S(1)}, u32[]{:S(2)}, u32[]{:S(2)}) %collective-permute-start.9) | collective-permute-done | bytes 589856 | tf_op jit(solution)/shard_map/ppermute | solution.py:373
  59.1 0.2 select_add_fusion
  59.3 0.0 copy-start.1
  59.4 4.3 %tone_systems.7 = (f32[2,288,256]{2,1,0:T(8,128)S(1)}, f32[2,288,256]{2,1,0:T(8,128)S(1)}) custom-call(s32[3]{0:T(128)S(1)} %get-tuple-element.36.place_ref, f32[16,32,1024]{2,1,0:T(8,128)S(1)} %pad_maximum_fusion.y_ref, f32[4,4,2,256,128]{4,3,2,1,0:T(8,128)S(1)} %get-tuple-element.25.lead, f32[4,4,2,256,128]{4,3,2,1,0:T(8,128)S(1)} %get-tuple-element.26.turn, ...), custom_call_target="tpu_custom_call" | custom-call | tf_op jit(solution)/shard_map/tone_systems/pallas_call | solution.py:212
  63.7 0.0 collective-permute-start.11
  63.7 0.4 collective-permute-start.12
  64.1 2.9 %collective-permute-start.13 = (f32[2,288,256]{2,1,0:T(8,128)S(1)}, f32[2,288,256]{2,1,0:T(8,128)S(1)}, u32[]{:S(2)}, u32[]{:S(2)}) collective-permute-start(f32[2,288,256]{2,1,0:T(8,128)S(1)} %get-tuple-element.45), channel_id=1, source_target_pairs={{0,48},{8,56},{16,0},{24,8},{32,16},{40,24},{48,32},{56,40},{64,11... | collective-permute-start | bytes 1769480 | tf_op jit(solution)/shard_map/ppermute | solution.py:367
  67.0 0.0 collective-permute-done.11
  67.0 13.6 %collective-permute-done.12 = f32[2,288,256]{2,1,0:T(8,128)S(1)} collective-permute-done((f32[2,288,256]{2,1,0:T(8,128)S(1)}, f32[2,288,256]{2,1,0:T(8,128)S(1)}, u32[]{:S(2)}, u32[]{:S(2)}) %collective-permute-start.12) | collective-permute-done | bytes 589856 | tf_op jit(solution)/shard_map/ppermute | solution.py:367
  80.6 0.0 collective-permute-done.13
  80.7 0.2 add_add_fusion
  80.9 1.1 %collective-permute-start.14 = (f32[1,288,256]{2,1,0:T(8,128)S(1)}, f32[1,288,256]{2,1,0:T(8,128)S(1)}, u32[]{:S(2)}, u32[]{:S(2)}) collective-permute-start(f32[1,288,256]{2,1,0:T(8,128)S(1)} %get-tuple-element.43), channel_id=1, source_target_pairs={{0,64},{8,72},{16,80},{24,88},{32,96},{40,104},{48,112},{56,120},{... | collective-permute-start | bytes 884744 | tf_op jit(solution)/shard_map/ppermute | solution.py:367
  82.0 7.5 %collective-permute-done.14.refs_1_ = f32[1,288,256]{2,1,0:T(8,128)S(1)} collective-permute-done((f32[1,288,256]{2,1,0:T(8,128)S(1)}, f32[1,288,256]{2,1,0:T(8,128)S(1)}, u32[]{:S(2)}, u32[]{:S(2)}) %collective-permute-start.14) | collective-permute-done | bytes 294944 | tf_op jit(solution)/shard_map/ppermute | solution.py:367
  89.4 0.0 copy-done.1
  89.4 4.6 %solved.1 = f32[32,256]{1,0:T(8,128)S(1)} custom-call(f32[1,288,256]{2,1,0:T(8,128)S(1)} %get-tuple-element.44.refs_0_, f32[1,288,256]{2,1,0:T(8,128)S(1)} %collective-permute-done.14.refs_1_, f32[1,256]{1,0:T(1,128)S(1)} %bitcast.25), custom_call_target="tpu_custom_call" | custom-call | tf_op jit(solution)/shard_map/solved/pallas_call | solution.py:332
  94.0 12.9 %all_to_all.5 = f32[8,32,256]{2,1,0:T(8,128)S(1)} all-to-all(f32[8,32,256]{2,1,0:T(8,128)S(1)} %broadcast_in_dim.13), channel_id=1, replica_groups={{0,16,32,48,64,80,96,112},{8,24,40,56,72,88,104,120},{1,17,33,49,65,81,..., dimensions={0} | all-to-all | bytes 524288 | tf_op jit(solution)/shard_map/all_to_all | solution.py:470
  106.9 0.0 collective-permute-start.15
  106.9 1.5 %collective-permute-done.15 = f32[8,32,256]{2,1,0:T(8,128)S(1)} collective-permute-done((f32[8,32,256]{2,1,0:T(8,128)S(1)}, f32[8,32,256]{2,1,0:T(8,128)S(1)}, u32[]{:S(2)}, u32[]{:S(2)}) %collective-permute-start.15) | collective-permute-done | bytes 262176 | tf_op jit(solution)/shard_map/ppermute | solution.py:367
  108.6 1.0 copy.25
  (6 shorter events, 0.2 us)
Async XLA Ops:
  1.0 14.9 %collective-permute-start.3 = (f32[16,32,128]{2,1,0:T(8,128)S(1)}, f32[16,32,128]{2,1,0:T(8,128)}, u32[]{:S(2)}, u32[]{:S(2)}) collective-permute-start(f32[16,32,128]{2,1,0:T(8,128)S(1)} %packed_tables.1.refs_0_), channel_id=1, source_target_pairs={{0,4},{1,5},{2,6},{3,7},{4,0},{5,1},{6,2},{7,3},{8,12},{9,13},{10,... | collective-permute-start | bytes 786440 | tf_op jit(solution)/shard_map/ppermute | solution.py:379
  5.0 9.0 %collective-permute-start = (f32[16,32,128]{2,1,0:T(8,128)S(1)}, f32[16,32,128]{2,1,0:T(8,128)S(1)}, u32[]{:S(2)}, u32[]{:S(2)}) collective-permute-start(f32[16,32,128]{2,1,0:T(8,128)S(1)} %packed_tables.1.refs_0_), channel_id=1, source_target_pairs={{0,1},{1,2},{2,3},{3,0},{4,5},{5,6},{6,7},{7,4},{8,9},{9,10},{10,1... | collective-permute-start | bytes 786440 | tf_op jit(solution)/shard_map/ppermute | solution.py:379
  6.5 7.5 %collective-permute-start.1 = (f32[16,32,128]{2,1,0:T(8,128)S(1)}, f32[16,32,128]{2,1,0:T(8,128)S(1)}, u32[]{:S(2)}, u32[]{:S(2)}) collective-permute-start(f32[16,32,128]{2,1,0:T(8,128)S(1)} %packed_tables.1.refs_0_), channel_id=1, source_target_pairs={{0,3},{1,0},{2,1},{3,2},{4,7},{5,4},{6,5},{7,6},{8,11},{9,8},{10,9... | collective-permute-start | bytes 786440 | tf_op jit(solution)/shard_map/ppermute | solution.py:379
  10.8 13.4 %copy-start = (s32[256,128]{1,0:T(8,128)S(1)}, s32[256,128]{1,0:T(8,128)}, u32[]{:S(2)}) copy-start(s32[256,128]{1,0:T(8,128)} %refs_4_.3) | copy-start | bytes 393220
  14.1 9.8 %collective-permute-start.2 = (f32[16,32,128]{2,1,0:T(8,128)S(1)}, f32[16,32,128]{2,1,0:T(8,128)S(1)}, u32[]{:S(2)}, u32[]{:S(2)}) collective-permute-start(f32[16,32,128]{2,1,0:T(8,128)S(1)} %broadcast_select_fusion), channel_id=1, source_target_pairs={{0,1},{1,2},{2,3},{3,0},{4,5},{5,6},{6,7},{7,4},{8,11},{9,8},{10,9... | collective-permute-start | bytes 786440 | tf_op jit(solution)/shard_map/ppermute | solution.py:391
  15.8 11.5 %collective-permute-start.4 = (f32[16,32,128]{2,1,0:T(8,128)}, f32[16,32,128]{2,1,0:T(8,128)S(1)}, u32[]{:S(2)}, u32[]{:S(2)}) collective-permute-start(f32[16,32,128]{2,1,0:T(8,128)} %collective-permute-done.3.refs_1_), channel_id=1, source_target_pairs={{0,1},{1,2},{2,3},{3,0},{4,5},{5,6},{6,7},{7,4},{8,9},{9,10},{10,1... | collective-permute-start | bytes 786440 | tf_op jit(solution)/shard_map/ppermute | solution.py:379
  17.1 10.2 %collective-permute-start.5 = (f32[16,32,128]{2,1,0:T(8,128)}, f32[16,32,128]{2,1,0:T(8,128)}, u32[]{:S(2)}, u32[]{:S(2)}) collective-permute-start(f32[16,32,128]{2,1,0:T(8,128)} %collective-permute-done.3.refs_1_), channel_id=1, source_target_pairs={{0,3},{1,0},{2,1},{3,2},{4,7},{5,4},{6,5},{7,6},{8,11},{9,8},{10,9... | collective-permute-start | bytes 786440 | tf_op jit(solution)/shard_map/ppermute | solution.py:379
  23.9 8.0 %collective-permute-start.6 = (f32[16,32,128]{2,1,0:T(8,128)S(1)}, f32[16,32,128]{2,1,0:T(8,128)}, u32[]{:S(2)}, u32[]{:S(2)}) collective-permute-start(f32[16,32,128]{2,1,0:T(8,128)S(1)} %collective-permute-done.2.refs_0_), channel_id=1, source_target_pairs={{0,4},{1,5},{2,6},{3,7},{4,0},{5,1},{6,2},{7,3},{8,12},{9,13},{10,... | collective-permute-start | bytes 786440 | tf_op jit(solution)/shard_map/ppermute | solution.py:379
  38.5 5.0 %collective-permute-start.8 = (f32[2,288,256]{2,1,0:T(8,128)S(1)}, f32[2,288,256]{2,1,0:T(8,128)S(1)}, u32[]{:S(2)}, u32[]{:S(2)}) collective-permute-start(f32[2,288,256]{2,1,0:T(8,128)S(1)} %get-tuple-element.32), channel_id=1, source_target_pairs={{0,8},{8,0},{16,24},{24,16},{32,40},{40,32},{48,56},{56,48},{64,72... | collective-permute-start | bytes 1769480 | tf_op jit(solution)/shard_map/ppermute | solution.py:367
  42.8 6.8 %collective-permute-start.7 = (f32[2,288,256]{2,1,0:T(8,128)S(1)}, f32[2,288,256]{2,1,0:T(8,128)S(1)}, u32[]{:S(2)}, u32[]{:S(2)}) collective-permute-start(f32[2,288,256]{2,1,0:T(8,128)S(1)} %get-tuple-element.31), channel_id=1, source_target_pairs={{0,8},{8,0},{16,24},{24,16},{32,40},{40,32},{48,56},{56,48},{64,72... | collective-permute-start | bytes 1769480 | tf_op jit(solution)/shard_map/ppermute | solution.py:367
  47.9 2.0 %collective-permute-start.10 = (f32[2,288,256]{2,1,0:T(8,128)S(1)}, f32[2,288,256]{2,1,0:T(8,128)S(1)}, u32[]{:S(2)}, u32[]{:S(2)}) collective-permute-start(f32[2,288,256]{2,1,0:T(8,128)S(1)} %get-tuple-element.35), channel_id=1, source_target_pairs={{0,8},{8,0},{16,24},{24,16},{32,40},{40,32},{48,56},{56,48},{64,72... | collective-permute-start | bytes 1769480 | tf_op jit(solution)/shard_map/ppermute | solution.py:367
  48.0 11.2 %collective-permute-start.9 = (f32[2,288,256]{2,1,0:T(8,128)S(1)}, f32[2,288,256]{2,1,0:T(8,128)S(1)}, u32[]{:S(2)}, u32[]{:S(2)}) collective-permute-start(f32[2,288,256]{2,1,0:T(8,128)S(1)} %add.72), channel_id=1, source_target_pairs={{0,16},{8,56},{16,32},{24,8},{32,48},{40,24},{48,0},{56,40},{64,80... | collective-permute-start | bytes 1769480 | tf_op jit(solution)/shard_map/ppermute | solution.py:373
  59.3 30.1 %copy-start.1 = (f32[256]{0:T(256)S(1)}, f32[256]{0:T(256)}, u32[]{:S(2)}) copy-start(f32[256]{0:T(256)} %param.13) | copy-start | bytes 3076
  63.7 3.3 %collective-permute-start.11 = (f32[2,288,256]{2,1,0:T(8,128)S(1)}, f32[2,288,256]{2,1,0:T(8,128)S(1)}, u32[]{:S(2)}, u32[]{:S(2)}) collective-permute-start(f32[2,288,256]{2,1,0:T(8,128)S(1)} %get-tuple-element.38), channel_id=1, source_target_pairs={{0,8},{8,0},{16,24},{24,16},{32,40},{40,32},{48,56},{56,48},{64,72... | collective-permute-start | bytes 1769480 | tf_op jit(solution)/shard_map/ppermute | solution.py:367
  63.7 17.0 %collective-permute-start.12 = (f32[2,288,256]{2,1,0:T(8,128)S(1)}, f32[2,288,256]{2,1,0:T(8,128)S(1)}, u32[]{:S(2)}, u32[]{:S(2)}) collective-permute-start(f32[2,288,256]{2,1,0:T(8,128)S(1)} %get-tuple-element.46), channel_id=1, source_target_pairs={{0,16},{8,24},{16,32},{24,40},{32,48},{40,56},{48,0},{56,8},{64,80... | collective-permute-start | bytes 1769480 | tf_op jit(solution)/shard_map/ppermute | solution.py:367
  64.1 16.5 %collective-permute-start.13 = (f32[2,288,256]{2,1,0:T(8,128)S(1)}, f32[2,288,256]{2,1,0:T(8,128)S(1)}, u32[]{:S(2)}, u32[]{:S(2)}) collective-permute-start(f32[2,288,256]{2,1,0:T(8,128)S(1)} %get-tuple-element.45), channel_id=1, source_target_pairs={{0,48},{8,56},{16,0},{24,8},{32,16},{40,24},{48,32},{56,40},{64,11... | collective-permute-start | bytes 1769480 | tf_op jit(solution)/shard_map/ppermute | solution.py:367
  80.9 8.6 %collective-permute-start.14 = (f32[1,288,256]{2,1,0:T(8,128)S(1)}, f32[1,288,256]{2,1,0:T(8,128)S(1)}, u32[]{:S(2)}, u32[]{:S(2)}) collective-permute-start(f32[1,288,256]{2,1,0:T(8,128)S(1)} %get-tuple-element.43), channel_id=1, source_target_pairs={{0,64},{8,72},{16,80},{24,88},{32,96},{40,104},{48,112},{56,120},{... | collective-permute-start | bytes 884744 | tf_op jit(solution)/shard_map/ppermute | solution.py:367
  106.9 1.5 %collective-permute-start.15 = (f32[8,32,256]{2,1,0:T(8,128)S(1)}, f32[8,32,256]{2,1,0:T(8,128)S(1)}, u32[]{:S(2)}, u32[]{:S(2)}) collective-permute-start(f32[8,32,256]{2,1,0:T(8,128)S(1)} %all_to_all.5), channel_id=1, source_target_pairs={{0,8},{8,0},{16,24},{24,16},{32,40},{40,32},{48,56},{56,48},{64,72... | collective-permute-start | bytes 786440 | tf_op jit(solution)/shard_map/ppermute | solution.py:367

commit v3 on v0

--- a/solution.py
+++ b/solution.py
@@ -23,7 +23,7 @@
 ROWS = 16
 HALF = 16
 SOLVE_STEPS = 60
-TOLERANCE = 2e-7
+TOLERANCE = 1e-6
 
 
 def turn_fit():
@@ -448,14 +448,22 @@
     upward = jnp.concatenate([upward[:, :top] + up, upward[:, top:]], 1)
     downward = last_kept + last_other
     downward = jnp.concatenate([downward[:, :top], downward[:, top:] + down], 1)
-    up, down = around(upward, 1), around(downward, -1)
+    up, down = around(upward[1:], 1), around(downward[1:], -1)
     kept, other = systems(0, upward, downward)
-    mine = (kept + other) + (up + down)
-    own_tone = solved([mine[:1], over_ap(mine[1:], 1, 0, 0)], regularizer)
-    length = lax.axis_size("ap")
-    every = lax.all_to_all(jnp.broadcast_to(own_tone[None], (length, *own_tone.shape)), "ap", 0, 0, tiled=True)
-    every = every.reshape(length // CORES, CORES, 2, HALF, users)[:, :, :, :samples]
-    every = jnp.concatenate([every[::-1, 0], every[:, 1]], 0)
+    upward, downward, kept = lax.optimization_barrier((upward[:1], downward[:1], kept))
+    own_up, own_down = around(upward, 1), around(downward, -1)
+    across = kept[1:] + other[1:] + (up + down)
+    across = over_ap(across, 1, 0, 0)
+    own_tone = solved([kept[:1], other[:1], own_up, own_down, across], regularizer)
+    chips = lax.axis_size("ap") // CORES
+    same = [[chip * CORES + c for chip in range(chips)] for c in range(CORES)]
+    same_core = lax.all_to_all(
+        jnp.broadcast_to(own_tone[None], (chips, *own_tone.shape)), "ap", 0, 0, tiled=True, axis_index_groups=same
+    )
+    other_core = over_ap(same_core, 0, 0, 1)
+    first = jnp.where(core == 0, same_core, other_core)[::-1]
+    second = jnp.where(core == 0, other_core, same_core)
+    every = jnp.concatenate([first, second], 0).reshape(tones, 2, HALF, users)[:, :, :samples]
     return jnp.transpose(every, (1, 2, 0, 3))
 
 

time: 110 us -> 101 us (0.918)
  waiting for transfers between devices: 32.3 us -> 22.7 us
  starting transfers between devices: 26 us -> 29.8 us
  blocking collectives: 16.1 us -> 13.9 us
  Pallas kernels: 28.9 us -> 27.5 us
    ppermute x9 -> x12, waiting for transfers between devices: 27.7 us -> 18 us  [over_ap(): return lax.ppermute(value, 'ap', pairs)]
    ppermute x9 -> x12, starting transfers between devices: 8.52 us -> 12.3 us  [over_ap(): return lax.ppermute(value, 'ap', pairs)]
    all_to_all x1, blocking collectives: 16.1 us -> 13.9 us  [all_steps(): lax.all_to_all(jnp.broadcast_to(own_tone[None], (chips, *own_tone.shape))...]
    pallas_call x1, Pallas kernels: 5.94 us -> 4.57 us  [solved(): pl.pallas_call(solve_kernel, in_specs=[vmem] * (len(systems) + 1), out_sp...]
  transfers between devices with their start and end apart: 18 -> 21, of which waited for: 8 -> 9; matrix products, arithmetic and copies ran while one was open for 4% -> 4% of each run, Pallas kernels for 14% -> 15%
where the time goes in v3:
time: 101 us; the launch traced here: 99.5 us
  starting transfers between devices  29.8 us (30%)
  Pallas kernels  27.5 us (27%)
  waiting for transfers between devices  22.7 us (22%)
  blocking collectives  13.9 us (14%)
  local copies, waits for them, and re-layouts  3.4 us (3%)
  other arithmetic  1.99 us (2%)
    ppermute x12, waiting for transfers between devices, over_ap(): return lax.ppermute(value, 'ap', pairs)  18 us
    ppermute x9, starting transfers between devices, over_sc(): return lax.ppermute(value, 'sc', pairs)  17.5 us
    pallas_call x4, Pallas kernels, tone_systems(): pl.pallas_call(tone_kernel, in_specs=[smem] + [vmem] * (1 + len(state)),...  17.5 us
    all_to_all x1, blocking collectives, all_steps(): lax.all_to_all(jnp.broadcast_to(own_tone[None], (chips, *own_tone.shape))...  13.9 us
    ppermute x12, starting transfers between devices, over_ap(): return lax.ppermute(value, 'ap', pairs)  12.3 us
    ppermute x9, waiting for transfers between devices, over_sc(): return lax.ppermute(value, 'sc', pairs)  4.67 us
    pallas_call x1, Pallas kernels, solved(): pl.pallas_call(solve_kernel, in_specs=[vmem] * (len(systems) + 1), out_sp...  4.57 us
    pallas_call x2, Pallas kernels, prepared(): pl.pallas_call(functools.partial(prepare_kernel, slots, len(tables)), in_...  4.55 us
  transfers between devices with their start and end apart: 21, of which 9 were waited for; matrix products, arithmetic and copies ran while one was open for 4% of the time, Pallas kernels for 15%

profile of v3, /device:TPU:0, one launch (start us, length us, event | category | flops | bytes accessed | tf_op | source)
XLA Modules:
  0.0 99.5 jit_solution(4727701263651075437)
XLA Ops:
  0.0 1.0 packed_tables.1.refs_0_
  1.0 4.1 %collective-permute-start.4 = (f32[16,32,128]{2,1,0:T(8,128)S(1)}, f32[16,32,128]{2,1,0:T(8,128)}, u32[]{:S(2)}, u32[]{:S(2)}) collective-permute-start(f32[16,32,128]{2,1,0:T(8,128)S(1)} %packed_tables.1.refs_0_), channel_id=1, source_target_pairs={{0,4},{1,5},{2,6},{3,7},{4,0},{5,1},{6,2},{7,3},{8,12},{9,13},{10,... | collective-permute-start | bytes 786440 | tf_op jit(solution)/shard_map/ppermute | solution.py:373
  5.0 1.5 %collective-permute-start = (f32[16,32,128]{2,1,0:T(8,128)S(1)}, f32[16,32,128]{2,1,0:T(8,128)S(1)}, u32[]{:S(2)}, u32[]{:S(2)}) collective-permute-start(f32[16,32,128]{2,1,0:T(8,128)S(1)} %packed_tables.1.refs_0_), channel_id=1, source_target_pairs={{0,1},{1,2},{2,3},{3,0},{4,5},{5,6},{6,7},{7,4},{8,9},{9,10},{10,1... | collective-permute-start | bytes 786440 | tf_op jit(solution)/shard_map/ppermute | solution.py:373
  6.5 1.7 %collective-permute-start.2 = (f32[16,32,128]{2,1,0:T(8,128)S(1)}, f32[16,32,128]{2,1,0:T(8,128)S(1)}, u32[]{:S(2)}, u32[]{:S(2)}) collective-permute-start(f32[16,32,128]{2,1,0:T(8,128)S(1)} %packed_tables.1.refs_0_), channel_id=1, source_target_pairs={{0,3},{1,0},{2,1},{3,2},{4,7},{5,4},{6,5},{7,6},{8,11},{9,8},{10,9... | collective-permute-start | bytes 786440 | tf_op jit(solution)/shard_map/ppermute | solution.py:373
  8.3 1.5 %reshape.10 = f32[16,2,14,512]{3,0,2,1:T(8,128)S(1)} reshape(f32[16,2,14,4,128]{4,3,0,2,1:T(4,128)} %bitcast.27) | data formatting | bytes 1835008 | tf_op jit(solution)/shard_map/reshape | solution.py:352
  9.8 0.1 fusion.6
  9.9 0.3 fusion.5
  10.2 0.5 copy_bitcast_fusion
  10.8 0.1 pad_add_fusion.4
  10.9 0.6 pad_add_fusion.3
  11.5 2.5 %collective-permute-done.refs_2_ = f32[16,32,128]{2,1,0:T(8,128)S(1)} collective-permute-done((f32[16,32,128]{2,1,0:T(8,128)S(1)}, f32[16,32,128]{2,1,0:T(8,128)S(1)}, u32[]{:S(2)}, u32[]{:S(2)}) %collective-permute-start) | collective-permute-done | bytes 262176 | tf_op jit(solution)/shard_map/ppermute | solution.py:373
  14.0 0.3 collective-permute-start.1
  14.4 0.0 collective-permute-done.2.refs_3_
  14.4 3.0 %collective-permute-start.3 = (f32[8,32,128]{2,1,0:T(8,128)S(1)}, f32[8,32,128]{2,1,0:T(8,128)}, u32[]{:S(2)}, u32[]{:S(2)}) collective-permute-start(f32[8,32,128]{2,1,0:T(8,128)S(1)} %slice.79), channel_id=1, source_target_pairs={{0,3},{1,0},{2,1},{3,2},{4,7},{5,4},{6,5},{7,6},{8,11},{9,8},{10,9... | collective-permute-start | bytes 393224 | tf_op jit(solution)/shard_map/ppermute | solution.py:373
  17.4 0.2 select_maximum_fusion.1
  17.6 0.0 collective-permute-done.4.refs_1_
  17.6 0.1 collective-permute-start.5
  17.7 3.2 %collective-permute-start.6 = (f32[16,32,128]{2,1,0:T(8,128)}, f32[16,32,128]{2,1,0:T(8,128)S(1)}, u32[]{:S(2)}, u32[]{:S(2)}) collective-permute-start(f32[16,32,128]{2,1,0:T(8,128)} %collective-permute-done.4.refs_1_), channel_id=1, source_target_pairs={{0,3},{1,0},{2,1},{3,2},{4,7},{5,4},{6,5},{7,6},{8,11},{9,8},{10,9... | collective-permute-start | bytes 786440 | tf_op jit(solution)/shard_map/ppermute | solution.py:373
  20.9 0.0 collective-permute-done.1.refs_0_
  20.9 0.4 collective-permute-start.7
  21.3 0.0 collective-permute-done.3.refs_1_
  21.3 3.2 %collective-permute-start.8 = (f32[8,32,128]{2,1,0:T(8,128)}, f32[8,32,128]{2,1,0:T(8,128)}, u32[]{:S(2)}, u32[]{:S(2)}) collective-permute-start(f32[8,32,128]{2,1,0:T(8,128)} %collective-permute-done.3.refs_1_), channel_id=1, source_target_pairs={{0,4},{1,5},{2,6},{3,7},{4,0},{5,1},{6,2},{7,3},{8,12},{9,13},{10,... | collective-permute-start | bytes 393224 | tf_op jit(solution)/shard_map/ppermute | solution.py:373
  24.5 0.1 pad_maximum_fusion.y_ref
  24.6 0.1 stack.66.place_ref
  24.7 0.1 pad_maximum_fusion.4.tone_ref
  24.8 2.2 %prepared.2 = (f32[4,4,2,256,128]{4,3,2,1,0:T(8,128)S(1)}, f32[4,4,2,256,128]{4,3,2,1,0:T(8,128)S(1)}, f32[4,2,256,128]{3,2,1,0:T(8,128)S(1)}) custom-call(s32[5]{0:T(128)S(1)} %stack.66.place_ref, f32[2]{0:T(128)S(1)} %pad_maximum_fusion.4.tone_ref, f32[16,32,128]{2,1,0:T(8,128)S(1)} %packed_tables.1.refs_0_, ...), custom_call_target="tpu_custom_call" | custom-call | tf_op jit(solution)/shard_map/prepared/pallas_call | solution.py:124
  27.0 0.7 collective-permute-done.7.refs_4_
  27.7 1.4 %collective-permute-done.8.refs_5_ = f32[8,32,128]{2,1,0:T(8,128)} collective-permute-done((f32[8,32,128]{2,1,0:T(8,128)}, f32[8,32,128]{2,1,0:T(8,128)}, u32[]{:S(2)}, u32[]{:S(2)}) %collective-permute-start.8) | collective-permute-done | bytes 131104 | tf_op jit(solution)/shard_map/ppermute | solution.py:373
  29.1 0.0 collective-permute-done.5.refs_2_
  29.1 2.3 %prepared.3 = (f32[4,4,2,256,128]{4,3,2,1,0:T(8,128)S(1)}, f32[4,4,2,256,128]{4,3,2,1,0:T(8,128)S(1)}, f32[4,2,256,128]{3,2,1,0:T(8,128)S(1)}) custom-call(s32[5]{0:T(128)S(1)} %stack.66.place_ref, f32[2]{0:T(128)S(1)} %pad_maximum_fusion.4.tone_ref, ...), custom_call_target="tpu_custom_call", output_to_operand_aliasing={{0}: (9, {}), {1}: (10, {}), {2}: (11, {})} | custom-call | tf_op jit(solution)/shard_map/prepared/pallas_call | solution.py:124
  31.5 4.4 %tone_systems.4 = (f32[2,288,256]{2,1,0:T(8,128)S(1)}, f32[2,288,256]{2,1,0:T(8,128)S(1)}) custom-call(s32[3]{0:T(128)S(1)} %copy-done.1, f32[16,32,1024]{2,1,0:T(8,128)S(1)} %pad_maximum_fusion.y_ref, f32[4,4,2,256,128]{4,3,2,1,0:T(8,128)S(1)} %get-tuple-element.28.lead, f32[4,4,2,256,128]{4,3,2,1,0:T(8,128)S(1)} %get-tuple-element.29.turn, ...), custom_call_target="tpu_custom_call" | custom-call | tf_op jit(solution)/shard_map/tone_systems/pallas_call | solution.py:212
  35.9 0.0 collective-permute-start.10
  35.9 4.4 %tone_systems.5 = (f32[2,288,256]{2,1,0:T(8,128)S(1)}, f32[2,288,256]{2,1,0:T(8,128)S(1)}) custom-call(s32[3]{0:T(128)S(1)} %get-tuple-element.32.place_ref, f32[16,32,1024]{2,1,0:T(8,128)S(1)} %pad_maximum_fusion.y_ref, f32[4,4,2,256,128]{4,3,2,1,0:T(8,128)S(1)} %get-tuple-element.28.lead, f32[4,4,2,256,128]{4,3,2,1,0:T(8,128)S(1)} %get-tuple-element.29.turn, ...), custom_call_target="tpu_custom_call" | custom-call | tf_op jit(solution)/shard_map/tone_systems/pallas_call | solution.py:212
  40.2 0.5 collective-permute-start.9
  40.8 0.1 add.72
  40.9 1.8 %collective-permute-start.11 = (f32[2,144,256]{2,1,0:T(8,128)S(1)}, f32[2,144,256]{2,1,0:T(8,128)S(1)}, u32[]{:S(2)}, u32[]{:S(2)}) collective-permute-start(f32[2,144,256]{2,1,0:T(8,128)S(1)} %get-tuple-element.59), channel_id=1, source_target_pairs={{0,16},{8,24},{16,32},{24,40},{32,48},{40,56},{48,0},{56,8},{64,80... | collective-permute-start | bytes 884744 | tf_op jit(solution)/shard_map/ppermute | solution.py:367
  42.7 4.4 %tone_systems.6 = (f32[2,288,256]{2,1,0:T(8,128)S(1)}, f32[2,288,256]{2,1,0:T(8,128)S(1)}) custom-call(s32[3]{0:T(128)S(1)} %get-tuple-element.36.place_ref, f32[16,32,1024]{2,1,0:T(8,128)S(1)} %pad_maximum_fusion.y_ref, f32[4,4,2,256,128]{4,3,2,1,0:T(8,128)S(1)} %get-tuple-element.28.lead, f32[4,4,2,256,128]{4,3,2,1,0:T(8,128)S(1)} %get-tuple-element.29.turn, ...), custom_call_target="tpu_custom_call" | custom-call | tf_op jit(solution)/shard_map/tone_systems/pallas_call | solution.py:212
  47.1 0.0 collective-permute-start.12
  47.1 4.4 %tone_systems.7 = (f32[2,288,256]{2,1,0:T(8,128)S(1)}, f32[2,288,256]{2,1,0:T(8,128)S(1)}) custom-call(s32[3]{0:T(128)S(1)} %get-tuple-element.39.place_ref, f32[16,32,1024]{2,1,0:T(8,128)S(1)} %pad_maximum_fusion.y_ref, f32[4,4,2,256,128]{4,3,2,1,0:T(8,128)S(1)} %get-tuple-element.28.lead, f32[4,4,2,256,128]{4,3,2,1,0:T(8,128)S(1)} %get-tuple-element.29.turn, ...), custom_call_target="tpu_custom_call" | custom-call | tf_op jit(solution)/shard_map/tone_systems/pallas_call | solution.py:212
  51.5 0.5 collective-permute-start.14
  52.0 1.7 %collective-permute-start.13 = (f32[2,144,256]{2,1,0:T(8,128)S(1)}, f32[2,144,256]{2,1,0:T(8,128)S(1)}, u32[]{:S(2)}, u32[]{:S(2)}) collective-permute-start(f32[2,144,256]{2,1,0:T(8,128)S(1)} %get-tuple-element.58), channel_id=1, source_target_pairs={{0,48},{8,56},{16,0},{24,8},{32,16},{40,24},{48,32},{56,40},{64,11... | collective-permute-start | bytes 884744 | tf_op jit(solution)/shard_map/ppermute | solution.py:367
  53.7 0.0 collective-permute-done.9
  53.7 0.1 add.71
  53.8 0.1 fusion.8
  53.8 0.0 copy-start.2
  53.9 0.4 collective-permute-start.17
  54.3 0.1 add.76
  54.4 6.6 %collective-permute-done.13 = f32[2,144,256]{2,1,0:T(8,128)S(1)} collective-permute-done((f32[2,144,256]{2,1,0:T(8,128)S(1)}, f32[2,144,256]{2,1,0:T(8,128)S(1)}, u32[]{:S(2)}, u32[]{:S(2)}) %collective-permute-start.13) | collective-permute-done | bytes 294944 | tf_op jit(solution)/shard_map/ppermute | solution.py:367
  61.0 0.1 slice_add_fusion.1
  61.1 2.9 %collective-permute-start.18 = (f32[1,288,256]{2,1,0:T(8,128)S(1)}, f32[1,288,256]{2,1,0:T(8,128)S(1)}, u32[]{:S(2)}, u32[]{:S(2)}) collective-permute-start(f32[1,288,256]{2,1,0:T(8,128)S(1)} %get-tuple-element.52), channel_id=1, source_target_pairs={{0,48},{8,56},{16,0},{24,8},{32,16},{40,24},{48,32},{56,40},{64,11... | collective-permute-start | bytes 884744 | tf_op jit(solution)/shard_map/ppermute | solution.py:367
  64.0 0.0 collective-permute-start.15
  64.1 3.2 %collective-permute-start.16 = (f32[1,288,256]{2,1,0:T(8,128)S(1)}, f32[1,288,256]{2,1,0:T(8,128)S(1)}, u32[]{:S(2)}, u32[]{:S(2)}) collective-permute-start(f32[1,288,256]{2,1,0:T(8,128)S(1)} %get-tuple-element.44), channel_id=1, source_target_pairs={{0,48},{8,56},{16,0},{24,8},{32,16},{40,24},{48,32},{56,40},{64,11... | collective-permute-start | bytes 884744 | tf_op jit(solution)/shard_map/ppermute | solution.py:367
  67.3 0.0 collective-permute-done.17
  67.3 4.2 %collective-permute-done.18 = f32[1,288,256]{2,1,0:T(8,128)S(1)} collective-permute-done((f32[1,288,256]{2,1,0:T(8,128)S(1)}, f32[1,288,256]{2,1,0:T(8,128)S(1)}, u32[]{:S(2)}, u32[]{:S(2)}) %collective-permute-start.18) | collective-permute-done | bytes 294944 | tf_op jit(solution)/shard_map/ppermute | solution.py:367
  71.4 0.1 fusion.4
  71.6 1.1 %collective-permute-start.19 = (f32[1,288,256]{2,1,0:T(8,128)S(1)}, f32[1,288,256]{2,1,0:T(8,128)S(1)}, u32[]{:S(2)}, u32[]{:S(2)}) collective-permute-start(f32[1,288,256]{2,1,0:T(8,128)S(1)} %get-tuple-element.49), channel_id=1, source_target_pairs={{0,64},{8,72},{16,80},{24,88},{32,96},{40,104},{48,112},{56,120},{... | collective-permute-start | bytes 884744 | tf_op jit(solution)/shard_map/ppermute | solution.py:367
  72.7 0.5 collective-permute-done.15.refs_2_
  73.1 2.9 %collective-permute-done.16.refs_3_ = f32[1,288,256]{2,1,0:T(8,128)S(1)} collective-permute-done((f32[1,288,256]{2,1,0:T(8,128)S(1)}, f32[1,288,256]{2,1,0:T(8,128)S(1)}, u32[]{:S(2)}, u32[]{:S(2)}) %collective-permute-start.16) | collective-permute-done | bytes 294944 | tf_op jit(solution)/shard_map/ppermute | solution.py:367
  76.0 2.4 %collective-permute-done.19.refs_4_ = f32[1,288,256]{2,1,0:T(8,128)S(1)} collective-permute-done((f32[1,288,256]{2,1,0:T(8,128)S(1)}, f32[1,288,256]{2,1,0:T(8,128)S(1)}, u32[]{:S(2)}, u32[]{:S(2)}) %collective-permute-start.19) | collective-permute-done | bytes 294944 | tf_op jit(solution)/shard_map/ppermute | solution.py:367
  78.4 4.6 %solved.1 = f32[32,256]{1,0:T(8,128)S(1)} custom-call(f32[1,288,256]{2,1,0:T(8,128)S(1)} %get-tuple-element.50.refs_0_, f32[1,288,256]{2,1,0:T(8,128)S(1)} %get-tuple-element.51.refs_1_, f32[1,288,256]{2,1,0:T(8,128)S(1)} %collective-permute-done.15.refs_2_, f32[1,288,256]{2,1,0:T(8,128)S(1)} %collective-permute-done.16.refs_3_, ...), custom_call_target="tpu_custom_call" | custom-call | tf_op jit(solution)/shard_map/solved/pallas_call | solution.py:332
  83.0 13.9 %all_to_all.5 = f32[8,32,256]{2,1,0:T(8,128)S(1)} all-to-all(f32[8,32,256]{2,1,0:T(8,128)S(1)} %broadcast_in_dim.2), channel_id=1, replica_groups={{0,16,32,48,64,80,96,112},{8,24,40,56,72,88,104,120},{1,17,33,49,65,81,..., dimensions={0} | all-to-all | bytes 524288 | tf_op jit(solution)/shard_map/all_to_all | solution.py:460
  96.8 0.0 collective-permute-start.20
  96.8 1.5 %collective-permute-done.20 = f32[8,32,256]{2,1,0:T(8,128)S(1)} collective-permute-done((f32[8,32,256]{2,1,0:T(8,128)S(1)}, f32[8,32,256]{2,1,0:T(8,128)S(1)}, u32[]{:S(2)}, u32[]{:S(2)}) %collective-permute-start.20) | collective-permute-done | bytes 262176 | tf_op jit(solution)/shard_map/ppermute | solution.py:367
  98.5 1.0 %copy.25 = f32[16,2,14,256]{3,0,2,1:T(8,128)} copy(f32[16,2,14,256]{3,2,1,0:T(8,128)S(1)} %bitcast.26) | data formatting | bytes 917504
  (19 shorter events, 0.3 us)
Async XLA Ops:
  1.0 16.6 %collective-permute-start.4 = (f32[16,32,128]{2,1,0:T(8,128)S(1)}, f32[16,32,128]{2,1,0:T(8,128)}, u32[]{:S(2)}, u32[]{:S(2)}) collective-permute-start(f32[16,32,128]{2,1,0:T(8,128)S(1)} %packed_tables.1.refs_0_), channel_id=1, source_target_pairs={{0,4},{1,5},{2,6},{3,7},{4,0},{5,1},{6,2},{7,3},{8,12},{9,13},{10,... | collective-permute-start | bytes 786440 | tf_op jit(solution)/shard_map/ppermute | solution.py:373
  5.0 9.0 %collective-permute-start = (f32[16,32,128]{2,1,0:T(8,128)S(1)}, f32[16,32,128]{2,1,0:T(8,128)S(1)}, u32[]{:S(2)}, u32[]{:S(2)}) collective-permute-start(f32[16,32,128]{2,1,0:T(8,128)S(1)} %packed_tables.1.refs_0_), channel_id=1, source_target_pairs={{0,1},{1,2},{2,3},{3,0},{4,5},{5,6},{6,7},{7,4},{8,9},{9,10},{10,1... | collective-permute-start | bytes 786440 | tf_op jit(solution)/shard_map/ppermute | solution.py:373
  6.5 7.9 %collective-permute-start.2 = (f32[16,32,128]{2,1,0:T(8,128)S(1)}, f32[16,32,128]{2,1,0:T(8,128)S(1)}, u32[]{:S(2)}, u32[]{:S(2)}) collective-permute-start(f32[16,32,128]{2,1,0:T(8,128)S(1)} %packed_tables.1.refs_0_), channel_id=1, source_target_pairs={{0,3},{1,0},{2,1},{3,2},{4,7},{5,4},{6,5},{7,6},{8,11},{9,8},{10,9... | collective-permute-start | bytes 786440 | tf_op jit(solution)/shard_map/ppermute | solution.py:373
  11.5 13.3 %copy-start = (s32[256,128]{1,0:T(8,128)S(1)}, s32[256,128]{1,0:T(8,128)}, u32[]{:S(2)}) copy-start(s32[256,128]{1,0:T(8,128)} %refs_6_.1) | copy-start | bytes 393220
  14.0 6.9 %collective-permute-start.1 = (f32[8,32,128]{2,1,0:T(8,128)S(1)}, f32[8,32,128]{2,1,0:T(8,128)}, u32[]{:S(2)}, u32[]{:S(2)}) collective-permute-start(f32[8,32,128]{2,1,0:T(8,128)S(1)} %slice.78), channel_id=1, source_target_pairs={{0,1},{1,2},{2,3},{3,0},{4,5},{5,6},{6,7},{7,4},{8,9},{9,10},{10,1... | collective-permute-start | bytes 393224 | tf_op jit(solution)/shard_map/ppermute | solution.py:373
  14.4 6.9 %collective-permute-start.3 = (f32[8,32,128]{2,1,0:T(8,128)S(1)}, f32[8,32,128]{2,1,0:T(8,128)}, u32[]{:S(2)}, u32[]{:S(2)}) collective-permute-start(f32[8,32,128]{2,1,0:T(8,128)S(1)} %slice.79), channel_id=1, source_target_pairs={{0,3},{1,0},{2,1},{3,2},{4,7},{5,4},{6,5},{7,6},{8,11},{9,8},{10,9... | collective-permute-start | bytes 393224 | tf_op jit(solution)/shard_map/ppermute | solution.py:373
  17.6 11.5 %collective-permute-start.5 = (f32[16,32,128]{2,1,0:T(8,128)}, f32[16,32,128]{2,1,0:T(8,128)S(1)}, u32[]{:S(2)}, u32[]{:S(2)}) collective-permute-start(f32[16,32,128]{2,1,0:T(8,128)} %collective-permute-done.4.refs_1_), channel_id=1, source_target_pairs={{0,1},{1,2},{2,3},{3,0},{4,5},{5,6},{6,7},{7,4},{8,9},{9,10},{10,1... | collective-permute-start | bytes 786440 | tf_op jit(solution)/shard_map/ppermute | solution.py:373
  17.7 11.4 %collective-permute-start.6 = (f32[16,32,128]{2,1,0:T(8,128)}, f32[16,32,128]{2,1,0:T(8,128)S(1)}, u32[]{:S(2)}, u32[]{:S(2)}) collective-permute-start(f32[16,32,128]{2,1,0:T(8,128)} %collective-permute-done.4.refs_1_), channel_id=1, source_target_pairs={{0,3},{1,0},{2,1},{3,2},{4,7},{5,4},{6,5},{7,6},{8,11},{9,8},{10,9... | collective-permute-start | bytes 786440 | tf_op jit(solution)/shard_map/ppermute | solution.py:373
  20.9 6.8 %collective-permute-start.7 = (f32[8,32,128]{2,1,0:T(8,128)}, f32[8,32,128]{2,1,0:T(8,128)}, u32[]{:S(2)}, u32[]{:S(2)}) collective-permute-start(f32[8,32,128]{2,1,0:T(8,128)} %collective-permute-done.1.refs_0_), channel_id=1, source_target_pairs={{0,4},{1,5},{2,6},{3,7},{4,0},{5,1},{6,2},{7,3},{8,12},{9,13},{10,... | collective-permute-start | bytes 393224 | tf_op jit(solution)/shard_map/ppermute | solution.py:373
  21.3 7.8 %collective-permute-start.8 = (f32[8,32,128]{2,1,0:T(8,128)}, f32[8,32,128]{2,1,0:T(8,128)}, u32[]{:S(2)}, u32[]{:S(2)}) collective-permute-start(f32[8,32,128]{2,1,0:T(8,128)} %collective-permute-done.3.refs_1_), channel_id=1, source_target_pairs={{0,4},{1,5},{2,6},{3,7},{4,0},{5,1},{6,2},{7,3},{8,12},{9,13},{10,... | collective-permute-start | bytes 393224 | tf_op jit(solution)/shard_map/ppermute | solution.py:373
  29.1 2.4 %copy-start.1 = (s32[3]{0:T(128)S(1)}, s32[3]{0:T(128)}, u32[]{:S(2)}) copy-start(s32[3]{0:T(128)} %get-tuple-element.67.place_ref) | copy-start | bytes 40
  35.9 4.9 %collective-permute-start.10 = (f32[2,288,256]{2,1,0:T(8,128)S(1)}, f32[2,288,256]{2,1,0:T(8,128)S(1)}, u32[]{:S(2)}, u32[]{:S(2)}) collective-permute-start(f32[2,288,256]{2,1,0:T(8,128)S(1)} %get-tuple-element.35), channel_id=1, source_target_pairs={{0,8},{8,0},{16,24},{24,16},{32,40},{40,32},{48,56},{56,48},{64,72... | collective-permute-start | bytes 1769480 | tf_op jit(solution)/shard_map/ppermute | solution.py:367
  40.2 13.4 %collective-permute-start.9 = (f32[2,288,256]{2,1,0:T(8,128)S(1)}, f32[2,288,256]{2,1,0:T(8,128)S(1)}, u32[]{:S(2)}, u32[]{:S(2)}) collective-permute-start(f32[2,288,256]{2,1,0:T(8,128)S(1)} %get-tuple-element.34), channel_id=1, source_target_pairs={{0,8},{8,0},{16,24},{24,16},{32,40},{40,32},{48,56},{56,48},{64,72... | collective-permute-start | bytes 1769480 | tf_op jit(solution)/shard_map/ppermute | solution.py:367
  40.9 12.9 %collective-permute-start.11 = (f32[2,144,256]{2,1,0:T(8,128)S(1)}, f32[2,144,256]{2,1,0:T(8,128)S(1)}, u32[]{:S(2)}, u32[]{:S(2)}) collective-permute-start(f32[2,144,256]{2,1,0:T(8,128)S(1)} %get-tuple-element.59), channel_id=1, source_target_pairs={{0,16},{8,24},{16,32},{24,40},{32,48},{40,56},{48,0},{56,8},{64,80... | collective-permute-start | bytes 884744 | tf_op jit(solution)/shard_map/ppermute | solution.py:367
  47.1 7.2 %collective-permute-start.12 = (f32[2,288,256]{2,1,0:T(8,128)S(1)}, f32[2,288,256]{2,1,0:T(8,128)S(1)}, u32[]{:S(2)}, u32[]{:S(2)}) collective-permute-start(f32[2,288,256]{2,1,0:T(8,128)S(1)} %get-tuple-element.38), channel_id=1, source_target_pairs={{0,8},{8,0},{16,24},{24,16},{32,40},{40,32},{48,56},{56,48},{64,72... | collective-permute-start | bytes 1769480 | tf_op jit(solution)/shard_map/ppermute | solution.py:367
  51.5 15.8 %collective-permute-start.14 = (f32[2,288,256]{2,1,0:T(8,128)S(1)}, f32[2,288,256]{2,1,0:T(8,128)S(1)}, u32[]{:S(2)}, u32[]{:S(2)}) collective-permute-start(f32[2,288,256]{2,1,0:T(8,128)S(1)} %get-tuple-element.42), channel_id=1, source_target_pairs={{0,8},{8,0},{16,24},{24,16},{32,40},{40,32},{48,56},{56,48},{64,72... | collective-permute-start | bytes 1769480 | tf_op jit(solution)/shard_map/ppermute | solution.py:367
  52.0 9.0 %collective-permute-start.13 = (f32[2,144,256]{2,1,0:T(8,128)S(1)}, f32[2,144,256]{2,1,0:T(8,128)S(1)}, u32[]{:S(2)}, u32[]{:S(2)}) collective-permute-start(f32[2,144,256]{2,1,0:T(8,128)S(1)} %get-tuple-element.58), channel_id=1, source_target_pairs={{0,48},{8,56},{16,0},{24,8},{32,16},{40,24},{48,32},{56,40},{64,11... | collective-permute-start | bytes 884744 | tf_op jit(solution)/shard_map/ppermute | solution.py:367
  53.8 24.5 %copy-start.2 = (f32[256]{0:T(256)S(1)}, f32[256]{0:T(256)}, u32[]{:S(2)}) copy-start(f32[256]{0:T(256)} %param.13) | copy-start | bytes 3076
  53.9 13.4 %collective-permute-start.17 = (f32[1,288,256]{2,1,0:T(8,128)S(1)}, f32[1,288,256]{2,1,0:T(8,128)S(1)}, u32[]{:S(2)}, u32[]{:S(2)}) collective-permute-start(f32[1,288,256]{2,1,0:T(8,128)S(1)} %get-tuple-element.54), channel_id=1, source_target_pairs={{0,16},{8,24},{16,32},{24,40},{32,48},{40,56},{48,0},{56,8},{64,80... | collective-permute-start | bytes 884744 | tf_op jit(solution)/shard_map/ppermute | solution.py:367
  61.1 10.3 %collective-permute-start.18 = (f32[1,288,256]{2,1,0:T(8,128)S(1)}, f32[1,288,256]{2,1,0:T(8,128)S(1)}, u32[]{:S(2)}, u32[]{:S(2)}) collective-permute-start(f32[1,288,256]{2,1,0:T(8,128)S(1)} %get-tuple-element.52), channel_id=1, source_target_pairs={{0,48},{8,56},{16,0},{24,8},{32,16},{40,24},{48,32},{56,40},{64,11... | collective-permute-start | bytes 884744 | tf_op jit(solution)/shard_map/ppermute | solution.py:367
  64.0 9.1 %collective-permute-start.15 = (f32[1,288,256]{2,1,0:T(8,128)S(1)}, f32[1,288,256]{2,1,0:T(8,128)S(1)}, u32[]{:S(2)}, u32[]{:S(2)}) collective-permute-start(f32[1,288,256]{2,1,0:T(8,128)S(1)} %get-tuple-element.43), channel_id=1, source_target_pairs={{0,16},{8,24},{16,32},{24,40},{32,48},{40,56},{48,0},{56,8},{64,80... | collective-permute-start | bytes 884744 | tf_op jit(solution)/shard_map/ppermute | solution.py:367
  64.1 12.0 %collective-permute-start.16 = (f32[1,288,256]{2,1,0:T(8,128)S(1)}, f32[1,288,256]{2,1,0:T(8,128)S(1)}, u32[]{:S(2)}, u32[]{:S(2)}) collective-permute-start(f32[1,288,256]{2,1,0:T(8,128)S(1)} %get-tuple-element.44), channel_id=1, source_target_pairs={{0,48},{8,56},{16,0},{24,8},{32,16},{40,24},{48,32},{56,40},{64,11... | collective-permute-start | bytes 884744 | tf_op jit(solution)/shard_map/ppermute | solution.py:367
  71.6 6.8 %collective-permute-start.19 = (f32[1,288,256]{2,1,0:T(8,128)S(1)}, f32[1,288,256]{2,1,0:T(8,128)S(1)}, u32[]{:S(2)}, u32[]{:S(2)}) collective-permute-start(f32[1,288,256]{2,1,0:T(8,128)S(1)} %get-tuple-element.49), channel_id=1, source_target_pairs={{0,64},{8,72},{16,80},{24,88},{32,96},{40,104},{48,112},{56,120},{... | collective-permute-start | bytes 884744 | tf_op jit(solution)/shard_map/ppermute | solution.py:367
  96.8 1.5 %collective-permute-start.20 = (f32[8,32,256]{2,1,0:T(8,128)S(1)}, f32[8,32,256]{2,1,0:T(8,128)S(1)}, u32[]{:S(2)}, u32[]{:S(2)}) collective-permute-start(f32[8,32,256]{2,1,0:T(8,128)S(1)} %all_to_all.5), channel_id=1, source_target_pairs={{0,8},{8,0},{16,24},{24,16},{32,40},{40,32},{48,56},{56,48},{64,72... | collective-permute-start | bytes 786440 | tf_op jit(solution)/shard_map/ppermute | solution.py:367

commit v4 on v3

--- a/solution.py
+++ b/solution.py
@@ -12,7 +12,7 @@
 CORES = 2
 OWNERS = 8
 NEAR_SLOTS = [((0, 0), 0, 0, 0, 8), ((1, 0), 1, 0, 1, 8), ((0, 1), 2, 0, 2, 8), ((0, 3), 3, 0, 3, 8)]
-FAR_SLOTS = [((0, 2), 0, 0, 1, 0), ((1, 1), 2, 0, 2, 8), ((1, 3), 3, 0, 3, 8), ((1, 2), 4, 0, 5, 0)]
+FAR_SLOTS = [((0, 2), 0, 0, 0, 8), ((1, 1), 1, 0, 1, 8), ((1, 3), 2, 0, 2, 8), ((1, 2), 3, 0, 3, 8)]
 Y_CHIPS = 4
 Z_CHIPS = 2
 X_CHIPS = 4
@@ -67,13 +67,14 @@
     return lax.dot_general(a, b, NT, preferred_element_type=jnp.float32)
 
 
-def prepare_kernel(slots, pieces, place_ref, tone_ref, *refs):
+def prepare_kernel(slots, pieces, tones, *refs):
     tab_refs, count_ref = refs[:pieces], refs[pieces]
-    lead, turn, four = refs[-3:]
+    lead, turn = refs[-2:]
     per_block = count_ref.shape[0] // OWNERS
-    sc_z, sc_x = place_ref[3], place_ref[4]
-    centre = tone_ref[0]
-    side = tone_ref[1]
+    sc = lax.axis_index("sc")
+    sc_z, sc_x = sc // X_CHIPS, sc % X_CHIPS
+    centre = ((sc * tones).astype(jnp.float32) + 0.5 * (tones - 1)) * (1.0 / FFT_LEN)
+    side = jnp.where(lax.axis_index("ap") % CORES == 0, -1.0, 1.0)
 
     def prepare(slot, block, carry):
         (across, along), angles, a_at, gains, g_at = slot
@@ -88,13 +89,12 @@
             alive = p < count
             re = jnp.where(alive, gains[g_at + p, inside, :], 0.0)
             im = jnp.where(alive, gains[g_at + PATHS + p, inside, :], 0.0)
-            tones = small_turn(delay * (side * (0.5 / FFT_LEN)))
-            one = doubled(*tones)
-            for y in range(Y_CHIPS):
-                turn[y, p, 0, here, :], turn[y, p, 1, here, :] = tones
-                if y + 1 < Y_CHIPS:
-                    tones = times(tones, one)
-            four[p, 0, here, :], four[p, 1, here, :] = doubled(*doubled(*one))
+            angle = small_turn(delay * (side * (0.5 / FFT_LEN)))
+            one = doubled(*angle)
+            for pair in range(tones // 2):
+                turn[pair, p, 0, here, :], turn[pair, p, 1, here, :] = angle
+                if pair + 1 < tones // 2:
+                    angle = times(angle, one)
             turns = delay * centre
             turns = turns - jnp.round(turns)
             c, s = doubled(*small_turn(0.5 * turns))
@@ -114,42 +114,43 @@
     return pltpu.with_memory_space_constraint(x, pltpu.VMEM)
 
 
-def prepared(place, centre, slots, tables, counts, state=None):
+def prepared(tones, slots, tables, counts, state=()):
     users, width = counts.shape
     f32 = jnp.float32
     vmem = pl.BlockSpec(memory_space=pltpu.VMEM)
-    smem = pl.BlockSpec(memory_space=pltpu.SMEM)
-    state = () if state is None else state
-    first = 3 + len(tables)
+    first = len(tables) + 1
     return pl.pallas_call(
-        functools.partial(prepare_kernel, slots, len(tables)),
-        in_specs=[smem, smem] + [vmem] * (len(tables) + 1 + len(state)),
-        out_specs=[vmem] * 3,
+        functools.partial(prepare_kernel, slots, len(tables), tones),
+        in_specs=[vmem] * (first + len(state)),
+        out_specs=[vmem] * 2,
         out_shape=[
             pltpu.VMEM((ANTENNAS, PATHS, 2, users, width), f32),
-            pltpu.VMEM((Y_CHIPS, PATHS, 2, users, width), f32),
-            pltpu.VMEM((PATHS, 2, users, width), f32),
+            pltpu.VMEM((tones // 2, PATHS, 2, users, width), f32),
         ],
         input_output_aliases={first + k: k for k in range(len(state))},
         compiler_params=pltpu.CompilerParams(vmem_limit_bytes=4 << 20),
         name="prepared",
-    )(place, centre, *[in_vmem(t) for t in tables], in_vmem(counts), *state)
-
-
-def tone_kernel(place_ref, y_ref, lead, turn, four, kept_ref, sent_ref, re_a, im_a, lo_a, re_b, im_b, lo_b):
-    users, width = four.shape[2:]
+    )(*[in_vmem(t) for t in tables], in_vmem(counts), *state)
+
+
+def tone_kernel(distance, planes, y_ref, lead, turn, kept_ref, sent_ref, *buffers):
+    users, width = lead.shape[3:]
     blocks = users // ROWS
     half = ANTENNAS * width
     pairs = Y_CHIPS * Z_CHIPS
-    core, chip_z, target_y = place_ref[0], place_ref[1], place_ref[2]
-
-    def build(buffers, block, second):
+    ap = lax.axis_index("ap")
+    core, chip = ap % CORES, ap // CORES
+    chip_z, target_y = chip // Y_CHIPS, (chip + distance) % Y_CHIPS
+
+    def pair_of(plane):
+        return jnp.abs(chip_z - plane) * Y_CHIPS + target_y
+
+    def build(buffers, block, plane):
+        pair = pair_of(plane)
         with_re, with_im, lo = buffers
         here = pl.ds(block * ROWS, ROWS)
         below = pl.ds(users + block * ROWS, ROWS)
-        cs = [(turn[target_y, p, 0, here, :], turn[target_y, p, 1, here, :]) for p in range(PATHS)]
-        if second:
-            cs = [times(cs[p], (four[p, 0, here, :], four[p, 1, here, :])) for p in range(PATHS)]
+        cs = [(turn[pair, p, 0, here, :], turn[pair, p, 1, here, :]) for p in range(PATHS)]
         for n in range(ANTENNAS):
             sums = None
             for p in range(PATHS):
@@ -167,10 +168,9 @@
                     rest = (value - packed.astype(jnp.float32)).astype(jnp.bfloat16)
                     lo[tone, here, slice(part * half + n * width, part * half + (n + 1) * width)] = rest
 
-    def multiply(buffers, z):
+    def multiply(buffers, plane, slot):
         with_re, with_im, lo = buffers
-        pair = z * Y_CHIPS + target_y
-        slot = jnp.abs(z - chip_z)
+        pair = pair_of(plane)
         plus, minus = pairs + pair, pairs - 1 - pair
         first = jnp.where(core == 0, plus, minus)
         for tone, (at, out_ref) in enumerate(((first, sent_ref), (plus + minus - first, kept_ref))):
@@ -188,36 +188,36 @@
             rest = product(y_hi, lo[tone])
             out_ref[slot, users:, :] = filtered[: 2 * HALF] + (filtered[2 * HALF :] + rest)
 
-    even, odd = (re_a, im_a, lo_a), (re_b, im_b, lo_b)
+    sides = [buffers[3 * k : 3 * k + 3] for k in range(len(planes))]
 
     def alone(block, carry):
-        build(even, block, False)
+        build(sides[0], block, planes[0])
         return carry
 
     lax.fori_loop(0, blocks, alone, 0, unroll=2)
-    multiply(even, 0)
-    for block in range(blocks):
-        build(odd, block, True)
-    multiply(odd, 1)
-
-
-def tone_systems(place, received, state):
-    users, _ = state[2].shape[2:]
+    for slot, plane in enumerate(planes):
+        multiply(sides[slot], plane, slot)
+        if slot + 1 < len(planes):
+            for block in range(blocks):
+                build(sides[slot + 1], block, planes[slot + 1])
+
+
+def tone_systems(distance, planes, received, state):
+    users, _ = state[0].shape[3:]
     wide = received.shape[2]
     f32, bf16 = jnp.float32, jnp.bfloat16
     vmem = pl.BlockSpec(memory_space=pltpu.VMEM)
-    smem = pl.BlockSpec(memory_space=pltpu.SMEM)
     channel = pltpu.VMEM((2, 2 * users + 4 * HALF, wide // 2), bf16)
     rest = pltpu.VMEM((2, users, wide), bf16)
     return pl.pallas_call(
-        tone_kernel,
-        in_specs=[smem] + [vmem] * (1 + len(state)),
+        functools.partial(tone_kernel, distance, planes),
+        in_specs=[vmem] * (1 + len(state)),
         out_specs=[vmem, vmem],
-        out_shape=[pltpu.VMEM((Z_CHIPS, users + 2 * HALF, users), f32)] * 2,
-        scratch_shapes=[channel, channel, rest] * 2,
+        out_shape=[pltpu.VMEM((len(planes), users + 2 * HALF, users), f32)] * 2,
+        scratch_shapes=[channel, channel, rest] * len(planes),
         compiler_params=pltpu.CompilerParams(vmem_limit_bytes=16 << 20),
         name="tone_systems",
-    )(place, in_vmem(received), *state)
+    )(in_vmem(received), *state)
 
 
 def three_parts(x):
@@ -379,8 +379,8 @@
     up, down = over_sc(own, 0, 1), over_sc(own, 0, -1)
     up_twice, down_twice = over_sc(up[:half], 0, 1), over_sc(down[half:], 0, -1)
     across_up, across_down = over_sc(across, 0, 1), over_sc(across, 0, -1)
-    far = over_sc(up_twice, 1, 0), over_sc(down_twice, 1, 0)
-    return [own, across, up, down], [up_twice, down_twice, across_up, across_down, *far]
+    opposite = jnp.concatenate([up_twice, down_twice], 0)
+    return [own, across, up, down], [opposite, across_up, across_down, over_sc(opposite, 1, 0)]
 
 
 def pack_kernel(*refs):
@@ -413,48 +413,45 @@
     tones = observed_signal.shape[2]
     samples = observed_signal.shape[1]
     users = counts.shape[0]
-    sc = lax.axis_index("sc")
-    ap = lax.axis_index("ap")
-    core = ap % CORES
-    chip = ap // CORES
-    place = jnp.stack([core, chip // Y_CHIPS, chip % Y_CHIPS, sc // X_CHIPS, sc % X_CHIPS]).astype(jnp.int32)
-    first = (sc * tones).astype(jnp.float32)
-    side = jnp.where(core == 0, -1.0, 1.0)
-    centre = jnp.stack([(first + 0.5 * (tones - 1)) * (1.0 / FFT_LEN), side])
+    core = lax.axis_index("ap") % CORES
     own = packed_tables([delays, sines, path_gain_real, path_gain_imaginary])
     near, far = gathered_tables(own)
-    state = prepared(place, centre, NEAR_SLOTS, near, counts)
-    state = prepared(place, centre, FAR_SLOTS, far, counts, state)
+    state = prepared(tones, NEAR_SLOTS, near, counts)
+    state = prepared(tones, FAR_SLOTS, far, counts, state)
     received = received_rows(observed_signal)
     rows = users + 2 * HALF
     top = rows // 2
 
-    def systems(distance, *after):
-        where = jnp.stack([core, chip // Y_CHIPS, (chip + distance) % Y_CHIPS]).astype(jnp.int32)
-        if after:
-            where = lax.optimization_barrier((where, *after))[0]
-        kept, sent = tone_systems(where, received, state)
+    def systems(distance, planes, *after):
+        y = lax.optimization_barrier((received, *after))[0] if after else received
+        kept, sent = tone_systems(distance, planes, y, state)
         return kept, over_ap(sent, 0, 0, 1)
 
     def around(value, step):
         return over_ap(value, 0, step, 0)
 
-    kept, other = systems(2)
-    next_kept, next_other = systems(1, kept)
+    def joined(pieces, passed, at):
+        total = pieces[0] + pieces[1]
+        if at == 0:
+            return jnp.concatenate([total[:, :top] + passed, total[:, top:]], 1)
+        return jnp.concatenate([total[:, :top], total[:, top:] + passed], 1)
+
+    kept, other = systems(2, (0, 1))
+    up_far = systems(1, (1,), kept)
     farthest = kept + other
     up, down = around(farthest[:, :top], 1), around(farthest[:, top:], -1)
-    last_kept, last_other = systems(3, farthest)
-    upward = next_kept + next_other
-    upward = jnp.concatenate([upward[:, :top] + up, upward[:, top:]], 1)
-    downward = last_kept + last_other
-    downward = jnp.concatenate([downward[:, :top], downward[:, top:] + down], 1)
-    up, down = around(upward[1:], 1), around(downward[1:], -1)
-    kept, other = systems(0, upward, downward)
-    upward, downward, kept = lax.optimization_barrier((upward[:1], downward[:1], kept))
-    own_up, own_down = around(upward, 1), around(downward, -1)
-    across = kept[1:] + other[1:] + (up + down)
+    up_own = systems(1, (0,), farthest, up_far[0])
+    kept, other = systems(3, (0, 1), up_own[0])
+    up_far, up_own = joined(up_far, up[1:], 0), joined(up_own, up[:1], 0)
+    down_far, down_own = joined((kept[1:], other[1:]), down[1:], 1), joined((kept[:1], other[:1]), down[:1], 1)
+    up, down = around(up_far, 1), around(down_far, -1)
+    kept, other = systems(0, (1,), up_far, down_far)
+    up_own, down_own, kept = lax.optimization_barrier((up_own, down_own, kept))
+    own_up, own_down = around(up_own, 1), around(down_own, -1)
+    across = (kept + other) + (up + down)
+    kept, other = systems(0, (0,), across)
     across = over_ap(across, 1, 0, 0)
-    own_tone = solved([kept[:1], other[:1], own_up, own_down, across], regularizer)
+    own_tone = solved([kept, other, own_up, own_down, across], regularizer)
     chips = lax.axis_size("ap") // CORES
     same = [[chip * CORES + c for chip in range(chips)] for c in range(CORES)]
     same_core = lax.all_to_all(

time: 101 us -> 100 us (0.990)
  waiting for transfers between devices: 22.7 us -> 30.3 us
  Pallas kernels: 27.5 us -> 23.7 us
  starting transfers between devices: 29.8 us -> 26.3 us
    ppermute x9 -> x8, waiting for transfers between devices: 4.67 us -> 9.27 us  [over_sc(): return lax.ppermute(value, 'sc', pairs)]
    pallas_call x6 -> x8, Pallas kernels: 22 us -> 18.2 us  [the longest x6 15.4 us: tone_systems(): pl.pallas_call(functools.partial(tone_kernel, distance, planes), in_specs...]
    ppermute x9 -> x8, starting transfers between devices: 17.5 us -> 14.4 us  [over_sc(): return lax.ppermute(value, 'sc', pairs)]
    ppermute x12 -> x14, waiting for transfers between devices: 18 us -> 21 us  [over_ap(): return lax.ppermute(value, 'ap', pairs)]
    ppermute x12 -> x14, starting transfers between devices: 12.3 us -> 11.9 us  [over_ap(): return lax.ppermute(value, 'ap', pairs)]
  transfers between devices with their start and end apart: 21 -> 22, of which waited for: 9 -> 9; matrix products, arithmetic and copies ran while one was open for 4% -> 3% of each run, Pallas kernels for 15% -> 13%
where the time goes in v4:
time: 100 us; the launch traced here: 99.1 us
  waiting for transfers between devices  30.3 us (30%)
  starting transfers between devices  26.3 us (26%)
  Pallas kernels  23.7 us (24%)
  blocking collectives  13.9 us (14%)
  local copies, waits for them, and re-layouts  3.32 us (3%)
  other arithmetic  1.28 us (1%)
    ppermute x14, waiting for transfers between devices, over_ap(): return lax.ppermute(value, 'ap', pairs)  21 us
    pallas_call x6, Pallas kernels, tone_systems(): pl.pallas_call(functools.partial(tone_kernel, distance, planes), in_specs...  15.4 us
    ppermute x8, starting transfers between devices, over_sc(): return lax.ppermute(value, 'sc', pairs)  14.4 us
    all_to_all x1, blocking collectives, all_steps(): lax.all_to_all(jnp.broadcast_to(own_tone[None], (chips, *own_tone.shape))...  13.9 us
    ppermute x14, starting transfers between devices, over_ap(): return lax.ppermute(value, 'ap', pairs)  11.9 us
    ppermute x8, waiting for transfers between devices, over_sc(): return lax.ppermute(value, 'sc', pairs)  9.27 us
    pallas_call x1, Pallas kernels, solved(): pl.pallas_call(solve_kernel, in_specs=[vmem] * (len(systems) + 1), out_sp...  4.57 us
    pallas_call x2, Pallas kernels, prepared(): pl.pallas_call(functools.partial(prepare_kernel, slots, len(tables), tone...  2.77 us
  transfers between devices with their start and end apart: 22, of which 9 were waited for; matrix products, arithmetic and copies ran while one was open for 3% of the time, Pallas kernels for 13%

profile of v4, /device:TPU:0, one launch (start us, length us, event | category | flops | bytes accessed | tf_op | source)
XLA Modules:
  0.0 99.1 jit_solution(3880032371416567592)
XLA Ops:
  0.0 1.0 packed_tables.1.refs_0_
  1.0 4.1 %collective-permute-start.4 = (f32[16,32,128]{2,1,0:T(8,128)S(1)}, f32[16,32,128]{2,1,0:T(8,128)S(1)}, u32[]{:S(2)}, u32[]{:S(2)}) collective-permute-start(f32[16,32,128]{2,1,0:T(8,128)S(1)} %packed_tables.1.refs_0_), channel_id=1, source_target_pairs={{0,4},{1,5},{2,6},{3,7},{4,0},{5,1},{6,2},{7,3},{8,12},{9,13},{10,... | collective-permute-start | bytes 786440 | tf_op jit(solution)/shard_map/ppermute | solution.py:373
  5.0 1.5 %collective-permute-start = (f32[16,32,128]{2,1,0:T(8,128)S(1)}, f32[16,32,128]{2,1,0:T(8,128)S(1)}, u32[]{:S(2)}, u32[]{:S(2)}) collective-permute-start(f32[16,32,128]{2,1,0:T(8,128)S(1)} %packed_tables.1.refs_0_), channel_id=1, source_target_pairs={{0,1},{1,2},{2,3},{3,0},{4,5},{5,6},{6,7},{7,4},{8,9},{9,10},{10,1... | collective-permute-start | bytes 786440 | tf_op jit(solution)/shard_map/ppermute | solution.py:373
  6.5 1.7 %collective-permute-start.2 = (f32[16,32,128]{2,1,0:T(8,128)S(1)}, f32[16,32,128]{2,1,0:T(8,128)S(1)}, u32[]{:S(2)}, u32[]{:S(2)}) collective-permute-start(f32[16,32,128]{2,1,0:T(8,128)S(1)} %packed_tables.1.refs_0_), channel_id=1, source_target_pairs={{0,3},{1,0},{2,1},{3,2},{4,7},{5,4},{6,5},{7,6},{8,11},{9,8},{10,9... | collective-permute-start | bytes 786440 | tf_op jit(solution)/shard_map/ppermute | solution.py:373
  8.3 1.5 %reshape.10 = f32[16,2,14,512]{3,0,2,1:T(8,128)S(1)} reshape(f32[16,2,14,4,128]{4,3,0,2,1:T(4,128)} %bitcast.17) | data formatting | bytes 1835008 | tf_op jit(solution)/shard_map/reshape | solution.py:352
  9.8 0.1 fusion.1
  9.9 0.5 copy_bitcast_fusion
  10.5 3.6 %collective-permute-done.refs_2_ = f32[16,32,128]{2,1,0:T(8,128)S(1)} collective-permute-done((f32[16,32,128]{2,1,0:T(8,128)S(1)}, f32[16,32,128]{2,1,0:T(8,128)S(1)}, u32[]{:S(2)}, u32[]{:S(2)}) %collective-permute-start) | collective-permute-done | bytes 262176 | tf_op jit(solution)/shard_map/ppermute | solution.py:373
  14.0 0.3 collective-permute-start.1
  14.4 0.0 collective-permute-done.2.refs_3_
  14.4 3.0 %collective-permute-start.3 = (f32[8,32,128]{2,1,0:T(8,128)S(1)}, f32[8,32,128]{2,1,0:T(8,128)S(1)}, u32[]{:S(2)}, u32[]{:S(2)}) collective-permute-start(f32[8,32,128]{2,1,0:T(8,128)S(1)} %slice.95), channel_id=1, source_target_pairs={{0,3},{1,0},{2,1},{3,2},{4,7},{5,4},{6,5},{7,6},{8,11},{9,8},{10,9... | collective-permute-start | bytes 393224 | tf_op jit(solution)/shard_map/ppermute | solution.py:373
  17.4 0.3 fusion
  17.7 0.0 copy-start
  17.7 0.0 collective-permute-done.4.refs_1_
  17.8 0.1 collective-permute-start.5
  17.8 3.2 %collective-permute-start.6 = (f32[16,32,128]{2,1,0:T(8,128)S(1)}, f32[16,32,128]{2,1,0:T(8,128)S(1)}, u32[]{:S(2)}, u32[]{:S(2)}) collective-permute-start(f32[16,32,128]{2,1,0:T(8,128)S(1)} %collective-permute-done.4.refs_1_), channel_id=1, source_target_pairs={{0,3},{1,0},{2,1},{3,2},{4,7},{5,4},{6,5},{7,6},{8,11},{9,8},{10,9... | collective-permute-start | bytes 786440 | tf_op jit(solution)/shard_map/ppermute | solution.py:373
  21.1 0.0 collective-permute-done.1
  21.1 0.0 collective-permute-done.3
  21.1 0.4 collective-permute-start.7
  21.6 0.3 select_maximum_fusion.1
  21.8 0.1 pad_maximum_fusion.y_ref
  22.0 1.4 %prepared.2 = (f32[4,4,2,256,128]{4,3,2,1,0:T(8,128)S(1)}, f32[8,4,2,256,128]{4,3,2,1,0:T(8,128)S(1)}) custom-call(f32[16,32,128]{2,1,0:T(8,128)S(1)} %packed_tables.1.refs_0_, f32[16,32,128]{2,1,0:T(8,128)S(1)} %collective-permute-done.4.refs_1_, f32[16,32,128]{2,1,0:T(8,128)S(1)} %collective-permute-done.refs_2_, ...), custom_call_target="tpu_custom_call" | custom-call | tf_op jit(solution)/shard_map/prepared/pallas_call | solution.py:122
  23.4 2.5 %collective-permute-done.5.refs_1_ = f32[16,32,128]{2,1,0:T(8,128)S(1)} collective-permute-done((f32[16,32,128]{2,1,0:T(8,128)S(1)}, f32[16,32,128]{2,1,0:T(8,128)S(1)}, u32[]{:S(2)}, u32[]{:S(2)}) %collective-permute-start.5) | collective-permute-done | bytes 262176 | tf_op jit(solution)/shard_map/ppermute | solution.py:373
  25.9 0.0 collective-permute-done.6.refs_2_
  25.9 3.2 %collective-permute-done.7.refs_3_ = f32[16,32,128]{2,1,0:T(8,128)S(1)} collective-permute-done((f32[16,32,128]{2,1,0:T(8,128)S(1)}, f32[16,32,128]{2,1,0:T(8,128)S(1)}, u32[]{:S(2)}, u32[]{:S(2)}) %collective-permute-start.7) | collective-permute-done | bytes 262176 | tf_op jit(solution)/shard_map/ppermute | solution.py:373
  29.1 1.4 %prepared.3 = (f32[4,4,2,256,128]{4,3,2,1,0:T(8,128)S(1)}, f32[8,4,2,256,128]{4,3,2,1,0:T(8,128)S(1)}) custom-call(f32[16,32,128]{2,1,0:T(8,128)S(1)} %constant_dynamic-update-slice_fusion.refs_0_, f32[16,32,128]{2,1,0:T(8,128)S(1)} %collective-permute-done.5.refs_1_, ...), custom_call_target="tpu_custom_call", output_to_operand_aliasing={{0}: (5, {}), {1}: (6, {})} | custom-call | tf_op jit(solution)/shard_map/prepared/pallas_call | solution.py:122
  30.4 3.6 %tone_systems.6 = (f32[2,288,256]{2,1,0:T(8,128)S(1)}, f32[2,288,256]{2,1,0:T(8,128)S(1)}) custom-call(f32[16,32,1024]{2,1,0:T(8,128)S(1)} %pad_maximum_fusion.y_ref, f32[4,4,2,256,128]{4,3,2,1,0:T(8,128)S(1)} %get-tuple-element.31.lead, f32[8,4,2,256,128]{4,3,2,1,0:T(8,128)S(1)} %get-tuple-element.32.turn), custom_call_target="tpu_custom_call" | custom-call | tf_op jit(solution)/shard_map/tone_systems/pallas_call | solution.py:212
  34.1 0.0 collective-permute-start.8
  34.1 2.0 %tone_systems.7 = (f32[1,288,256]{2,1,0:T(8,128)S(1)}, f32[1,288,256]{2,1,0:T(8,128)S(1)}) custom-call(f32[16,32,1024]{2,1,0:T(8,128)S(1)} %pad_maximum_fusion.y_ref, f32[4,4,2,256,128]{4,3,2,1,0:T(8,128)S(1)} %get-tuple-element.31.lead, f32[8,4,2,256,128]{4,3,2,1,0:T(8,128)S(1)} %get-tuple-element.32.turn), custom_call_target="tpu_custom_call" | custom-call | tf_op jit(solution)/shard_map/tone_systems/pallas_call | solution.py:212
  36.1 0.5 collective-permute-start.13
  36.6 0.0 collective-permute-done.8
  36.6 0.1 add.45
  36.8 2.0 %tone_systems.8 = (f32[1,288,256]{2,1,0:T(8,128)S(1)}, f32[1,288,256]{2,1,0:T(8,128)S(1)}) custom-call(f32[16,32,1024]{2,1,0:T(8,128)S(1)} %pad_maximum_fusion.y_ref, f32[4,4,2,256,128]{4,3,2,1,0:T(8,128)S(1)} %get-tuple-element.31.lead, f32[8,4,2,256,128]{4,3,2,1,0:T(8,128)S(1)} %get-tuple-element.32.turn), custom_call_target="tpu_custom_call" | custom-call | tf_op jit(solution)/shard_map/tone_systems/pallas_call | solution.py:212
  38.8 0.1 collective-permute-start.9
  38.9 1.8 %collective-permute-start.10 = (f32[2,144,256]{2,1,0:T(8,128)S(1)}, f32[2,144,256]{2,1,0:T(8,128)S(1)}, u32[]{:S(2)}, u32[]{:S(2)}) collective-permute-start(f32[2,144,256]{2,1,0:T(8,128)S(1)} %get-tuple-element.58), channel_id=1, source_target_pairs={{0,16},{8,24},{16,32},{24,40},{32,48},{40,56},{48,0},{56,8},{64,80... | collective-permute-start | bytes 884744 | tf_op jit(solution)/shard_map/ppermute | solution.py:367
  40.7 3.6 %tone_systems.9 = (f32[2,288,256]{2,1,0:T(8,128)S(1)}, f32[2,288,256]{2,1,0:T(8,128)S(1)}) custom-call(f32[16,32,1024]{2,1,0:T(8,128)S(1)} %pad_maximum_fusion.y_ref, f32[4,4,2,256,128]{4,3,2,1,0:T(8,128)S(1)} %get-tuple-element.31.lead, f32[8,4,2,256,128]{4,3,2,1,0:T(8,128)S(1)} %get-tuple-element.32.turn), custom_call_target="tpu_custom_call" | custom-call | tf_op jit(solution)/shard_map/tone_systems/pallas_call | solution.py:212
  44.2 0.0 collective-permute-start.11
  44.3 0.0 collective-permute-done.13
  44.3 1.8 %collective-permute-start.12 = (f32[2,144,256]{2,1,0:T(8,128)S(1)}, f32[2,144,256]{2,1,0:T(8,128)S(1)}, u32[]{:S(2)}, u32[]{:S(2)}) collective-permute-start(f32[2,144,256]{2,1,0:T(8,128)S(1)} %get-tuple-element.57), channel_id=1, source_target_pairs={{0,48},{8,56},{16,0},{24,8},{32,16},{40,24},{48,32},{56,40},{64,11... | collective-permute-start | bytes 884744 | tf_op jit(solution)/shard_map/ppermute | solution.py:367
  46.1 0.0 collective-permute-done.9
  46.2 3.4 %collective-permute-done.10 = f32[2,144,256]{2,1,0:T(8,128)S(1)} collective-permute-done((f32[2,144,256]{2,1,0:T(8,128)S(1)}, f32[2,144,256]{2,1,0:T(8,128)S(1)}, u32[]{:S(2)}, u32[]{:S(2)}) %collective-permute-start.10) | collective-permute-done | bytes 294944 | tf_op jit(solution)/shard_map/ppermute | solution.py:367
  49.6 0.1 slice_add_fusion.5
  49.7 0.4 collective-permute-start.15
  50.0 0.0 collective-permute-done.11
  50.0 0.1 slice_add_fusion.1
  50.1 3.7 %collective-permute-done.12 = f32[2,144,256]{2,1,0:T(8,128)S(1)} collective-permute-done((f32[2,144,256]{2,1,0:T(8,128)S(1)}, f32[2,144,256]{2,1,0:T(8,128)S(1)}, u32[]{:S(2)}, u32[]{:S(2)}) %collective-permute-start.12) | collective-permute-done | bytes 294944 | tf_op jit(solution)/shard_map/ppermute | solution.py:367
  53.8 0.1 fusion.3
  53.9 2.1 %tone_systems.10 = (f32[1,288,256]{2,1,0:T(8,128)S(1)}, f32[1,288,256]{2,1,0:T(8,128)S(1)}) custom-call(f32[16,32,1024]{2,1,0:T(8,128)S(1)} %pad_maximum_fusion.y_ref, f32[4,4,2,256,128]{4,3,2,1,0:T(8,128)S(1)} %get-tuple-element.31.lead, f32[8,4,2,256,128]{4,3,2,1,0:T(8,128)S(1)} %get-tuple-element.32.turn), custom_call_target="tpu_custom_call" | custom-call | tf_op jit(solution)/shard_map/tone_systems/pallas_call | solution.py:212
  55.9 0.0 collective-permute-start.14
  56.0 2.9 %collective-permute-start.16 = (f32[1,288,256]{2,1,0:T(8,128)S(1)}, f32[1,288,256]{2,1,0:T(8,128)S(1)}, u32[]{:S(2)}, u32[]{:S(2)}) collective-permute-start(f32[1,288,256]{2,1,0:T(8,128)S(1)} %pad_maximum_fusion.5), channel_id=1, source_target_pairs={{0,48},{8,56},{16,0},{24,8},{32,16},{40,24},{48,32},{56,40},{64,11... | collective-permute-start | bytes 884744 | tf_op jit(solution)/shard_map/ppermute | solution.py:367
  59.0 0.1 collective-permute-start.18
  59.0 3.2 %collective-permute-start.19 = (f32[1,288,256]{2,1,0:T(8,128)S(1)}, f32[1,288,256]{2,1,0:T(8,128)S(1)}, u32[]{:S(2)}, u32[]{:S(2)}) collective-permute-start(f32[1,288,256]{2,1,0:T(8,128)S(1)} %pad_maximum_fusion.3), channel_id=1, source_target_pairs={{0,48},{8,56},{16,0},{24,8},{32,16},{40,24},{48,32},{56,40},{64,11... | collective-permute-start | bytes 884744 | tf_op jit(solution)/shard_map/ppermute | solution.py:367
  62.3 0.0 collective-permute-done.15
  62.3 4.0 %collective-permute-done.16 = f32[1,288,256]{2,1,0:T(8,128)S(1)} collective-permute-done((f32[1,288,256]{2,1,0:T(8,128)S(1)}, f32[1,288,256]{2,1,0:T(8,128)S(1)}, u32[]{:S(2)}, u32[]{:S(2)}) %collective-permute-start.16) | collective-permute-done | bytes 294944 | tf_op jit(solution)/shard_map/ppermute | solution.py:367
  66.3 0.1 add_add_fusion
  66.4 0.0 copy-start.1
  66.4 2.1 %tone_systems.11 = (f32[1,288,256]{2,1,0:T(8,128)S(1)}, f32[1,288,256]{2,1,0:T(8,128)S(1)}) custom-call(f32[16,32,1024]{2,1,0:T(8,128)S(1)} %pad_maximum_fusion.y_ref, f32[4,4,2,256,128]{4,3,2,1,0:T(8,128)S(1)} %get-tuple-element.31.lead, f32[8,4,2,256,128]{4,3,2,1,0:T(8,128)S(1)} %get-tuple-element.32.turn), custom_call_target="tpu_custom_call" | custom-call | tf_op jit(solution)/shard_map/tone_systems/pallas_call | solution.py:212
  68.5 1.1 %collective-permute-start.20 = (f32[1,288,256]{2,1,0:T(8,128)S(1)}, f32[1,288,256]{2,1,0:T(8,128)S(1)}, u32[]{:S(2)}, u32[]{:S(2)}) collective-permute-start(f32[1,288,256]{2,1,0:T(8,128)S(1)} %add_add_fusion), channel_id=1, source_target_pairs={{0,64},{8,72},{16,80},{24,88},{32,96},{40,104},{48,112},{56,120},{... | collective-permute-start | bytes 884744 | tf_op jit(solution)/shard_map/ppermute | solution.py:367
  69.6 2.6 %collective-permute-done.19.refs_3_ = f32[1,288,256]{2,1,0:T(8,128)S(1)} collective-permute-done((f32[1,288,256]{2,1,0:T(8,128)S(1)}, f32[1,288,256]{2,1,0:T(8,128)S(1)}, u32[]{:S(2)}, u32[]{:S(2)}) %collective-permute-start.19) | collective-permute-done | bytes 294944 | tf_op jit(solution)/shard_map/ppermute | solution.py:367
  72.1 5.8 %collective-permute-done.20.refs_4_ = f32[1,288,256]{2,1,0:T(8,128)S(1)} collective-permute-done((f32[1,288,256]{2,1,0:T(8,128)S(1)}, f32[1,288,256]{2,1,0:T(8,128)S(1)}, u32[]{:S(2)}, u32[]{:S(2)}) %collective-permute-start.20) | collective-permute-done | bytes 294944 | tf_op jit(solution)/shard_map/ppermute | solution.py:367
  77.9 4.6 %solved.1 = f32[32,256]{1,0:T(8,128)S(1)} custom-call(f32[1,288,256]{2,1,0:T(8,128)S(1)} %get-tuple-element.49.refs_0_, f32[1,288,256]{2,1,0:T(8,128)S(1)} %collective-permute-done.17.refs_1_, f32[1,288,256]{2,1,0:T(8,128)S(1)} %collective-permute-done.18.refs_2_, f32[1,288,256]{2,1,0:T(8,128)S(1)} %collective-permute-done.19.refs_3_, ...), custom_call_target="tpu_custom_call" | custom-call | tf_op jit(solution)/shard_map/solved/pallas_call | solution.py:332
  82.5 13.9 %all_to_all.5 = f32[8,32,256]{2,1,0:T(8,128)S(1)} all-to-all(f32[8,32,256]{2,1,0:T(8,128)S(1)} %broadcast_in_dim.2), channel_id=1, replica_groups={{0,16,32,48,64,80,96,112},{8,24,40,56,72,88,104,120},{1,17,33,49,65,81,..., dimensions={0} | all-to-all | bytes 524288 | tf_op jit(solution)/shard_map/all_to_all | solution.py:457
  96.4 1.5 %collective-permute-done.21 = f32[8,32,256]{2,1,0:T(8,128)S(1)} collective-permute-done((f32[8,32,256]{2,1,0:T(8,128)S(1)}, f32[8,32,256]{2,1,0:T(8,128)S(1)}, u32[]{:S(2)}, u32[]{:S(2)}) %collective-permute-start.21) | collective-permute-done | bytes 262176 | tf_op jit(solution)/shard_map/ppermute | solution.py:367
  98.0 1.0 %copy.24 = f32[16,2,14,256]{3,0,2,1:T(8,128)} copy(f32[16,2,14,256]{3,2,1,0:T(8,128)S(1)} %bitcast.16) | data formatting | bytes 917504
  (22 shorter events, 0.4 us)
Async XLA Ops:
  1.0 16.8 %collective-permute-start.4 = (f32[16,32,128]{2,1,0:T(8,128)S(1)}, f32[16,32,128]{2,1,0:T(8,128)S(1)}, u32[]{:S(2)}, u32[]{:S(2)}) collective-permute-start(f32[16,32,128]{2,1,0:T(8,128)S(1)} %packed_tables.1.refs_0_), channel_id=1, source_target_pairs={{0,4},{1,5},{2,6},{3,7},{4,0},{5,1},{6,2},{7,3},{8,12},{9,13},{10,... | collective-permute-start | bytes 786440 | tf_op jit(solution)/shard_map/ppermute | solution.py:373
  5.0 9.0 %collective-permute-start = (f32[16,32,128]{2,1,0:T(8,128)S(1)}, f32[16,32,128]{2,1,0:T(8,128)S(1)}, u32[]{:S(2)}, u32[]{:S(2)}) collective-permute-start(f32[16,32,128]{2,1,0:T(8,128)S(1)} %packed_tables.1.refs_0_), channel_id=1, source_target_pairs={{0,1},{1,2},{2,3},{3,0},{4,5},{5,6},{6,7},{7,4},{8,9},{9,10},{10,1... | collective-permute-start | bytes 786440 | tf_op jit(solution)/shard_map/ppermute | solution.py:373
  6.5 7.9 %collective-permute-start.2 = (f32[16,32,128]{2,1,0:T(8,128)S(1)}, f32[16,32,128]{2,1,0:T(8,128)S(1)}, u32[]{:S(2)}, u32[]{:S(2)}) collective-permute-start(f32[16,32,128]{2,1,0:T(8,128)S(1)} %packed_tables.1.refs_0_), channel_id=1, source_target_pairs={{0,3},{1,0},{2,1},{3,2},{4,7},{5,4},{6,5},{7,6},{8,11},{9,8},{10,9... | collective-permute-start | bytes 786440 | tf_op jit(solution)/shard_map/ppermute | solution.py:373
  14.0 7.0 %collective-permute-start.1 = (f32[8,32,128]{2,1,0:T(8,128)S(1)}, f32[8,32,128]{2,1,0:T(8,128)S(1)}, u32[]{:S(2)}, u32[]{:S(2)}) collective-permute-start(f32[8,32,128]{2,1,0:T(8,128)S(1)} %slice.94), channel_id=1, source_target_pairs={{0,1},{1,2},{2,3},{3,0},{4,5},{5,6},{6,7},{7,4},{8,9},{9,10},{10,1... | collective-permute-start | bytes 393224 | tf_op jit(solution)/shard_map/ppermute | solution.py:373
  14.4 6.7 %collective-permute-start.3 = (f32[8,32,128]{2,1,0:T(8,128)S(1)}, f32[8,32,128]{2,1,0:T(8,128)S(1)}, u32[]{:S(2)}, u32[]{:S(2)}) collective-permute-start(f32[8,32,128]{2,1,0:T(8,128)S(1)} %slice.95), channel_id=1, source_target_pairs={{0,3},{1,0},{2,1},{3,2},{4,7},{5,4},{6,5},{7,6},{8,11},{9,8},{10,9... | collective-permute-start | bytes 393224 | tf_op jit(solution)/shard_map/ppermute | solution.py:373
  17.7 4.2 %copy-start = (s32[256,128]{1,0:T(8,128)S(1)}, s32[256,128]{1,0:T(8,128)}, u32[]{:S(2)}) copy-start(s32[256,128]{1,0:T(8,128)} %refs_4_.3) | copy-start | bytes 393220
  17.8 8.1 %collective-permute-start.5 = (f32[16,32,128]{2,1,0:T(8,128)S(1)}, f32[16,32,128]{2,1,0:T(8,128)S(1)}, u32[]{:S(2)}, u32[]{:S(2)}) collective-permute-start(f32[16,32,128]{2,1,0:T(8,128)S(1)} %collective-permute-done.4.refs_1_), channel_id=1, source_target_pairs={{0,1},{1,2},{2,3},{3,0},{4,5},{5,6},{6,7},{7,4},{8,9},{9,10},{10,1... | collective-permute-start | bytes 786440 | tf_op jit(solution)/shard_map/ppermute | solution.py:373
  17.8 8.1 %collective-permute-start.6 = (f32[16,32,128]{2,1,0:T(8,128)S(1)}, f32[16,32,128]{2,1,0:T(8,128)S(1)}, u32[]{:S(2)}, u32[]{:S(2)}) collective-permute-start(f32[16,32,128]{2,1,0:T(8,128)S(1)} %collective-permute-done.4.refs_1_), channel_id=1, source_target_pairs={{0,3},{1,0},{2,1},{3,2},{4,7},{5,4},{6,5},{7,6},{8,11},{9,8},{10,9... | collective-permute-start | bytes 786440 | tf_op jit(solution)/shard_map/ppermute | solution.py:373
  21.1 8.0 %collective-permute-start.7 = (f32[16,32,128]{2,1,0:T(8,128)S(1)}, f32[16,32,128]{2,1,0:T(8,128)S(1)}, u32[]{:S(2)}, u32[]{:S(2)}) collective-permute-start(f32[16,32,128]{2,1,0:T(8,128)S(1)} %constant_dynamic-update-slice_fusion.refs_0_), channel_id=1, source_target_pairs={{0,4},{1,5},{2,6},{3,7},{4,0},{5,1},{6,2},{7,3},{8,12},{9,13},{10,... | collective-permute-start | bytes 786440 | tf_op jit(solution)/shard_map/ppermute | solution.py:373
  34.1 2.6 %collective-permute-start.8 = (f32[2,288,256]{2,1,0:T(8,128)S(1)}, f32[2,288,256]{2,1,0:T(8,128)S(1)}, u32[]{:S(2)}, u32[]{:S(2)}) collective-permute-start(f32[2,288,256]{2,1,0:T(8,128)S(1)} %get-tuple-element.34), channel_id=1, source_target_pairs={{0,8},{8,0},{16,24},{24,16},{32,40},{40,32},{48,56},{56,48},{64,72... | collective-permute-start | bytes 1769480 | tf_op jit(solution)/shard_map/ppermute | solution.py:367
  36.1 8.2 %collective-permute-start.13 = (f32[1,288,256]{2,1,0:T(8,128)S(1)}, f32[1,288,256]{2,1,0:T(8,128)S(1)}, u32[]{:S(2)}, u32[]{:S(2)}) collective-permute-start(f32[1,288,256]{2,1,0:T(8,128)S(1)} %get-tuple-element.43), channel_id=1, source_target_pairs={{0,8},{8,0},{16,24},{24,16},{32,40},{40,32},{48,56},{56,48},{64,72... | collective-permute-start | bytes 884744 | tf_op jit(solution)/shard_map/ppermute | solution.py:367
  38.8 7.3 %collective-permute-start.9 = (f32[1,288,256]{2,1,0:T(8,128)S(1)}, f32[1,288,256]{2,1,0:T(8,128)S(1)}, u32[]{:S(2)}, u32[]{:S(2)}) collective-permute-start(f32[1,288,256]{2,1,0:T(8,128)S(1)} %get-tuple-element.39), channel_id=1, source_target_pairs={{0,8},{8,0},{16,24},{24,16},{32,40},{40,32},{48,56},{56,48},{64,72... | collective-permute-start | bytes 884744 | tf_op jit(solution)/shard_map/ppermute | solution.py:367
  38.9 10.7 %collective-permute-start.10 = (f32[2,144,256]{2,1,0:T(8,128)S(1)}, f32[2,144,256]{2,1,0:T(8,128)S(1)}, u32[]{:S(2)}, u32[]{:S(2)}) collective-permute-start(f32[2,144,256]{2,1,0:T(8,128)S(1)} %get-tuple-element.58), channel_id=1, source_target_pairs={{0,16},{8,24},{16,32},{24,40},{32,48},{40,56},{48,0},{56,8},{64,80... | collective-permute-start | bytes 884744 | tf_op jit(solution)/shard_map/ppermute | solution.py:367
  44.2 5.8 %collective-permute-start.11 = (f32[2,288,256]{2,1,0:T(8,128)S(1)}, f32[2,288,256]{2,1,0:T(8,128)S(1)}, u32[]{:S(2)}, u32[]{:S(2)}) collective-permute-start(f32[2,288,256]{2,1,0:T(8,128)S(1)} %get-tuple-element.42), channel_id=1, source_target_pairs={{0,8},{8,0},{16,24},{24,16},{32,40},{40,32},{48,56},{56,48},{64,72... | collective-permute-start | bytes 1769480 | tf_op jit(solution)/shard_map/ppermute | solution.py:367
  44.3 9.5 %collective-permute-start.12 = (f32[2,144,256]{2,1,0:T(8,128)S(1)}, f32[2,144,256]{2,1,0:T(8,128)S(1)}, u32[]{:S(2)}, u32[]{:S(2)}) collective-permute-start(f32[2,144,256]{2,1,0:T(8,128)S(1)} %get-tuple-element.57), channel_id=1, source_target_pairs={{0,48},{8,56},{16,0},{24,8},{32,16},{40,24},{48,32},{56,40},{64,11... | collective-permute-start | bytes 884744 | tf_op jit(solution)/shard_map/ppermute | solution.py:367
  49.7 12.6 %collective-permute-start.15 = (f32[1,288,256]{2,1,0:T(8,128)S(1)}, f32[1,288,256]{2,1,0:T(8,128)S(1)}, u32[]{:S(2)}, u32[]{:S(2)}) collective-permute-start(f32[1,288,256]{2,1,0:T(8,128)S(1)} %pad_maximum_fusion.4), channel_id=1, source_target_pairs={{0,16},{8,24},{16,32},{24,40},{32,48},{40,56},{48,0},{56,8},{64,80... | collective-permute-start | bytes 884744 | tf_op jit(solution)/shard_map/ppermute | solution.py:367
  55.9 6.3 %collective-permute-start.14 = (f32[1,288,256]{2,1,0:T(8,128)S(1)}, f32[1,288,256]{2,1,0:T(8,128)S(1)}, u32[]{:S(2)}, u32[]{:S(2)}) collective-permute-start(f32[1,288,256]{2,1,0:T(8,128)S(1)} %get-tuple-element.47), channel_id=1, source_target_pairs={{0,8},{8,0},{16,24},{24,16},{32,40},{40,32},{48,56},{56,48},{64,72... | collective-permute-start | bytes 884744 | tf_op jit(solution)/shard_map/ppermute | solution.py:367
  56.0 10.3 %collective-permute-start.16 = (f32[1,288,256]{2,1,0:T(8,128)S(1)}, f32[1,288,256]{2,1,0:T(8,128)S(1)}, u32[]{:S(2)}, u32[]{:S(2)}) collective-permute-start(f32[1,288,256]{2,1,0:T(8,128)S(1)} %pad_maximum_fusion.5), channel_id=1, source_target_pairs={{0,48},{8,56},{16,0},{24,8},{32,16},{40,24},{48,32},{56,40},{64,11... | collective-permute-start | bytes 884744 | tf_op jit(solution)/shard_map/ppermute | solution.py:367
  59.0 10.6 %collective-permute-start.18 = (f32[1,288,256]{2,1,0:T(8,128)S(1)}, f32[1,288,256]{2,1,0:T(8,128)S(1)}, u32[]{:S(2)}, u32[]{:S(2)}) collective-permute-start(f32[1,288,256]{2,1,0:T(8,128)S(1)} %pad_maximum_fusion.2), channel_id=1, source_target_pairs={{0,16},{8,24},{16,32},{24,40},{32,48},{40,56},{48,0},{56,8},{64,80... | collective-permute-start | bytes 884744 | tf_op jit(solution)/shard_map/ppermute | solution.py:367
  59.0 13.1 %collective-permute-start.19 = (f32[1,288,256]{2,1,0:T(8,128)S(1)}, f32[1,288,256]{2,1,0:T(8,128)S(1)}, u32[]{:S(2)}, u32[]{:S(2)}) collective-permute-start(f32[1,288,256]{2,1,0:T(8,128)S(1)} %pad_maximum_fusion.3), channel_id=1, source_target_pairs={{0,48},{8,56},{16,0},{24,8},{32,16},{40,24},{48,32},{56,40},{64,11... | collective-permute-start | bytes 884744 | tf_op jit(solution)/shard_map/ppermute | solution.py:367
  66.4 11.5 %copy-start.1 = (f32[256]{0:T(256)S(1)}, f32[256]{0:T(256)}, u32[]{:S(2)}) copy-start(f32[256]{0:T(256)} %param.13) | copy-start | bytes 3076
  68.4 3.7 %collective-permute-start.17 = (f32[1,288,256]{2,1,0:T(8,128)S(1)}, f32[1,288,256]{2,1,0:T(8,128)S(1)}, u32[]{:S(2)}, u32[]{:S(2)}) collective-permute-start(f32[1,288,256]{2,1,0:T(8,128)S(1)} %get-tuple-element.50), channel_id=1, source_target_pairs={{0,8},{8,0},{16,24},{24,16},{32,40},{40,32},{48,56},{56,48},{64,72... | collective-permute-start | bytes 884744 | tf_op jit(solution)/shard_map/ppermute | solution.py:367
  68.5 9.5 %collective-permute-start.20 = (f32[1,288,256]{2,1,0:T(8,128)S(1)}, f32[1,288,256]{2,1,0:T(8,128)S(1)}, u32[]{:S(2)}, u32[]{:S(2)}) collective-permute-start(f32[1,288,256]{2,1,0:T(8,128)S(1)} %add_add_fusion), channel_id=1, source_target_pairs={{0,64},{8,72},{16,80},{24,88},{32,96},{40,104},{48,112},{56,120},{... | collective-permute-start | bytes 884744 | tf_op jit(solution)/shard_map/ppermute | solution.py:367
  96.4 1.5 %collective-permute-start.21 = (f32[8,32,256]{2,1,0:T(8,128)S(1)}, f32[8,32,256]{2,1,0:T(8,128)S(1)}, u32[]{:S(2)}, u32[]{:S(2)}) collective-permute-start(f32[8,32,256]{2,1,0:T(8,128)S(1)} %all_to_all.5), channel_id=1, source_target_pairs={{0,8},{8,0},{16,24},{24,16},{32,40},{40,32},{48,56},{56,48},{64,72... | collective-permute-start | bytes 786440 | tf_op jit(solution)/shard_map/ppermute | solution.py:367

commit v5 on v4

--- a/solution.py
+++ b/solution.py
@@ -22,7 +22,7 @@
 FIT_POINTS = 4001
 ROWS = 16
 HALF = 16
-SOLVE_STEPS = 60
+SOLVE_STEPS = 40
 TOLERANCE = 1e-6
 
 
@@ -161,10 +161,11 @@
             a, b, c, d = sums
             columns = slice(n * width, (n + 1) * width)
             for tone, (re, im) in enumerate(((a - b, c + d), (a + b, c - d))):
-                for part, (value, top, bottom) in enumerate(((re, with_re, with_im), (im, with_im, with_re))):
+                for part, (value, ref) in enumerate(((re, with_re), (im, with_im))):
                     packed = value.astype(jnp.bfloat16)
-                    top[tone, here, columns] = packed
-                    bottom[tone, below, columns] = packed
+                    ref[tone, here, columns] = packed
+                    if part == 0:
+                        with_im[tone, below, columns] = packed
                     rest = (value - packed.astype(jnp.float32)).astype(jnp.bfloat16)
                     lo[tone, here, slice(part * half + n * width, part * half + (n + 1) * width)] = rest
 
@@ -178,13 +179,14 @@
             y_hi = y.astype(jnp.bfloat16)
             y_lo = (y - y_hi.astype(jnp.float32)).astype(jnp.bfloat16)
             for part, ref in enumerate((with_re, with_im)):
-                ref[tone, 2 * users : 2 * users + 2 * HALF] = y_hi[:, part * half : (part + 1) * half]
-                ref[tone, 2 * users + 2 * HALF :] = y_lo[:, part * half : (part + 1) * half]
+                end = ref.shape[1]
+                ref[tone, end - 4 * HALF : end - 2 * HALF] = y_hi[:, part * half : (part + 1) * half]
+                ref[tone, end - 2 * HALF :] = y_lo[:, part * half : (part + 1) * half]
             by_re = product(with_re[tone], with_re[tone, :users])
             by_im = product(with_im[tone], with_im[tone, :users])
-            plain, crossed = by_re[:users] + by_im[:users], by_im[users : 2 * users] - by_re[users : 2 * users]
-            out_ref[slot, :users, :] = plain + crossed
-            filtered = by_re[2 * users :] + by_im[2 * users :]
+            crossed = by_im[users : 2 * users]
+            out_ref[slot, :users, :] = (by_re[:users] + by_im[:users]) + (crossed - crossed.T)
+            filtered = by_re[users:] + by_im[2 * users :]
             rest = product(y_hi, lo[tone])
             out_ref[slot, users:, :] = filtered[: 2 * HALF] + (filtered[2 * HALF :] + rest)
 
@@ -207,14 +209,15 @@
     wide = received.shape[2]
     f32, bf16 = jnp.float32, jnp.bfloat16
     vmem = pl.BlockSpec(memory_space=pltpu.VMEM)
-    channel = pltpu.VMEM((2, 2 * users + 4 * HALF, wide // 2), bf16)
+    channel_re = pltpu.VMEM((2, users + 4 * HALF, wide // 2), bf16)
+    channel_im = pltpu.VMEM((2, 2 * users + 4 * HALF, wide // 2), bf16)
     rest = pltpu.VMEM((2, users, wide), bf16)
     return pl.pallas_call(
         functools.partial(tone_kernel, distance, planes),
         in_specs=[vmem] * (1 + len(state)),
         out_specs=[vmem, vmem],
         out_shape=[pltpu.VMEM((len(planes), users + 2 * HALF, users), f32)] * 2,
-        scratch_shapes=[channel, channel, rest] * len(planes),
+        scratch_shapes=[channel_re, channel_im, rest] * len(planes),
         compiler_params=pltpu.CompilerParams(vmem_limit_bytes=16 << 20),
         name="tone_systems",
     )(in_vmem(received), *state)
@@ -228,7 +231,7 @@
 
 
 def solve_kernel(*refs):
-    *part_refs, regularizer_ref, out_ref, system_ref, parts, x_ref, r_ref, p_ref, work = refs
+    *part_refs, regularizer_ref, out_ref, system_ref, parts, x_ref, r_ref, p_ref, q_ref, work = refs
     system_ref[...] = sum(ref[0] for ref in part_refs)
     users = regularizer_ref.shape[1]
     f32 = jnp.float32
@@ -273,30 +276,34 @@
 
     norm = together(right * right)
     goal = norm * (TOLERANCE * TOLERANCE)
-    x_ref[...] = jnp.zeros_like(right)
+    nothing = jnp.zeros_like(right)
+    x_ref[...], p_ref[...], q_ref[...] = nothing, nothing, nothing
     r_ref[...] = right
-    p_ref[...] = right
 
     def advance(state):
-        done, _, rr = state
+        done, _, earlier, alpha = state
         for _ in range(2):
-            p = p_ref[...]
-            q = applied(p)
-            pq = together(p * q)
-            alpha = jnp.where(pq > 0.0, rr / pq, 0.0)
+            r = r_ref[...]
+            applied_r = applied(r)
+            rr = together(r * r)
+            curvature = together(r * applied_r)
+            beta = jnp.where(earlier > 0.0, rr / earlier, 0.0)
+            curvature = curvature - jnp.where(alpha > 0.0, beta * rr / alpha, 0.0)
+            alpha = jnp.where(curvature > 0.0, rr / curvature, 0.0)
+            p = r + beta * p_ref[...]
+            q = applied_r + beta * q_ref[...]
+            p_ref[...], q_ref[...] = p, q
             x_ref[...] += alpha * p
-            r = r_ref[...] - alpha * q
-            r_ref[...] = r
-            latest = together(r * r)
-            p_ref[...] = r + jnp.where(rr > 0.0, latest / rr, 0.0) * p
-            rr = latest
-        return done + 2, jnp.max(jnp.where(rr <= goal, 0, 1)), rr
+            r_ref[...] = r - alpha * q
+            earlier = rr
+        r = r_ref[...]
+        return done + 2, jnp.max(jnp.where(together(r * r) <= goal, 0, 1)), earlier, alpha
 
     def unfinished(state):
-        done, left, _ = state
-        return (left > 0) & (done < SOLVE_STEPS)
-
-    _, left, _ = lax.while_loop(unfinished, advance, (0, jnp.max(jnp.where(norm <= goal, 0, 1)), norm))
+        return (state[1] > 0) & (state[0] < SOLVE_STEPS)
+
+    zero = jnp.zeros_like(norm)
+    _, left, _, _ = lax.while_loop(unfinished, advance, (0, jnp.max(jnp.where(norm <= goal, 0, 1)), zero, zero))
     out_ref[...] = x_ref[...] * across
 
     @pl.when(left > 0)
@@ -340,6 +347,7 @@
             pair,
             pair,
             pair,
+            pair,
             pltpu.VMEM((2, users + HALF, users), f32),
         ],
         compiler_params=pltpu.CompilerParams(vmem_limit_bytes=12 << 20),
@@ -375,6 +383,7 @@
 
 def gathered_tables(own):
     half = own.shape[0] // 2
+
     across = over_sc(own, 1, 0)
     up, down = over_sc(own, 0, 1), over_sc(own, 0, -1)
     up_twice, down_twice = over_sc(up[:half], 0, 1), over_sc(down[half:], 0, -1)
@@ -442,13 +451,12 @@
     up, down = around(farthest[:, :top], 1), around(farthest[:, top:], -1)
     up_own = systems(1, (0,), farthest, up_far[0])
     kept, other = systems(3, (0, 1), up_own[0])
+    last_kept, last_other = systems(0, (1,), kept)
     up_far, up_own = joined(up_far, up[1:], 0), joined(up_own, up[:1], 0)
     down_far, down_own = joined((kept[1:], other[1:]), down[1:], 1), joined((kept[:1], other[:1]), down[:1], 1)
     up, down = around(up_far, 1), around(down_far, -1)
-    kept, other = systems(0, (1,), up_far, down_far)
-    up_own, down_own, kept = lax.optimization_barrier((up_own, down_own, kept))
     own_up, own_down = around(up_own, 1), around(down_own, -1)
-    across = (kept + other) + (up + down)
+    across = (last_kept + last_other) + (up + down)
     kept, other = systems(0, (0,), across)
     across = over_ap(across, 1, 0, 0)
     own_tone = solved([kept, other, own_up, own_down, across], regularizer)

time: 100 us -> 96.8 us (0.968)
  waiting for transfers between devices: 30.3 us -> 28.1 us
  Pallas kernels: 23.7 us -> 22.2 us
    ppermute x14, waiting for transfers between devices: 21 us -> 18.9 us  [over_ap(): return lax.ppermute(value, 'ap', pairs)]
    pallas_call x6, Pallas kernels: 15.4 us -> 14.3 us  [tone_systems(): pl.pallas_call(functools.partial(tone_kernel, distance, planes), in_specs...]
  transfers between devices with their start and end apart: 22 -> 22, of which waited for: 9 -> 9; matrix products, arithmetic and copies ran while one was open for 3% -> 4% of each run, Pallas kernels for 13% -> 13%
where the time goes in v5:
time: 96.8 us; the launch traced here: 95.6 us
  waiting for transfers between devices  28.1 us (29%)
  starting transfers between devices  26.7 us (28%)
  Pallas kernels  22.2 us (23%)
  blocking collectives  13.7 us (14%)
  local copies, waits for them, and re-layouts  3.32 us (3%)
  other arithmetic  1.28 us (1%)
    ppermute x14, waiting for transfers between devices, over_ap(): return lax.ppermute(value, 'ap', pairs)  18.9 us
    ppermute x8, starting transfers between devices, over_sc(): return lax.ppermute(value, 'sc', pairs)  14.4 us
    pallas_call x6, Pallas kernels, tone_systems(): pl.pallas_call(functools.partial(tone_kernel, distance, planes), in_specs...  14.3 us
    all_to_all x1, blocking collectives, all_steps(): lax.all_to_all(jnp.broadcast_to(own_tone[None], (chips, *own_tone.shape))...  13.7 us
    ppermute x14, starting transfers between devices, over_ap(): return lax.ppermute(value, 'ap', pairs)  12.2 us
    ppermute x8, waiting for transfers between devices, over_sc(): return lax.ppermute(value, 'sc', pairs)  9.27 us
    pallas_call x1, Pallas kernels, solved(): pl.pallas_call(solve_kernel, in_specs=[vmem] * (len(systems) + 1), out_sp...  4.14 us
    pallas_call x2, Pallas kernels, prepared(): pl.pallas_call(functools.partial(prepare_kernel, slots, len(tables), tone...  2.77 us
  transfers between devices with their start and end apart: 22, of which 9 were waited for; matrix products, arithmetic and copies ran while one was open for 4% of the time, Pallas kernels for 13%

profile of v5, /device:TPU:0, one launch (start us, length us, event | category | flops | bytes accessed | tf_op | source)
XLA Modules:
  0.0 95.6 jit_solution(13311099954575031232)
XLA Ops:
  0.0 1.0 %packed_tables.1.refs_0_ = f32[16,32,128]{2,1,0:T(8,128)S(1)} custom-call(f32[4,32,128]{2,1,0:T(8,128)} %refs_0_.1, f32[4,32,128]{2,1,0:T(8,128)} %refs_1_.1, f32[4,32,128]{2,1,0:T(8,128)} %refs_2_.1, f32[4,32,128]{2,1,0:T(8,128)} %refs_3_.1), custom_call_target="tpu_custom_call" | custom-call | tf_op jit(solution)/shard_map/packed_tables/pallas_call | solution.py:410
  1.0 4.1 %collective-permute-start.4 = (f32[16,32,128]{2,1,0:T(8,128)S(1)}, f32[16,32,128]{2,1,0:T(8,128)S(1)}, u32[]{:S(2)}, u32[]{:S(2)}) collective-permute-start(f32[16,32,128]{2,1,0:T(8,128)S(1)} %packed_tables.1.refs_0_), channel_id=1, source_target_pairs={{0,4},{1,5},{2,6},{3,7},{4,0},{5,1},{6,2},{7,3},{8,12},{9,13},{10,... | collective-permute-start | bytes 786440 | tf_op jit(solution)/shard_map/ppermute | solution.py:381
  5.0 1.5 %collective-permute-start = (f32[16,32,128]{2,1,0:T(8,128)S(1)}, f32[16,32,128]{2,1,0:T(8,128)S(1)}, u32[]{:S(2)}, u32[]{:S(2)}) collective-permute-start(f32[16,32,128]{2,1,0:T(8,128)S(1)} %packed_tables.1.refs_0_), channel_id=1, source_target_pairs={{0,1},{1,2},{2,3},{3,0},{4,5},{5,6},{6,7},{7,4},{8,9},{9,10},{10,1... | collective-permute-start | bytes 786440 | tf_op jit(solution)/shard_map/ppermute | solution.py:381
  6.5 1.7 %collective-permute-start.2 = (f32[16,32,128]{2,1,0:T(8,128)S(1)}, f32[16,32,128]{2,1,0:T(8,128)S(1)}, u32[]{:S(2)}, u32[]{:S(2)}) collective-permute-start(f32[16,32,128]{2,1,0:T(8,128)S(1)} %packed_tables.1.refs_0_), channel_id=1, source_target_pairs={{0,3},{1,0},{2,1},{3,2},{4,7},{5,4},{6,5},{7,6},{8,11},{9,8},{10,9... | collective-permute-start | bytes 786440 | tf_op jit(solution)/shard_map/ppermute | solution.py:381
  8.3 1.5 %reshape.10 = f32[16,2,14,512]{3,0,2,1:T(8,128)S(1)} reshape(f32[16,2,14,4,128]{4,3,0,2,1:T(4,128)} %bitcast.17) | data formatting | bytes 1835008 | tf_op jit(solution)/shard_map/reshape | solution.py:360
  9.8 0.1 fusion.1
  9.9 0.5 copy_bitcast_fusion
  10.5 3.6 %collective-permute-done.refs_2_ = f32[16,32,128]{2,1,0:T(8,128)S(1)} collective-permute-done((f32[16,32,128]{2,1,0:T(8,128)S(1)}, f32[16,32,128]{2,1,0:T(8,128)S(1)}, u32[]{:S(2)}, u32[]{:S(2)}) %collective-permute-start) | collective-permute-done | bytes 262176 | tf_op jit(solution)/shard_map/ppermute | solution.py:381
  14.0 0.3 collective-permute-start.1
  14.4 0.0 collective-permute-done.2.refs_3_
  14.4 3.0 %collective-permute-start.3 = (f32[8,32,128]{2,1,0:T(8,128)S(1)}, f32[8,32,128]{2,1,0:T(8,128)S(1)}, u32[]{:S(2)}, u32[]{:S(2)}) collective-permute-start(f32[8,32,128]{2,1,0:T(8,128)S(1)} %slice.95), channel_id=1, source_target_pairs={{0,3},{1,0},{2,1},{3,2},{4,7},{5,4},{6,5},{7,6},{8,11},{9,8},{10,9... | collective-permute-start | bytes 393224 | tf_op jit(solution)/shard_map/ppermute | solution.py:381
  17.4 0.3 fusion
  17.7 0.0 copy-start
  17.7 0.0 collective-permute-done.4.refs_1_
  17.8 0.1 collective-permute-start.5
  17.8 3.2 %collective-permute-start.6 = (f32[16,32,128]{2,1,0:T(8,128)S(1)}, f32[16,32,128]{2,1,0:T(8,128)S(1)}, u32[]{:S(2)}, u32[]{:S(2)}) collective-permute-start(f32[16,32,128]{2,1,0:T(8,128)S(1)} %collective-permute-done.4.refs_1_), channel_id=1, source_target_pairs={{0,3},{1,0},{2,1},{3,2},{4,7},{5,4},{6,5},{7,6},{8,11},{9,8},{10,9... | collective-permute-start | bytes 786440 | tf_op jit(solution)/shard_map/ppermute | solution.py:381
  21.1 0.0 collective-permute-done.1
  21.1 0.0 collective-permute-done.3
  21.1 0.4 collective-permute-start.7
  21.6 0.3 select_maximum_fusion.1
  21.8 0.1 pad_maximum_fusion.y_ref
  22.0 1.4 %prepared.2 = (f32[4,4,2,256,128]{4,3,2,1,0:T(8,128)S(1)}, f32[8,4,2,256,128]{4,3,2,1,0:T(8,128)S(1)}) custom-call(f32[16,32,128]{2,1,0:T(8,128)S(1)} %packed_tables.1.refs_0_, f32[16,32,128]{2,1,0:T(8,128)S(1)} %collective-permute-done.4.refs_1_, f32[16,32,128]{2,1,0:T(8,128)S(1)} %collective-permute-done.refs_2_, ...), custom_call_target="tpu_custom_call" | custom-call | tf_op jit(solution)/shard_map/prepared/pallas_call | solution.py:122
  23.4 2.5 %collective-permute-done.5.refs_1_ = f32[16,32,128]{2,1,0:T(8,128)S(1)} collective-permute-done((f32[16,32,128]{2,1,0:T(8,128)S(1)}, f32[16,32,128]{2,1,0:T(8,128)S(1)}, u32[]{:S(2)}, u32[]{:S(2)}) %collective-permute-start.5) | collective-permute-done | bytes 262176 | tf_op jit(solution)/shard_map/ppermute | solution.py:381
  25.9 0.0 collective-permute-done.6.refs_2_
  25.9 3.2 %collective-permute-done.7.refs_3_ = f32[16,32,128]{2,1,0:T(8,128)S(1)} collective-permute-done((f32[16,32,128]{2,1,0:T(8,128)S(1)}, f32[16,32,128]{2,1,0:T(8,128)S(1)}, u32[]{:S(2)}, u32[]{:S(2)}) %collective-permute-start.7) | collective-permute-done | bytes 262176 | tf_op jit(solution)/shard_map/ppermute | solution.py:381
  29.1 1.4 %prepared.3 = (f32[4,4,2,256,128]{4,3,2,1,0:T(8,128)S(1)}, f32[8,4,2,256,128]{4,3,2,1,0:T(8,128)S(1)}) custom-call(f32[16,32,128]{2,1,0:T(8,128)S(1)} %constant_dynamic-update-slice_fusion.refs_0_, f32[16,32,128]{2,1,0:T(8,128)S(1)} %collective-permute-done.5.refs_1_, ...), custom_call_target="tpu_custom_call", output_to_operand_aliasing={{0}: (5, {}), {1}: (6, {})} | custom-call | tf_op jit(solution)/shard_map/prepared/pallas_call | solution.py:122
  30.4 3.4 %tone_systems.6 = (f32[2,288,256]{2,1,0:T(8,128)S(1)}, f32[2,288,256]{2,1,0:T(8,128)S(1)}) custom-call(f32[16,32,1024]{2,1,0:T(8,128)S(1)} %pad_maximum_fusion.y_ref, f32[4,4,2,256,128]{4,3,2,1,0:T(8,128)S(1)} %get-tuple-element.28.lead, f32[8,4,2,256,128]{4,3,2,1,0:T(8,128)S(1)} %get-tuple-element.29.turn), custom_call_target="tpu_custom_call" | custom-call | tf_op jit(solution)/shard_map/tone_systems/pallas_call | solution.py:215
  33.8 0.1 collective-permute-start.8
  33.9 1.9 %tone_systems.7 = (f32[1,288,256]{2,1,0:T(8,128)S(1)}, f32[1,288,256]{2,1,0:T(8,128)S(1)}) custom-call(f32[16,32,1024]{2,1,0:T(8,128)S(1)} %pad_maximum_fusion.y_ref, f32[4,4,2,256,128]{4,3,2,1,0:T(8,128)S(1)} %get-tuple-element.28.lead, f32[8,4,2,256,128]{4,3,2,1,0:T(8,128)S(1)} %get-tuple-element.29.turn), custom_call_target="tpu_custom_call" | custom-call | tf_op jit(solution)/shard_map/tone_systems/pallas_call | solution.py:215
  35.8 0.5 collective-permute-start.10
  36.3 0.1 add.45
  36.4 1.9 %tone_systems.8 = (f32[1,288,256]{2,1,0:T(8,128)S(1)}, f32[1,288,256]{2,1,0:T(8,128)S(1)}) custom-call(f32[16,32,1024]{2,1,0:T(8,128)S(1)} %pad_maximum_fusion.y_ref, f32[4,4,2,256,128]{4,3,2,1,0:T(8,128)S(1)} %get-tuple-element.28.lead, f32[8,4,2,256,128]{4,3,2,1,0:T(8,128)S(1)} %get-tuple-element.29.turn), custom_call_target="tpu_custom_call" | custom-call | tf_op jit(solution)/shard_map/tone_systems/pallas_call | solution.py:215
  38.3 0.1 collective-permute-start.17
  38.4 1.8 %collective-permute-start.11 = (f32[2,144,256]{2,1,0:T(8,128)S(1)}, f32[2,144,256]{2,1,0:T(8,128)S(1)}, u32[]{:S(2)}, u32[]{:S(2)}) collective-permute-start(f32[2,144,256]{2,1,0:T(8,128)S(1)} %get-tuple-element.52), channel_id=1, source_target_pairs={{0,16},{8,24},{16,32},{24,40},{32,48},{40,56},{48,0},{56,8},{64,80... | collective-permute-start | bytes 884744 | tf_op jit(solution)/shard_map/ppermute | solution.py:375
  40.2 3.3 %tone_systems.9 = (f32[2,288,256]{2,1,0:T(8,128)S(1)}, f32[2,288,256]{2,1,0:T(8,128)S(1)}) custom-call(f32[16,32,1024]{2,1,0:T(8,128)S(1)} %pad_maximum_fusion.y_ref, f32[4,4,2,256,128]{4,3,2,1,0:T(8,128)S(1)} %get-tuple-element.28.lead, f32[8,4,2,256,128]{4,3,2,1,0:T(8,128)S(1)} %get-tuple-element.29.turn), custom_call_target="tpu_custom_call" | custom-call | tf_op jit(solution)/shard_map/tone_systems/pallas_call | solution.py:215
  43.5 0.1 collective-permute-start.13
  43.7 1.7 %collective-permute-start.14 = (f32[2,144,256]{2,1,0:T(8,128)S(1)}, f32[2,144,256]{2,1,0:T(8,128)S(1)}, u32[]{:S(2)}, u32[]{:S(2)}) collective-permute-start(f32[2,144,256]{2,1,0:T(8,128)S(1)} %get-tuple-element.51), channel_id=1, source_target_pairs={{0,48},{8,56},{16,0},{24,8},{32,16},{40,24},{48,32},{56,40},{64,11... | collective-permute-start | bytes 884744 | tf_op jit(solution)/shard_map/ppermute | solution.py:375
  45.4 1.9 %tone_systems.10 = (f32[1,288,256]{2,1,0:T(8,128)S(1)}, f32[1,288,256]{2,1,0:T(8,128)S(1)}) custom-call(f32[16,32,1024]{2,1,0:T(8,128)S(1)} %pad_maximum_fusion.y_ref, f32[4,4,2,256,128]{4,3,2,1,0:T(8,128)S(1)} %get-tuple-element.28.lead, f32[8,4,2,256,128]{4,3,2,1,0:T(8,128)S(1)} %get-tuple-element.29.turn), custom_call_target="tpu_custom_call" | custom-call | tf_op jit(solution)/shard_map/tone_systems/pallas_call | solution.py:215
  47.3 0.2 collective-permute-start.9
  47.5 0.0 collective-permute-done.17
  47.5 1.5 %collective-permute-done.11 = f32[2,144,256]{2,1,0:T(8,128)S(1)} collective-permute-done((f32[2,144,256]{2,1,0:T(8,128)S(1)}, f32[2,144,256]{2,1,0:T(8,128)S(1)}, u32[]{:S(2)}, u32[]{:S(2)}) %collective-permute-start.11) | collective-permute-done | bytes 294944 | tf_op jit(solution)/shard_map/ppermute | solution.py:375
  49.0 0.1 slice_add_fusion.3
  49.1 0.4 collective-permute-start.12
  49.5 0.1 slice_add_fusion
  49.6 3.5 %collective-permute-done.14 = f32[2,144,256]{2,1,0:T(8,128)S(1)} collective-permute-done((f32[2,144,256]{2,1,0:T(8,128)S(1)}, f32[2,144,256]{2,1,0:T(8,128)S(1)}, u32[]{:S(2)}, u32[]{:S(2)}) %collective-permute-start.14) | collective-permute-done | bytes 294944 | tf_op jit(solution)/shard_map/ppermute | solution.py:375
  53.1 0.1 fusion.3
  53.2 2.9 %collective-permute-start.15 = (f32[1,288,256]{2,1,0:T(8,128)S(1)}, f32[1,288,256]{2,1,0:T(8,128)S(1)}, u32[]{:S(2)}, u32[]{:S(2)}) collective-permute-start(f32[1,288,256]{2,1,0:T(8,128)S(1)} %pad_maximum_fusion.3), channel_id=1, source_target_pairs={{0,48},{8,56},{16,0},{24,8},{32,16},{40,24},{48,32},{56,40},{64,11... | collective-permute-start | bytes 884744 | tf_op jit(solution)/shard_map/ppermute | solution.py:375
  56.2 0.1 collective-permute-start.18
  56.3 3.3 %collective-permute-start.19 = (f32[1,288,256]{2,1,0:T(8,128)S(1)}, f32[1,288,256]{2,1,0:T(8,128)S(1)}, u32[]{:S(2)}, u32[]{:S(2)}) collective-permute-start(f32[1,288,256]{2,1,0:T(8,128)S(1)} %pad_maximum_fusion.5), channel_id=1, source_target_pairs={{0,48},{8,56},{16,0},{24,8},{32,16},{40,24},{48,32},{56,40},{64,11... | collective-permute-start | bytes 884744 | tf_op jit(solution)/shard_map/ppermute | solution.py:375
  59.6 4.0 %collective-permute-done.15 = f32[1,288,256]{2,1,0:T(8,128)S(1)} collective-permute-done((f32[1,288,256]{2,1,0:T(8,128)S(1)}, f32[1,288,256]{2,1,0:T(8,128)S(1)}, u32[]{:S(2)}, u32[]{:S(2)}) %collective-permute-start.15) | collective-permute-done | bytes 294944 | tf_op jit(solution)/shard_map/ppermute | solution.py:375
  63.6 0.1 add_add_fusion
  63.6 0.0 copy-start.1
  63.7 1.9 %tone_systems.11 = (f32[1,288,256]{2,1,0:T(8,128)S(1)}, f32[1,288,256]{2,1,0:T(8,128)S(1)}) custom-call(f32[16,32,1024]{2,1,0:T(8,128)S(1)} %pad_maximum_fusion.y_ref, f32[4,4,2,256,128]{4,3,2,1,0:T(8,128)S(1)} %get-tuple-element.28.lead, f32[8,4,2,256,128]{4,3,2,1,0:T(8,128)S(1)} %get-tuple-element.29.turn), custom_call_target="tpu_custom_call" | custom-call | tf_op jit(solution)/shard_map/tone_systems/pallas_call | solution.py:215
  65.6 0.0 collective-permute-start.16
  65.6 1.1 %collective-permute-start.20 = (f32[1,288,256]{2,1,0:T(8,128)S(1)}, f32[1,288,256]{2,1,0:T(8,128)S(1)}, u32[]{:S(2)}, u32[]{:S(2)}) collective-permute-start(f32[1,288,256]{2,1,0:T(8,128)S(1)} %add_add_fusion), channel_id=1, source_target_pairs={{0,64},{8,72},{16,80},{24,88},{32,96},{40,104},{48,112},{56,120},{... | collective-permute-start | bytes 884744 | tf_op jit(solution)/shard_map/ppermute | solution.py:375
  66.7 0.0 collective-permute-done.18.refs_2_
  66.7 1.8 %collective-permute-done.19.refs_3_ = f32[1,288,256]{2,1,0:T(8,128)S(1)} collective-permute-done((f32[1,288,256]{2,1,0:T(8,128)S(1)}, f32[1,288,256]{2,1,0:T(8,128)S(1)}, u32[]{:S(2)}, u32[]{:S(2)}) %collective-permute-start.19) | collective-permute-done | bytes 294944 | tf_op jit(solution)/shard_map/ppermute | solution.py:375
  68.5 0.0 collective-permute-done.16.refs_1_
  68.5 6.5 %collective-permute-done.20.refs_4_ = f32[1,288,256]{2,1,0:T(8,128)S(1)} collective-permute-done((f32[1,288,256]{2,1,0:T(8,128)S(1)}, f32[1,288,256]{2,1,0:T(8,128)S(1)}, u32[]{:S(2)}, u32[]{:S(2)}) %collective-permute-start.20) | collective-permute-done | bytes 294944 | tf_op jit(solution)/shard_map/ppermute | solution.py:375
  75.0 4.1 %solved.1 = f32[32,256]{1,0:T(8,128)S(1)} custom-call(f32[1,288,256]{2,1,0:T(8,128)S(1)} %get-tuple-element.44.refs_0_, f32[1,288,256]{2,1,0:T(8,128)S(1)} %collective-permute-done.16.refs_1_, f32[1,288,256]{2,1,0:T(8,128)S(1)} %collective-permute-done.18.refs_2_, f32[1,288,256]{2,1,0:T(8,128)S(1)} %collective-permute-done.19.refs_3_, ...), custom_call_target="tpu_custom_call" | custom-call | tf_op jit(solution)/shard_map/solved/pallas_call | solution.py:339
  79.2 13.7 %all_to_all.5 = f32[8,32,256]{2,1,0:T(8,128)S(1)} all-to-all(f32[8,32,256]{2,1,0:T(8,128)S(1)} %broadcast_in_dim.2), channel_id=1, replica_groups={{0,16,32,48,64,80,96,112},{8,24,40,56,72,88,104,120},{1,17,33,49,65,81,..., dimensions={0} | all-to-all | bytes 524288 | tf_op jit(solution)/shard_map/all_to_all | solution.py:465
  92.9 0.0 collective-permute-start.21
  92.9 1.5 %collective-permute-done.21 = f32[8,32,256]{2,1,0:T(8,128)S(1)} collective-permute-done((f32[8,32,256]{2,1,0:T(8,128)S(1)}, f32[8,32,256]{2,1,0:T(8,128)S(1)}, u32[]{:S(2)}, u32[]{:S(2)}) %collective-permute-start.21) | collective-permute-done | bytes 262176 | tf_op jit(solution)/shard_map/ppermute | solution.py:375
  94.6 1.0 %copy.24 = f32[16,2,14,256]{3,0,2,1:T(8,128)} copy(f32[16,2,14,256]{3,2,1,0:T(8,128)S(1)} %bitcast.16) | data formatting | bytes 917504
  (22 shorter events, 0.4 us)
Async XLA Ops:
  1.0 16.8 %collective-permute-start.4 = (f32[16,32,128]{2,1,0:T(8,128)S(1)}, f32[16,32,128]{2,1,0:T(8,128)S(1)}, u32[]{:S(2)}, u32[]{:S(2)}) collective-permute-start(f32[16,32,128]{2,1,0:T(8,128)S(1)} %packed_tables.1.refs_0_), channel_id=1, source_target_pairs={{0,4},{1,5},{2,6},{3,7},{4,0},{5,1},{6,2},{7,3},{8,12},{9,13},{10,... | collective-permute-start | bytes 786440 | tf_op jit(solution)/shard_map/ppermute | solution.py:381
  5.0 9.0 %collective-permute-start = (f32[16,32,128]{2,1,0:T(8,128)S(1)}, f32[16,32,128]{2,1,0:T(8,128)S(1)}, u32[]{:S(2)}, u32[]{:S(2)}) collective-permute-start(f32[16,32,128]{2,1,0:T(8,128)S(1)} %packed_tables.1.refs_0_), channel_id=1, source_target_pairs={{0,1},{1,2},{2,3},{3,0},{4,5},{5,6},{6,7},{7,4},{8,9},{9,10},{10,1... | collective-permute-start | bytes 786440 | tf_op jit(solution)/shard_map/ppermute | solution.py:381
  6.5 7.9 %collective-permute-start.2 = (f32[16,32,128]{2,1,0:T(8,128)S(1)}, f32[16,32,128]{2,1,0:T(8,128)S(1)}, u32[]{:S(2)}, u32[]{:S(2)}) collective-permute-start(f32[16,32,128]{2,1,0:T(8,128)S(1)} %packed_tables.1.refs_0_), channel_id=1, source_target_pairs={{0,3},{1,0},{2,1},{3,2},{4,7},{5,4},{6,5},{7,6},{8,11},{9,8},{10,9... | collective-permute-start | bytes 786440 | tf_op jit(solution)/shard_map/ppermute | solution.py:381
  14.0 7.0 %collective-permute-start.1 = (f32[8,32,128]{2,1,0:T(8,128)S(1)}, f32[8,32,128]{2,1,0:T(8,128)S(1)}, u32[]{:S(2)}, u32[]{:S(2)}) collective-permute-start(f32[8,32,128]{2,1,0:T(8,128)S(1)} %slice.94), channel_id=1, source_target_pairs={{0,1},{1,2},{2,3},{3,0},{4,5},{5,6},{6,7},{7,4},{8,9},{9,10},{10,1... | collective-permute-start | bytes 393224 | tf_op jit(solution)/shard_map/ppermute | solution.py:381
  14.4 6.7 %collective-permute-start.3 = (f32[8,32,128]{2,1,0:T(8,128)S(1)}, f32[8,32,128]{2,1,0:T(8,128)S(1)}, u32[]{:S(2)}, u32[]{:S(2)}) collective-permute-start(f32[8,32,128]{2,1,0:T(8,128)S(1)} %slice.95), channel_id=1, source_target_pairs={{0,3},{1,0},{2,1},{3,2},{4,7},{5,4},{6,5},{7,6},{8,11},{9,8},{10,9... | collective-permute-start | bytes 393224 | tf_op jit(solution)/shard_map/ppermute | solution.py:381
  17.7 4.2 %copy-start = (s32[256,128]{1,0:T(8,128)S(1)}, s32[256,128]{1,0:T(8,128)}, u32[]{:S(2)}) copy-start(s32[256,128]{1,0:T(8,128)} %refs_4_.3) | copy-start | bytes 393220
  17.8 8.1 %collective-permute-start.5 = (f32[16,32,128]{2,1,0:T(8,128)S(1)}, f32[16,32,128]{2,1,0:T(8,128)S(1)}, u32[]{:S(2)}, u32[]{:S(2)}) collective-permute-start(f32[16,32,128]{2,1,0:T(8,128)S(1)} %collective-permute-done.4.refs_1_), channel_id=1, source_target_pairs={{0,1},{1,2},{2,3},{3,0},{4,5},{5,6},{6,7},{7,4},{8,9},{9,10},{10,1... | collective-permute-start | bytes 786440 | tf_op jit(solution)/shard_map/ppermute | solution.py:381
  17.8 8.1 %collective-permute-start.6 = (f32[16,32,128]{2,1,0:T(8,128)S(1)}, f32[16,32,128]{2,1,0:T(8,128)S(1)}, u32[]{:S(2)}, u32[]{:S(2)}) collective-permute-start(f32[16,32,128]{2,1,0:T(8,128)S(1)} %collective-permute-done.4.refs_1_), channel_id=1, source_target_pairs={{0,3},{1,0},{2,1},{3,2},{4,7},{5,4},{6,5},{7,6},{8,11},{9,8},{10,9... | collective-permute-start | bytes 786440 | tf_op jit(solution)/shard_map/ppermute | solution.py:381
  21.1 8.0 %collective-permute-start.7 = (f32[16,32,128]{2,1,0:T(8,128)S(1)}, f32[16,32,128]{2,1,0:T(8,128)S(1)}, u32[]{:S(2)}, u32[]{:S(2)}) collective-permute-start(f32[16,32,128]{2,1,0:T(8,128)S(1)} %constant_dynamic-update-slice_fusion.refs_0_), channel_id=1, source_target_pairs={{0,4},{1,5},{2,6},{3,7},{4,0},{5,1},{6,2},{7,3},{8,12},{9,13},{10,... | collective-permute-start | bytes 786440 | tf_op jit(solution)/shard_map/ppermute | solution.py:381
  33.8 2.5 %collective-permute-start.8 = (f32[2,288,256]{2,1,0:T(8,128)S(1)}, f32[2,288,256]{2,1,0:T(8,128)S(1)}, u32[]{:S(2)}, u32[]{:S(2)}) collective-permute-start(f32[2,288,256]{2,1,0:T(8,128)S(1)} %get-tuple-element.31), channel_id=1, source_target_pairs={{0,8},{8,0},{16,24},{24,16},{32,40},{40,32},{48,56},{56,48},{64,72... | collective-permute-start | bytes 1769480 | tf_op jit(solution)/shard_map/ppermute | solution.py:375
  35.8 7.8 %collective-permute-start.10 = (f32[1,288,256]{2,1,0:T(8,128)S(1)}, f32[1,288,256]{2,1,0:T(8,128)S(1)}, u32[]{:S(2)}, u32[]{:S(2)}) collective-permute-start(f32[1,288,256]{2,1,0:T(8,128)S(1)} %get-tuple-element.41), channel_id=1, source_target_pairs={{0,8},{8,0},{16,24},{24,16},{32,40},{40,32},{48,56},{56,48},{64,72... | collective-permute-start | bytes 884744 | tf_op jit(solution)/shard_map/ppermute | solution.py:375
  38.3 9.2 %collective-permute-start.17 = (f32[1,288,256]{2,1,0:T(8,128)S(1)}, f32[1,288,256]{2,1,0:T(8,128)S(1)}, u32[]{:S(2)}, u32[]{:S(2)}) collective-permute-start(f32[1,288,256]{2,1,0:T(8,128)S(1)} %get-tuple-element.46), channel_id=1, source_target_pairs={{0,8},{8,0},{16,24},{24,16},{32,40},{40,32},{48,56},{56,48},{64,72... | collective-permute-start | bytes 884744 | tf_op jit(solution)/shard_map/ppermute | solution.py:375
  38.4 10.7 %collective-permute-start.11 = (f32[2,144,256]{2,1,0:T(8,128)S(1)}, f32[2,144,256]{2,1,0:T(8,128)S(1)}, u32[]{:S(2)}, u32[]{:S(2)}) collective-permute-start(f32[2,144,256]{2,1,0:T(8,128)S(1)} %get-tuple-element.52), channel_id=1, source_target_pairs={{0,16},{8,24},{16,32},{24,40},{32,48},{40,56},{48,0},{56,8},{64,80... | collective-permute-start | bytes 884744 | tf_op jit(solution)/shard_map/ppermute | solution.py:375
  43.5 6.0 %collective-permute-start.13 = (f32[2,288,256]{2,1,0:T(8,128)S(1)}, f32[2,288,256]{2,1,0:T(8,128)S(1)}, u32[]{:S(2)}, u32[]{:S(2)}) collective-permute-start(f32[2,288,256]{2,1,0:T(8,128)S(1)} %get-tuple-element.42), channel_id=1, source_target_pairs={{0,8},{8,0},{16,24},{24,16},{32,40},{40,32},{48,56},{56,48},{64,72... | collective-permute-start | bytes 1769480 | tf_op jit(solution)/shard_map/ppermute | solution.py:375
  43.7 9.5 %collective-permute-start.14 = (f32[2,144,256]{2,1,0:T(8,128)S(1)}, f32[2,144,256]{2,1,0:T(8,128)S(1)}, u32[]{:S(2)}, u32[]{:S(2)}) collective-permute-start(f32[2,144,256]{2,1,0:T(8,128)S(1)} %get-tuple-element.51), channel_id=1, source_target_pairs={{0,48},{8,56},{16,0},{24,8},{32,16},{40,24},{48,32},{56,40},{64,11... | collective-permute-start | bytes 884744 | tf_op jit(solution)/shard_map/ppermute | solution.py:375
  47.3 12.3 %collective-permute-start.9 = (f32[1,288,256]{2,1,0:T(8,128)S(1)}, f32[1,288,256]{2,1,0:T(8,128)S(1)}, u32[]{:S(2)}, u32[]{:S(2)}) collective-permute-start(f32[1,288,256]{2,1,0:T(8,128)S(1)} %get-tuple-element.40), channel_id=1, source_target_pairs={{0,8},{8,0},{16,24},{24,16},{32,40},{40,32},{48,56},{56,48},{64,72... | collective-permute-start | bytes 884744 | tf_op jit(solution)/shard_map/ppermute | solution.py:375
  49.1 10.5 %collective-permute-start.12 = (f32[1,288,256]{2,1,0:T(8,128)S(1)}, f32[1,288,256]{2,1,0:T(8,128)S(1)}, u32[]{:S(2)}, u32[]{:S(2)}) collective-permute-start(f32[1,288,256]{2,1,0:T(8,128)S(1)} %pad_maximum_fusion.2), channel_id=1, source_target_pairs={{0,16},{8,24},{16,32},{24,40},{32,48},{40,56},{48,0},{56,8},{64,80... | collective-permute-start | bytes 884744 | tf_op jit(solution)/shard_map/ppermute | solution.py:375
  53.2 10.3 %collective-permute-start.15 = (f32[1,288,256]{2,1,0:T(8,128)S(1)}, f32[1,288,256]{2,1,0:T(8,128)S(1)}, u32[]{:S(2)}, u32[]{:S(2)}) collective-permute-start(f32[1,288,256]{2,1,0:T(8,128)S(1)} %pad_maximum_fusion.3), channel_id=1, source_target_pairs={{0,48},{8,56},{16,0},{24,8},{32,16},{40,24},{48,32},{56,40},{64,11... | collective-permute-start | bytes 884744 | tf_op jit(solution)/shard_map/ppermute | solution.py:375
  56.2 10.5 %collective-permute-start.18 = (f32[1,288,256]{2,1,0:T(8,128)S(1)}, f32[1,288,256]{2,1,0:T(8,128)S(1)}, u32[]{:S(2)}, u32[]{:S(2)}) collective-permute-start(f32[1,288,256]{2,1,0:T(8,128)S(1)} %pad_maximum_fusion.4), channel_id=1, source_target_pairs={{0,16},{8,24},{16,32},{24,40},{32,48},{40,56},{48,0},{56,8},{64,80... | collective-permute-start | bytes 884744 | tf_op jit(solution)/shard_map/ppermute | solution.py:375
  56.3 12.2 %collective-permute-start.19 = (f32[1,288,256]{2,1,0:T(8,128)S(1)}, f32[1,288,256]{2,1,0:T(8,128)S(1)}, u32[]{:S(2)}, u32[]{:S(2)}) collective-permute-start(f32[1,288,256]{2,1,0:T(8,128)S(1)} %pad_maximum_fusion.5), channel_id=1, source_target_pairs={{0,48},{8,56},{16,0},{24,8},{32,16},{40,24},{48,32},{56,40},{64,11... | collective-permute-start | bytes 884744 | tf_op jit(solution)/shard_map/ppermute | solution.py:375
  63.6 11.4 %copy-start.1 = (f32[256]{0:T(256)S(1)}, f32[256]{0:T(256)}, u32[]{:S(2)}) copy-start(f32[256]{0:T(256)} %param.13) | copy-start | bytes 3076
  65.6 3.0 %collective-permute-start.16 = (f32[1,288,256]{2,1,0:T(8,128)S(1)}, f32[1,288,256]{2,1,0:T(8,128)S(1)}, u32[]{:S(2)}, u32[]{:S(2)}) collective-permute-start(f32[1,288,256]{2,1,0:T(8,128)S(1)} %get-tuple-element.45), channel_id=1, source_target_pairs={{0,8},{8,0},{16,24},{24,16},{32,40},{40,32},{48,56},{56,48},{64,72... | collective-permute-start | bytes 884744 | tf_op jit(solution)/shard_map/ppermute | solution.py:375
  65.6 9.4 %collective-permute-start.20 = (f32[1,288,256]{2,1,0:T(8,128)S(1)}, f32[1,288,256]{2,1,0:T(8,128)S(1)}, u32[]{:S(2)}, u32[]{:S(2)}) collective-permute-start(f32[1,288,256]{2,1,0:T(8,128)S(1)} %add_add_fusion), channel_id=1, source_target_pairs={{0,64},{8,72},{16,80},{24,88},{32,96},{40,104},{48,112},{56,120},{... | collective-permute-start | bytes 884744 | tf_op jit(solution)/shard_map/ppermute | solution.py:375
  92.9 1.5 %collective-permute-start.21 = (f32[8,32,256]{2,1,0:T(8,128)S(1)}, f32[8,32,256]{2,1,0:T(8,128)S(1)}, u32[]{:S(2)}, u32[]{:S(2)}) collective-permute-start(f32[8,32,256]{2,1,0:T(8,128)S(1)} %all_to_all.5), channel_id=1, source_target_pairs={{0,8},{8,0},{16,24},{24,16},{32,40},{40,32},{48,56},{56,48},{64,72... | collective-permute-start | bytes 786440 | tf_op jit(solution)/shard_map/ppermute | solution.py:375

commit v6 on v5

--- a/solution.py
+++ b/solution.py
@@ -445,20 +445,26 @@
             return jnp.concatenate([total[:, :top] + passed, total[:, top:]], 1)
         return jnp.concatenate([total[:, :top], total[:, top:] + passed], 1)
 
+    def across_z(value):
+        return over_ap(value, 1, 0, 0)
+
     kept, other = systems(2, (0, 1))
     up_far = systems(1, (1,), kept)
     farthest = kept + other
     up, down = around(farthest[:, :top], 1), around(farthest[:, top:], -1)
     up_own = systems(1, (0,), farthest, up_far[0])
-    kept, other = systems(3, (0, 1), up_own[0])
-    last_kept, last_other = systems(0, (1,), kept)
-    up_far, up_own = joined(up_far, up[1:], 0), joined(up_own, up[:1], 0)
-    down_far, down_own = joined((kept[1:], other[1:]), down[1:], 1), joined((kept[:1], other[:1]), down[:1], 1)
-    up, down = around(up_far, 1), around(down_far, -1)
+    up_across = across_z(up_far[0] + up_far[1])
+    down_far = systems(3, (1,), up_own[0])
+    down_own = systems(3, (0,), down_far[0])
+    down_across = across_z(down_far[0] + down_far[1])
+    far_kept, far_other = systems(0, (1,), down_own[0])
+    far_up, far_down = around(up[1:], 1), around(down[1:], -1)
+    kept, other = systems(0, (0,), far_kept)
+    up_own = joined(up_own, up[:1], 0) + up_across
+    down_own = joined(down_own, down[:1], 1) + down_across
+    up_own, kept = lax.optimization_barrier((up_own, kept))
     own_up, own_down = around(up_own, 1), around(down_own, -1)
-    across = (last_kept + last_other) + (up + down)
-    kept, other = systems(0, (0,), across)
-    across = over_ap(across, 1, 0, 0)
+    across = across_z((far_kept + far_other) + jnp.concatenate([far_up, far_down], 1))
     own_tone = solved([kept, other, own_up, own_down, across], regularizer)
     chips = lax.axis_size("ap") // CORES
     same = [[chip * CORES + c for chip in range(chips)] for c in range(CORES)]

time: 96.8 us -> 96.4 us (level)
  waiting for transfers between devices: 28.1 us -> 26.2 us
  starting transfers between devices: 26.7 us -> 27.8 us
    ppermute x14 -> x17, waiting for transfers between devices: 18.9 us -> 16.9 us  [over_ap(): return lax.ppermute(value, 'ap', pairs)]
    ppermute x14 -> x17, starting transfers between devices: 12.2 us -> 13.3 us  [over_ap(): return lax.ppermute(value, 'ap', pairs)]
    pallas_call x6 -> x7, Pallas kernels: 14.3 us -> 14.7 us  [tone_systems(): pl.pallas_call(functools.partial(tone_kernel, distance, planes), in_specs...]
  transfers between devices with their start and end apart: 22 -> 25, of which waited for: 9 -> 11; matrix products, arithmetic and copies ran while one was open for 4% -> 4% of each run, Pallas kernels for 13% -> 13%
where the time goes in v6:
time: 96.4 us; the launch traced here: 95.1 us
  starting transfers between devices  27.8 us (29%)
  waiting for transfers between devices  26.2 us (27%)
  Pallas kernels  22.6 us (23%)
  blocking collectives  13.7 us (14%)
  local copies, waits for them, and re-layouts  3.32 us (3%)
  other arithmetic  1.22 us (1%)
    ppermute x17, waiting for transfers between devices, over_ap(): return lax.ppermute(value, 'ap', pairs)  16.9 us
    pallas_call x7, Pallas kernels, tone_systems(): pl.pallas_call(functools.partial(tone_kernel, distance, planes), in_specs...  14.7 us
    ppermute x8, starting transfers between devices, over_sc(): return lax.ppermute(value, 'sc', pairs)  14.4 us
    all_to_all x1, blocking collectives, all_steps(): lax.all_to_all(jnp.broadcast_to(own_tone[None], (chips, *own_tone.shape))...  13.7 us
    ppermute x17, starting transfers between devices, over_ap(): return lax.ppermute(value, 'ap', pairs)  13.3 us
    ppermute x8, waiting for transfers between devices, over_sc(): return lax.ppermute(value, 'sc', pairs)  9.27 us
    pallas_call x1, Pallas kernels, solved(): pl.pallas_call(solve_kernel, in_specs=[vmem] * (len(systems) + 1), out_sp...  4.15 us
    pallas_call x2, Pallas kernels, prepared(): pl.pallas_call(functools.partial(prepare_kernel, slots, len(tables), tone...  2.77 us
  transfers between devices with their start and end apart: 25, of which 11 were waited for; matrix products, arithmetic and copies ran while one was open for 4% of the time, Pallas kernels for 13%

profile of v6, /device:TPU:0, one launch (start us, length us, event | category | flops | bytes accessed | tf_op | source)
XLA Modules:
  0.0 95.1 jit_solution(2148775051053686150)
XLA Ops:
  0.0 1.0 %packed_tables.1.refs_0_ = f32[16,32,128]{2,1,0:T(8,128)S(1)} custom-call(f32[4,32,128]{2,1,0:T(8,128)} %refs_0_.1, f32[4,32,128]{2,1,0:T(8,128)} %refs_1_.1, f32[4,32,128]{2,1,0:T(8,128)} %refs_2_.1, f32[4,32,128]{2,1,0:T(8,128)} %refs_3_.1), custom_call_target="tpu_custom_call" | custom-call | tf_op jit(solution)/shard_map/packed_tables/pallas_call | solution.py:410
  1.0 4.1 %collective-permute-start.4 = (f32[16,32,128]{2,1,0:T(8,128)S(1)}, f32[16,32,128]{2,1,0:T(8,128)S(1)}, u32[]{:S(2)}, u32[]{:S(2)}) collective-permute-start(f32[16,32,128]{2,1,0:T(8,128)S(1)} %packed_tables.1.refs_0_), channel_id=1, source_target_pairs={{0,4},{1,5},{2,6},{3,7},{4,0},{5,1},{6,2},{7,3},{8,12},{9,13},{10,... | collective-permute-start | bytes 786440 | tf_op jit(solution)/shard_map/ppermute | solution.py:381
  5.0 1.5 %collective-permute-start = (f32[16,32,128]{2,1,0:T(8,128)S(1)}, f32[16,32,128]{2,1,0:T(8,128)S(1)}, u32[]{:S(2)}, u32[]{:S(2)}) collective-permute-start(f32[16,32,128]{2,1,0:T(8,128)S(1)} %packed_tables.1.refs_0_), channel_id=1, source_target_pairs={{0,1},{1,2},{2,3},{3,0},{4,5},{5,6},{6,7},{7,4},{8,9},{9,10},{10,1... | collective-permute-start | bytes 786440 | tf_op jit(solution)/shard_map/ppermute | solution.py:381
  6.5 1.7 %collective-permute-start.2 = (f32[16,32,128]{2,1,0:T(8,128)S(1)}, f32[16,32,128]{2,1,0:T(8,128)S(1)}, u32[]{:S(2)}, u32[]{:S(2)}) collective-permute-start(f32[16,32,128]{2,1,0:T(8,128)S(1)} %packed_tables.1.refs_0_), channel_id=1, source_target_pairs={{0,3},{1,0},{2,1},{3,2},{4,7},{5,4},{6,5},{7,6},{8,11},{9,8},{10,9... | collective-permute-start | bytes 786440 | tf_op jit(solution)/shard_map/ppermute | solution.py:381
  8.3 1.5 %reshape.10 = f32[16,2,14,512]{3,0,2,1:T(8,128)S(1)} reshape(f32[16,2,14,4,128]{4,3,0,2,1:T(4,128)} %bitcast.17) | data formatting | bytes 1835008 | tf_op jit(solution)/shard_map/reshape | solution.py:360
  9.8 0.1 fusion.1
  9.9 0.5 copy_bitcast_fusion
  10.5 3.6 %collective-permute-done.refs_2_ = f32[16,32,128]{2,1,0:T(8,128)S(1)} collective-permute-done((f32[16,32,128]{2,1,0:T(8,128)S(1)}, f32[16,32,128]{2,1,0:T(8,128)S(1)}, u32[]{:S(2)}, u32[]{:S(2)}) %collective-permute-start) | collective-permute-done | bytes 262176 | tf_op jit(solution)/shard_map/ppermute | solution.py:381
  14.0 0.3 collective-permute-start.1
  14.4 3.0 %collective-permute-start.3 = (f32[8,32,128]{2,1,0:T(8,128)S(1)}, f32[8,32,128]{2,1,0:T(8,128)S(1)}, u32[]{:S(2)}, u32[]{:S(2)}) collective-permute-start(f32[8,32,128]{2,1,0:T(8,128)S(1)} %slice.63), channel_id=1, source_target_pairs={{0,3},{1,0},{2,1},{3,2},{4,7},{5,4},{6,5},{7,6},{8,11},{9,8},{10,9... | collective-permute-start | bytes 393224 | tf_op jit(solution)/shard_map/ppermute | solution.py:381
  17.4 0.3 fusion
  17.7 0.0 copy-start
  17.8 0.1 collective-permute-start.5
  17.8 3.2 %collective-permute-start.6 = (f32[16,32,128]{2,1,0:T(8,128)S(1)}, f32[16,32,128]{2,1,0:T(8,128)S(1)}, u32[]{:S(2)}, u32[]{:S(2)}) collective-permute-start(f32[16,32,128]{2,1,0:T(8,128)S(1)} %collective-permute-done.4.refs_1_), channel_id=1, source_target_pairs={{0,3},{1,0},{2,1},{3,2},{4,7},{5,4},{6,5},{7,6},{8,11},{9,8},{10,9... | collective-permute-start | bytes 786440 | tf_op jit(solution)/shard_map/ppermute | solution.py:381
  21.1 0.4 collective-permute-start.7
  21.6 0.3 select_maximum_fusion.1
  21.8 0.1 pad_maximum_fusion.y_ref
  22.0 1.4 %prepared.2 = (f32[4,4,2,256,128]{4,3,2,1,0:T(8,128)S(1)}, f32[8,4,2,256,128]{4,3,2,1,0:T(8,128)S(1)}) custom-call(f32[16,32,128]{2,1,0:T(8,128)S(1)} %packed_tables.1.refs_0_, f32[16,32,128]{2,1,0:T(8,128)S(1)} %collective-permute-done.4.refs_1_, f32[16,32,128]{2,1,0:T(8,128)S(1)} %collective-permute-done.refs_2_, ...), custom_call_target="tpu_custom_call" | custom-call | tf_op jit(solution)/shard_map/prepared/pallas_call | solution.py:122
  23.4 2.5 %collective-permute-done.5.refs_1_ = f32[16,32,128]{2,1,0:T(8,128)S(1)} collective-permute-done((f32[16,32,128]{2,1,0:T(8,128)S(1)}, f32[16,32,128]{2,1,0:T(8,128)S(1)}, u32[]{:S(2)}, u32[]{:S(2)}) %collective-permute-start.5) | collective-permute-done | bytes 262176 | tf_op jit(solution)/shard_map/ppermute | solution.py:381
  25.9 0.0 collective-permute-done.6.refs_2_
  25.9 3.2 %collective-permute-done.7.refs_3_ = f32[16,32,128]{2,1,0:T(8,128)S(1)} collective-permute-done((f32[16,32,128]{2,1,0:T(8,128)S(1)}, f32[16,32,128]{2,1,0:T(8,128)S(1)}, u32[]{:S(2)}, u32[]{:S(2)}) %collective-permute-start.7) | collective-permute-done | bytes 262176 | tf_op jit(solution)/shard_map/ppermute | solution.py:381
  29.1 1.4 %prepared.3 = (f32[4,4,2,256,128]{4,3,2,1,0:T(8,128)S(1)}, f32[8,4,2,256,128]{4,3,2,1,0:T(8,128)S(1)}) custom-call(f32[16,32,128]{2,1,0:T(8,128)S(1)} %constant_dynamic-update-slice_fusion.refs_0_, f32[16,32,128]{2,1,0:T(8,128)S(1)} %collective-permute-done.5.refs_1_, ...), custom_call_target="tpu_custom_call", output_to_operand_aliasing={{0}: (5, {}), {1}: (6, {})} | custom-call | tf_op jit(solution)/shard_map/prepared/pallas_call | solution.py:122
  30.4 3.4 %tone_systems.7 = (f32[2,288,256]{2,1,0:T(8,128)S(1)}, f32[2,288,256]{2,1,0:T(8,128)S(1)}) custom-call(f32[16,32,1024]{2,1,0:T(8,128)S(1)} %pad_maximum_fusion.y_ref, f32[4,4,2,256,128]{4,3,2,1,0:T(8,128)S(1)} %get-tuple-element.33.lead, f32[8,4,2,256,128]{4,3,2,1,0:T(8,128)S(1)} %get-tuple-element.34.turn), custom_call_target="tpu_custom_call" | custom-call | tf_op jit(solution)/shard_map/tone_systems/pallas_call | solution.py:215
  33.8 0.1 collective-permute-start.8
  33.9 1.9 %tone_systems.8 = (f32[1,288,256]{2,1,0:T(8,128)S(1)}, f32[1,288,256]{2,1,0:T(8,128)S(1)}) custom-call(f32[16,32,1024]{2,1,0:T(8,128)S(1)} %pad_maximum_fusion.y_ref, f32[4,4,2,256,128]{4,3,2,1,0:T(8,128)S(1)} %get-tuple-element.33.lead, f32[8,4,2,256,128]{4,3,2,1,0:T(8,128)S(1)} %get-tuple-element.34.turn), custom_call_target="tpu_custom_call" | custom-call | tf_op jit(solution)/shard_map/tone_systems/pallas_call | solution.py:215
  35.8 0.5 collective-permute-start.11
  36.3 0.1 add.42
  36.4 1.9 %tone_systems.9 = (f32[1,288,256]{2,1,0:T(8,128)S(1)}, f32[1,288,256]{2,1,0:T(8,128)S(1)}) custom-call(f32[16,32,1024]{2,1,0:T(8,128)S(1)} %pad_maximum_fusion.y_ref, f32[4,4,2,256,128]{4,3,2,1,0:T(8,128)S(1)} %get-tuple-element.33.lead, f32[8,4,2,256,128]{4,3,2,1,0:T(8,128)S(1)} %get-tuple-element.34.turn), custom_call_target="tpu_custom_call" | custom-call | tf_op jit(solution)/shard_map/tone_systems/pallas_call | solution.py:215
  38.3 1.9 %tone_systems.10 = (f32[1,288,256]{2,1,0:T(8,128)S(1)}, f32[1,288,256]{2,1,0:T(8,128)S(1)}) custom-call(f32[16,32,1024]{2,1,0:T(8,128)S(1)} %pad_maximum_fusion.y_ref, f32[4,4,2,256,128]{4,3,2,1,0:T(8,128)S(1)} %get-tuple-element.33.lead, f32[8,4,2,256,128]{4,3,2,1,0:T(8,128)S(1)} %get-tuple-element.34.turn), custom_call_target="tpu_custom_call" | custom-call | tf_op jit(solution)/shard_map/tone_systems/pallas_call | solution.py:215
  40.2 1.9 %tone_systems.11 = (f32[1,288,256]{2,1,0:T(8,128)S(1)}, f32[1,288,256]{2,1,0:T(8,128)S(1)}) custom-call(f32[16,32,1024]{2,1,0:T(8,128)S(1)} %pad_maximum_fusion.y_ref, f32[4,4,2,256,128]{4,3,2,1,0:T(8,128)S(1)} %get-tuple-element.33.lead, f32[8,4,2,256,128]{4,3,2,1,0:T(8,128)S(1)} %get-tuple-element.34.turn), custom_call_target="tpu_custom_call" | custom-call | tf_op jit(solution)/shard_map/tone_systems/pallas_call | solution.py:215
  42.1 0.2 collective-permute-start.15
  42.4 3.1 %collective-permute-start.16 = (f32[2,144,256]{2,1,0:T(8,128)S(1)}, f32[2,144,256]{2,1,0:T(8,128)S(1)}, u32[]{:S(2)}, u32[]{:S(2)}) collective-permute-start(f32[2,144,256]{2,1,0:T(8,128)S(1)} %get-tuple-element.59), channel_id=1, source_target_pairs={{0,48},{8,56},{16,0},{24,8},{32,16},{40,24},{48,32},{56,40},{64,11... | collective-permute-start | bytes 884744 | tf_op jit(solution)/shard_map/ppermute | solution.py:375
  45.5 0.2 collective-permute-start.9
  45.6 0.0 collective-permute-start.10
  45.7 1.1 %collective-permute-start.12 = (f32[1,288,256]{2,1,0:T(8,128)S(1)}, f32[1,288,256]{2,1,0:T(8,128)S(1)}, u32[]{:S(2)}, u32[]{:S(2)}) collective-permute-start(f32[1,288,256]{2,1,0:T(8,128)S(1)} %add.45), channel_id=1, source_target_pairs={{0,64},{8,72},{16,80},{24,88},{32,96},{40,104},{48,112},{56,120},{... | collective-permute-start | bytes 884744 | tf_op jit(solution)/shard_map/ppermute | solution.py:375
  46.8 1.9 %tone_systems.12 = (f32[1,288,256]{2,1,0:T(8,128)S(1)}, f32[1,288,256]{2,1,0:T(8,128)S(1)}) custom-call(f32[16,32,1024]{2,1,0:T(8,128)S(1)} %pad_maximum_fusion.y_ref, f32[4,4,2,256,128]{4,3,2,1,0:T(8,128)S(1)} %get-tuple-element.33.lead, f32[8,4,2,256,128]{4,3,2,1,0:T(8,128)S(1)} %get-tuple-element.34.turn), custom_call_target="tpu_custom_call" | custom-call | tf_op jit(solution)/shard_map/tone_systems/pallas_call | solution.py:215
  48.7 1.9 %tone_systems.13 = (f32[1,288,256]{2,1,0:T(8,128)S(1)}, f32[1,288,256]{2,1,0:T(8,128)S(1)}) custom-call(f32[16,32,1024]{2,1,0:T(8,128)S(1)} %pad_maximum_fusion.y_ref, f32[4,4,2,256,128]{4,3,2,1,0:T(8,128)S(1)} %get-tuple-element.33.lead, f32[8,4,2,256,128]{4,3,2,1,0:T(8,128)S(1)} %get-tuple-element.34.turn), custom_call_target="tpu_custom_call" | custom-call | tf_op jit(solution)/shard_map/tone_systems/pallas_call | solution.py:215
  50.5 0.0 collective-permute-done.15
  50.6 0.1 collective-permute-start.20
  50.7 1.6 %collective-permute-done.16 = f32[2,144,256]{2,1,0:T(8,128)S(1)} collective-permute-done((f32[2,144,256]{2,1,0:T(8,128)S(1)}, f32[2,144,256]{2,1,0:T(8,128)S(1)}, u32[]{:S(2)}, u32[]{:S(2)}) %collective-permute-start.16) | collective-permute-done | bytes 294944 | tf_op jit(solution)/shard_map/ppermute | solution.py:375
  52.4 0.0 collective-permute-start.17
  52.4 0.0 collective-permute-done.9
  52.4 0.6 collective-permute-start.13
  53.0 3.1 %collective-permute-done.10 = f32[2,144,256]{2,1,0:T(8,128)S(1)} collective-permute-done((f32[2,144,256]{2,1,0:T(8,128)S(1)}, f32[2,144,256]{2,1,0:T(8,128)S(1)}, u32[]{:S(2)}, u32[]{:S(2)}) %collective-permute-start.10) | collective-permute-done | bytes 294944 | tf_op jit(solution)/shard_map/ppermute | solution.py:375
  56.1 0.7 collective-permute-start.22
  56.9 0.0 collective-permute-done.17
  56.9 1.4 %collective-permute-start.21 = (f32[1,144,256]{2,1,0:T(8,128)S(1)}, f32[1,144,256]{2,1,0:T(8,128)S(1)}, u32[]{:S(2)}, u32[]{:S(2)}) collective-permute-start(f32[1,144,256]{2,1,0:T(8,128)S(1)} %get-tuple-element.65), channel_id=1, source_target_pairs={{0,16},{8,24},{16,32},{24,40},{32,48},{40,56},{48,0},{56,8},{64,80... | collective-permute-start | bytes 442376 | tf_op jit(solution)/shard_map/ppermute | solution.py:375
  58.3 1.1 %collective-permute-start.18 = (f32[1,288,256]{2,1,0:T(8,128)S(1)}, f32[1,288,256]{2,1,0:T(8,128)S(1)}, u32[]{:S(2)}, u32[]{:S(2)}) collective-permute-start(f32[1,288,256]{2,1,0:T(8,128)S(1)} %add.49), channel_id=1, source_target_pairs={{0,64},{8,72},{16,80},{24,88},{32,96},{40,104},{48,112},{56,120},{... | collective-permute-start | bytes 884744 | tf_op jit(solution)/shard_map/ppermute | solution.py:375
  59.4 0.0 collective-permute-done.20
  59.4 0.1 collective-permute-start.14
  59.5 1.8 %collective-permute-done.22 = f32[1,144,256]{2,1,0:T(8,128)S(1)} collective-permute-done((f32[1,144,256]{2,1,0:T(8,128)S(1)}, f32[1,144,256]{2,1,0:T(8,128)S(1)}, u32[]{:S(2)}, u32[]{:S(2)}) %collective-permute-start.22) | collective-permute-done | bytes 147488 | tf_op jit(solution)/shard_map/ppermute | solution.py:375
  61.3 3.5 %collective-permute-done.21 = f32[1,144,256]{2,1,0:T(8,128)S(1)} collective-permute-done((f32[1,144,256]{2,1,0:T(8,128)S(1)}, f32[1,144,256]{2,1,0:T(8,128)S(1)}, u32[]{:S(2)}, u32[]{:S(2)}) %collective-permute-start.21) | collective-permute-done | bytes 147488 | tf_op jit(solution)/shard_map/ppermute | solution.py:375
  64.9 0.1 maximum_add_fusion.2
  64.9 1.1 %collective-permute-start.23 = (f32[1,288,256]{2,1,0:T(8,128)S(1)}, f32[1,288,256]{2,1,0:T(8,128)S(1)}, u32[]{:S(2)}, u32[]{:S(2)}) collective-permute-start(f32[1,288,256]{2,1,0:T(8,128)S(1)} %maximum_add_fusion.2), channel_id=1, source_target_pairs={{0,64},{8,72},{16,80},{24,88},{32,96},{40,104},{48,112},{56,120},{... | collective-permute-start | bytes 884744 | tf_op jit(solution)/shard_map/ppermute | solution.py:375
  66.0 1.1 %collective-permute-done.18 = f32[1,288,256]{2,1,0:T(8,128)S(1)} collective-permute-done((f32[1,288,256]{2,1,0:T(8,128)S(1)}, f32[1,288,256]{2,1,0:T(8,128)S(1)}, u32[]{:S(2)}, u32[]{:S(2)}) %collective-permute-start.18) | collective-permute-done | bytes 294944 | tf_op jit(solution)/shard_map/ppermute | solution.py:375
  67.2 3.1 %collective-permute-start.19 = (f32[1,288,256]{2,1,0:T(8,128)S(1)}, f32[1,288,256]{2,1,0:T(8,128)S(1)}, u32[]{:S(2)}, u32[]{:S(2)}) collective-permute-start(f32[1,288,256]{2,1,0:T(8,128)S(1)} %maximum_add_fusion.1), channel_id=1, source_target_pairs={{0,48},{8,56},{16,0},{24,8},{32,16},{40,24},{48,32},{56,40},{64,11... | collective-permute-start | bytes 884744 | tf_op jit(solution)/shard_map/ppermute | solution.py:375
  70.3 0.0 collective-permute-done.14.refs_2_
  70.3 2.2 %collective-permute-done.23.refs_4_ = f32[1,288,256]{2,1,0:T(8,128)S(1)} collective-permute-done((f32[1,288,256]{2,1,0:T(8,128)S(1)}, f32[1,288,256]{2,1,0:T(8,128)S(1)}, u32[]{:S(2)}, u32[]{:S(2)}) %collective-permute-start.23) | collective-permute-done | bytes 294944 | tf_op jit(solution)/shard_map/ppermute | solution.py:375
  72.5 2.0 %collective-permute-done.19.refs_3_ = f32[1,288,256]{2,1,0:T(8,128)S(1)} collective-permute-done((f32[1,288,256]{2,1,0:T(8,128)S(1)}, f32[1,288,256]{2,1,0:T(8,128)S(1)}, u32[]{:S(2)}, u32[]{:S(2)}) %collective-permute-start.19) | collective-permute-done | bytes 294944 | tf_op jit(solution)/shard_map/ppermute | solution.py:375
  74.5 4.2 %solved.1 = f32[32,256]{1,0:T(8,128)S(1)} custom-call(f32[1,288,256]{2,1,0:T(8,128)S(1)} %get-tuple-element.51.refs_0_, f32[1,288,256]{2,1,0:T(8,128)S(1)} %collective-permute-done.13.refs_1_, f32[1,288,256]{2,1,0:T(8,128)S(1)} %collective-permute-done.14.refs_2_, f32[1,288,256]{2,1,0:T(8,128)S(1)} %collective-permute-done.19.refs_3_, ...), custom_call_target="tpu_custom_call" | custom-call | tf_op jit(solution)/shard_map/solved/pallas_call | solution.py:339
  78.7 13.7 %all_to_all.5 = f32[8,32,256]{2,1,0:T(8,128)S(1)} all-to-all(f32[8,32,256]{2,1,0:T(8,128)S(1)} %broadcast_in_dim.2), channel_id=1, replica_groups={{0,16,32,48,64,80,96,112},{8,24,40,56,72,88,104,120},{1,17,33,49,65,81,..., dimensions={0} | all-to-all | bytes 524288 | tf_op jit(solution)/shard_map/all_to_all | solution.py:471
  92.4 0.0 collective-permute-start.24
  92.4 1.5 %collective-permute-done.24 = f32[8,32,256]{2,1,0:T(8,128)S(1)} collective-permute-done((f32[8,32,256]{2,1,0:T(8,128)S(1)}, f32[8,32,256]{2,1,0:T(8,128)S(1)}, u32[]{:S(2)}, u32[]{:S(2)}) %collective-permute-start.24) | collective-permute-done | bytes 262176 | tf_op jit(solution)/shard_map/ppermute | solution.py:375
  94.1 1.0 %copy.24 = f32[16,2,14,256]{3,0,2,1:T(8,128)} copy(f32[16,2,14,256]{3,2,1,0:T(8,128)S(1)} %bitcast.16) | data formatting | bytes 917504
  (28 shorter events, 0.5 us)
Async XLA Ops:
  1.0 16.8 %collective-permute-start.4 = (f32[16,32,128]{2,1,0:T(8,128)S(1)}, f32[16,32,128]{2,1,0:T(8,128)S(1)}, u32[]{:S(2)}, u32[]{:S(2)}) collective-permute-start(f32[16,32,128]{2,1,0:T(8,128)S(1)} %packed_tables.1.refs_0_), channel_id=1, source_target_pairs={{0,4},{1,5},{2,6},{3,7},{4,0},{5,1},{6,2},{7,3},{8,12},{9,13},{10,... | collective-permute-start | bytes 786440 | tf_op jit(solution)/shard_map/ppermute | solution.py:381
  5.0 9.0 %collective-permute-start = (f32[16,32,128]{2,1,0:T(8,128)S(1)}, f32[16,32,128]{2,1,0:T(8,128)S(1)}, u32[]{:S(2)}, u32[]{:S(2)}) collective-permute-start(f32[16,32,128]{2,1,0:T(8,128)S(1)} %packed_tables.1.refs_0_), channel_id=1, source_target_pairs={{0,1},{1,2},{2,3},{3,0},{4,5},{5,6},{6,7},{7,4},{8,9},{9,10},{10,1... | collective-permute-start | bytes 786440 | tf_op jit(solution)/shard_map/ppermute | solution.py:381
  6.5 7.9 %collective-permute-start.2 = (f32[16,32,128]{2,1,0:T(8,128)S(1)}, f32[16,32,128]{2,1,0:T(8,128)S(1)}, u32[]{:S(2)}, u32[]{:S(2)}) collective-permute-start(f32[16,32,128]{2,1,0:T(8,128)S(1)} %packed_tables.1.refs_0_), channel_id=1, source_target_pairs={{0,3},{1,0},{2,1},{3,2},{4,7},{5,4},{6,5},{7,6},{8,11},{9,8},{10,9... | collective-permute-start | bytes 786440 | tf_op jit(solution)/shard_map/ppermute | solution.py:381
  14.0 7.0 %collective-permute-start.1 = (f32[8,32,128]{2,1,0:T(8,128)S(1)}, f32[8,32,128]{2,1,0:T(8,128)S(1)}, u32[]{:S(2)}, u32[]{:S(2)}) collective-permute-start(f32[8,32,128]{2,1,0:T(8,128)S(1)} %slice.62), channel_id=1, source_target_pairs={{0,1},{1,2},{2,3},{3,0},{4,5},{5,6},{6,7},{7,4},{8,9},{9,10},{10,1... | collective-permute-start | bytes 393224 | tf_op jit(solution)/shard_map/ppermute | solution.py:381
  14.4 6.7 %collective-permute-start.3 = (f32[8,32,128]{2,1,0:T(8,128)S(1)}, f32[8,32,128]{2,1,0:T(8,128)S(1)}, u32[]{:S(2)}, u32[]{:S(2)}) collective-permute-start(f32[8,32,128]{2,1,0:T(8,128)S(1)} %slice.63), channel_id=1, source_target_pairs={{0,3},{1,0},{2,1},{3,2},{4,7},{5,4},{6,5},{7,6},{8,11},{9,8},{10,9... | collective-permute-start | bytes 393224 | tf_op jit(solution)/shard_map/ppermute | solution.py:381
  17.7 4.2 %copy-start = (s32[256,128]{1,0:T(8,128)S(1)}, s32[256,128]{1,0:T(8,128)}, u32[]{:S(2)}) copy-start(s32[256,128]{1,0:T(8,128)} %refs_4_.3) | copy-start | bytes 393220
  17.8 8.1 %collective-permute-start.5 = (f32[16,32,128]{2,1,0:T(8,128)S(1)}, f32[16,32,128]{2,1,0:T(8,128)S(1)}, u32[]{:S(2)}, u32[]{:S(2)}) collective-permute-start(f32[16,32,128]{2,1,0:T(8,128)S(1)} %collective-permute-done.4.refs_1_), channel_id=1, source_target_pairs={{0,1},{1,2},{2,3},{3,0},{4,5},{5,6},{6,7},{7,4},{8,9},{9,10},{10,1... | collective-permute-start | bytes 786440 | tf_op jit(solution)/shard_map/ppermute | solution.py:381
  17.8 8.1 %collective-permute-start.6 = (f32[16,32,128]{2,1,0:T(8,128)S(1)}, f32[16,32,128]{2,1,0:T(8,128)S(1)}, u32[]{:S(2)}, u32[]{:S(2)}) collective-permute-start(f32[16,32,128]{2,1,0:T(8,128)S(1)} %collective-permute-done.4.refs_1_), channel_id=1, source_target_pairs={{0,3},{1,0},{2,1},{3,2},{4,7},{5,4},{6,5},{7,6},{8,11},{9,8},{10,9... | collective-permute-start | bytes 786440 | tf_op jit(solution)/shard_map/ppermute | solution.py:381
  21.1 8.0 %collective-permute-start.7 = (f32[16,32,128]{2,1,0:T(8,128)S(1)}, f32[16,32,128]{2,1,0:T(8,128)S(1)}, u32[]{:S(2)}, u32[]{:S(2)}) collective-permute-start(f32[16,32,128]{2,1,0:T(8,128)S(1)} %constant_dynamic-update-slice_fusion.refs_0_), channel_id=1, source_target_pairs={{0,4},{1,5},{2,6},{3,7},{4,0},{5,1},{6,2},{7,3},{8,12},{9,13},{10,... | collective-permute-start | bytes 786440 | tf_op jit(solution)/shard_map/ppermute | solution.py:381
  33.8 2.5 %collective-permute-start.8 = (f32[2,288,256]{2,1,0:T(8,128)S(1)}, f32[2,288,256]{2,1,0:T(8,128)S(1)}, u32[]{:S(2)}, u32[]{:S(2)}) collective-permute-start(f32[2,288,256]{2,1,0:T(8,128)S(1)} %get-tuple-element.36), channel_id=1, source_target_pairs={{0,8},{8,0},{16,24},{24,16},{32,40},{40,32},{48,56},{56,48},{64,72... | collective-permute-start | bytes 1769480 | tf_op jit(solution)/shard_map/ppermute | solution.py:375
  35.8 9.8 %collective-permute-start.11 = (f32[1,288,256]{2,1,0:T(8,128)S(1)}, f32[1,288,256]{2,1,0:T(8,128)S(1)}, u32[]{:S(2)}, u32[]{:S(2)}) collective-permute-start(f32[1,288,256]{2,1,0:T(8,128)S(1)} %get-tuple-element.42), channel_id=1, source_target_pairs={{0,8},{8,0},{16,24},{24,16},{32,40},{40,32},{48,56},{56,48},{64,72... | collective-permute-start | bytes 884744 | tf_op jit(solution)/shard_map/ppermute | solution.py:375
  42.1 8.5 %collective-permute-start.15 = (f32[1,288,256]{2,1,0:T(8,128)S(1)}, f32[1,288,256]{2,1,0:T(8,128)S(1)}, u32[]{:S(2)}, u32[]{:S(2)}) collective-permute-start(f32[1,288,256]{2,1,0:T(8,128)S(1)} %get-tuple-element.54), channel_id=1, source_target_pairs={{0,8},{8,0},{16,24},{24,16},{32,40},{40,32},{48,56},{56,48},{64,72... | collective-permute-start | bytes 884744 | tf_op jit(solution)/shard_map/ppermute | solution.py:375
  42.4 10.0 %collective-permute-start.16 = (f32[2,144,256]{2,1,0:T(8,128)S(1)}, f32[2,144,256]{2,1,0:T(8,128)S(1)}, u32[]{:S(2)}, u32[]{:S(2)}) collective-permute-start(f32[2,144,256]{2,1,0:T(8,128)S(1)} %get-tuple-element.59), channel_id=1, source_target_pairs={{0,48},{8,56},{16,0},{24,8},{32,16},{40,24},{48,32},{56,40},{64,11... | collective-permute-start | bytes 884744 | tf_op jit(solution)/shard_map/ppermute | solution.py:375
  45.5 6.9 %collective-permute-start.9 = (f32[1,288,256]{2,1,0:T(8,128)S(1)}, f32[1,288,256]{2,1,0:T(8,128)S(1)}, u32[]{:S(2)}, u32[]{:S(2)}) collective-permute-start(f32[1,288,256]{2,1,0:T(8,128)S(1)} %get-tuple-element.41), channel_id=1, source_target_pairs={{0,8},{8,0},{16,24},{24,16},{32,40},{40,32},{48,56},{56,48},{64,72... | collective-permute-start | bytes 884744 | tf_op jit(solution)/shard_map/ppermute | solution.py:375
  45.6 10.4 %collective-permute-start.10 = (f32[2,144,256]{2,1,0:T(8,128)S(1)}, f32[2,144,256]{2,1,0:T(8,128)S(1)}, u32[]{:S(2)}, u32[]{:S(2)}) collective-permute-start(f32[2,144,256]{2,1,0:T(8,128)S(1)} %get-tuple-element.60), channel_id=1, source_target_pairs={{0,16},{8,24},{16,32},{24,40},{32,48},{40,56},{48,0},{56,8},{64,80... | collective-permute-start | bytes 884744 | tf_op jit(solution)/shard_map/ppermute | solution.py:375
  45.7 12.6 %collective-permute-start.12 = (f32[1,288,256]{2,1,0:T(8,128)S(1)}, f32[1,288,256]{2,1,0:T(8,128)S(1)}, u32[]{:S(2)}, u32[]{:S(2)}) collective-permute-start(f32[1,288,256]{2,1,0:T(8,128)S(1)} %add.45), channel_id=1, source_target_pairs={{0,64},{8,72},{16,80},{24,88},{32,96},{40,104},{48,112},{56,120},{... | collective-permute-start | bytes 884744 | tf_op jit(solution)/shard_map/ppermute | solution.py:375
  50.5 24.0 %copy-start.1 = (f32[256]{0:T(256)S(1)}, f32[256]{0:T(256)}, u32[]{:S(2)}) copy-start(f32[256]{0:T(256)} %param.13) | copy-start | bytes 3076
  50.6 8.9 %collective-permute-start.20 = (f32[1,288,256]{2,1,0:T(8,128)S(1)}, f32[1,288,256]{2,1,0:T(8,128)S(1)}, u32[]{:S(2)}, u32[]{:S(2)}) collective-permute-start(f32[1,288,256]{2,1,0:T(8,128)S(1)} %get-tuple-element.56), channel_id=1, source_target_pairs={{0,8},{8,0},{16,24},{24,16},{32,40},{40,32},{48,56},{56,48},{64,72... | collective-permute-start | bytes 884744 | tf_op jit(solution)/shard_map/ppermute | solution.py:375
  52.4 4.5 %collective-permute-start.17 = (f32[1,288,256]{2,1,0:T(8,128)S(1)}, f32[1,288,256]{2,1,0:T(8,128)S(1)}, u32[]{:S(2)}, u32[]{:S(2)}) collective-permute-start(f32[1,288,256]{2,1,0:T(8,128)S(1)} %get-tuple-element.55), channel_id=1, source_target_pairs={{0,8},{8,0},{16,24},{24,16},{32,40},{40,32},{48,56},{56,48},{64,72... | collective-permute-start | bytes 884744 | tf_op jit(solution)/shard_map/ppermute | solution.py:375
  52.4 17.9 %collective-permute-start.13 = (f32[1,288,256]{2,1,0:T(8,128)S(1)}, f32[1,288,256]{2,1,0:T(8,128)S(1)}, u32[]{:S(2)}, u32[]{:S(2)}) collective-permute-start(f32[1,288,256]{2,1,0:T(8,128)S(1)} %get-tuple-element.52), channel_id=1, source_target_pairs={{0,8},{8,0},{16,24},{24,16},{32,40},{40,32},{48,56},{56,48},{64,72... | collective-permute-start | bytes 884744 | tf_op jit(solution)/shard_map/ppermute | solution.py:375
  56.1 5.2 %collective-permute-start.22 = (f32[1,144,256]{2,1,0:T(8,128)S(1)}, f32[1,144,256]{2,1,0:T(8,128)S(1)}, u32[]{:S(2)}, u32[]{:S(2)}) collective-permute-start(f32[1,144,256]{2,1,0:T(8,128)S(1)} %get-tuple-element.68), channel_id=1, source_target_pairs={{0,48},{8,56},{16,0},{24,8},{32,16},{40,24},{48,32},{56,40},{64,11... | collective-permute-start | bytes 442376 | tf_op jit(solution)/shard_map/ppermute | solution.py:375
  56.9 8.0 %collective-permute-start.21 = (f32[1,144,256]{2,1,0:T(8,128)S(1)}, f32[1,144,256]{2,1,0:T(8,128)S(1)}, u32[]{:S(2)}, u32[]{:S(2)}) collective-permute-start(f32[1,144,256]{2,1,0:T(8,128)S(1)} %get-tuple-element.65), channel_id=1, source_target_pairs={{0,16},{8,24},{16,32},{24,40},{32,48},{40,56},{48,0},{56,8},{64,80... | collective-permute-start | bytes 442376 | tf_op jit(solution)/shard_map/ppermute | solution.py:375
  58.3 8.8 %collective-permute-start.18 = (f32[1,288,256]{2,1,0:T(8,128)S(1)}, f32[1,288,256]{2,1,0:T(8,128)S(1)}, u32[]{:S(2)}, u32[]{:S(2)}) collective-permute-start(f32[1,288,256]{2,1,0:T(8,128)S(1)} %add.49), channel_id=1, source_target_pairs={{0,64},{8,72},{16,80},{24,88},{32,96},{40,104},{48,112},{56,120},{... | collective-permute-start | bytes 884744 | tf_op jit(solution)/shard_map/ppermute | solution.py:375
  59.4 10.9 %collective-permute-start.14 = (f32[1,288,256]{2,1,0:T(8,128)S(1)}, f32[1,288,256]{2,1,0:T(8,128)S(1)}, u32[]{:S(2)}, u32[]{:S(2)}) collective-permute-start(f32[1,288,256]{2,1,0:T(8,128)S(1)} %maximum_add_fusion), channel_id=1, source_target_pairs={{0,16},{8,24},{16,32},{24,40},{32,48},{40,56},{48,0},{56,8},{64,80... | collective-permute-start | bytes 884744 | tf_op jit(solution)/shard_map/ppermute | solution.py:375
  64.9 7.6 %collective-permute-start.23 = (f32[1,288,256]{2,1,0:T(8,128)S(1)}, f32[1,288,256]{2,1,0:T(8,128)S(1)}, u32[]{:S(2)}, u32[]{:S(2)}) collective-permute-start(f32[1,288,256]{2,1,0:T(8,128)S(1)} %maximum_add_fusion.2), channel_id=1, source_target_pairs={{0,64},{8,72},{16,80},{24,88},{32,96},{40,104},{48,112},{56,120},{... | collective-permute-start | bytes 884744 | tf_op jit(solution)/shard_map/ppermute | solution.py:375
  67.2 7.4 %collective-permute-start.19 = (f32[1,288,256]{2,1,0:T(8,128)S(1)}, f32[1,288,256]{2,1,0:T(8,128)S(1)}, u32[]{:S(2)}, u32[]{:S(2)}) collective-permute-start(f32[1,288,256]{2,1,0:T(8,128)S(1)} %maximum_add_fusion.1), channel_id=1, source_target_pairs={{0,48},{8,56},{16,0},{24,8},{32,16},{40,24},{48,32},{56,40},{64,11... | collective-permute-start | bytes 884744 | tf_op jit(solution)/shard_map/ppermute | solution.py:375
  92.4 1.5 %collective-permute-start.24 = (f32[8,32,256]{2,1,0:T(8,128)S(1)}, f32[8,32,256]{2,1,0:T(8,128)S(1)}, u32[]{:S(2)}, u32[]{:S(2)}) collective-permute-start(f32[8,32,256]{2,1,0:T(8,128)S(1)} %all_to_all.5), channel_id=1, source_target_pairs={{0,8},{8,0},{16,24},{24,16},{32,40},{40,32},{48,56},{56,48},{64,72... | collective-permute-start | bytes 786440 | tf_op jit(solution)/shard_map/ppermute | solution.py:375

commit v7 on v6

--- a/solution.py
+++ b/solution.py
@@ -22,7 +22,8 @@
 FIT_POINTS = 4001
 ROWS = 16
 HALF = 16
-SOLVE_STEPS = 40
+SOLVE_STEPS = 42
+STEPS_A_CHECK = 3
 TOLERANCE = 1e-6
 
 
@@ -282,7 +283,7 @@
 
     def advance(state):
         done, _, earlier, alpha = state
-        for _ in range(2):
+        for _ in range(STEPS_A_CHECK):
             r = r_ref[...]
             applied_r = applied(r)
             rr = together(r * r)
@@ -297,7 +298,7 @@
             r_ref[...] = r - alpha * q
             earlier = rr
         r = r_ref[...]
-        return done + 2, jnp.max(jnp.where(together(r * r) <= goal, 0, 1)), earlier, alpha
+        return done + STEPS_A_CHECK, jnp.max(jnp.where(together(r * r) <= goal, 0, 1)), earlier, alpha
 
     def unfinished(state):
         return (state[1] > 0) & (state[0] < SOLVE_STEPS)

time: 96.4 us -> 96.3 us (level)
  no operation moved by 1% of the time
where the time goes in v7:
time: 96.3 us; the launch traced here: 95 us
  starting transfers between devices  27.8 us (29%)
  waiting for transfers between devices  26.2 us (27%)
  Pallas kernels  22.2 us (23%)
  blocking collectives  14.1 us (15%)
  local copies, waits for them, and re-layouts  3.32 us (3%)
  other arithmetic  1.22 us (1%)
    ppermute x17, waiting for transfers between devices, over_ap(): return lax.ppermute(value, 'ap', pairs)  16.9 us
    pallas_call x7, Pallas kernels, tone_systems(): pl.pallas_call(functools.partial(tone_kernel, distance, planes), in_specs...  14.7 us
    ppermute x8, starting transfers between devices, over_sc(): return lax.ppermute(value, 'sc', pairs)  14.4 us
    all_to_all x1, blocking collectives, all_steps(): lax.all_to_all(jnp.broadcast_to(own_tone[None], (chips, *own_tone.shape))...  14.1 us
    ppermute x17, starting transfers between devices, over_ap(): return lax.ppermute(value, 'ap', pairs)  13.3 us
    ppermute x8, waiting for transfers between devices, over_sc(): return lax.ppermute(value, 'sc', pairs)  9.27 us
    pallas_call x1, Pallas kernels, solved(): pl.pallas_call(solve_kernel, in_specs=[vmem] * (len(systems) + 1), out_sp...  3.69 us
    pallas_call x2, Pallas kernels, prepared(): pl.pallas_call(functools.partial(prepare_kernel, slots, len(tables), tone...  2.77 us
  transfers between devices with their start and end apart: 25, of which 11 were waited for; matrix products, arithmetic and copies ran while one was open for 4% of the time, Pallas kernels for 13%

profile of v7, /device:TPU:0, one launch (start us, length us, event | category | flops | bytes accessed | tf_op | source)
XLA Modules:
  0.0 95.0 jit_solution(2976174816371634785)
XLA Ops:
  0.0 1.0 %packed_tables.1.refs_0_ = f32[16,32,128]{2,1,0:T(8,128)S(1)} custom-call(f32[4,32,128]{2,1,0:T(8,128)} %refs_0_.1, f32[4,32,128]{2,1,0:T(8,128)} %refs_1_.1, f32[4,32,128]{2,1,0:T(8,128)} %refs_2_.1, f32[4,32,128]{2,1,0:T(8,128)} %refs_3_.1), custom_call_target="tpu_custom_call" | custom-call | tf_op jit(solution)/shard_map/packed_tables/pallas_call | solution.py:411
  1.0 4.1 %collective-permute-start.4 = (f32[16,32,128]{2,1,0:T(8,128)S(1)}, f32[16,32,128]{2,1,0:T(8,128)S(1)}, u32[]{:S(2)}, u32[]{:S(2)}) collective-permute-start(f32[16,32,128]{2,1,0:T(8,128)S(1)} %packed_tables.1.refs_0_), channel_id=1, source_target_pairs={{0,4},{1,5},{2,6},{3,7},{4,0},{5,1},{6,2},{7,3},{8,12},{9,13},{10,... | collective-permute-start | bytes 786440 | tf_op jit(solution)/shard_map/ppermute | solution.py:382
  5.0 1.5 %collective-permute-start = (f32[16,32,128]{2,1,0:T(8,128)S(1)}, f32[16,32,128]{2,1,0:T(8,128)S(1)}, u32[]{:S(2)}, u32[]{:S(2)}) collective-permute-start(f32[16,32,128]{2,1,0:T(8,128)S(1)} %packed_tables.1.refs_0_), channel_id=1, source_target_pairs={{0,1},{1,2},{2,3},{3,0},{4,5},{5,6},{6,7},{7,4},{8,9},{9,10},{10,1... | collective-permute-start | bytes 786440 | tf_op jit(solution)/shard_map/ppermute | solution.py:382
  6.5 1.7 %collective-permute-start.2 = (f32[16,32,128]{2,1,0:T(8,128)S(1)}, f32[16,32,128]{2,1,0:T(8,128)S(1)}, u32[]{:S(2)}, u32[]{:S(2)}) collective-permute-start(f32[16,32,128]{2,1,0:T(8,128)S(1)} %packed_tables.1.refs_0_), channel_id=1, source_target_pairs={{0,3},{1,0},{2,1},{3,2},{4,7},{5,4},{6,5},{7,6},{8,11},{9,8},{10,9... | collective-permute-start | bytes 786440 | tf_op jit(solution)/shard_map/ppermute | solution.py:382
  8.3 1.5 %reshape.10 = f32[16,2,14,512]{3,0,2,1:T(8,128)S(1)} reshape(f32[16,2,14,4,128]{4,3,0,2,1:T(4,128)} %bitcast.17) | data formatting | bytes 1835008 | tf_op jit(solution)/shard_map/reshape | solution.py:361
  9.8 0.1 fusion.1
  9.9 0.5 copy_bitcast_fusion
  10.5 3.6 %collective-permute-done.refs_2_ = f32[16,32,128]{2,1,0:T(8,128)S(1)} collective-permute-done((f32[16,32,128]{2,1,0:T(8,128)S(1)}, f32[16,32,128]{2,1,0:T(8,128)S(1)}, u32[]{:S(2)}, u32[]{:S(2)}) %collective-permute-start) | collective-permute-done | bytes 262176 | tf_op jit(solution)/shard_map/ppermute | solution.py:382
  14.0 0.3 collective-permute-start.1
  14.4 0.0 collective-permute-done.2.refs_3_
  14.4 3.0 %collective-permute-start.3 = (f32[8,32,128]{2,1,0:T(8,128)S(1)}, f32[8,32,128]{2,1,0:T(8,128)S(1)}, u32[]{:S(2)}, u32[]{:S(2)}) collective-permute-start(f32[8,32,128]{2,1,0:T(8,128)S(1)} %slice.63), channel_id=1, source_target_pairs={{0,3},{1,0},{2,1},{3,2},{4,7},{5,4},{6,5},{7,6},{8,11},{9,8},{10,9... | collective-permute-start | bytes 393224 | tf_op jit(solution)/shard_map/ppermute | solution.py:382
  17.4 0.3 fusion
  17.7 0.0 copy-start
  17.8 0.1 collective-permute-start.5
  17.8 3.2 %collective-permute-start.6 = (f32[16,32,128]{2,1,0:T(8,128)S(1)}, f32[16,32,128]{2,1,0:T(8,128)S(1)}, u32[]{:S(2)}, u32[]{:S(2)}) collective-permute-start(f32[16,32,128]{2,1,0:T(8,128)S(1)} %collective-permute-done.4.refs_1_), channel_id=1, source_target_pairs={{0,3},{1,0},{2,1},{3,2},{4,7},{5,4},{6,5},{7,6},{8,11},{9,8},{10,9... | collective-permute-start | bytes 786440 | tf_op jit(solution)/shard_map/ppermute | solution.py:382
  21.1 0.4 collective-permute-start.7
  21.6 0.3 select_maximum_fusion.1
  21.8 0.1 pad_maximum_fusion.y_ref
  22.0 1.4 %prepared.2 = (f32[4,4,2,256,128]{4,3,2,1,0:T(8,128)S(1)}, f32[8,4,2,256,128]{4,3,2,1,0:T(8,128)S(1)}) custom-call(f32[16,32,128]{2,1,0:T(8,128)S(1)} %packed_tables.1.refs_0_, f32[16,32,128]{2,1,0:T(8,128)S(1)} %collective-permute-done.4.refs_1_, f32[16,32,128]{2,1,0:T(8,128)S(1)} %collective-permute-done.refs_2_, ...), custom_call_target="tpu_custom_call" | custom-call | tf_op jit(solution)/shard_map/prepared/pallas_call | solution.py:123
  23.4 2.5 %collective-permute-done.5.refs_1_ = f32[16,32,128]{2,1,0:T(8,128)S(1)} collective-permute-done((f32[16,32,128]{2,1,0:T(8,128)S(1)}, f32[16,32,128]{2,1,0:T(8,128)S(1)}, u32[]{:S(2)}, u32[]{:S(2)}) %collective-permute-start.5) | collective-permute-done | bytes 262176 | tf_op jit(solution)/shard_map/ppermute | solution.py:382
  25.9 0.0 collective-permute-done.6.refs_2_
  25.9 3.2 %collective-permute-done.7.refs_3_ = f32[16,32,128]{2,1,0:T(8,128)S(1)} collective-permute-done((f32[16,32,128]{2,1,0:T(8,128)S(1)}, f32[16,32,128]{2,1,0:T(8,128)S(1)}, u32[]{:S(2)}, u32[]{:S(2)}) %collective-permute-start.7) | collective-permute-done | bytes 262176 | tf_op jit(solution)/shard_map/ppermute | solution.py:382
  29.1 1.4 %prepared.3 = (f32[4,4,2,256,128]{4,3,2,1,0:T(8,128)S(1)}, f32[8,4,2,256,128]{4,3,2,1,0:T(8,128)S(1)}) custom-call(f32[16,32,128]{2,1,0:T(8,128)S(1)} %constant_dynamic-update-slice_fusion.refs_0_, f32[16,32,128]{2,1,0:T(8,128)S(1)} %collective-permute-done.5.refs_1_, ...), custom_call_target="tpu_custom_call", output_to_operand_aliasing={{0}: (5, {}), {1}: (6, {})} | custom-call | tf_op jit(solution)/shard_map/prepared/pallas_call | solution.py:123
  30.4 3.4 %tone_systems.7 = (f32[2,288,256]{2,1,0:T(8,128)S(1)}, f32[2,288,256]{2,1,0:T(8,128)S(1)}) custom-call(f32[16,32,1024]{2,1,0:T(8,128)S(1)} %pad_maximum_fusion.y_ref, f32[4,4,2,256,128]{4,3,2,1,0:T(8,128)S(1)} %get-tuple-element.33.lead, f32[8,4,2,256,128]{4,3,2,1,0:T(8,128)S(1)} %get-tuple-element.34.turn), custom_call_target="tpu_custom_call" | custom-call | tf_op jit(solution)/shard_map/tone_systems/pallas_call | solution.py:216
  33.8 0.1 collective-permute-start.8
  33.9 1.9 %tone_systems.8 = (f32[1,288,256]{2,1,0:T(8,128)S(1)}, f32[1,288,256]{2,1,0:T(8,128)S(1)}) custom-call(f32[16,32,1024]{2,1,0:T(8,128)S(1)} %pad_maximum_fusion.y_ref, f32[4,4,2,256,128]{4,3,2,1,0:T(8,128)S(1)} %get-tuple-element.33.lead, f32[8,4,2,256,128]{4,3,2,1,0:T(8,128)S(1)} %get-tuple-element.34.turn), custom_call_target="tpu_custom_call" | custom-call | tf_op jit(solution)/shard_map/tone_systems/pallas_call | solution.py:216
  35.8 0.5 collective-permute-start.11
  36.3 0.1 add.42
  36.4 1.9 %tone_systems.9 = (f32[1,288,256]{2,1,0:T(8,128)S(1)}, f32[1,288,256]{2,1,0:T(8,128)S(1)}) custom-call(f32[16,32,1024]{2,1,0:T(8,128)S(1)} %pad_maximum_fusion.y_ref, f32[4,4,2,256,128]{4,3,2,1,0:T(8,128)S(1)} %get-tuple-element.33.lead, f32[8,4,2,256,128]{4,3,2,1,0:T(8,128)S(1)} %get-tuple-element.34.turn), custom_call_target="tpu_custom_call" | custom-call | tf_op jit(solution)/shard_map/tone_systems/pallas_call | solution.py:216
  38.3 1.9 %tone_systems.10 = (f32[1,288,256]{2,1,0:T(8,128)S(1)}, f32[1,288,256]{2,1,0:T(8,128)S(1)}) custom-call(f32[16,32,1024]{2,1,0:T(8,128)S(1)} %pad_maximum_fusion.y_ref, f32[4,4,2,256,128]{4,3,2,1,0:T(8,128)S(1)} %get-tuple-element.33.lead, f32[8,4,2,256,128]{4,3,2,1,0:T(8,128)S(1)} %get-tuple-element.34.turn), custom_call_target="tpu_custom_call" | custom-call | tf_op jit(solution)/shard_map/tone_systems/pallas_call | solution.py:216
  40.2 1.9 %tone_systems.11 = (f32[1,288,256]{2,1,0:T(8,128)S(1)}, f32[1,288,256]{2,1,0:T(8,128)S(1)}) custom-call(f32[16,32,1024]{2,1,0:T(8,128)S(1)} %pad_maximum_fusion.y_ref, f32[4,4,2,256,128]{4,3,2,1,0:T(8,128)S(1)} %get-tuple-element.33.lead, f32[8,4,2,256,128]{4,3,2,1,0:T(8,128)S(1)} %get-tuple-element.34.turn), custom_call_target="tpu_custom_call" | custom-call | tf_op jit(solution)/shard_map/tone_systems/pallas_call | solution.py:216
  42.1 0.2 collective-permute-start.15
  42.4 3.1 %collective-permute-start.16 = (f32[2,144,256]{2,1,0:T(8,128)S(1)}, f32[2,144,256]{2,1,0:T(8,128)S(1)}, u32[]{:S(2)}, u32[]{:S(2)}) collective-permute-start(f32[2,144,256]{2,1,0:T(8,128)S(1)} %get-tuple-element.59), channel_id=1, source_target_pairs={{0,48},{8,56},{16,0},{24,8},{32,16},{40,24},{48,32},{56,40},{64,11... | collective-permute-start | bytes 884744 | tf_op jit(solution)/shard_map/ppermute | solution.py:376
  45.5 0.2 collective-permute-start.9
  45.6 0.0 collective-permute-start.10
  45.7 1.1 %collective-permute-start.12 = (f32[1,288,256]{2,1,0:T(8,128)S(1)}, f32[1,288,256]{2,1,0:T(8,128)S(1)}, u32[]{:S(2)}, u32[]{:S(2)}) collective-permute-start(f32[1,288,256]{2,1,0:T(8,128)S(1)} %add.45), channel_id=1, source_target_pairs={{0,64},{8,72},{16,80},{24,88},{32,96},{40,104},{48,112},{56,120},{... | collective-permute-start | bytes 884744 | tf_op jit(solution)/shard_map/ppermute | solution.py:376
  46.8 1.9 %tone_systems.12 = (f32[1,288,256]{2,1,0:T(8,128)S(1)}, f32[1,288,256]{2,1,0:T(8,128)S(1)}) custom-call(f32[16,32,1024]{2,1,0:T(8,128)S(1)} %pad_maximum_fusion.y_ref, f32[4,4,2,256,128]{4,3,2,1,0:T(8,128)S(1)} %get-tuple-element.33.lead, f32[8,4,2,256,128]{4,3,2,1,0:T(8,128)S(1)} %get-tuple-element.34.turn), custom_call_target="tpu_custom_call" | custom-call | tf_op jit(solution)/shard_map/tone_systems/pallas_call | solution.py:216
  48.7 1.9 %tone_systems.13 = (f32[1,288,256]{2,1,0:T(8,128)S(1)}, f32[1,288,256]{2,1,0:T(8,128)S(1)}) custom-call(f32[16,32,1024]{2,1,0:T(8,128)S(1)} %pad_maximum_fusion.y_ref, f32[4,4,2,256,128]{4,3,2,1,0:T(8,128)S(1)} %get-tuple-element.33.lead, f32[8,4,2,256,128]{4,3,2,1,0:T(8,128)S(1)} %get-tuple-element.34.turn), custom_call_target="tpu_custom_call" | custom-call | tf_op jit(solution)/shard_map/tone_systems/pallas_call | solution.py:216
  50.5 0.0 collective-permute-done.15
  50.6 0.1 collective-permute-start.20
  50.7 1.6 %collective-permute-done.16 = f32[2,144,256]{2,1,0:T(8,128)S(1)} collective-permute-done((f32[2,144,256]{2,1,0:T(8,128)S(1)}, f32[2,144,256]{2,1,0:T(8,128)S(1)}, u32[]{:S(2)}, u32[]{:S(2)}) %collective-permute-start.16) | collective-permute-done | bytes 294944 | tf_op jit(solution)/shard_map/ppermute | solution.py:376
  52.4 0.0 collective-permute-start.17
  52.4 0.0 collective-permute-done.9
  52.4 0.6 collective-permute-start.13
  53.0 3.1 %collective-permute-done.10 = f32[2,144,256]{2,1,0:T(8,128)S(1)} collective-permute-done((f32[2,144,256]{2,1,0:T(8,128)S(1)}, f32[2,144,256]{2,1,0:T(8,128)S(1)}, u32[]{:S(2)}, u32[]{:S(2)}) %collective-permute-start.10) | collective-permute-done | bytes 294944 | tf_op jit(solution)/shard_map/ppermute | solution.py:376
  56.1 0.7 collective-permute-start.22
  56.9 0.0 collective-permute-done.17
  56.9 1.4 %collective-permute-start.21 = (f32[1,144,256]{2,1,0:T(8,128)S(1)}, f32[1,144,256]{2,1,0:T(8,128)S(1)}, u32[]{:S(2)}, u32[]{:S(2)}) collective-permute-start(f32[1,144,256]{2,1,0:T(8,128)S(1)} %get-tuple-element.65), channel_id=1, source_target_pairs={{0,16},{8,24},{16,32},{24,40},{32,48},{40,56},{48,0},{56,8},{64,80... | collective-permute-start | bytes 442376 | tf_op jit(solution)/shard_map/ppermute | solution.py:376
  58.3 1.1 %collective-permute-start.18 = (f32[1,288,256]{2,1,0:T(8,128)S(1)}, f32[1,288,256]{2,1,0:T(8,128)S(1)}, u32[]{:S(2)}, u32[]{:S(2)}) collective-permute-start(f32[1,288,256]{2,1,0:T(8,128)S(1)} %add.49), channel_id=1, source_target_pairs={{0,64},{8,72},{16,80},{24,88},{32,96},{40,104},{48,112},{56,120},{... | collective-permute-start | bytes 884744 | tf_op jit(solution)/shard_map/ppermute | solution.py:376
  59.4 0.0 collective-permute-done.20
  59.4 0.1 collective-permute-start.14
  59.5 1.8 %collective-permute-done.22 = f32[1,144,256]{2,1,0:T(8,128)S(1)} collective-permute-done((f32[1,144,256]{2,1,0:T(8,128)S(1)}, f32[1,144,256]{2,1,0:T(8,128)S(1)}, u32[]{:S(2)}, u32[]{:S(2)}) %collective-permute-start.22) | collective-permute-done | bytes 147488 | tf_op jit(solution)/shard_map/ppermute | solution.py:376
  61.3 3.5 %collective-permute-done.21 = f32[1,144,256]{2,1,0:T(8,128)S(1)} collective-permute-done((f32[1,144,256]{2,1,0:T(8,128)S(1)}, f32[1,144,256]{2,1,0:T(8,128)S(1)}, u32[]{:S(2)}, u32[]{:S(2)}) %collective-permute-start.21) | collective-permute-done | bytes 147488 | tf_op jit(solution)/shard_map/ppermute | solution.py:376
  64.9 0.1 maximum_add_fusion.2
  64.9 1.1 %collective-permute-start.23 = (f32[1,288,256]{2,1,0:T(8,128)S(1)}, f32[1,288,256]{2,1,0:T(8,128)S(1)}, u32[]{:S(2)}, u32[]{:S(2)}) collective-permute-start(f32[1,288,256]{2,1,0:T(8,128)S(1)} %maximum_add_fusion.2), channel_id=1, source_target_pairs={{0,64},{8,72},{16,80},{24,88},{32,96},{40,104},{48,112},{56,120},{... | collective-permute-start | bytes 884744 | tf_op jit(solution)/shard_map/ppermute | solution.py:376
  66.0 1.1 %collective-permute-done.18 = f32[1,288,256]{2,1,0:T(8,128)S(1)} collective-permute-done((f32[1,288,256]{2,1,0:T(8,128)S(1)}, f32[1,288,256]{2,1,0:T(8,128)S(1)}, u32[]{:S(2)}, u32[]{:S(2)}) %collective-permute-start.18) | collective-permute-done | bytes 294944 | tf_op jit(solution)/shard_map/ppermute | solution.py:376
  67.2 3.1 %collective-permute-start.19 = (f32[1,288,256]{2,1,0:T(8,128)S(1)}, f32[1,288,256]{2,1,0:T(8,128)S(1)}, u32[]{:S(2)}, u32[]{:S(2)}) collective-permute-start(f32[1,288,256]{2,1,0:T(8,128)S(1)} %maximum_add_fusion.1), channel_id=1, source_target_pairs={{0,48},{8,56},{16,0},{24,8},{32,16},{40,24},{48,32},{56,40},{64,11... | collective-permute-start | bytes 884744 | tf_op jit(solution)/shard_map/ppermute | solution.py:376
  70.3 0.0 collective-permute-done.14.refs_2_
  70.3 2.2 %collective-permute-done.23.refs_4_ = f32[1,288,256]{2,1,0:T(8,128)S(1)} collective-permute-done((f32[1,288,256]{2,1,0:T(8,128)S(1)}, f32[1,288,256]{2,1,0:T(8,128)S(1)}, u32[]{:S(2)}, u32[]{:S(2)}) %collective-permute-start.23) | collective-permute-done | bytes 294944 | tf_op jit(solution)/shard_map/ppermute | solution.py:376
  72.5 2.0 %collective-permute-done.19.refs_3_ = f32[1,288,256]{2,1,0:T(8,128)S(1)} collective-permute-done((f32[1,288,256]{2,1,0:T(8,128)S(1)}, f32[1,288,256]{2,1,0:T(8,128)S(1)}, u32[]{:S(2)}, u32[]{:S(2)}) %collective-permute-start.19) | collective-permute-done | bytes 294944 | tf_op jit(solution)/shard_map/ppermute | solution.py:376
  74.5 3.7 %solved.1 = f32[32,256]{1,0:T(8,128)S(1)} custom-call(f32[1,288,256]{2,1,0:T(8,128)S(1)} %get-tuple-element.51.refs_0_, f32[1,288,256]{2,1,0:T(8,128)S(1)} %collective-permute-done.13.refs_1_, f32[1,288,256]{2,1,0:T(8,128)S(1)} %collective-permute-done.14.refs_2_, f32[1,288,256]{2,1,0:T(8,128)S(1)} %collective-permute-done.19.refs_3_, ...), custom_call_target="tpu_custom_call" | custom-call | tf_op jit(solution)/shard_map/solved/pallas_call | solution.py:340
  78.3 14.1 %all_to_all.5 = f32[8,32,256]{2,1,0:T(8,128)S(1)} all-to-all(f32[8,32,256]{2,1,0:T(8,128)S(1)} %broadcast_in_dim.2), channel_id=1, replica_groups={{0,16,32,48,64,80,96,112},{8,24,40,56,72,88,104,120},{1,17,33,49,65,81,..., dimensions={0} | all-to-all | bytes 524288 | tf_op jit(solution)/shard_map/all_to_all | solution.py:472
  92.4 1.5 %collective-permute-done.24 = f32[8,32,256]{2,1,0:T(8,128)S(1)} collective-permute-done((f32[8,32,256]{2,1,0:T(8,128)S(1)}, f32[8,32,256]{2,1,0:T(8,128)S(1)}, u32[]{:S(2)}, u32[]{:S(2)}) %collective-permute-start.24) | collective-permute-done | bytes 262176 | tf_op jit(solution)/shard_map/ppermute | solution.py:376
  94.0 1.0 %copy.24 = f32[16,2,14,256]{3,0,2,1:T(8,128)} copy(f32[16,2,14,256]{3,2,1,0:T(8,128)S(1)} %bitcast.16) | data formatting | bytes 917504
  (28 shorter events, 0.5 us)
Async XLA Ops:
  1.0 16.8 %collective-permute-start.4 = (f32[16,32,128]{2,1,0:T(8,128)S(1)}, f32[16,32,128]{2,1,0:T(8,128)S(1)}, u32[]{:S(2)}, u32[]{:S(2)}) collective-permute-start(f32[16,32,128]{2,1,0:T(8,128)S(1)} %packed_tables.1.refs_0_), channel_id=1, source_target_pairs={{0,4},{1,5},{2,6},{3,7},{4,0},{5,1},{6,2},{7,3},{8,12},{9,13},{10,... | collective-permute-start | bytes 786440 | tf_op jit(solution)/shard_map/ppermute | solution.py:382
  5.0 9.0 %collective-permute-start = (f32[16,32,128]{2,1,0:T(8,128)S(1)}, f32[16,32,128]{2,1,0:T(8,128)S(1)}, u32[]{:S(2)}, u32[]{:S(2)}) collective-permute-start(f32[16,32,128]{2,1,0:T(8,128)S(1)} %packed_tables.1.refs_0_), channel_id=1, source_target_pairs={{0,1},{1,2},{2,3},{3,0},{4,5},{5,6},{6,7},{7,4},{8,9},{9,10},{10,1... | collective-permute-start | bytes 786440 | tf_op jit(solution)/shard_map/ppermute | solution.py:382
  6.5 7.9 %collective-permute-start.2 = (f32[16,32,128]{2,1,0:T(8,128)S(1)}, f32[16,32,128]{2,1,0:T(8,128)S(1)}, u32[]{:S(2)}, u32[]{:S(2)}) collective-permute-start(f32[16,32,128]{2,1,0:T(8,128)S(1)} %packed_tables.1.refs_0_), channel_id=1, source_target_pairs={{0,3},{1,0},{2,1},{3,2},{4,7},{5,4},{6,5},{7,6},{8,11},{9,8},{10,9... | collective-permute-start | bytes 786440 | tf_op jit(solution)/shard_map/ppermute | solution.py:382
  14.0 7.0 %collective-permute-start.1 = (f32[8,32,128]{2,1,0:T(8,128)S(1)}, f32[8,32,128]{2,1,0:T(8,128)S(1)}, u32[]{:S(2)}, u32[]{:S(2)}) collective-permute-start(f32[8,32,128]{2,1,0:T(8,128)S(1)} %slice.62), channel_id=1, source_target_pairs={{0,1},{1,2},{2,3},{3,0},{4,5},{5,6},{6,7},{7,4},{8,9},{9,10},{10,1... | collective-permute-start | bytes 393224 | tf_op jit(solution)/shard_map/ppermute | solution.py:382
  14.4 6.7 %collective-permute-start.3 = (f32[8,32,128]{2,1,0:T(8,128)S(1)}, f32[8,32,128]{2,1,0:T(8,128)S(1)}, u32[]{:S(2)}, u32[]{:S(2)}) collective-permute-start(f32[8,32,128]{2,1,0:T(8,128)S(1)} %slice.63), channel_id=1, source_target_pairs={{0,3},{1,0},{2,1},{3,2},{4,7},{5,4},{6,5},{7,6},{8,11},{9,8},{10,9... | collective-permute-start | bytes 393224 | tf_op jit(solution)/shard_map/ppermute | solution.py:382
  17.7 4.2 %copy-start = (s32[256,128]{1,0:T(8,128)S(1)}, s32[256,128]{1,0:T(8,128)}, u32[]{:S(2)}) copy-start(s32[256,128]{1,0:T(8,128)} %refs_4_.3) | copy-start | bytes 393220
  17.8 8.1 %collective-permute-start.5 = (f32[16,32,128]{2,1,0:T(8,128)S(1)}, f32[16,32,128]{2,1,0:T(8,128)S(1)}, u32[]{:S(2)}, u32[]{:S(2)}) collective-permute-start(f32[16,32,128]{2,1,0:T(8,128)S(1)} %collective-permute-done.4.refs_1_), channel_id=1, source_target_pairs={{0,1},{1,2},{2,3},{3,0},{4,5},{5,6},{6,7},{7,4},{8,9},{9,10},{10,1... | collective-permute-start | bytes 786440 | tf_op jit(solution)/shard_map/ppermute | solution.py:382
  17.8 8.1 %collective-permute-start.6 = (f32[16,32,128]{2,1,0:T(8,128)S(1)}, f32[16,32,128]{2,1,0:T(8,128)S(1)}, u32[]{:S(2)}, u32[]{:S(2)}) collective-permute-start(f32[16,32,128]{2,1,0:T(8,128)S(1)} %collective-permute-done.4.refs_1_), channel_id=1, source_target_pairs={{0,3},{1,0},{2,1},{3,2},{4,7},{5,4},{6,5},{7,6},{8,11},{9,8},{10,9... | collective-permute-start | bytes 786440 | tf_op jit(solution)/shard_map/ppermute | solution.py:382
  21.1 8.0 %collective-permute-start.7 = (f32[16,32,128]{2,1,0:T(8,128)S(1)}, f32[16,32,128]{2,1,0:T(8,128)S(1)}, u32[]{:S(2)}, u32[]{:S(2)}) collective-permute-start(f32[16,32,128]{2,1,0:T(8,128)S(1)} %constant_dynamic-update-slice_fusion.refs_0_), channel_id=1, source_target_pairs={{0,4},{1,5},{2,6},{3,7},{4,0},{5,1},{6,2},{7,3},{8,12},{9,13},{10,... | collective-permute-start | bytes 786440 | tf_op jit(solution)/shard_map/ppermute | solution.py:382
  33.8 2.5 %collective-permute-start.8 = (f32[2,288,256]{2,1,0:T(8,128)S(1)}, f32[2,288,256]{2,1,0:T(8,128)S(1)}, u32[]{:S(2)}, u32[]{:S(2)}) collective-permute-start(f32[2,288,256]{2,1,0:T(8,128)S(1)} %get-tuple-element.36), channel_id=1, source_target_pairs={{0,8},{8,0},{16,24},{24,16},{32,40},{40,32},{48,56},{56,48},{64,72... | collective-permute-start | bytes 1769480 | tf_op jit(solution)/shard_map/ppermute | solution.py:376
  35.8 9.8 %collective-permute-start.11 = (f32[1,288,256]{2,1,0:T(8,128)S(1)}, f32[1,288,256]{2,1,0:T(8,128)S(1)}, u32[]{:S(2)}, u32[]{:S(2)}) collective-permute-start(f32[1,288,256]{2,1,0:T(8,128)S(1)} %get-tuple-element.42), channel_id=1, source_target_pairs={{0,8},{8,0},{16,24},{24,16},{32,40},{40,32},{48,56},{56,48},{64,72... | collective-permute-start | bytes 884744 | tf_op jit(solution)/shard_map/ppermute | solution.py:376
  42.1 8.5 %collective-permute-start.15 = (f32[1,288,256]{2,1,0:T(8,128)S(1)}, f32[1,288,256]{2,1,0:T(8,128)S(1)}, u32[]{:S(2)}, u32[]{:S(2)}) collective-permute-start(f32[1,288,256]{2,1,0:T(8,128)S(1)} %get-tuple-element.54), channel_id=1, source_target_pairs={{0,8},{8,0},{16,24},{24,16},{32,40},{40,32},{48,56},{56,48},{64,72... | collective-permute-start | bytes 884744 | tf_op jit(solution)/shard_map/ppermute | solution.py:376
  42.4 10.0 %collective-permute-start.16 = (f32[2,144,256]{2,1,0:T(8,128)S(1)}, f32[2,144,256]{2,1,0:T(8,128)S(1)}, u32[]{:S(2)}, u32[]{:S(2)}) collective-permute-start(f32[2,144,256]{2,1,0:T(8,128)S(1)} %get-tuple-element.59), channel_id=1, source_target_pairs={{0,48},{8,56},{16,0},{24,8},{32,16},{40,24},{48,32},{56,40},{64,11... | collective-permute-start | bytes 884744 | tf_op jit(solution)/shard_map/ppermute | solution.py:376
  45.5 6.9 %collective-permute-start.9 = (f32[1,288,256]{2,1,0:T(8,128)S(1)}, f32[1,288,256]{2,1,0:T(8,128)S(1)}, u32[]{:S(2)}, u32[]{:S(2)}) collective-permute-start(f32[1,288,256]{2,1,0:T(8,128)S(1)} %get-tuple-element.41), channel_id=1, source_target_pairs={{0,8},{8,0},{16,24},{24,16},{32,40},{40,32},{48,56},{56,48},{64,72... | collective-permute-start | bytes 884744 | tf_op jit(solution)/shard_map/ppermute | solution.py:376
  45.6 10.4 %collective-permute-start.10 = (f32[2,144,256]{2,1,0:T(8,128)S(1)}, f32[2,144,256]{2,1,0:T(8,128)S(1)}, u32[]{:S(2)}, u32[]{:S(2)}) collective-permute-start(f32[2,144,256]{2,1,0:T(8,128)S(1)} %get-tuple-element.60), channel_id=1, source_target_pairs={{0,16},{8,24},{16,32},{24,40},{32,48},{40,56},{48,0},{56,8},{64,80... | collective-permute-start | bytes 884744 | tf_op jit(solution)/shard_map/ppermute | solution.py:376
  45.7 12.6 %collective-permute-start.12 = (f32[1,288,256]{2,1,0:T(8,128)S(1)}, f32[1,288,256]{2,1,0:T(8,128)S(1)}, u32[]{:S(2)}, u32[]{:S(2)}) collective-permute-start(f32[1,288,256]{2,1,0:T(8,128)S(1)} %add.45), channel_id=1, source_target_pairs={{0,64},{8,72},{16,80},{24,88},{32,96},{40,104},{48,112},{56,120},{... | collective-permute-start | bytes 884744 | tf_op jit(solution)/shard_map/ppermute | solution.py:376
  50.5 24.0 %copy-start.1 = (f32[256]{0:T(256)S(1)}, f32[256]{0:T(256)}, u32[]{:S(2)}) copy-start(f32[256]{0:T(256)} %param.13) | copy-start | bytes 3076
  50.6 8.9 %collective-permute-start.20 = (f32[1,288,256]{2,1,0:T(8,128)S(1)}, f32[1,288,256]{2,1,0:T(8,128)S(1)}, u32[]{:S(2)}, u32[]{:S(2)}) collective-permute-start(f32[1,288,256]{2,1,0:T(8,128)S(1)} %get-tuple-element.56), channel_id=1, source_target_pairs={{0,8},{8,0},{16,24},{24,16},{32,40},{40,32},{48,56},{56,48},{64,72... | collective-permute-start | bytes 884744 | tf_op jit(solution)/shard_map/ppermute | solution.py:376
  52.4 4.5 %collective-permute-start.17 = (f32[1,288,256]{2,1,0:T(8,128)S(1)}, f32[1,288,256]{2,1,0:T(8,128)S(1)}, u32[]{:S(2)}, u32[]{:S(2)}) collective-permute-start(f32[1,288,256]{2,1,0:T(8,128)S(1)} %get-tuple-element.55), channel_id=1, source_target_pairs={{0,8},{8,0},{16,24},{24,16},{32,40},{40,32},{48,56},{56,48},{64,72... | collective-permute-start | bytes 884744 | tf_op jit(solution)/shard_map/ppermute | solution.py:376
  52.4 17.9 %collective-permute-start.13 = (f32[1,288,256]{2,1,0:T(8,128)S(1)}, f32[1,288,256]{2,1,0:T(8,128)S(1)}, u32[]{:S(2)}, u32[]{:S(2)}) collective-permute-start(f32[1,288,256]{2,1,0:T(8,128)S(1)} %get-tuple-element.52), channel_id=1, source_target_pairs={{0,8},{8,0},{16,24},{24,16},{32,40},{40,32},{48,56},{56,48},{64,72... | collective-permute-start | bytes 884744 | tf_op jit(solution)/shard_map/ppermute | solution.py:376
  56.1 5.2 %collective-permute-start.22 = (f32[1,144,256]{2,1,0:T(8,128)S(1)}, f32[1,144,256]{2,1,0:T(8,128)S(1)}, u32[]{:S(2)}, u32[]{:S(2)}) collective-permute-start(f32[1,144,256]{2,1,0:T(8,128)S(1)} %get-tuple-element.68), channel_id=1, source_target_pairs={{0,48},{8,56},{16,0},{24,8},{32,16},{40,24},{48,32},{56,40},{64,11... | collective-permute-start | bytes 442376 | tf_op jit(solution)/shard_map/ppermute | solution.py:376
  56.9 8.0 %collective-permute-start.21 = (f32[1,144,256]{2,1,0:T(8,128)S(1)}, f32[1,144,256]{2,1,0:T(8,128)S(1)}, u32[]{:S(2)}, u32[]{:S(2)}) collective-permute-start(f32[1,144,256]{2,1,0:T(8,128)S(1)} %get-tuple-element.65), channel_id=1, source_target_pairs={{0,16},{8,24},{16,32},{24,40},{32,48},{40,56},{48,0},{56,8},{64,80... | collective-permute-start | bytes 442376 | tf_op jit(solution)/shard_map/ppermute | solution.py:376
  58.3 8.8 %collective-permute-start.18 = (f32[1,288,256]{2,1,0:T(8,128)S(1)}, f32[1,288,256]{2,1,0:T(8,128)S(1)}, u32[]{:S(2)}, u32[]{:S(2)}) collective-permute-start(f32[1,288,256]{2,1,0:T(8,128)S(1)} %add.49), channel_id=1, source_target_pairs={{0,64},{8,72},{16,80},{24,88},{32,96},{40,104},{48,112},{56,120},{... | collective-permute-start | bytes 884744 | tf_op jit(solution)/shard_map/ppermute | solution.py:376
  59.4 10.9 %collective-permute-start.14 = (f32[1,288,256]{2,1,0:T(8,128)S(1)}, f32[1,288,256]{2,1,0:T(8,128)S(1)}, u32[]{:S(2)}, u32[]{:S(2)}) collective-permute-start(f32[1,288,256]{2,1,0:T(8,128)S(1)} %maximum_add_fusion), channel_id=1, source_target_pairs={{0,16},{8,24},{16,32},{24,40},{32,48},{40,56},{48,0},{56,8},{64,80... | collective-permute-start | bytes 884744 | tf_op jit(solution)/shard_map/ppermute | solution.py:376
  64.9 7.6 %collective-permute-start.23 = (f32[1,288,256]{2,1,0:T(8,128)S(1)}, f32[1,288,256]{2,1,0:T(8,128)S(1)}, u32[]{:S(2)}, u32[]{:S(2)}) collective-permute-start(f32[1,288,256]{2,1,0:T(8,128)S(1)} %maximum_add_fusion.2), channel_id=1, source_target_pairs={{0,64},{8,72},{16,80},{24,88},{32,96},{40,104},{48,112},{56,120},{... | collective-permute-start | bytes 884744 | tf_op jit(solution)/shard_map/ppermute | solution.py:376
  67.2 7.4 %collective-permute-start.19 = (f32[1,288,256]{2,1,0:T(8,128)S(1)}, f32[1,288,256]{2,1,0:T(8,128)S(1)}, u32[]{:S(2)}, u32[]{:S(2)}) collective-permute-start(f32[1,288,256]{2,1,0:T(8,128)S(1)} %maximum_add_fusion.1), channel_id=1, source_target_pairs={{0,48},{8,56},{16,0},{24,8},{32,16},{40,24},{48,32},{56,40},{64,11... | collective-permute-start | bytes 884744 | tf_op jit(solution)/shard_map/ppermute | solution.py:376
  92.4 1.5 %collective-permute-start.24 = (f32[8,32,256]{2,1,0:T(8,128)S(1)}, f32[8,32,256]{2,1,0:T(8,128)S(1)}, u32[]{:S(2)}, u32[]{:S(2)}) collective-permute-start(f32[8,32,256]{2,1,0:T(8,128)S(1)} %all_to_all.5), channel_id=1, source_target_pairs={{0,8},{8,0},{16,24},{24,16},{32,40},{40,32},{48,56},{56,48},{64,72... | collective-permute-start | bytes 786440 | tf_op jit(solution)/shard_map/ppermute | solution.py:376

commit v8 on v5

--- a/solution.py
+++ b/solution.py
@@ -445,20 +445,26 @@
             return jnp.concatenate([total[:, :top] + passed, total[:, top:]], 1)
         return jnp.concatenate([total[:, :top], total[:, top:] + passed], 1)
 
-    kept, other = systems(2, (0, 1))
-    up_far = systems(1, (1,), kept)
-    farthest = kept + other
-    up, down = around(farthest[:, :top], 1), around(farthest[:, top:], -1)
-    up_own = systems(1, (0,), farthest, up_far[0])
-    kept, other = systems(3, (0, 1), up_own[0])
-    last_kept, last_other = systems(0, (1,), kept)
-    up_far, up_own = joined(up_far, up[1:], 0), joined(up_own, up[:1], 0)
-    down_far, down_own = joined((kept[1:], other[1:]), down[1:], 1), joined((kept[:1], other[:1]), down[:1], 1)
-    up, down = around(up_far, 1), around(down_far, -1)
+    def across_z(value):
+        return over_ap(value, 1, 0, 0)
+
+    far2 = systems(2, (1,))
+    own2 = systems(2, (0,), far2[0])
+    first = across_z(far2[0] + far2[1])
+    far1 = systems(1, (1,), own2[0])
+    own1 = systems(1, (0,), far1[0])
+    up_across = across_z(far1[0] + far1[1])
+    far3 = systems(3, (1,), own1[0])
+    own3 = systems(3, (0,), far3[0])
+    down_across = across_z(far3[0] + far3[1])
+    passing = (own2[0] + own2[1]) + first
+    up, down = around(passing[:, :top], 1), around(passing[:, top:], -1)
+    far0 = systems(0, (1,), own3[0])
+    kept, other = systems(0, (0,), far0[0])
+    across = across_z(far0[0] + far0[1])
+    up_own = joined(own1, up, 0) + up_across
+    down_own = joined(own3, down, 1) + down_across
     own_up, own_down = around(up_own, 1), around(down_own, -1)
-    across = (last_kept + last_other) + (up + down)
-    kept, other = systems(0, (0,), across)
-    across = over_ap(across, 1, 0, 0)
     own_tone = solved([kept, other, own_up, own_down, across], regularizer)
     chips = lax.axis_size("ap") // CORES
     same = [[chip * CORES + c for chip in range(chips)] for c in range(CORES)]

time: 96.8 us -> 101 us (1.043)
  waiting for transfers between devices: 28.1 us -> 36.1 us
  blocking collectives: 13.7 us -> 10.6 us
  starting transfers between devices: 26.7 us -> 24.6 us
    ppermute x14 -> x17, waiting for transfers between devices: 18.9 us -> 26.9 us  [over_ap(): return lax.ppermute(value, 'ap', pairs)]
    all_to_all x1, blocking collectives: 13.7 us -> 10.6 us  [all_steps(): lax.all_to_all(jnp.broadcast_to(own_tone[None], (chips, *own_tone.shape))...]
    ppermute x14 -> x17, starting transfers between devices: 12.2 us -> 10.2 us  [over_ap(): return lax.ppermute(value, 'ap', pairs)]
    pallas_call x6 -> x8, Pallas kernels: 14.3 us -> 15.2 us  [tone_systems(): pl.pallas_call(functools.partial(tone_kernel, distance, planes), in_specs...]
  transfers between devices with their start and end apart: 22 -> 25, of which waited for: 9 -> 9; matrix products, arithmetic and copies ran while one was open for 4% -> 3% of each run, Pallas kernels for 13% -> 15%
where the time goes in v8:
time: 101 us; the launch traced here: 99.3 us
  waiting for transfers between devices  36.1 us (36%)
  starting transfers between devices  24.6 us (24%)
  Pallas kernels  23.1 us (23%)
  blocking collectives  10.6 us (10%)
  local copies, waits for them, and re-layouts  3.3 us (3%)
  other arithmetic  1.21 us (1%)
    ppermute x17, waiting for transfers between devices, over_ap(): return lax.ppermute(value, 'ap', pairs)  26.9 us
    pallas_call x8, Pallas kernels, tone_systems(): pl.pallas_call(functools.partial(tone_kernel, distance, planes), in_specs...  15.2 us
    ppermute x8, starting transfers between devices, over_sc(): return lax.ppermute(value, 'sc', pairs)  14.4 us
    all_to_all x1, blocking collectives, all_steps(): lax.all_to_all(jnp.broadcast_to(own_tone[None], (chips, *own_tone.shape))...  10.6 us
    ppermute x17, starting transfers between devices, over_ap(): return lax.ppermute(value, 'ap', pairs)  10.2 us
    ppermute x8, waiting for transfers between devices, over_sc(): return lax.ppermute(value, 'sc', pairs)  9.27 us
    pallas_call x1, Pallas kernels, solved(): pl.pallas_call(solve_kernel, in_specs=[vmem] * (len(systems) + 1), out_sp...  4.15 us
    pallas_call x2, Pallas kernels, prepared(): pl.pallas_call(functools.partial(prepare_kernel, slots, len(tables), tone...  2.77 us
  transfers between devices with their start and end apart: 25, of which 9 were waited for; matrix products, arithmetic and copies ran while one was open for 3% of the time, Pallas kernels for 15%

profile of v8, /device:TPU:0, one launch (start us, length us, event | category | flops | bytes accessed | tf_op | source)
XLA Modules:
  0.0 99.3 jit_solution(4597786486969208673)
XLA Ops:
  0.0 1.0 packed_tables.1.refs_0_
  1.0 4.1 %collective-permute-start.4 = (f32[16,32,128]{2,1,0:T(8,128)S(1)}, f32[16,32,128]{2,1,0:T(8,128)S(1)}, u32[]{:S(2)}, u32[]{:S(2)}) collective-permute-start(f32[16,32,128]{2,1,0:T(8,128)S(1)} %packed_tables.1.refs_0_), channel_id=1, source_target_pairs={{0,4},{1,5},{2,6},{3,7},{4,0},{5,1},{6,2},{7,3},{8,12},{9,13},{10,... | collective-permute-start | bytes 786440 | tf_op jit(solution)/shard_map/ppermute | solution.py:381
  5.0 1.5 %collective-permute-start = (f32[16,32,128]{2,1,0:T(8,128)S(1)}, f32[16,32,128]{2,1,0:T(8,128)S(1)}, u32[]{:S(2)}, u32[]{:S(2)}) collective-permute-start(f32[16,32,128]{2,1,0:T(8,128)S(1)} %packed_tables.1.refs_0_), channel_id=1, source_target_pairs={{0,1},{1,2},{2,3},{3,0},{4,5},{5,6},{6,7},{7,4},{8,9},{9,10},{10,1... | collective-permute-start | bytes 786440 | tf_op jit(solution)/shard_map/ppermute | solution.py:381
  6.5 1.7 %collective-permute-start.2 = (f32[16,32,128]{2,1,0:T(8,128)S(1)}, f32[16,32,128]{2,1,0:T(8,128)S(1)}, u32[]{:S(2)}, u32[]{:S(2)}) collective-permute-start(f32[16,32,128]{2,1,0:T(8,128)S(1)} %packed_tables.1.refs_0_), channel_id=1, source_target_pairs={{0,3},{1,0},{2,1},{3,2},{4,7},{5,4},{6,5},{7,6},{8,11},{9,8},{10,9... | collective-permute-start | bytes 786440 | tf_op jit(solution)/shard_map/ppermute | solution.py:381
  8.3 1.5 %reshape.10 = f32[16,2,14,512]{3,0,2,1:T(8,128)S(1)} reshape(f32[16,2,14,4,128]{4,3,0,2,1:T(4,128)} %bitcast.17) | data formatting | bytes 1835008 | tf_op jit(solution)/shard_map/reshape | solution.py:360
  9.8 0.1 fusion.1
  9.9 0.5 copy_bitcast_fusion
  10.5 3.6 %collective-permute-done.refs_2_ = f32[16,32,128]{2,1,0:T(8,128)S(1)} collective-permute-done((f32[16,32,128]{2,1,0:T(8,128)S(1)}, f32[16,32,128]{2,1,0:T(8,128)S(1)}, u32[]{:S(2)}, u32[]{:S(2)}) %collective-permute-start) | collective-permute-done | bytes 262176 | tf_op jit(solution)/shard_map/ppermute | solution.py:381
  14.0 0.3 collective-permute-start.1
  14.4 3.0 %collective-permute-start.3 = (f32[8,32,128]{2,1,0:T(8,128)S(1)}, f32[8,32,128]{2,1,0:T(8,128)S(1)}, u32[]{:S(2)}, u32[]{:S(2)}) collective-permute-start(f32[8,32,128]{2,1,0:T(8,128)S(1)} %slice.47), channel_id=1, source_target_pairs={{0,3},{1,0},{2,1},{3,2},{4,7},{5,4},{6,5},{7,6},{8,11},{9,8},{10,9... | collective-permute-start | bytes 393224 | tf_op jit(solution)/shard_map/ppermute | solution.py:381
  17.4 0.3 fusion
  17.7 0.0 copy-start
  17.8 0.1 collective-permute-start.5
  17.8 3.2 %collective-permute-start.6 = (f32[16,32,128]{2,1,0:T(8,128)S(1)}, f32[16,32,128]{2,1,0:T(8,128)S(1)}, u32[]{:S(2)}, u32[]{:S(2)}) collective-permute-start(f32[16,32,128]{2,1,0:T(8,128)S(1)} %collective-permute-done.4.refs_1_), channel_id=1, source_target_pairs={{0,3},{1,0},{2,1},{3,2},{4,7},{5,4},{6,5},{7,6},{8,11},{9,8},{10,9... | collective-permute-start | bytes 786440 | tf_op jit(solution)/shard_map/ppermute | solution.py:381
  21.1 0.4 collective-permute-start.7
  21.6 0.3 select_maximum_fusion.1
  21.8 0.1 pad_maximum_fusion.y_ref
  22.0 1.4 %prepared.2 = (f32[4,4,2,256,128]{4,3,2,1,0:T(8,128)S(1)}, f32[8,4,2,256,128]{4,3,2,1,0:T(8,128)S(1)}) custom-call(f32[16,32,128]{2,1,0:T(8,128)S(1)} %packed_tables.1.refs_0_, f32[16,32,128]{2,1,0:T(8,128)S(1)} %collective-permute-done.4.refs_1_, f32[16,32,128]{2,1,0:T(8,128)S(1)} %collective-permute-done.refs_2_, ...), custom_call_target="tpu_custom_call" | custom-call | tf_op jit(solution)/shard_map/prepared/pallas_call | solution.py:122
  23.4 2.5 %collective-permute-done.5.refs_1_ = f32[16,32,128]{2,1,0:T(8,128)S(1)} collective-permute-done((f32[16,32,128]{2,1,0:T(8,128)S(1)}, f32[16,32,128]{2,1,0:T(8,128)S(1)}, u32[]{:S(2)}, u32[]{:S(2)}) %collective-permute-start.5) | collective-permute-done | bytes 262176 | tf_op jit(solution)/shard_map/ppermute | solution.py:381
  25.9 0.0 collective-permute-done.6.refs_2_
  25.9 3.2 %collective-permute-done.7.refs_3_ = f32[16,32,128]{2,1,0:T(8,128)S(1)} collective-permute-done((f32[16,32,128]{2,1,0:T(8,128)S(1)}, f32[16,32,128]{2,1,0:T(8,128)S(1)}, u32[]{:S(2)}, u32[]{:S(2)}) %collective-permute-start.7) | collective-permute-done | bytes 262176 | tf_op jit(solution)/shard_map/ppermute | solution.py:381
  29.1 1.4 %prepared.3 = (f32[4,4,2,256,128]{4,3,2,1,0:T(8,128)S(1)}, f32[8,4,2,256,128]{4,3,2,1,0:T(8,128)S(1)}) custom-call(f32[16,32,128]{2,1,0:T(8,128)S(1)} %constant_dynamic-update-slice_fusion.refs_0_, f32[16,32,128]{2,1,0:T(8,128)S(1)} %collective-permute-done.5.refs_1_, ...), custom_call_target="tpu_custom_call", output_to_operand_aliasing={{0}: (5, {}), {1}: (6, {})} | custom-call | tf_op jit(solution)/shard_map/prepared/pallas_call | solution.py:122
  30.4 1.9 %tone_systems.8 = (f32[1,288,256]{2,1,0:T(8,128)S(1)}, f32[1,288,256]{2,1,0:T(8,128)S(1)}) custom-call(f32[16,32,1024]{2,1,0:T(8,128)S(1)} %pad_maximum_fusion.y_ref, f32[4,4,2,256,128]{4,3,2,1,0:T(8,128)S(1)} %get-tuple-element.34.lead, f32[8,4,2,256,128]{4,3,2,1,0:T(8,128)S(1)} %get-tuple-element.35.turn), custom_call_target="tpu_custom_call" | custom-call | tf_op jit(solution)/shard_map/tone_systems/pallas_call | solution.py:215
  32.4 0.0 collective-permute-start.11
  32.4 1.9 %tone_systems.9 = (f32[1,288,256]{2,1,0:T(8,128)S(1)}, f32[1,288,256]{2,1,0:T(8,128)S(1)}) custom-call(f32[16,32,1024]{2,1,0:T(8,128)S(1)} %pad_maximum_fusion.y_ref, f32[4,4,2,256,128]{4,3,2,1,0:T(8,128)S(1)} %get-tuple-element.34.lead, f32[8,4,2,256,128]{4,3,2,1,0:T(8,128)S(1)} %get-tuple-element.35.turn), custom_call_target="tpu_custom_call" | custom-call | tf_op jit(solution)/shard_map/tone_systems/pallas_call | solution.py:215
  34.3 0.5 collective-permute-start.10
  34.8 0.0 collective-permute-done.11
  34.8 1.3 %collective-permute-start.12 = (f32[1,288,256]{2,1,0:T(8,128)S(1)}, f32[1,288,256]{2,1,0:T(8,128)S(1)}, u32[]{:S(2)}, u32[]{:S(2)}) collective-permute-start(f32[1,288,256]{2,1,0:T(8,128)S(1)} %add.47), channel_id=1, source_target_pairs={{0,64},{8,72},{16,80},{24,88},{32,96},{40,104},{48,112},{56,120},{... | collective-permute-start | bytes 884744 | tf_op jit(solution)/shard_map/ppermute | solution.py:375
  36.1 1.9 %tone_systems.10 = (f32[1,288,256]{2,1,0:T(8,128)S(1)}, f32[1,288,256]{2,1,0:T(8,128)S(1)}) custom-call(f32[16,32,1024]{2,1,0:T(8,128)S(1)} %pad_maximum_fusion.y_ref, f32[4,4,2,256,128]{4,3,2,1,0:T(8,128)S(1)} %get-tuple-element.34.lead, f32[8,4,2,256,128]{4,3,2,1,0:T(8,128)S(1)} %get-tuple-element.35.turn), custom_call_target="tpu_custom_call" | custom-call | tf_op jit(solution)/shard_map/tone_systems/pallas_call | solution.py:215
  38.0 1.9 %tone_systems.11 = (f32[1,288,256]{2,1,0:T(8,128)S(1)}, f32[1,288,256]{2,1,0:T(8,128)S(1)}) custom-call(f32[16,32,1024]{2,1,0:T(8,128)S(1)} %pad_maximum_fusion.y_ref, f32[4,4,2,256,128]{4,3,2,1,0:T(8,128)S(1)} %get-tuple-element.34.lead, f32[8,4,2,256,128]{4,3,2,1,0:T(8,128)S(1)} %get-tuple-element.35.turn), custom_call_target="tpu_custom_call" | custom-call | tf_op jit(solution)/shard_map/tone_systems/pallas_call | solution.py:215
  39.9 1.9 %tone_systems.12 = (f32[1,288,256]{2,1,0:T(8,128)S(1)}, f32[1,288,256]{2,1,0:T(8,128)S(1)}) custom-call(f32[16,32,1024]{2,1,0:T(8,128)S(1)} %pad_maximum_fusion.y_ref, f32[4,4,2,256,128]{4,3,2,1,0:T(8,128)S(1)} %get-tuple-element.34.lead, f32[8,4,2,256,128]{4,3,2,1,0:T(8,128)S(1)} %get-tuple-element.35.turn), custom_call_target="tpu_custom_call" | custom-call | tf_op jit(solution)/shard_map/tone_systems/pallas_call | solution.py:215
  41.8 1.9 %tone_systems.13 = (f32[1,288,256]{2,1,0:T(8,128)S(1)}, f32[1,288,256]{2,1,0:T(8,128)S(1)}) custom-call(f32[16,32,1024]{2,1,0:T(8,128)S(1)} %pad_maximum_fusion.y_ref, f32[4,4,2,256,128]{4,3,2,1,0:T(8,128)S(1)} %get-tuple-element.34.lead, f32[8,4,2,256,128]{4,3,2,1,0:T(8,128)S(1)} %get-tuple-element.35.turn), custom_call_target="tpu_custom_call" | custom-call | tf_op jit(solution)/shard_map/tone_systems/pallas_call | solution.py:215
  43.7 1.9 %tone_systems.14 = (f32[1,288,256]{2,1,0:T(8,128)S(1)}, f32[1,288,256]{2,1,0:T(8,128)S(1)}) custom-call(f32[16,32,1024]{2,1,0:T(8,128)S(1)} %pad_maximum_fusion.y_ref, f32[4,4,2,256,128]{4,3,2,1,0:T(8,128)S(1)} %get-tuple-element.34.lead, f32[8,4,2,256,128]{4,3,2,1,0:T(8,128)S(1)} %get-tuple-element.35.turn), custom_call_target="tpu_custom_call" | custom-call | tf_op jit(solution)/shard_map/tone_systems/pallas_call | solution.py:215
  45.6 0.0 collective-permute-start.22
  45.6 0.5 collective-permute-start.17
  46.1 0.1 collective-permute-start.19
  46.2 0.0 collective-permute-done.10
  46.2 0.4 collective-permute-start.9
  46.6 0.0 collective-permute-done.12
  46.6 0.1 collective-permute-start.14
  46.7 0.1 add_add_fusion
  46.8 1.2 %collective-permute-done.19 = f32[1,288,256]{2,1,0:T(8,128)S(1)} collective-permute-done((f32[1,288,256]{2,1,0:T(8,128)S(1)}, f32[1,288,256]{2,1,0:T(8,128)S(1)}, u32[]{:S(2)}, u32[]{:S(2)}) %collective-permute-start.19) | collective-permute-done | bytes 294944 | tf_op jit(solution)/shard_map/ppermute | solution.py:375
  48.0 3.0 %collective-permute-start.18 = (f32[1,144,256]{2,1,0:T(8,128)S(1)}, f32[1,144,256]{2,1,0:T(8,128)S(1)}, u32[]{:S(2)}, u32[]{:S(2)}) collective-permute-start(f32[1,144,256]{2,1,0:T(8,128)S(1)} %get-tuple-element.67), channel_id=1, source_target_pairs={{0,48},{8,56},{16,0},{24,8},{32,16},{40,24},{48,32},{56,40},{64,11... | collective-permute-start | bytes 442376 | tf_op jit(solution)/shard_map/ppermute | solution.py:375
  51.1 1.1 %collective-permute-start.20 = (f32[1,288,256]{2,1,0:T(8,128)S(1)}, f32[1,288,256]{2,1,0:T(8,128)S(1)}, u32[]{:S(2)}, u32[]{:S(2)}) collective-permute-start(f32[1,288,256]{2,1,0:T(8,128)S(1)} %add.54), channel_id=1, source_target_pairs={{0,64},{8,72},{16,80},{24,88},{32,96},{40,104},{48,112},{56,120},{... | collective-permute-start | bytes 884744 | tf_op jit(solution)/shard_map/ppermute | solution.py:375
  52.2 1.9 %tone_systems.15 = (f32[1,288,256]{2,1,0:T(8,128)S(1)}, f32[1,288,256]{2,1,0:T(8,128)S(1)}) custom-call(f32[16,32,1024]{2,1,0:T(8,128)S(1)} %pad_maximum_fusion.y_ref, f32[4,4,2,256,128]{4,3,2,1,0:T(8,128)S(1)} %get-tuple-element.34.lead, f32[8,4,2,256,128]{4,3,2,1,0:T(8,128)S(1)} %get-tuple-element.35.turn), custom_call_target="tpu_custom_call" | custom-call | tf_op jit(solution)/shard_map/tone_systems/pallas_call | solution.py:215
  54.1 0.1 collective-permute-start.8
  54.2 0.0 collective-permute-done.14
  54.3 1.1 %collective-permute-start.23 = (f32[1,288,256]{2,1,0:T(8,128)S(1)}, f32[1,288,256]{2,1,0:T(8,128)S(1)}, u32[]{:S(2)}, u32[]{:S(2)}) collective-permute-start(f32[1,288,256]{2,1,0:T(8,128)S(1)} %add.56), channel_id=1, source_target_pairs={{0,64},{8,72},{16,80},{24,88},{32,96},{40,104},{48,112},{56,120},{... | collective-permute-start | bytes 884744 | tf_op jit(solution)/shard_map/ppermute | solution.py:375
  55.4 1.1 %collective-permute-start.15 = (f32[1,288,256]{2,1,0:T(8,128)S(1)}, f32[1,288,256]{2,1,0:T(8,128)S(1)}, u32[]{:S(2)}, u32[]{:S(2)}) collective-permute-start(f32[1,288,256]{2,1,0:T(8,128)S(1)} %add.50), channel_id=1, source_target_pairs={{0,64},{8,72},{16,80},{24,88},{32,96},{40,104},{48,112},{56,120},{... | collective-permute-start | bytes 884744 | tf_op jit(solution)/shard_map/ppermute | solution.py:375
  56.5 0.0 collective-permute-done.18
  56.5 0.1 collective-permute-start.13
  56.7 4.4 %collective-permute-done.20 = f32[1,288,256]{2,1,0:T(8,128)S(1)} collective-permute-done((f32[1,288,256]{2,1,0:T(8,128)S(1)}, f32[1,288,256]{2,1,0:T(8,128)S(1)}, u32[]{:S(2)}, u32[]{:S(2)}) %collective-permute-start.20) | collective-permute-done | bytes 294944 | tf_op jit(solution)/shard_map/ppermute | solution.py:375
  61.1 0.8 collective-permute-start.21
  61.9 1.6 %collective-permute-done.13 = f32[1,144,256]{2,1,0:T(8,128)S(1)} collective-permute-done((f32[1,144,256]{2,1,0:T(8,128)S(1)}, f32[1,144,256]{2,1,0:T(8,128)S(1)}, u32[]{:S(2)}, u32[]{:S(2)}) %collective-permute-start.13) | collective-permute-done | bytes 147488 | tf_op jit(solution)/shard_map/ppermute | solution.py:375
  63.5 9.0 %collective-permute-done.15 = f32[1,288,256]{2,1,0:T(8,128)S(1)} collective-permute-done((f32[1,288,256]{2,1,0:T(8,128)S(1)}, f32[1,288,256]{2,1,0:T(8,128)S(1)}, u32[]{:S(2)}, u32[]{:S(2)}) %collective-permute-start.15) | collective-permute-done | bytes 294944 | tf_op jit(solution)/shard_map/ppermute | solution.py:375
  72.6 0.1 collective-permute-start.16
  72.7 0.0 collective-permute-done.8.refs_1_
  72.7 0.0 collective-permute-done.23.refs_4_
  72.7 9.1 %collective-permute-done.16.refs_2_ = f32[1,288,256]{2,1,0:T(8,128)S(1)} collective-permute-done((f32[1,288,256]{2,1,0:T(8,128)S(1)}, f32[1,288,256]{2,1,0:T(8,128)S(1)}, u32[]{:S(2)}, u32[]{:S(2)}) %collective-permute-start.16) | collective-permute-done | bytes 294944 | tf_op jit(solution)/shard_map/ppermute | solution.py:375
  81.8 4.2 %solved.1 = f32[32,256]{1,0:T(8,128)S(1)} custom-call(f32[1,288,256]{2,1,0:T(8,128)S(1)} %get-tuple-element.50.refs_0_, f32[1,288,256]{2,1,0:T(8,128)S(1)} %collective-permute-done.8.refs_1_, f32[1,288,256]{2,1,0:T(8,128)S(1)} %collective-permute-done.16.refs_2_, f32[1,288,256]{2,1,0:T(8,128)S(1)} %collective-permute-done.21.refs_3_, ...), custom_call_target="tpu_custom_call" | custom-call | tf_op jit(solution)/shard_map/solved/pallas_call | solution.py:339
  86.0 10.6 %all_to_all.5 = f32[8,32,256]{2,1,0:T(8,128)S(1)} all-to-all(f32[8,32,256]{2,1,0:T(8,128)S(1)} %broadcast_in_dim.2), channel_id=1, replica_groups={{0,16,32,48,64,80,96,112},{8,24,40,56,72,88,104,120},{1,17,33,49,65,81,..., dimensions={0} | all-to-all | bytes 524288 | tf_op jit(solution)/shard_map/all_to_all | solution.py:471
  96.6 0.0 collective-permute-start.24
  96.6 1.5 %collective-permute-done.24 = f32[8,32,256]{2,1,0:T(8,128)S(1)} collective-permute-done((f32[8,32,256]{2,1,0:T(8,128)S(1)}, f32[8,32,256]{2,1,0:T(8,128)S(1)}, u32[]{:S(2)}, u32[]{:S(2)}) %collective-permute-start.24) | collective-permute-done | bytes 262176 | tf_op jit(solution)/shard_map/ppermute | solution.py:375
  98.2 1.0 %copy.24 = f32[16,2,14,256]{3,0,2,1:T(8,128)} copy(f32[16,2,14,256]{3,2,1,0:T(8,128)S(1)} %bitcast.16) | data formatting | bytes 917504
  (30 shorter events, 0.6 us)
Async XLA Ops:
  1.0 16.8 %collective-permute-start.4 = (f32[16,32,128]{2,1,0:T(8,128)S(1)}, f32[16,32,128]{2,1,0:T(8,128)S(1)}, u32[]{:S(2)}, u32[]{:S(2)}) collective-permute-start(f32[16,32,128]{2,1,0:T(8,128)S(1)} %packed_tables.1.refs_0_), channel_id=1, source_target_pairs={{0,4},{1,5},{2,6},{3,7},{4,0},{5,1},{6,2},{7,3},{8,12},{9,13},{10,... | collective-permute-start | bytes 786440 | tf_op jit(solution)/shard_map/ppermute | solution.py:381
  5.0 9.0 %collective-permute-start = (f32[16,32,128]{2,1,0:T(8,128)S(1)}, f32[16,32,128]{2,1,0:T(8,128)S(1)}, u32[]{:S(2)}, u32[]{:S(2)}) collective-permute-start(f32[16,32,128]{2,1,0:T(8,128)S(1)} %packed_tables.1.refs_0_), channel_id=1, source_target_pairs={{0,1},{1,2},{2,3},{3,0},{4,5},{5,6},{6,7},{7,4},{8,9},{9,10},{10,1... | collective-permute-start | bytes 786440 | tf_op jit(solution)/shard_map/ppermute | solution.py:381
  6.5 7.9 %collective-permute-start.2 = (f32[16,32,128]{2,1,0:T(8,128)S(1)}, f32[16,32,128]{2,1,0:T(8,128)S(1)}, u32[]{:S(2)}, u32[]{:S(2)}) collective-permute-start(f32[16,32,128]{2,1,0:T(8,128)S(1)} %packed_tables.1.refs_0_), channel_id=1, source_target_pairs={{0,3},{1,0},{2,1},{3,2},{4,7},{5,4},{6,5},{7,6},{8,11},{9,8},{10,9... | collective-permute-start | bytes 786440 | tf_op jit(solution)/shard_map/ppermute | solution.py:381
  14.0 7.0 %collective-permute-start.1 = (f32[8,32,128]{2,1,0:T(8,128)S(1)}, f32[8,32,128]{2,1,0:T(8,128)S(1)}, u32[]{:S(2)}, u32[]{:S(2)}) collective-permute-start(f32[8,32,128]{2,1,0:T(8,128)S(1)} %slice.46), channel_id=1, source_target_pairs={{0,1},{1,2},{2,3},{3,0},{4,5},{5,6},{6,7},{7,4},{8,9},{9,10},{10,1... | collective-permute-start | bytes 393224 | tf_op jit(solution)/shard_map/ppermute | solution.py:381
  14.4 6.7 %collective-permute-start.3 = (f32[8,32,128]{2,1,0:T(8,128)S(1)}, f32[8,32,128]{2,1,0:T(8,128)S(1)}, u32[]{:S(2)}, u32[]{:S(2)}) collective-permute-start(f32[8,32,128]{2,1,0:T(8,128)S(1)} %slice.47), channel_id=1, source_target_pairs={{0,3},{1,0},{2,1},{3,2},{4,7},{5,4},{6,5},{7,6},{8,11},{9,8},{10,9... | collective-permute-start | bytes 393224 | tf_op jit(solution)/shard_map/ppermute | solution.py:381
  17.7 4.2 %copy-start = (s32[256,128]{1,0:T(8,128)S(1)}, s32[256,128]{1,0:T(8,128)}, u32[]{:S(2)}) copy-start(s32[256,128]{1,0:T(8,128)} %refs_4_.3) | copy-start | bytes 393220
  17.8 8.1 %collective-permute-start.5 = (f32[16,32,128]{2,1,0:T(8,128)S(1)}, f32[16,32,128]{2,1,0:T(8,128)S(1)}, u32[]{:S(2)}, u32[]{:S(2)}) collective-permute-start(f32[16,32,128]{2,1,0:T(8,128)S(1)} %collective-permute-done.4.refs_1_), channel_id=1, source_target_pairs={{0,1},{1,2},{2,3},{3,0},{4,5},{5,6},{6,7},{7,4},{8,9},{9,10},{10,1... | collective-permute-start | bytes 786440 | tf_op jit(solution)/shard_map/ppermute | solution.py:381
  17.8 8.1 %collective-permute-start.6 = (f32[16,32,128]{2,1,0:T(8,128)S(1)}, f32[16,32,128]{2,1,0:T(8,128)S(1)}, u32[]{:S(2)}, u32[]{:S(2)}) collective-permute-start(f32[16,32,128]{2,1,0:T(8,128)S(1)} %collective-permute-done.4.refs_1_), channel_id=1, source_target_pairs={{0,3},{1,0},{2,1},{3,2},{4,7},{5,4},{6,5},{7,6},{8,11},{9,8},{10,9... | collective-permute-start | bytes 786440 | tf_op jit(solution)/shard_map/ppermute | solution.py:381
  21.1 8.0 %collective-permute-start.7 = (f32[16,32,128]{2,1,0:T(8,128)S(1)}, f32[16,32,128]{2,1,0:T(8,128)S(1)}, u32[]{:S(2)}, u32[]{:S(2)}) collective-permute-start(f32[16,32,128]{2,1,0:T(8,128)S(1)} %constant_dynamic-update-slice_fusion.refs_0_), channel_id=1, source_target_pairs={{0,4},{1,5},{2,6},{3,7},{4,0},{5,1},{6,2},{7,3},{8,12},{9,13},{10,... | collective-permute-start | bytes 786440 | tf_op jit(solution)/shard_map/ppermute | solution.py:381
  32.4 2.4 %collective-permute-start.11 = (f32[1,288,256]{2,1,0:T(8,128)S(1)}, f32[1,288,256]{2,1,0:T(8,128)S(1)}, u32[]{:S(2)}, u32[]{:S(2)}) collective-permute-start(f32[1,288,256]{2,1,0:T(8,128)S(1)} %get-tuple-element.54), channel_id=1, source_target_pairs={{0,8},{8,0},{16,24},{24,16},{32,40},{40,32},{48,56},{56,48},{64,72... | collective-permute-start | bytes 884744 | tf_op jit(solution)/shard_map/ppermute | solution.py:375
  34.3 11.9 %collective-permute-start.10 = (f32[1,288,256]{2,1,0:T(8,128)S(1)}, f32[1,288,256]{2,1,0:T(8,128)S(1)}, u32[]{:S(2)}, u32[]{:S(2)}) collective-permute-start(f32[1,288,256]{2,1,0:T(8,128)S(1)} %get-tuple-element.53), channel_id=1, source_target_pairs={{0,8},{8,0},{16,24},{24,16},{32,40},{40,32},{48,56},{56,48},{64,72... | collective-permute-start | bytes 884744 | tf_op jit(solution)/shard_map/ppermute | solution.py:375
  34.8 11.8 %collective-permute-start.12 = (f32[1,288,256]{2,1,0:T(8,128)S(1)}, f32[1,288,256]{2,1,0:T(8,128)S(1)}, u32[]{:S(2)}, u32[]{:S(2)}) collective-permute-start(f32[1,288,256]{2,1,0:T(8,128)S(1)} %add.47), channel_id=1, source_target_pairs={{0,64},{8,72},{16,80},{24,88},{32,96},{40,104},{48,112},{56,120},{... | collective-permute-start | bytes 884744 | tf_op jit(solution)/shard_map/ppermute | solution.py:375
  45.6 5.5 %collective-permute-start.22 = (f32[1,288,256]{2,1,0:T(8,128)S(1)}, f32[1,288,256]{2,1,0:T(8,128)S(1)}, u32[]{:S(2)}, u32[]{:S(2)}) collective-permute-start(f32[1,288,256]{2,1,0:T(8,128)S(1)} %get-tuple-element.58), channel_id=1, source_target_pairs={{0,8},{8,0},{16,24},{24,16},{32,40},{40,32},{48,56},{56,48},{64,72... | collective-permute-start | bytes 884744 | tf_op jit(solution)/shard_map/ppermute | solution.py:375
  45.6 8.5 %collective-permute-start.17 = (f32[1,288,256]{2,1,0:T(8,128)S(1)}, f32[1,288,256]{2,1,0:T(8,128)S(1)}, u32[]{:S(2)}, u32[]{:S(2)}) collective-permute-start(f32[1,288,256]{2,1,0:T(8,128)S(1)} %get-tuple-element.56), channel_id=1, source_target_pairs={{0,8},{8,0},{16,24},{24,16},{32,40},{40,32},{48,56},{56,48},{64,72... | collective-permute-start | bytes 884744 | tf_op jit(solution)/shard_map/ppermute | solution.py:375
  46.1 1.9 %collective-permute-start.19 = (f32[1,288,256]{2,1,0:T(8,128)S(1)}, f32[1,288,256]{2,1,0:T(8,128)S(1)}, u32[]{:S(2)}, u32[]{:S(2)}) collective-permute-start(f32[1,288,256]{2,1,0:T(8,128)S(1)} %get-tuple-element.57), channel_id=1, source_target_pairs={{0,8},{8,0},{16,24},{24,16},{32,40},{40,32},{48,56},{56,48},{64,72... | collective-permute-start | bytes 884744 | tf_op jit(solution)/shard_map/ppermute | solution.py:375
  46.2 9.2 %collective-permute-start.9 = (f32[1,288,256]{2,1,0:T(8,128)S(1)}, f32[1,288,256]{2,1,0:T(8,128)S(1)}, u32[]{:S(2)}, u32[]{:S(2)}) collective-permute-start(f32[1,288,256]{2,1,0:T(8,128)S(1)} %get-tuple-element.52), channel_id=1, source_target_pairs={{0,8},{8,0},{16,24},{24,16},{32,40},{40,32},{48,56},{56,48},{64,72... | collective-permute-start | bytes 884744 | tf_op jit(solution)/shard_map/ppermute | solution.py:375
  46.6 7.6 %collective-permute-start.14 = (f32[1,288,256]{2,1,0:T(8,128)S(1)}, f32[1,288,256]{2,1,0:T(8,128)S(1)}, u32[]{:S(2)}, u32[]{:S(2)}) collective-permute-start(f32[1,288,256]{2,1,0:T(8,128)S(1)} %get-tuple-element.55), channel_id=1, source_target_pairs={{0,8},{8,0},{16,24},{24,16},{32,40},{40,32},{48,56},{56,48},{64,72... | collective-permute-start | bytes 884744 | tf_op jit(solution)/shard_map/ppermute | solution.py:375
  48.0 8.5 %collective-permute-start.18 = (f32[1,144,256]{2,1,0:T(8,128)S(1)}, f32[1,144,256]{2,1,0:T(8,128)S(1)}, u32[]{:S(2)}, u32[]{:S(2)}) collective-permute-start(f32[1,144,256]{2,1,0:T(8,128)S(1)} %get-tuple-element.67), channel_id=1, source_target_pairs={{0,48},{8,56},{16,0},{24,8},{32,16},{40,24},{48,32},{56,40},{64,11... | collective-permute-start | bytes 442376 | tf_op jit(solution)/shard_map/ppermute | solution.py:375
  51.1 10.0 %collective-permute-start.20 = (f32[1,288,256]{2,1,0:T(8,128)S(1)}, f32[1,288,256]{2,1,0:T(8,128)S(1)}, u32[]{:S(2)}, u32[]{:S(2)}) collective-permute-start(f32[1,288,256]{2,1,0:T(8,128)S(1)} %add.54), channel_id=1, source_target_pairs={{0,64},{8,72},{16,80},{24,88},{32,96},{40,104},{48,112},{56,120},{... | collective-permute-start | bytes 884744 | tf_op jit(solution)/shard_map/ppermute | solution.py:375
  54.0 27.8 %copy-start.1 = (f32[256]{0:T(256)S(1)}, f32[256]{0:T(256)}, u32[]{:S(2)}) copy-start(f32[256]{0:T(256)} %param.13) | copy-start | bytes 3076
  54.1 18.6 %collective-permute-start.8 = (f32[1,288,256]{2,1,0:T(8,128)S(1)}, f32[1,288,256]{2,1,0:T(8,128)S(1)}, u32[]{:S(2)}, u32[]{:S(2)}) collective-permute-start(f32[1,288,256]{2,1,0:T(8,128)S(1)} %get-tuple-element.51), channel_id=1, source_target_pairs={{0,8},{8,0},{16,24},{24,16},{32,40},{40,32},{48,56},{56,48},{64,72... | collective-permute-start | bytes 884744 | tf_op jit(solution)/shard_map/ppermute | solution.py:375
  54.3 18.5 %collective-permute-start.23 = (f32[1,288,256]{2,1,0:T(8,128)S(1)}, f32[1,288,256]{2,1,0:T(8,128)S(1)}, u32[]{:S(2)}, u32[]{:S(2)}) collective-permute-start(f32[1,288,256]{2,1,0:T(8,128)S(1)} %add.56), channel_id=1, source_target_pairs={{0,64},{8,72},{16,80},{24,88},{32,96},{40,104},{48,112},{56,120},{... | collective-permute-start | bytes 884744 | tf_op jit(solution)/shard_map/ppermute | solution.py:375
  55.4 17.2 %collective-permute-start.15 = (f32[1,288,256]{2,1,0:T(8,128)S(1)}, f32[1,288,256]{2,1,0:T(8,128)S(1)}, u32[]{:S(2)}, u32[]{:S(2)}) collective-permute-start(f32[1,288,256]{2,1,0:T(8,128)S(1)} %add.50), channel_id=1, source_target_pairs={{0,64},{8,72},{16,80},{24,88},{32,96},{40,104},{48,112},{56,120},{... | collective-permute-start | bytes 884744 | tf_op jit(solution)/shard_map/ppermute | solution.py:375
  56.5 7.0 %collective-permute-start.13 = (f32[1,144,256]{2,1,0:T(8,128)S(1)}, f32[1,144,256]{2,1,0:T(8,128)S(1)}, u32[]{:S(2)}, u32[]{:S(2)}) collective-permute-start(f32[1,144,256]{2,1,0:T(8,128)S(1)} %get-tuple-element.68), channel_id=1, source_target_pairs={{0,16},{8,24},{16,32},{24,40},{32,48},{40,56},{48,0},{56,8},{64,80... | collective-permute-start | bytes 442376 | tf_op jit(solution)/shard_map/ppermute | solution.py:375
  61.1 11.6 %collective-permute-start.21 = (f32[1,288,256]{2,1,0:T(8,128)S(1)}, f32[1,288,256]{2,1,0:T(8,128)S(1)}, u32[]{:S(2)}, u32[]{:S(2)}) collective-permute-start(f32[1,288,256]{2,1,0:T(8,128)S(1)} %maximum_add_fusion.1), channel_id=1, source_target_pairs={{0,48},{8,56},{16,0},{24,8},{32,16},{40,24},{48,32},{56,40},{64,11... | collective-permute-start | bytes 884744 | tf_op jit(solution)/shard_map/ppermute | solution.py:375
  72.6 9.2 %collective-permute-start.16 = (f32[1,288,256]{2,1,0:T(8,128)S(1)}, f32[1,288,256]{2,1,0:T(8,128)S(1)}, u32[]{:S(2)}, u32[]{:S(2)}) collective-permute-start(f32[1,288,256]{2,1,0:T(8,128)S(1)} %maximum_add_fusion), channel_id=1, source_target_pairs={{0,16},{8,24},{16,32},{24,40},{32,48},{40,56},{48,0},{56,8},{64,80... | collective-permute-start | bytes 884744 | tf_op jit(solution)/shard_map/ppermute | solution.py:375
  96.6 1.5 %collective-permute-start.24 = (f32[8,32,256]{2,1,0:T(8,128)S(1)}, f32[8,32,256]{2,1,0:T(8,128)S(1)}, u32[]{:S(2)}, u32[]{:S(2)}) collective-permute-start(f32[8,32,256]{2,1,0:T(8,128)S(1)} %all_to_all.5), channel_id=1, source_target_pairs={{0,8},{8,0},{16,24},{24,16},{32,40},{40,32},{48,56},{56,48},{64,72... | collective-permute-start | bytes 786440 | tf_op jit(solution)/shard_map/ppermute | solution.py:375

commit v9 on v8

--- a/solution.py
+++ b/solution.py
@@ -23,6 +23,7 @@
 ROWS = 16
 HALF = 16
 SOLVE_STEPS = 40
+STEPS_A_CHECK = 5
 TOLERANCE = 1e-6
 
 
@@ -282,7 +283,7 @@
 
     def advance(state):
         done, _, earlier, alpha = state
-        for _ in range(2):
+        for _ in range(STEPS_A_CHECK):
             r = r_ref[...]
             applied_r = applied(r)
             rr = together(r * r)
@@ -297,7 +298,7 @@
             r_ref[...] = r - alpha * q
             earlier = rr
         r = r_ref[...]
-        return done + 2, jnp.max(jnp.where(together(r * r) <= goal, 0, 1)), earlier, alpha
+        return done + STEPS_A_CHECK, jnp.max(jnp.where(together(r * r) <= goal, 0, 1)), earlier, alpha
 
     def unfinished(state):
         return (state[1] > 0) & (state[0] < SOLVE_STEPS)

time: 101 us -> 101 us (level)
  Pallas kernels: 23.1 us -> 24.4 us
    pallas_call x1, Pallas kernels: 4.15 us -> 5.5 us  [solved(): pl.pallas_call(solve_kernel, in_specs=[vmem] * (len(systems) + 1), out_sp...]
where the time goes in v9:
time: 101 us; the launch traced here: 99.7 us
  waiting for transfers between devices  36.1 us (36%)
  starting transfers between devices  24.6 us (24%)
  Pallas kernels  24.4 us (24%)
  blocking collectives  9.7 us (10%)
  local copies, waits for them, and re-layouts  3.3 us (3%)
  other arithmetic  1.21 us (1%)
    ppermute x17, waiting for transfers between devices, over_ap(): return lax.ppermute(value, 'ap', pairs)  26.9 us
    pallas_call x8, Pallas kernels, tone_systems(): pl.pallas_call(functools.partial(tone_kernel, distance, planes), in_specs...  15.2 us
    ppermute x8, starting transfers between devices, over_sc(): return lax.ppermute(value, 'sc', pairs)  14.4 us
    ppermute x17, starting transfers between devices, over_ap(): return lax.ppermute(value, 'ap', pairs)  10.2 us
    all_to_all x1, blocking collectives, all_steps(): lax.all_to_all(jnp.broadcast_to(own_tone[None], (chips, *own_tone.shape))...  9.7 us
    ppermute x8, waiting for transfers between devices, over_sc(): return lax.ppermute(value, 'sc', pairs)  9.27 us
    pallas_call x1, Pallas kernels, solved(): pl.pallas_call(solve_kernel, in_specs=[vmem] * (len(systems) + 1), out_sp...  5.5 us
    pallas_call x2, Pallas kernels, prepared(): pl.pallas_call(functools.partial(prepare_kernel, slots, len(tables), tone...  2.77 us
  transfers between devices with their start and end apart: 25, of which 9 were waited for; matrix products, arithmetic and copies ran while one was open for 3% of the time, Pallas kernels for 15%

profile of v9, /device:TPU:0, one launch (start us, length us, event | category | flops | bytes accessed | tf_op | source)
XLA Modules:
  0.0 99.7 jit_solution(1658848204325989464)
XLA Ops:
  0.0 1.0 packed_tables.1.refs_0_
  1.0 4.1 %collective-permute-start.4 = (f32[16,32,128]{2,1,0:T(8,128)S(1)}, f32[16,32,128]{2,1,0:T(8,128)S(1)}, u32[]{:S(2)}, u32[]{:S(2)}) collective-permute-start(f32[16,32,128]{2,1,0:T(8,128)S(1)} %packed_tables.1.refs_0_), channel_id=1, source_target_pairs={{0,4},{1,5},{2,6},{3,7},{4,0},{5,1},{6,2},{7,3},{8,12},{9,13},{10,... | collective-permute-start | bytes 786440 | tf_op jit(solution)/shard_map/ppermute | solution.py:382
  5.0 1.5 %collective-permute-start = (f32[16,32,128]{2,1,0:T(8,128)S(1)}, f32[16,32,128]{2,1,0:T(8,128)S(1)}, u32[]{:S(2)}, u32[]{:S(2)}) collective-permute-start(f32[16,32,128]{2,1,0:T(8,128)S(1)} %packed_tables.1.refs_0_), channel_id=1, source_target_pairs={{0,1},{1,2},{2,3},{3,0},{4,5},{5,6},{6,7},{7,4},{8,9},{9,10},{10,1... | collective-permute-start | bytes 786440 | tf_op jit(solution)/shard_map/ppermute | solution.py:382
  6.5 1.7 %collective-permute-start.2 = (f32[16,32,128]{2,1,0:T(8,128)S(1)}, f32[16,32,128]{2,1,0:T(8,128)S(1)}, u32[]{:S(2)}, u32[]{:S(2)}) collective-permute-start(f32[16,32,128]{2,1,0:T(8,128)S(1)} %packed_tables.1.refs_0_), channel_id=1, source_target_pairs={{0,3},{1,0},{2,1},{3,2},{4,7},{5,4},{6,5},{7,6},{8,11},{9,8},{10,9... | collective-permute-start | bytes 786440 | tf_op jit(solution)/shard_map/ppermute | solution.py:382
  8.3 1.5 %reshape.10 = f32[16,2,14,512]{3,0,2,1:T(8,128)S(1)} reshape(f32[16,2,14,4,128]{4,3,0,2,1:T(4,128)} %bitcast.17) | data formatting | bytes 1835008 | tf_op jit(solution)/shard_map/reshape | solution.py:361
  9.8 0.1 fusion.1
  9.9 0.5 copy_bitcast_fusion
  10.5 3.6 %collective-permute-done.refs_2_ = f32[16,32,128]{2,1,0:T(8,128)S(1)} collective-permute-done((f32[16,32,128]{2,1,0:T(8,128)S(1)}, f32[16,32,128]{2,1,0:T(8,128)S(1)}, u32[]{:S(2)}, u32[]{:S(2)}) %collective-permute-start) | collective-permute-done | bytes 262176 | tf_op jit(solution)/shard_map/ppermute | solution.py:382
  14.0 0.3 collective-permute-start.1
  14.4 3.0 %collective-permute-start.3 = (f32[8,32,128]{2,1,0:T(8,128)S(1)}, f32[8,32,128]{2,1,0:T(8,128)S(1)}, u32[]{:S(2)}, u32[]{:S(2)}) collective-permute-start(f32[8,32,128]{2,1,0:T(8,128)S(1)} %slice.47), channel_id=1, source_target_pairs={{0,3},{1,0},{2,1},{3,2},{4,7},{5,4},{6,5},{7,6},{8,11},{9,8},{10,9... | collective-permute-start | bytes 393224 | tf_op jit(solution)/shard_map/ppermute | solution.py:382
  17.4 0.3 fusion
  17.7 0.0 copy-start
  17.8 0.1 collective-permute-start.5
  17.8 3.2 %collective-permute-start.6 = (f32[16,32,128]{2,1,0:T(8,128)S(1)}, f32[16,32,128]{2,1,0:T(8,128)S(1)}, u32[]{:S(2)}, u32[]{:S(2)}) collective-permute-start(f32[16,32,128]{2,1,0:T(8,128)S(1)} %collective-permute-done.4.refs_1_), channel_id=1, source_target_pairs={{0,3},{1,0},{2,1},{3,2},{4,7},{5,4},{6,5},{7,6},{8,11},{9,8},{10,9... | collective-permute-start | bytes 786440 | tf_op jit(solution)/shard_map/ppermute | solution.py:382
  21.1 0.4 collective-permute-start.7
  21.6 0.3 select_maximum_fusion.1
  21.8 0.1 pad_maximum_fusion.y_ref
  22.0 1.4 %prepared.2 = (f32[4,4,2,256,128]{4,3,2,1,0:T(8,128)S(1)}, f32[8,4,2,256,128]{4,3,2,1,0:T(8,128)S(1)}) custom-call(f32[16,32,128]{2,1,0:T(8,128)S(1)} %packed_tables.1.refs_0_, f32[16,32,128]{2,1,0:T(8,128)S(1)} %collective-permute-done.4.refs_1_, f32[16,32,128]{2,1,0:T(8,128)S(1)} %collective-permute-done.refs_2_, ...), custom_call_target="tpu_custom_call" | custom-call | tf_op jit(solution)/shard_map/prepared/pallas_call | solution.py:123
  23.4 2.5 %collective-permute-done.5.refs_1_ = f32[16,32,128]{2,1,0:T(8,128)S(1)} collective-permute-done((f32[16,32,128]{2,1,0:T(8,128)S(1)}, f32[16,32,128]{2,1,0:T(8,128)S(1)}, u32[]{:S(2)}, u32[]{:S(2)}) %collective-permute-start.5) | collective-permute-done | bytes 262176 | tf_op jit(solution)/shard_map/ppermute | solution.py:382
  25.9 0.0 collective-permute-done.6.refs_2_
  25.9 3.2 %collective-permute-done.7.refs_3_ = f32[16,32,128]{2,1,0:T(8,128)S(1)} collective-permute-done((f32[16,32,128]{2,1,0:T(8,128)S(1)}, f32[16,32,128]{2,1,0:T(8,128)S(1)}, u32[]{:S(2)}, u32[]{:S(2)}) %collective-permute-start.7) | collective-permute-done | bytes 262176 | tf_op jit(solution)/shard_map/ppermute | solution.py:382
  29.1 1.4 %prepared.3 = (f32[4,4,2,256,128]{4,3,2,1,0:T(8,128)S(1)}, f32[8,4,2,256,128]{4,3,2,1,0:T(8,128)S(1)}) custom-call(f32[16,32,128]{2,1,0:T(8,128)S(1)} %constant_dynamic-update-slice_fusion.refs_0_, f32[16,32,128]{2,1,0:T(8,128)S(1)} %collective-permute-done.5.refs_1_, ...), custom_call_target="tpu_custom_call", output_to_operand_aliasing={{0}: (5, {}), {1}: (6, {})} | custom-call | tf_op jit(solution)/shard_map/prepared/pallas_call | solution.py:123
  30.4 1.9 %tone_systems.8 = (f32[1,288,256]{2,1,0:T(8,128)S(1)}, f32[1,288,256]{2,1,0:T(8,128)S(1)}) custom-call(f32[16,32,1024]{2,1,0:T(8,128)S(1)} %pad_maximum_fusion.y_ref, f32[4,4,2,256,128]{4,3,2,1,0:T(8,128)S(1)} %get-tuple-element.34.lead, f32[8,4,2,256,128]{4,3,2,1,0:T(8,128)S(1)} %get-tuple-element.35.turn), custom_call_target="tpu_custom_call" | custom-call | tf_op jit(solution)/shard_map/tone_systems/pallas_call | solution.py:216
  32.4 0.0 collective-permute-start.11
  32.4 1.9 %tone_systems.9 = (f32[1,288,256]{2,1,0:T(8,128)S(1)}, f32[1,288,256]{2,1,0:T(8,128)S(1)}) custom-call(f32[16,32,1024]{2,1,0:T(8,128)S(1)} %pad_maximum_fusion.y_ref, f32[4,4,2,256,128]{4,3,2,1,0:T(8,128)S(1)} %get-tuple-element.34.lead, f32[8,4,2,256,128]{4,3,2,1,0:T(8,128)S(1)} %get-tuple-element.35.turn), custom_call_target="tpu_custom_call" | custom-call | tf_op jit(solution)/shard_map/tone_systems/pallas_call | solution.py:216
  34.3 0.5 collective-permute-start.10
  34.8 0.0 collective-permute-done.11
  34.8 1.3 %collective-permute-start.12 = (f32[1,288,256]{2,1,0:T(8,128)S(1)}, f32[1,288,256]{2,1,0:T(8,128)S(1)}, u32[]{:S(2)}, u32[]{:S(2)}) collective-permute-start(f32[1,288,256]{2,1,0:T(8,128)S(1)} %add.47), channel_id=1, source_target_pairs={{0,64},{8,72},{16,80},{24,88},{32,96},{40,104},{48,112},{56,120},{... | collective-permute-start | bytes 884744 | tf_op jit(solution)/shard_map/ppermute | solution.py:376
  36.1 1.9 %tone_systems.10 = (f32[1,288,256]{2,1,0:T(8,128)S(1)}, f32[1,288,256]{2,1,0:T(8,128)S(1)}) custom-call(f32[16,32,1024]{2,1,0:T(8,128)S(1)} %pad_maximum_fusion.y_ref, f32[4,4,2,256,128]{4,3,2,1,0:T(8,128)S(1)} %get-tuple-element.34.lead, f32[8,4,2,256,128]{4,3,2,1,0:T(8,128)S(1)} %get-tuple-element.35.turn), custom_call_target="tpu_custom_call" | custom-call | tf_op jit(solution)/shard_map/tone_systems/pallas_call | solution.py:216
  38.0 1.9 %tone_systems.11 = (f32[1,288,256]{2,1,0:T(8,128)S(1)}, f32[1,288,256]{2,1,0:T(8,128)S(1)}) custom-call(f32[16,32,1024]{2,1,0:T(8,128)S(1)} %pad_maximum_fusion.y_ref, f32[4,4,2,256,128]{4,3,2,1,0:T(8,128)S(1)} %get-tuple-element.34.lead, f32[8,4,2,256,128]{4,3,2,1,0:T(8,128)S(1)} %get-tuple-element.35.turn), custom_call_target="tpu_custom_call" | custom-call | tf_op jit(solution)/shard_map/tone_systems/pallas_call | solution.py:216
  39.9 1.9 %tone_systems.12 = (f32[1,288,256]{2,1,0:T(8,128)S(1)}, f32[1,288,256]{2,1,0:T(8,128)S(1)}) custom-call(f32[16,32,1024]{2,1,0:T(8,128)S(1)} %pad_maximum_fusion.y_ref, f32[4,4,2,256,128]{4,3,2,1,0:T(8,128)S(1)} %get-tuple-element.34.lead, f32[8,4,2,256,128]{4,3,2,1,0:T(8,128)S(1)} %get-tuple-element.35.turn), custom_call_target="tpu_custom_call" | custom-call | tf_op jit(solution)/shard_map/tone_systems/pallas_call | solution.py:216
  41.8 1.9 %tone_systems.13 = (f32[1,288,256]{2,1,0:T(8,128)S(1)}, f32[1,288,256]{2,1,0:T(8,128)S(1)}) custom-call(f32[16,32,1024]{2,1,0:T(8,128)S(1)} %pad_maximum_fusion.y_ref, f32[4,4,2,256,128]{4,3,2,1,0:T(8,128)S(1)} %get-tuple-element.34.lead, f32[8,4,2,256,128]{4,3,2,1,0:T(8,128)S(1)} %get-tuple-element.35.turn), custom_call_target="tpu_custom_call" | custom-call | tf_op jit(solution)/shard_map/tone_systems/pallas_call | solution.py:216
  43.7 1.9 %tone_systems.14 = (f32[1,288,256]{2,1,0:T(8,128)S(1)}, f32[1,288,256]{2,1,0:T(8,128)S(1)}) custom-call(f32[16,32,1024]{2,1,0:T(8,128)S(1)} %pad_maximum_fusion.y_ref, f32[4,4,2,256,128]{4,3,2,1,0:T(8,128)S(1)} %get-tuple-element.34.lead, f32[8,4,2,256,128]{4,3,2,1,0:T(8,128)S(1)} %get-tuple-element.35.turn), custom_call_target="tpu_custom_call" | custom-call | tf_op jit(solution)/shard_map/tone_systems/pallas_call | solution.py:216
  45.6 0.0 collective-permute-start.22
  45.6 0.5 collective-permute-start.17
  46.1 0.1 collective-permute-start.19
  46.2 0.0 collective-permute-done.10
  46.2 0.4 collective-permute-start.9
  46.6 0.0 collective-permute-done.12
  46.6 0.1 collective-permute-start.14
  46.7 0.1 add_add_fusion
  46.8 1.2 %collective-permute-done.19 = f32[1,288,256]{2,1,0:T(8,128)S(1)} collective-permute-done((f32[1,288,256]{2,1,0:T(8,128)S(1)}, f32[1,288,256]{2,1,0:T(8,128)S(1)}, u32[]{:S(2)}, u32[]{:S(2)}) %collective-permute-start.19) | collective-permute-done | bytes 294944 | tf_op jit(solution)/shard_map/ppermute | solution.py:376
  48.0 3.0 %collective-permute-start.18 = (f32[1,144,256]{2,1,0:T(8,128)S(1)}, f32[1,144,256]{2,1,0:T(8,128)S(1)}, u32[]{:S(2)}, u32[]{:S(2)}) collective-permute-start(f32[1,144,256]{2,1,0:T(8,128)S(1)} %get-tuple-element.67), channel_id=1, source_target_pairs={{0,48},{8,56},{16,0},{24,8},{32,16},{40,24},{48,32},{56,40},{64,11... | collective-permute-start | bytes 442376 | tf_op jit(solution)/shard_map/ppermute | solution.py:376
  51.1 1.1 %collective-permute-start.20 = (f32[1,288,256]{2,1,0:T(8,128)S(1)}, f32[1,288,256]{2,1,0:T(8,128)S(1)}, u32[]{:S(2)}, u32[]{:S(2)}) collective-permute-start(f32[1,288,256]{2,1,0:T(8,128)S(1)} %add.54), channel_id=1, source_target_pairs={{0,64},{8,72},{16,80},{24,88},{32,96},{40,104},{48,112},{56,120},{... | collective-permute-start | bytes 884744 | tf_op jit(solution)/shard_map/ppermute | solution.py:376
  52.2 1.9 %tone_systems.15 = (f32[1,288,256]{2,1,0:T(8,128)S(1)}, f32[1,288,256]{2,1,0:T(8,128)S(1)}) custom-call(f32[16,32,1024]{2,1,0:T(8,128)S(1)} %pad_maximum_fusion.y_ref, f32[4,4,2,256,128]{4,3,2,1,0:T(8,128)S(1)} %get-tuple-element.34.lead, f32[8,4,2,256,128]{4,3,2,1,0:T(8,128)S(1)} %get-tuple-element.35.turn), custom_call_target="tpu_custom_call" | custom-call | tf_op jit(solution)/shard_map/tone_systems/pallas_call | solution.py:216
  54.1 0.1 collective-permute-start.8
  54.2 0.0 collective-permute-done.14
  54.3 1.1 %collective-permute-start.23 = (f32[1,288,256]{2,1,0:T(8,128)S(1)}, f32[1,288,256]{2,1,0:T(8,128)S(1)}, u32[]{:S(2)}, u32[]{:S(2)}) collective-permute-start(f32[1,288,256]{2,1,0:T(8,128)S(1)} %add.56), channel_id=1, source_target_pairs={{0,64},{8,72},{16,80},{24,88},{32,96},{40,104},{48,112},{56,120},{... | collective-permute-start | bytes 884744 | tf_op jit(solution)/shard_map/ppermute | solution.py:376
  55.4 1.1 %collective-permute-start.15 = (f32[1,288,256]{2,1,0:T(8,128)S(1)}, f32[1,288,256]{2,1,0:T(8,128)S(1)}, u32[]{:S(2)}, u32[]{:S(2)}) collective-permute-start(f32[1,288,256]{2,1,0:T(8,128)S(1)} %add.50), channel_id=1, source_target_pairs={{0,64},{8,72},{16,80},{24,88},{32,96},{40,104},{48,112},{56,120},{... | collective-permute-start | bytes 884744 | tf_op jit(solution)/shard_map/ppermute | solution.py:376
  56.5 0.0 collective-permute-done.18
  56.5 0.1 collective-permute-start.13
  56.7 4.4 %collective-permute-done.20 = f32[1,288,256]{2,1,0:T(8,128)S(1)} collective-permute-done((f32[1,288,256]{2,1,0:T(8,128)S(1)}, f32[1,288,256]{2,1,0:T(8,128)S(1)}, u32[]{:S(2)}, u32[]{:S(2)}) %collective-permute-start.20) | collective-permute-done | bytes 294944 | tf_op jit(solution)/shard_map/ppermute | solution.py:376
  61.1 0.8 collective-permute-start.21
  61.9 1.6 %collective-permute-done.13 = f32[1,144,256]{2,1,0:T(8,128)S(1)} collective-permute-done((f32[1,144,256]{2,1,0:T(8,128)S(1)}, f32[1,144,256]{2,1,0:T(8,128)S(1)}, u32[]{:S(2)}, u32[]{:S(2)}) %collective-permute-start.13) | collective-permute-done | bytes 147488 | tf_op jit(solution)/shard_map/ppermute | solution.py:376
  63.5 9.0 %collective-permute-done.15 = f32[1,288,256]{2,1,0:T(8,128)S(1)} collective-permute-done((f32[1,288,256]{2,1,0:T(8,128)S(1)}, f32[1,288,256]{2,1,0:T(8,128)S(1)}, u32[]{:S(2)}, u32[]{:S(2)}) %collective-permute-start.15) | collective-permute-done | bytes 294944 | tf_op jit(solution)/shard_map/ppermute | solution.py:376
  72.6 0.1 collective-permute-start.16
  72.7 0.0 collective-permute-done.8.refs_1_
  72.7 0.0 collective-permute-done.23.refs_4_
  72.7 9.1 %collective-permute-done.16.refs_2_ = f32[1,288,256]{2,1,0:T(8,128)S(1)} collective-permute-done((f32[1,288,256]{2,1,0:T(8,128)S(1)}, f32[1,288,256]{2,1,0:T(8,128)S(1)}, u32[]{:S(2)}, u32[]{:S(2)}) %collective-permute-start.16) | collective-permute-done | bytes 294944 | tf_op jit(solution)/shard_map/ppermute | solution.py:376
  81.8 5.5 %solved.1 = f32[32,256]{1,0:T(8,128)S(1)} custom-call(f32[1,288,256]{2,1,0:T(8,128)S(1)} %get-tuple-element.50.refs_0_, f32[1,288,256]{2,1,0:T(8,128)S(1)} %collective-permute-done.8.refs_1_, f32[1,288,256]{2,1,0:T(8,128)S(1)} %collective-permute-done.16.refs_2_, f32[1,288,256]{2,1,0:T(8,128)S(1)} %collective-permute-done.21.refs_3_, ...), custom_call_target="tpu_custom_call" | custom-call | tf_op jit(solution)/shard_map/solved/pallas_call | solution.py:340
  87.3 9.7 %all_to_all.5 = f32[8,32,256]{2,1,0:T(8,128)S(1)} all-to-all(f32[8,32,256]{2,1,0:T(8,128)S(1)} %broadcast_in_dim.2), channel_id=1, replica_groups={{0,16,32,48,64,80,96,112},{8,24,40,56,72,88,104,120},{1,17,33,49,65,81,..., dimensions={0} | all-to-all | bytes 524288 | tf_op jit(solution)/shard_map/all_to_all | solution.py:472
  97.0 0.0 collective-permute-start.24
  97.0 1.5 %collective-permute-done.24 = f32[8,32,256]{2,1,0:T(8,128)S(1)} collective-permute-done((f32[8,32,256]{2,1,0:T(8,128)S(1)}, f32[8,32,256]{2,1,0:T(8,128)S(1)}, u32[]{:S(2)}, u32[]{:S(2)}) %collective-permute-start.24) | collective-permute-done | bytes 262176 | tf_op jit(solution)/shard_map/ppermute | solution.py:376
  98.7 1.0 %copy.24 = f32[16,2,14,256]{3,0,2,1:T(8,128)} copy(f32[16,2,14,256]{3,2,1,0:T(8,128)S(1)} %bitcast.16) | data formatting | bytes 917504
  (30 shorter events, 0.6 us)
Async XLA Ops:
  1.0 16.8 %collective-permute-start.4 = (f32[16,32,128]{2,1,0:T(8,128)S(1)}, f32[16,32,128]{2,1,0:T(8,128)S(1)}, u32[]{:S(2)}, u32[]{:S(2)}) collective-permute-start(f32[16,32,128]{2,1,0:T(8,128)S(1)} %packed_tables.1.refs_0_), channel_id=1, source_target_pairs={{0,4},{1,5},{2,6},{3,7},{4,0},{5,1},{6,2},{7,3},{8,12},{9,13},{10,... | collective-permute-start | bytes 786440 | tf_op jit(solution)/shard_map/ppermute | solution.py:382
  5.0 9.0 %collective-permute-start = (f32[16,32,128]{2,1,0:T(8,128)S(1)}, f32[16,32,128]{2,1,0:T(8,128)S(1)}, u32[]{:S(2)}, u32[]{:S(2)}) collective-permute-start(f32[16,32,128]{2,1,0:T(8,128)S(1)} %packed_tables.1.refs_0_), channel_id=1, source_target_pairs={{0,1},{1,2},{2,3},{3,0},{4,5},{5,6},{6,7},{7,4},{8,9},{9,10},{10,1... | collective-permute-start | bytes 786440 | tf_op jit(solution)/shard_map/ppermute | solution.py:382
  6.5 7.9 %collective-permute-start.2 = (f32[16,32,128]{2,1,0:T(8,128)S(1)}, f32[16,32,128]{2,1,0:T(8,128)S(1)}, u32[]{:S(2)}, u32[]{:S(2)}) collective-permute-start(f32[16,32,128]{2,1,0:T(8,128)S(1)} %packed_tables.1.refs_0_), channel_id=1, source_target_pairs={{0,3},{1,0},{2,1},{3,2},{4,7},{5,4},{6,5},{7,6},{8,11},{9,8},{10,9... | collective-permute-start | bytes 786440 | tf_op jit(solution)/shard_map/ppermute | solution.py:382
  14.0 7.0 %collective-permute-start.1 = (f32[8,32,128]{2,1,0:T(8,128)S(1)}, f32[8,32,128]{2,1,0:T(8,128)S(1)}, u32[]{:S(2)}, u32[]{:S(2)}) collective-permute-start(f32[8,32,128]{2,1,0:T(8,128)S(1)} %slice.46), channel_id=1, source_target_pairs={{0,1},{1,2},{2,3},{3,0},{4,5},{5,6},{6,7},{7,4},{8,9},{9,10},{10,1... | collective-permute-start | bytes 393224 | tf_op jit(solution)/shard_map/ppermute | solution.py:382
  14.4 6.7 %collective-permute-start.3 = (f32[8,32,128]{2,1,0:T(8,128)S(1)}, f32[8,32,128]{2,1,0:T(8,128)S(1)}, u32[]{:S(2)}, u32[]{:S(2)}) collective-permute-start(f32[8,32,128]{2,1,0:T(8,128)S(1)} %slice.47), channel_id=1, source_target_pairs={{0,3},{1,0},{2,1},{3,2},{4,7},{5,4},{6,5},{7,6},{8,11},{9,8},{10,9... | collective-permute-start | bytes 393224 | tf_op jit(solution)/shard_map/ppermute | solution.py:382
  17.7 4.2 %copy-start = (s32[256,128]{1,0:T(8,128)S(1)}, s32[256,128]{1,0:T(8,128)}, u32[]{:S(2)}) copy-start(s32[256,128]{1,0:T(8,128)} %refs_4_.3) | copy-start | bytes 393220
  17.8 8.1 %collective-permute-start.5 = (f32[16,32,128]{2,1,0:T(8,128)S(1)}, f32[16,32,128]{2,1,0:T(8,128)S(1)}, u32[]{:S(2)}, u32[]{:S(2)}) collective-permute-start(f32[16,32,128]{2,1,0:T(8,128)S(1)} %collective-permute-done.4.refs_1_), channel_id=1, source_target_pairs={{0,1},{1,2},{2,3},{3,0},{4,5},{5,6},{6,7},{7,4},{8,9},{9,10},{10,1... | collective-permute-start | bytes 786440 | tf_op jit(solution)/shard_map/ppermute | solution.py:382
  17.8 8.1 %collective-permute-start.6 = (f32[16,32,128]{2,1,0:T(8,128)S(1)}, f32[16,32,128]{2,1,0:T(8,128)S(1)}, u32[]{:S(2)}, u32[]{:S(2)}) collective-permute-start(f32[16,32,128]{2,1,0:T(8,128)S(1)} %collective-permute-done.4.refs_1_), channel_id=1, source_target_pairs={{0,3},{1,0},{2,1},{3,2},{4,7},{5,4},{6,5},{7,6},{8,11},{9,8},{10,9... | collective-permute-start | bytes 786440 | tf_op jit(solution)/shard_map/ppermute | solution.py:382
  21.1 8.0 %collective-permute-start.7 = (f32[16,32,128]{2,1,0:T(8,128)S(1)}, f32[16,32,128]{2,1,0:T(8,128)S(1)}, u32[]{:S(2)}, u32[]{:S(2)}) collective-permute-start(f32[16,32,128]{2,1,0:T(8,128)S(1)} %constant_dynamic-update-slice_fusion.refs_0_), channel_id=1, source_target_pairs={{0,4},{1,5},{2,6},{3,7},{4,0},{5,1},{6,2},{7,3},{8,12},{9,13},{10,... | collective-permute-start | bytes 786440 | tf_op jit(solution)/shard_map/ppermute | solution.py:382
  32.4 2.4 %collective-permute-start.11 = (f32[1,288,256]{2,1,0:T(8,128)S(1)}, f32[1,288,256]{2,1,0:T(8,128)S(1)}, u32[]{:S(2)}, u32[]{:S(2)}) collective-permute-start(f32[1,288,256]{2,1,0:T(8,128)S(1)} %get-tuple-element.54), channel_id=1, source_target_pairs={{0,8},{8,0},{16,24},{24,16},{32,40},{40,32},{48,56},{56,48},{64,72... | collective-permute-start | bytes 884744 | tf_op jit(solution)/shard_map/ppermute | solution.py:376
  34.3 11.9 %collective-permute-start.10 = (f32[1,288,256]{2,1,0:T(8,128)S(1)}, f32[1,288,256]{2,1,0:T(8,128)S(1)}, u32[]{:S(2)}, u32[]{:S(2)}) collective-permute-start(f32[1,288,256]{2,1,0:T(8,128)S(1)} %get-tuple-element.53), channel_id=1, source_target_pairs={{0,8},{8,0},{16,24},{24,16},{32,40},{40,32},{48,56},{56,48},{64,72... | collective-permute-start | bytes 884744 | tf_op jit(solution)/shard_map/ppermute | solution.py:376
  34.8 11.8 %collective-permute-start.12 = (f32[1,288,256]{2,1,0:T(8,128)S(1)}, f32[1,288,256]{2,1,0:T(8,128)S(1)}, u32[]{:S(2)}, u32[]{:S(2)}) collective-permute-start(f32[1,288,256]{2,1,0:T(8,128)S(1)} %add.47), channel_id=1, source_target_pairs={{0,64},{8,72},{16,80},{24,88},{32,96},{40,104},{48,112},{56,120},{... | collective-permute-start | bytes 884744 | tf_op jit(solution)/shard_map/ppermute | solution.py:376
  45.6 5.5 %collective-permute-start.22 = (f32[1,288,256]{2,1,0:T(8,128)S(1)}, f32[1,288,256]{2,1,0:T(8,128)S(1)}, u32[]{:S(2)}, u32[]{:S(2)}) collective-permute-start(f32[1,288,256]{2,1,0:T(8,128)S(1)} %get-tuple-element.58), channel_id=1, source_target_pairs={{0,8},{8,0},{16,24},{24,16},{32,40},{40,32},{48,56},{56,48},{64,72... | collective-permute-start | bytes 884744 | tf_op jit(solution)/shard_map/ppermute | solution.py:376
  45.6 8.5 %collective-permute-start.17 = (f32[1,288,256]{2,1,0:T(8,128)S(1)}, f32[1,288,256]{2,1,0:T(8,128)S(1)}, u32[]{:S(2)}, u32[]{:S(2)}) collective-permute-start(f32[1,288,256]{2,1,0:T(8,128)S(1)} %get-tuple-element.56), channel_id=1, source_target_pairs={{0,8},{8,0},{16,24},{24,16},{32,40},{40,32},{48,56},{56,48},{64,72... | collective-permute-start | bytes 884744 | tf_op jit(solution)/shard_map/ppermute | solution.py:376
  46.1 1.9 %collective-permute-start.19 = (f32[1,288,256]{2,1,0:T(8,128)S(1)}, f32[1,288,256]{2,1,0:T(8,128)S(1)}, u32[]{:S(2)}, u32[]{:S(2)}) collective-permute-start(f32[1,288,256]{2,1,0:T(8,128)S(1)} %get-tuple-element.57), channel_id=1, source_target_pairs={{0,8},{8,0},{16,24},{24,16},{32,40},{40,32},{48,56},{56,48},{64,72... | collective-permute-start | bytes 884744 | tf_op jit(solution)/shard_map/ppermute | solution.py:376
  46.2 9.2 %collective-permute-start.9 = (f32[1,288,256]{2,1,0:T(8,128)S(1)}, f32[1,288,256]{2,1,0:T(8,128)S(1)}, u32[]{:S(2)}, u32[]{:S(2)}) collective-permute-start(f32[1,288,256]{2,1,0:T(8,128)S(1)} %get-tuple-element.52), channel_id=1, source_target_pairs={{0,8},{8,0},{16,24},{24,16},{32,40},{40,32},{48,56},{56,48},{64,72... | collective-permute-start | bytes 884744 | tf_op jit(solution)/shard_map/ppermute | solution.py:376
  46.6 7.6 %collective-permute-start.14 = (f32[1,288,256]{2,1,0:T(8,128)S(1)}, f32[1,288,256]{2,1,0:T(8,128)S(1)}, u32[]{:S(2)}, u32[]{:S(2)}) collective-permute-start(f32[1,288,256]{2,1,0:T(8,128)S(1)} %get-tuple-element.55), channel_id=1, source_target_pairs={{0,8},{8,0},{16,24},{24,16},{32,40},{40,32},{48,56},{56,48},{64,72... | collective-permute-start | bytes 884744 | tf_op jit(solution)/shard_map/ppermute | solution.py:376
  48.0 8.5 %collective-permute-start.18 = (f32[1,144,256]{2,1,0:T(8,128)S(1)}, f32[1,144,256]{2,1,0:T(8,128)S(1)}, u32[]{:S(2)}, u32[]{:S(2)}) collective-permute-start(f32[1,144,256]{2,1,0:T(8,128)S(1)} %get-tuple-element.67), channel_id=1, source_target_pairs={{0,48},{8,56},{16,0},{24,8},{32,16},{40,24},{48,32},{56,40},{64,11... | collective-permute-start | bytes 442376 | tf_op jit(solution)/shard_map/ppermute | solution.py:376
  51.1 10.0 %collective-permute-start.20 = (f32[1,288,256]{2,1,0:T(8,128)S(1)}, f32[1,288,256]{2,1,0:T(8,128)S(1)}, u32[]{:S(2)}, u32[]{:S(2)}) collective-permute-start(f32[1,288,256]{2,1,0:T(8,128)S(1)} %add.54), channel_id=1, source_target_pairs={{0,64},{8,72},{16,80},{24,88},{32,96},{40,104},{48,112},{56,120},{... | collective-permute-start | bytes 884744 | tf_op jit(solution)/shard_map/ppermute | solution.py:376
  54.0 27.8 %copy-start.1 = (f32[256]{0:T(256)S(1)}, f32[256]{0:T(256)}, u32[]{:S(2)}) copy-start(f32[256]{0:T(256)} %param.13) | copy-start | bytes 3076
  54.1 18.6 %collective-permute-start.8 = (f32[1,288,256]{2,1,0:T(8,128)S(1)}, f32[1,288,256]{2,1,0:T(8,128)S(1)}, u32[]{:S(2)}, u32[]{:S(2)}) collective-permute-start(f32[1,288,256]{2,1,0:T(8,128)S(1)} %get-tuple-element.51), channel_id=1, source_target_pairs={{0,8},{8,0},{16,24},{24,16},{32,40},{40,32},{48,56},{56,48},{64,72... | collective-permute-start | bytes 884744 | tf_op jit(solution)/shard_map/ppermute | solution.py:376
  54.3 18.5 %collective-permute-start.23 = (f32[1,288,256]{2,1,0:T(8,128)S(1)}, f32[1,288,256]{2,1,0:T(8,128)S(1)}, u32[]{:S(2)}, u32[]{:S(2)}) collective-permute-start(f32[1,288,256]{2,1,0:T(8,128)S(1)} %add.56), channel_id=1, source_target_pairs={{0,64},{8,72},{16,80},{24,88},{32,96},{40,104},{48,112},{56,120},{... | collective-permute-start | bytes 884744 | tf_op jit(solution)/shard_map/ppermute | solution.py:376
  55.4 17.2 %collective-permute-start.15 = (f32[1,288,256]{2,1,0:T(8,128)S(1)}, f32[1,288,256]{2,1,0:T(8,128)S(1)}, u32[]{:S(2)}, u32[]{:S(2)}) collective-permute-start(f32[1,288,256]{2,1,0:T(8,128)S(1)} %add.50), channel_id=1, source_target_pairs={{0,64},{8,72},{16,80},{24,88},{32,96},{40,104},{48,112},{56,120},{... | collective-permute-start | bytes 884744 | tf_op jit(solution)/shard_map/ppermute | solution.py:376
  56.5 7.0 %collective-permute-start.13 = (f32[1,144,256]{2,1,0:T(8,128)S(1)}, f32[1,144,256]{2,1,0:T(8,128)S(1)}, u32[]{:S(2)}, u32[]{:S(2)}) collective-permute-start(f32[1,144,256]{2,1,0:T(8,128)S(1)} %get-tuple-element.68), channel_id=1, source_target_pairs={{0,16},{8,24},{16,32},{24,40},{32,48},{40,56},{48,0},{56,8},{64,80... | collective-permute-start | bytes 442376 | tf_op jit(solution)/shard_map/ppermute | solution.py:376
  61.1 11.6 %collective-permute-start.21 = (f32[1,288,256]{2,1,0:T(8,128)S(1)}, f32[1,288,256]{2,1,0:T(8,128)S(1)}, u32[]{:S(2)}, u32[]{:S(2)}) collective-permute-start(f32[1,288,256]{2,1,0:T(8,128)S(1)} %maximum_add_fusion.1), channel_id=1, source_target_pairs={{0,48},{8,56},{16,0},{24,8},{32,16},{40,24},{48,32},{56,40},{64,11... | collective-permute-start | bytes 884744 | tf_op jit(solution)/shard_map/ppermute | solution.py:376
  72.6 9.2 %collective-permute-start.16 = (f32[1,288,256]{2,1,0:T(8,128)S(1)}, f32[1,288,256]{2,1,0:T(8,128)S(1)}, u32[]{:S(2)}, u32[]{:S(2)}) collective-permute-start(f32[1,288,256]{2,1,0:T(8,128)S(1)} %maximum_add_fusion), channel_id=1, source_target_pairs={{0,16},{8,24},{16,32},{24,40},{32,48},{40,56},{48,0},{56,8},{64,80... | collective-permute-start | bytes 884744 | tf_op jit(solution)/shard_map/ppermute | solution.py:376
  97.0 1.5 %collective-permute-start.24 = (f32[8,32,256]{2,1,0:T(8,128)S(1)}, f32[8,32,256]{2,1,0:T(8,128)S(1)}, u32[]{:S(2)}, u32[]{:S(2)}) collective-permute-start(f32[8,32,256]{2,1,0:T(8,128)S(1)} %all_to_all.5), channel_id=1, source_target_pairs={{0,8},{8,0},{16,24},{24,16},{32,40},{40,32},{48,56},{56,48},{64,72... | collective-permute-start | bytes 786440 | tf_op jit(solution)/shard_map/ppermute | solution.py:376
